TPU v7x, 32 devices: a whole 2x2x4 slice. The times are simulated.
32 devices in a mesh: dp: 2 (over x), ctx: 4 (over y, core), tp: 4 (over z).
Axes of the slice: x: 2, y: 2, z: 4, core: 2. Of those that a mesh axis runs over, the one named last changes fastest.
Arguments:
- inputs: bfloat16 [2, 2048, 768], P('dp', 'ctx'), may hold values from -6 to 6
- teacher_states: bfloat16 [2, 2048, 768], P('dp', 'ctx'), may hold values from -6 to 6
- lengths: int32 [2], P('dp'), may hold values from 512 to 2048, as said below
- prev_logits: bfloat16 [2, 12, 2048, 2048], P('dp', 'tp', 'ctx'), may hold values from -6 to 6
- w_query: bfloat16 [768, 768], P('dp', 'tp'), may hold values from -0.21875 to 0.21875
- w_key: bfloat16 [768, 768], P('dp', 'tp'), may hold values from -0.21875 to 0.21875
- w_value: bfloat16 [768, 768], P('dp', 'tp'), may hold values from -0.21875 to 0.21875
- w_output: bfloat16 [768, 768], P('tp', 'dp'), may hold values from -2.5 to 2.5
- w_inner: bfloat16 [768, 3072], P('dp', 'tp'), may hold values from -0.21875 to 0.21875
- w_outer: bfloat16 [3072, 768], P('tp', 'dp'), may hold values from -0.15625 to 0.15625
- bias_query: float32 [768], P('tp'), may hold values from -3 to 3
- bias_value: float32 [768], P('tp'), may hold values from -3 to 3
- bias_output: float32 [768], replicated, may hold values from -2 to 2
- bias_inner: float32 [3072], P('tp'), may hold values from -3 to 3
- bias_outer: float32 [768], replicated, may hold values from -2 to 2
- gain_first: float32 [768], replicated, may hold values from 0.5 to 1.5
- shift_first: float32 [768], replicated, may hold values from -2 to 2
- gain_second: float32 [768], replicated, may hold values from 0.5 to 1.5
- shift_second: float32 [768], replicated, may hold values from -2 to 2
Outputs:
- outputs: float32 [2, 2048, 768], P('dp', 'ctx')
- logits: bfloat16 [2, 12, 2048, 2048], P('dp', 'tp', 'ctx')
- loss_value: float32 [], replicated
- grad_inputs: float32 [2, 2048, 768], P('dp', 'ctx')
- grad_logits_in: bfloat16 [2, 12, 2048, 2048], P('dp', 'tp', 'ctx')
- grad_w_query: float32 [768, 768], P('dp', 'tp')
- grad_w_key: float32 [768, 768], P('dp', 'tp')
- grad_w_value: float32 [768, 768], P('dp', 'tp')
- grad_w_output: float32 [768, 768], P('tp', 'dp')
- grad_w_inner: float32 [768, 3072], P('dp', 'tp')
- grad_w_outer: float32 [3072, 768], P('tp', 'dp')
- grad_bias_query: float32 [768], P('tp')
- grad_bias_value: float32 [768], P('tp')
- grad_bias_output: float32 [768], replicated
- grad_bias_inner: float32 [3072], P('tp')
- grad_bias_outer: float32 [768], replicated
- grad_gain_first: float32 [768], replicated
- grad_shift_first: float32 [768], replicated
- grad_gain_second: float32 [768], replicated
- grad_shift_second: float32 [768], replicated
Inputs may be any that keep to these rules, and one draw needn't show every extreme that they name: lengths[s] counts the leading valid tokens of sequence s; in every draw some sequence is full, with 2048 valid tokens.
All inputs are finite; a program needn't handle non-finite values.
Results may differ from a plain program's by a relative error of at most 0.018.
Values may be sent and summed in bfloat16 or wider, within the bound.
No kernel may reach another device: no remote copies, remote signals or barrier semaphores. Data moves between devices by JAX's collectives and lax.ppermute only.
A program may use at most 128 MiB of HBM per device.

v0:
```python
from functools import partial
import math

import jax
import jax.numpy as jnp
from jax import lax
from jax.experimental import pallas as pl
from jax.experimental.pallas import tpu as pltpu
from jax.sharding import PartitionSpec as P

BLK = 256


EPS = 1e-06
MASKED = -1e30


def norm_forward(total, gain_vec, shift_vec):
    center = total - jnp.mean(total, -1, keepdims=True)
    spread = lax.rsqrt(jnp.mean(center * center, -1, keepdims=True) + EPS)
    normed = center * spread
    return (normed, spread, normed * gain_vec + shift_vec)


def norm_backward(gradient, normed, spread, gain_vec):
    scaled = gradient * gain_vec
    inner_term = (
        scaled
        - jnp.mean(scaled, -1, keepdims=True)
        - normed * jnp.mean(scaled * normed, -1, keepdims=True)
    )
    return (inner_term * spread, jnp.sum(gradient * normed, 0), jnp.sum(gradient, 0))


F32, BF16 = jnp.float32, jnp.bfloat16


def dot32(left, right, dims):
    return lax.dot_general(left, right, (dims, ((), ())), preferred_element_type=F32)


def shifted(block, axis, step):
    size = lax.axis_size(axis)
    return lax.ppermute(block, axis, [(i, (i + step) % size) for i in range(size)])


def flipped(block, axis, bit):
    size = lax.axis_size(axis)
    return lax.ppermute(block, axis, [(i, i ^ bit) for i in range(size)])


def tie(*values):
    return lax.optimization_barrier(values)


def own_first(array):
    if lax.axis_size("dp") != 2:
        return array
    half = array.shape[-1] // 2
    turned = jnp.concatenate([array[..., half:], array[..., :half]], -1)
    return jnp.where(lax.axis_index("dp") == 0, array, turned)


def gather_weight(shard, dim):
    if lax.axis_size("dp") != 2:
        return lax.all_gather(shard, "dp", axis=dim, tiled=True)
    return jnp.concatenate([shard, flipped(shard, "dp", 1)], dim)


def gather_late(shard, dim):
    if lax.axis_size("dp") != 2:
        return gather_weight(shard, dim), lambda moved: moved
    moved = flipped(shard, "dp", 1)
    return moved, lambda moved: jnp.concatenate([shard, moved], dim)


class WeightSum:
    def __init__(self, gradient, dim, far_first=False):
        self.bits = []
        bit = 1
        while bit < lax.axis_size("ctx"):
            self.bits.append(bit)
            bit *= 2
        if far_first:
            self.bits.reverse()
        if lax.axis_size("dp") == 2:
            kept, given = jnp.split(gradient, 2, dim)
            self.kept, self.moved = kept, flipped(given.astype(BF16), "dp", 1)
        else:
            low = gradient.astype(BF16)
            self.moved = lax.psum_scatter(low, "dp", scatter_dimension=dim, tiled=True)
            self.kept = jnp.zeros(self.moved.shape, F32)

    def step(self):
        low = (self.kept.astype(F32) + self.moved.astype(F32)).astype(BF16)
        self.kept, self.moved = low, flipped(low, "ctx", self.bits.pop(0))

    def total(self):
        while self.bits:
            self.step()
        return self.kept.astype(F32) + self.moved.astype(F32)


class VectorSum:
    def __init__(self, vector, axes):
        self.bits = []
        for axis in axes:
            bit = 1
            while bit < lax.axis_size(axis):
                self.bits.append((axis, bit))
                bit *= 2
        self.kept, self.moved = vector, flipped(vector, *self.bits.pop(0))

    def step(self):
        summed = self.kept + self.moved
        self.kept, self.moved = summed, flipped(summed, *self.bits.pop(0))

    def total(self):
        while self.bits:
            self.step()
        return self.kept + self.moved


def ctx_order():
    order, bit = [0], lax.axis_size("ctx") // 2
    while bit:
        order = order + [e ^ bit for e in order]
        bit //= 2
    return order


def gather_parts(block):
    held, bit = [block[None]], lax.axis_size("ctx") // 2
    while bit:
        sent = held[0] if len(held) == 1 else jnp.concatenate(held, 0)
        held.append(flipped(sent, "ctx", bit))
        bit //= 2
    return held


def scatter_parts(blocks):
    size, bit = lax.axis_size("ctx"), 1
    while bit < size:
        half = blocks.shape[0] // 2
        moved = flipped(blocks[half:].astype(BF16), "ctx", bit)
        blocks = blocks[:half].astype(F32) + moved.astype(F32)
        bit *= 2
    return blocks[0]


def rows_turn(block):
    size = lax.axis_size("tp")
    place = lax.axis_index("tp")
    blocks = block.reshape((size, block.shape[0] // size) + block.shape[1:])
    return jnp.concatenate(
        [
            lax.dynamic_index_in_dim(blocks, lax.rem(place - e + size, size), 0, False)
            for e in range(size)
        ],
        0,
    )


def rows_sum(total):
    size = lax.axis_size("tp")
    rows = total.shape[0] // size
    low = total.astype(BF16)
    moved = [shifted(low[e * rows : (e + 1) * rows], "tp", size - e) for e in range(1, size)]
    kept = total[:rows]
    for block in moved:
        kept = kept + block.astype(F32)
    return kept


def rows_moved(block):
    moved = []
    for e in range(1, lax.axis_size("tp")):
        moved.append(shifted(block, "tp", e))
    return moved


def rows_gather(block):
    return jnp.concatenate([block] + rows_moved(block), 0)


def rows_exchange(blocks):
    size = lax.axis_size("tp")
    return [blocks[0]] + [shifted(blocks[size - j], "tp", j) for j in range(1, size)]


TILE = 128


def blocks_of(refs):
    return [ref.at[b] for ref in refs for b in range(ref.shape[0])]


def attend_kernel(heads, parts, limits, starts, query, prior, *refs):
    kv, (logits, weights, context, inverse) = blocks_of(refs[:parts]), refs[parts:]
    limit = limits[pl.program_id(0)]
    rows, width = query.shape
    size = width // heads
    block = kv[0].shape[0]
    column = lax.broadcasted_iota(jnp.int32, (rows, block), 1)
    spans = [pl.ds(pl.multiple_of(starts[e], block), block) for e in range(len(kv))]
    for h in range(heads):
        own = slice(h * size, (h + 1) * size)
        masked = []
        for e, span in enumerate(spans):
            raw = lax.dot_general(
                query[:, own], kv[e][:, own], (((1,), (1,)), ((), ())), preferred_element_type=F32
            )
            score = prior[0, h, :, span].astype(F32) + raw
            logits[0, h, :, span] = score.astype(BF16)
            masked.append(jnp.where(column < limit - starts[e], score, MASKED))
        top = jnp.max(masked[0], -1, keepdims=True)
        for part in masked[1:]:
            top = jnp.maximum(top, jnp.max(part, -1, keepdims=True))
        count = jnp.zeros((rows, 1), F32)
        mixed = jnp.zeros((rows, size), F32)
        for e, span in enumerate(spans):
            exponent = jnp.exp(masked[e] - top)
            count = count + jnp.sum(exponent, -1, keepdims=True)
            low = exponent.astype(BF16)
            weights[h, :, span] = low
            mixed = mixed + jnp.dot(
                low, kv[e][:, width + h * size : width + (h + 1) * size], preferred_element_type=F32
            )
        scale = 1.0 / count
        context[:, own] = (mixed * scale).astype(BF16)
        inverse[:, own] = jnp.broadcast_to(scale, (rows, size))


def attend(query, kv, starts, prior, limits, heads):
    rows, width = query.shape
    keys = prior.shape[3]
    tile = lambda i, *scalars: (i, 0)
    whole = lambda i, *scalars: (0, 0, 0)
    cube = lambda i, *scalars: (0, i, 0)
    quad = lambda i, *scalars: (0, 0, i, 0)
    return pl.pallas_call(
        partial(attend_kernel, heads, len(kv)),
        grid_spec=pltpu.PrefetchScalarGridSpec(
            num_scalar_prefetch=2,
            grid=(rows // TILE,),
            in_specs=[pl.BlockSpec((TILE, width), tile), pl.BlockSpec((1, heads, TILE, keys), quad)]
            + [pl.BlockSpec(part.shape, whole) for part in kv],
            out_specs=[
                pl.BlockSpec((1, heads, TILE, keys), quad),
                pl.BlockSpec((heads, TILE, keys), cube),
                pl.BlockSpec((TILE, width), tile),
                pl.BlockSpec((TILE, width), tile),
            ],
        ),
        out_shape=[
            jax.ShapeDtypeStruct((1, heads, rows, keys), BF16),
            jax.ShapeDtypeStruct((heads, rows, keys), BF16),
            jax.ShapeDtypeStruct((rows, width), BF16),
            jax.ShapeDtypeStruct((rows, width), F32),
        ],
        cost_estimate=pl.CostEstimate(
            flops=4 * rows * keys * width, transcendentals=heads * rows * keys, bytes_accessed=6 * heads * rows * keys
        ),
        name="attend",
    )(limits, starts, query, prior, *kv)


def attend_back_kernel(heads, scale, parts, starts, weights, context, d_mixed, inverse, query, *refs):
    kv, (d_scores, d_query, d_kv, total) = blocks_of(refs[:parts]), refs[parts:]
    width = context.shape[1]
    size = width // heads
    block = kv[0].shape[0]
    step = pl.program_id(0)
    spans = [pl.ds(pl.multiple_of(starts[e], block), block) for e in range(len(kv))]

    @pl.when(step == 0)
    def _():
        total[...] = jnp.zeros_like(total)

    scaled = d_mixed[...].astype(F32) * inverse[...]
    product = scaled * context[...].astype(F32)
    d_context = scaled.astype(BF16)
    for h in range(heads):
        own = slice(h * size, (h + 1) * size)
        other = slice(width + h * size, width + (h + 1) * size)
        mean = jnp.sum(product[:, own], -1, keepdims=True)
        d_head = jnp.zeros((context.shape[0], size), F32)
        for e, span in enumerate(spans):
            d_weights = lax.dot_general(
                d_context[:, own], kv[e][:, other], (((1,), (1,)), ((), ())), preferred_element_type=F32
            )
            low = weights[h, :, span]
            change = (low.astype(F32) * (d_weights - mean)).astype(BF16)
            d_scores[0, h, :, span] = change
            d_head = d_head + jnp.dot(change, kv[e][:, own], preferred_element_type=F32)
            total[e, own, :] += lax.dot_general(
                query[:, own], change, (((0,), (0,)), ((), ())), preferred_element_type=F32
            )
            total[e, other, :] += lax.dot_general(
                d_context[:, own], low, (((0,), (0,)), ((), ())), preferred_element_type=F32
            )
        d_query[:, own] = scale * d_head

    @pl.when(step == pl.num_programs(0) - 1)
    def _():
        d_kv[...] = total[...].astype(BF16)


def attend_back(weights, kv, starts, context, d_mixed, inverse, query, scale):
    heads, rows, keys = weights.shape
    width = context.shape[1]
    block = kv[0].shape[1]
    tile = lambda i, *scalars: (i, 0)
    whole = lambda i, *scalars: (0, 0, 0)
    shape = (keys // block, 2 * width, block)
    return pl.pallas_call(
        partial(attend_back_kernel, heads, scale, len(kv)),
        grid_spec=pltpu.PrefetchScalarGridSpec(
            num_scalar_prefetch=1,
            grid=(rows // TILE,),
            in_specs=[pl.BlockSpec((heads, TILE, keys), lambda i, *scalars: (0, i, 0))]
            + [pl.BlockSpec((TILE, width), tile)] * 4
            + [pl.BlockSpec(part.shape, whole) for part in kv],
            out_specs=[
                pl.BlockSpec((1, heads, TILE, keys), lambda i, *scalars: (0, 0, i, 0)),
                pl.BlockSpec((TILE, width), tile),
                pl.BlockSpec(shape, whole),
            ],
            scratch_shapes=[pltpu.VMEM(shape, F32)],
        ),
        out_shape=[
            jax.ShapeDtypeStruct((1, heads, rows, keys), BF16),
            jax.ShapeDtypeStruct((rows, width), F32),
            jax.ShapeDtypeStruct(shape, BF16),
        ],
        cost_estimate=pl.CostEstimate(
            flops=10 * rows * keys * width, transcendentals=0, bytes_accessed=6 * heads * rows * keys
        ),
        name="attend_back",
    )(starts, weights, context, d_mixed, inverse, query, *kv)


def pack_kernel(lead, place, squared, *refs):
    vectors, placed, out = refs[:-2], refs[-2], refs[-1]
    out[...] = jnp.zeros_like(out)
    for i, vector in enumerate(vectors):
        out[i : i + 1, :] = vector[...]
    out[len(vectors) : len(vectors) + 1, :] = jnp.broadcast_to(squared[...], (1, out.shape[1]))
    for p in range((out.shape[0] - lead) // placed.shape[0]):

        @pl.when(place[0] == p)
        def _():
            first = lead + p * placed.shape[0]
            out[first : first + placed.shape[0], :] = placed[...]


def pack(vectors, squared, placed, place, places):
    width = vectors[0].shape[0]
    vmem = pl.BlockSpec(memory_space=pltpu.VMEM)
    rows = placed.reshape(-1, width)
    return pl.pallas_call(
        partial(pack_kernel, 8),
        in_specs=[pl.BlockSpec(memory_space=pltpu.SMEM)] + [vmem] * (len(vectors) + 2),
        out_specs=vmem,
        out_shape=jax.ShapeDtypeStruct((8 + places * rows.shape[0], width), F32),
        name="pack",
    )(place.reshape(1), squared.reshape(1, 1), *[v.reshape(1, width) for v in vectors], rows)


def per_device(
    inputs,
    teacher_states,
    lengths,
    prev_logits,
    w_query,
    w_key,
    w_value,
    w_output,
    w_inner,
    w_outer,
    bias_query,
    bias_value,
    bias_output,
    bias_inner,
    bias_outer,
    gain_first,
    shift_first,
    gain_second,
    shift_second,
):
    tokens = inputs[0]
    row_count, model_width = tokens.shape
    heads_local = prev_logits.shape[1]
    width_local = w_query.shape[1]
    score_scale = 1.0 / math.sqrt(width_local // heads_local)
    seq_length = lengths[0]
    ctx_place, tp_place = lax.axis_index("ctx"), lax.axis_index("tp")
    tp_size = lax.axis_size("tp")
    part_rows = row_count // tp_size

    qkv_shard = jnp.concatenate([w_query.T, w_key.T, w_value.T], 0)
    full_qkv = gather_weight(qkv_shard, 1)
    output_half = jnp.concatenate([w_output] + rows_moved(w_output), 0)
    row_pos = ctx_place * row_count + jnp.arange(row_count, dtype=jnp.int32)
    limits = jnp.minimum((row_pos[::TILE] // BLK + 1) * BLK, seq_length)

    def own_rows(array):
        return lax.dynamic_slice_in_dim(array, tp_place * part_rows, part_rows, 0)

    tokens_first = own_first(tokens)
    projected = dot32(tokens_first, full_qkv, ((1,), (1,)))
    query_local = (projected[:, :width_local] + bias_query).astype(BF16)
    kv_local = jnp.concatenate(
        [projected[:, width_local : 2 * width_local], projected[:, 2 * width_local :] + bias_value], 1
    ).astype(BF16)
    kv_local, output_half = tie(kv_local, output_half)
    output_moved, join_output = gather_late(output_half, 1)
    kv_all = gather_parts(kv_local)
    starts = (ctx_place ^ jnp.asarray(ctx_order(), jnp.int32)) * row_count
    all_count = VectorSum(seq_length.astype(F32), ("dp",)).total()

    query_scaled = (query_local.astype(F32) * score_scale).astype(BF16)
    logits, weights, context, inverse = attend(
        query_scaled, kv_all, starts, prev_logits, limits, heads_local
    )
    context_turned = rows_turn(context)
    context_turned, output_moved, w_inner, w_outer = tie(
        context_turned, output_moved, w_inner, w_outer
    )
    full_output = join_output(output_moved)
    inner_moved, join_inner = gather_late(w_inner, 0)
    outer_moved, join_outer = gather_late(w_outer, 1)
    context_mine = jnp.concatenate(rows_exchange(jnp.split(context_turned, tp_size, 0)), 1)
    attended = own_first(dot32(context_mine, full_output, ((1,), (0,))))
    first_sum = own_rows(tokens).astype(F32) + attended + bias_output
    normed_first, spread_first, hidden = norm_forward(first_sum, gain_first, shift_first)
    hidden_first = own_first(hidden.astype(BF16))
    hidden_moved = rows_moved(hidden_first)
    full_inner, full_outer = join_inner(inner_moved), join_outer(outer_moved)
    hidden_low = jnp.concatenate([hidden_first] + hidden_moved, 0)
    pre_act = dot32(hidden_low, full_inner, ((1,), (0,))) + bias_inner
    act_low = jax.nn.gelu(pre_act, approximate=False).astype(BF16)
    fed = own_first(rows_sum(dot32(act_low, full_outer, ((1,), (0,)))))
    second_sum = hidden + fed + bias_outer
    normed_second, spread_second, result = norm_forward(second_sum, gain_second, shift_second)
    valid_rows = (own_rows(row_pos) < seq_length).astype(F32)
    deviation = result - own_rows(teacher_states[0]).astype(F32)
    local_squared = jnp.sum(valid_rows[:, None] * deviation * deviation)
    token_total = row_count * lax.axis_size("ctx") * lax.axis_size("dp")
    d_out = 2.0 * token_total / all_count * valid_rows[:, None] * deviation
    d_second, grad_gain_second, grad_shift_second = norm_backward(
        d_out, normed_second, spread_second, gain_second
    )
    grad_bias_outer = jnp.sum(d_second, 0)
    d_second_low = rows_gather(own_first(d_second.astype(BF16)))
    d_act = dot32(d_second_low, full_outer, ((1,), (1,)))
    gelu_back = jax.vjp(partial(jax.nn.gelu, approximate=False), pre_act)[1]
    d_pre = gelu_back(d_act)[0]
    grad_bias_inner = jnp.sum(d_pre, 0)
    d_pre_low = d_pre.astype(BF16)
    hidden_part = rows_sum(dot32(d_pre_low, full_inner, ((1,), (1,))))
    outer_sum = WeightSum(dot32(act_low, d_second_low, ((0,), (0,))), 1)
    inner_sum = WeightSum(dot32(hidden_low, d_pre_low, ((0,), (0,))), 0)
    d_hidden = d_second + own_first(hidden_part)
    d_first, grad_gain_first, grad_shift_first = norm_backward(
        d_hidden, normed_first, spread_first, gain_first
    )
    grad_bias_output = jnp.sum(d_first, 0)
    d_first, outer_sum.moved = tie(d_first, outer_sum.moved)
    outer_sum.step()
    d_first_low = own_first(d_first.astype(BF16))
    d_context_mine = dot32(d_first_low, full_output, ((1,), (1,))).astype(BF16)
    d_context = jnp.concatenate(rows_exchange(jnp.split(d_context_mine, tp_size, 1)), 0)
    d_context = rows_turn(d_context)

    early_sum = VectorSum(
        pack(
            [
                grad_bias_output,
                grad_bias_outer,
                grad_gain_first,
                grad_shift_first,
                grad_gain_second,
                grad_shift_second,
            ],
            local_squared,
            grad_bias_inner,
            tp_place,
            tp_size,
        ),
        ("dp", "ctx", "tp"),
    )
    d_context, outer_sum.moved, inner_sum.moved, early_sum.moved = tie(
        d_context, outer_sum.moved, inner_sum.moved, early_sum.moved
    )
    outer_sum.step()
    inner_sum.step()
    early_sum.step()
    result_mine, d_first_low, _ = tie(result.astype(BF16), d_first_low, d_context)
    d_first_moved = rows_moved(d_first_low)
    result_moved = rows_moved(result_mine)
    d_scores, d_query, d_kv_parts = attend_back(
        weights, kv_all, starts, context, d_context, inverse, query_scaled, score_scale
    )
    d_kv_parts, outer_sum.moved, inner_sum.moved, early_sum.moved = tie(
        d_kv_parts, outer_sum.moved, inner_sum.moved, early_sum.moved
    )
    early_sum.step()
    d_kv = scatter_parts(d_kv_parts)
    d_query_low = d_query.astype(BF16)
    d_kv_low, inner_sum.moved, early_sum.moved = tie(
        d_kv.astype(BF16), inner_sum.moved, early_sum.moved
    )
    inner_sum.step()
    early_sum.step()
    d_kv_low, *d_first_moved = tie(d_kv_low, *d_first_moved)
    d_first_all = jnp.concatenate([d_first_low] + d_first_moved, 0)
    output_sum = WeightSum(dot32(context_turned, d_first_all, ((0,), (0,))), 1, True)
    d_qkv_low = jnp.concatenate([d_query_low, d_kv_low.T], 1)
    tokens_part = rows_sum(dot32(rows_turn(d_qkv_low), full_qkv, ((1,), (0,))))
    qkv_sum = WeightSum(dot32(d_qkv_low, tokens_first, ((0,), (0,))), 1, True)
    late_sum = VectorSum(
        jnp.concatenate([jnp.sum(d_query, 0), jnp.sum(d_kv[width_local:], 1)]), ("dp", "ctx")
    )
    grad_mine = (d_first + own_first(tokens_part)).astype(BF16)
    sums = (inner_sum, output_sum, early_sum, qkv_sum, late_sum)
    grad_mine, *moved = tie(grad_mine, *[one.moved for one in sums])
    for one, value in zip(sums, moved):
        one.moved = value
    for one in (output_sum, early_sum, qkv_sum, late_sum):
        one.step()
    grad_mine, *result_moved = tie(grad_mine, *result_moved)
    result_all = rows_turn(jnp.concatenate([result_mine] + result_moved, 0)).astype(F32)
    grad_inputs = rows_turn(rows_gather(grad_mine)).astype(F32)
    output_shard = output_sum.total()
    shard_qkv = qkv_sum.total()
    early = early_sum.total()
    loss_value = early[6, 0] / (all_count * model_width)
    inner_rows = grad_bias_inner.shape[0] // model_width
    sum_bias_inner = lax.dynamic_slice_in_dim(early, 8 + tp_place * inner_rows, inner_rows, 0).reshape(-1)
    late = late_sum.total()
    return (
        result_all[None],
        logits,
        loss_value,
        grad_inputs[None],
        d_scores,
        shard_qkv[:width_local].T,
        shard_qkv[width_local : 2 * width_local].T,
        shard_qkv[2 * width_local :].T,
        output_shard,
        inner_sum.total(),
        outer_sum.total(),
        late[:width_local],
        late[width_local:],
        early[0],
        sum_bias_inner,
        early[1],
        early[2],
        early[3],
        early[4],
        early[5],
    )


def solution(mesh):
    placed = (
        P("dp", "ctx", None),
        P("dp", "ctx", None),
        P("dp"),
        P("dp", "tp", "ctx", None),
        P("dp", "tp"),
        P("dp", "tp"),
        P("dp", "tp"),
        P("tp", "dp"),
        P("dp", "tp"),
        P("tp", "dp"),
        P("tp"),
        P("tp"),
        P(),
        P("tp"),
        P(),
        P(),
        P(),
        P(),
        P(),
    )
    return jax.shard_map(
        per_device,
        mesh=mesh,
        in_specs=placed,
        out_specs=(
            P("dp", "ctx", None),
            P("dp", "tp", "ctx", None),
            P(),
            P("dp", "ctx", None),
            P("dp", "tp", "ctx", None),
            P("dp", "tp"),
            P("dp", "tp"),
            P("dp", "tp"),
            P("tp", "dp"),
            P("dp", "tp"),
            P("tp", "dp"),
            P("tp"),
            P("tp"),
            P(),
            P("tp"),
            P(),
            P(),
            P(),
            P(),
            P(),
        ),
        check_vma=False,
    )
```

profile of v0, /device:TPU:0, one launch (start us, length us, event | category | flops | bytes accessed | tf_op | source)
XLA Modules:
  0.0 329.7 jit_solution(13229347661587674659)
XLA Ops:
  1.9 3.0 collective-permute-start
  4.9 1.6 collective-permute-start.1
  6.5 2.6 collective-permute-start.2
  11.6 2.1 collective-permute-done.1
  13.7 5.0 %collective-permute-done.2 = bf16[192,384]{1,0:T(8,128)(2,1)S(1)} collective-permute-done((bf16[192,384]{1,0:T(8,128)(2,1)}, bf16[192,384]{1,0:T(8,128)(2,1)S(1)}, u32[]{:S(2)}, u32[]{:S(2)}) %collective-permute-start.2) | collective-permute-done | bytes 147488 | tf_op jit(solution)/shard_map/ppermute | solution.py:44
  18.8 1.7 fusion.54
  21.9 1.6 collective-permute-start.4
  24.2 1.9 collective-permute-start.18
  26.2 6.8 %collective-permute-done.4.refs_1_ = bf16[1,512,384]{2,1,0:T(8,128)(2,1)S(1)} collective-permute-done((bf16[1,512,384]{2,1,0:T(8,128)(2,1)S(1)}, bf16[1,512,384]{2,1,0:T(8,128)(2,1)S(1)}, u32[]{:S(2)}, u32[]{:S(2)}) %collective-permute-start.4) | collective-permute-done | bytes 393248 | tf_op jit(solution)/shard_map/ppermute | solution.py:49
  35.6 2.0 copy.60
  37.6 1.8 multiply_convert_fusion.1.query
  40.3 13.1 %attend.1 = (bf16[1,3,512,2048]{3,2,1,0:T(8,128)(2,1)}, bf16[3,512,2048]{2,1,0:T(8,128)(2,1)}, bf16[512,192]{1,0:T(8,128)(2,1)}, f32[512,192]{1,0:T(8,128)}) custom-call(s32[4]{0:T(128)} %multiply_minimum_fusion.limits, s32[4]{0:T(128)} %xor_multiply_fusion.starts, bf16[512,192]{1,0:T(8,128)(2,1)} %multiply_convert_fusion.1.query, ...), custom_call_target="tpu_custom_call" | custom-call | flops 805306368 | bytes 18874368 | tf_op jit(solution)/shard_map/attend/pallas_call | solution.py:241
  55.7 1.6 collective-permute-start.14
  57.3 3.8 %collective-permute-start.7 = (bf16[128,192]{1,0:T(8,128)(2,1)S(1)}, bf16[128,192]{1,0:T(8,128)(2,1)S(1)}, u32[]{:S(2)}, u32[]{:S(2)}) collective-permute-start(bf16[128,192]{1,0:T(8,128)(2,1)S(1)} %get-tuple-element.177), channel_id=1, source_target_pairs={{0,1},{1,2},{2,3},{3,0},{4,5},{5,6},{6,7},{7,4},{8,9},{9,10},{10,1... | collective-permute-start | bytes 147464 | tf_op jit(solution)/shard_map/ppermute | solution.py:44
  61.3 2.1 collective-permute-start.9
  65.3 1.8 collective-permute-done.8
  69.3 1.7 collective-permute-start.10
  71.0 1.6 collective-permute-start.11
  72.6 2.8 collective-permute-start.12
  75.5 8.3 %collective-permute-done.13 = bf16[384,768]{1,0:T(8,128)(2,1)S(1)} collective-permute-done((bf16[384,768]{1,0:T(8,128)(2,1)S(1)}, bf16[384,768]{1,0:T(8,128)(2,1)S(1)}, u32[]{:S(2)}, u32[]{:S(2)}) %collective-permute-start.13) | collective-permute-done | bytes 589856 | tf_op jit(solution)/shard_map/ppermute | solution.py:49
  83.9 2.0 collective-permute-done.11
  85.9 5.6 %multiply_convert_fusion = (bf16[512,768]{1,0:T(8,128)(2,1)S(1)}, f32[512,768]{1,0:T(8,128)}, f32[512,768]{1,0:T(8,128)}) fusion(f32[768]{0:T(1024)S(1)} %copy-done.55, bf16[768,768]{1,0:T(8,128)(2,1)S(1)} %constant_dynamic-update-slice_fusion.2, bf16[128,768]{1,0:T(8,128)(2,1)S(1)} %collective-permute-done.12, ...), kind=kOutput, calls=%fused_computation.4 | convolution fusion | flops 633077760 | bytes 5901312 | tf_op jit(solution)/shard_map/dot_general | solution.py:39
  91.6 1.9 fusion.94
  94.3 4.9 %collective-permute-start.15 = (bf16[128,768]{1,0:T(8,128)(2,1)}, bf16[128,768]{1,0:T(8,128)(2,1)}, u32[]{:S(2)}, u32[]{:S(2)}) collective-permute-start(bf16[128,768]{1,0:T(8,128)(2,1)} %get-tuple-element.152), channel_id=1, source_target_pairs={{0,3},{1,0},{2,1},{3,2},{4,7},{5,4},{6,5},{7,6},{8,11},{9,8},{10,9... | collective-permute-start | bytes 589832 | tf_op jit(solution)/shard_map/ppermute | solution.py:44
  101.1 3.7 %collective-permute-done.15 = bf16[128,768]{1,0:T(8,128)(2,1)} collective-permute-done((bf16[128,768]{1,0:T(8,128)(2,1)}, bf16[128,768]{1,0:T(8,128)(2,1)}, u32[]{:S(2)}, u32[]{:S(2)}) %collective-permute-start.15) | collective-permute-done | bytes 196640 | tf_op jit(solution)/shard_map/ppermute | solution.py:44
  104.8 13.3 %collective-permute-done.16 = bf16[128,768]{1,0:T(8,128)(2,1)} collective-permute-done((bf16[128,768]{1,0:T(8,128)(2,1)S(1)}, bf16[128,768]{1,0:T(8,128)(2,1)}, u32[]{:S(2)}, u32[]{:S(2)}) %collective-permute-start.16) | collective-permute-done | bytes 196640 | tf_op jit(solution)/shard_map/ppermute | solution.py:44
  123.2 3.2 collective-permute-start.21
  126.4 5.8 %collective-permute-done.19 = bf16[128,768]{1,0:T(8,128)(2,1)S(1)} collective-permute-done((bf16[128,768]{1,0:T(8,128)(2,1)S(1)}, bf16[128,768]{1,0:T(8,128)(2,1)S(1)}, u32[]{:S(2)}, u32[]{:S(2)}) %collective-permute-start.19) | collective-permute-done | bytes 196640 | tf_op jit(solution)/shard_map/ppermute | solution.py:44
  132.3 6.7 %collective-permute-done.20 = bf16[128,768]{1,0:T(8,128)(2,1)S(1)} collective-permute-done((bf16[128,768]{1,0:T(8,128)(2,1)S(1)}, bf16[128,768]{1,0:T(8,128)(2,1)S(1)}, u32[]{:S(2)}, u32[]{:S(2)}) %collective-permute-start.20) | collective-permute-done | bytes 196640 | tf_op jit(solution)/shard_map/ppermute | solution.py:44
  141.1 4.2 %collective-permute-start.22 = (bf16[128,768]{1,0:T(8,128)(2,1)S(1)}, bf16[128,768]{1,0:T(8,128)(2,1)S(1)}, u32[]{:S(2)}, u32[]{:S(2)}) collective-permute-start(bf16[128,768]{1,0:T(8,128)(2,1)S(1)} %get-tuple-element.149), channel_id=1, source_target_pairs={{0,3},{1,0},{2,1},{3,2},{4,7},{5,4},{6,5},{7,6},{8,11},{9,8},{10,9... | collective-permute-start | bytes 589832 | tf_op jit(solution)/shard_map/ppermute | solution.py:44
  149.7 1.6 collective-permute-start.25
  151.3 11.8 %collective-permute-done.23 = bf16[128,768]{1,0:T(8,128)(2,1)S(1)} collective-permute-done((bf16[128,768]{1,0:T(8,128)(2,1)S(1)}, bf16[128,768]{1,0:T(8,128)(2,1)S(1)}, u32[]{:S(2)}, u32[]{:S(2)}) %collective-permute-start.23) | collective-permute-done | bytes 196640 | tf_op jit(solution)/shard_map/ppermute | solution.py:44
  163.6 11.3 %collective-permute-done.25 = bf16[768,384]{1,0:T(8,128)(2,1)S(1)} collective-permute-done((bf16[768,384]{1,0:T(8,128)(2,1)S(1)}, bf16[768,384]{1,0:T(8,128)(2,1)S(1)}, u32[]{:S(2)}, u32[]{:S(2)}) %collective-permute-start.25) | collective-permute-done | bytes 589856 | tf_op jit(solution)/shard_map/ppermute | solution.py:49
  176.0 1.6 collective-permute-start.26
  177.6 2.5 collective-permute-start.27
  184.6 2.1 pack.1
  188.1 2.9 collective-permute-done.31
  191.8 1.5 fusion.6
  194.6 1.5 collective-permute-start.32
  196.4 17.7 %attend_back.1 = (bf16[1,3,512,2048]{3,2,1,0:T(8,128)(2,1)}, f32[512,192]{1,0:T(8,128)}, bf16[4,384,512]{2,1,0:T(8,128)(2,1)}) custom-call(s32[4]{0:T(128)} %xor_multiply_fusion.starts, bf16[3,512,2048]{2,1,0:T(8,128)(2,1)} %get-tuple-element.73.weights, bf16[512,192]{1,0:T(8,128)(2,1)} %get-tuple-element.63.context, ...), custom_call_target="tpu_custom_call" | custom-call | flops 2013265920 | bytes 18874368 | tf_op jit(solution)/shard_map/attend_back/pallas_call | solution.py:316
  217.4 2.0 collective-permute-done.35
  221.0 1.7 collective-permute-start.38
  223.1 2.2 collective-permute-start.40
  225.3 1.8 copy.55
  228.3 1.5 collective-permute-start.37
  229.8 2.2 convert_add_fusion.1
  233.7 4.8 %collective-permute-done.39 = bf16[128,768]{1,0:T(8,128)(2,1)} collective-permute-done((bf16[128,768]{1,0:T(8,128)(2,1)}, bf16[128,768]{1,0:T(8,128)(2,1)}, u32[]{:S(2)}, u32[]{:S(2)}) %collective-permute-start.39) | collective-permute-done | bytes 196640 | tf_op jit(solution)/shard_map/ppermute | solution.py:44
  240.0 1.5 collective-permute-start.47
  241.6 1.5 fusion.9
  246.1 1.8 fusion.97
  248.0 4.6 %collective-permute-start.41 = (bf16[128,768]{1,0:T(8,128)(2,1)S(1)}, bf16[128,768]{1,0:T(8,128)(2,1)S(1)}, u32[]{:S(2)}, u32[]{:S(2)}) collective-permute-start(bf16[128,768]{1,0:T(8,128)(2,1)S(1)} %get-tuple-element.146), channel_id=1, source_target_pairs={{0,3},{1,0},{2,1},{3,2},{4,7},{5,4},{6,5},{7,6},{8,11},{9,8},{10,9... | collective-permute-start | bytes 589832 | tf_op jit(solution)/shard_map/ppermute | solution.py:44
  252.7 1.5 collective-permute-start.42
  254.4 3.6 %collective-permute-done.41 = bf16[128,768]{1,0:T(8,128)(2,1)S(1)} collective-permute-done((bf16[128,768]{1,0:T(8,128)(2,1)S(1)}, bf16[128,768]{1,0:T(8,128)(2,1)S(1)}, u32[]{:S(2)}, u32[]{:S(2)}) %collective-permute-start.41) | collective-permute-done | bytes 196640 | tf_op jit(solution)/shard_map/ppermute | solution.py:44
  258.0 11.0 %collective-permute-start.46 = (f32[12,768]{1,0:T(8,128)S(1)}, f32[12,768]{1,0:T(8,128)S(1)}, u32[]{:S(2)}, u32[]{:S(2)}) collective-permute-start(f32[12,768]{1,0:T(8,128)S(1)} %add.318), channel_id=1, source_target_pairs={{0,1},{1,0},{2,3},{3,2},{4,5},{5,4},{6,7},{7,6},{8,9},{9,8},{10,11... | collective-permute-start | bytes 110600 | tf_op jit(solution)/shard_map/ppermute | solution.py:49
  269.0 2.2 collective-permute-done.42
  271.7 1.6 collective-permute-start.44
  273.6 2.7 collective-permute-done.45
  277.5 7.7 %collective-permute-done.44 = bf16[384,768]{1,0:T(8,128)(2,1)S(1)} collective-permute-done((bf16[384,768]{1,0:T(8,128)(2,1)S(1)}, bf16[384,768]{1,0:T(8,128)(2,1)S(1)}, u32[]{:S(2)}, u32[]{:S(2)}) %collective-permute-start.44) | collective-permute-done | bytes 589856 | tf_op jit(solution)/shard_map/ppermute | solution.py:49
  285.2 3.5 %collective-permute-done.50 = bf16[128,768]{1,0:T(8,128)(2,1)S(1)} collective-permute-done((bf16[128,768]{1,0:T(8,128)(2,1)S(1)}, bf16[128,768]{1,0:T(8,128)(2,1)S(1)}, u32[]{:S(2)}, u32[]{:S(2)}) %collective-permute-start.50) | collective-permute-done | bytes 196640 | tf_op jit(solution)/shard_map/ppermute | solution.py:44
  288.7 3.9 %collective-permute-start.53 = (bf16[128,768]{1,0:T(8,128)(2,1)S(1)}, bf16[128,768]{1,0:T(8,128)(2,1)S(1)}, u32[]{:S(2)}, u32[]{:S(2)}) collective-permute-start(bf16[128,768]{1,0:T(8,128)(2,1)S(1)} %fusion.38), channel_id=1, source_target_pairs={{0,1},{1,2},{2,3},{3,0},{4,5},{5,6},{6,7},{7,4},{8,9},{9,10},{10,1... | collective-permute-start | bytes 589832 | tf_op jit(solution)/shard_map/ppermute | solution.py:44
  296.8 1.7 collective-permute-start.61
  298.5 4.0 %collective-permute-done.61 = f32[384]{0:T(512)S(1)} collective-permute-done((f32[384]{0:T(512)S(1)}, f32[384]{0:T(512)S(1)}, u32[]{:S(2)}, u32[]{:S(2)}) %collective-permute-start.61) | collective-permute-done | bytes 1568 | tf_op jit(solution)/shard_map/ppermute | solution.py:49
  303.8 8.3 %collective-permute-done.52 = f32[12,768]{1,0:T(8,128)S(1)} collective-permute-done((f32[12,768]{1,0:T(8,128)S(1)}, f32[12,768]{1,0:T(8,128)S(1)}, u32[]{:S(2)}, u32[]{:S(2)}) %collective-permute-start.52) | collective-permute-done | bytes 36896 | tf_op jit(solution)/shard_map/ppermute | solution.py:49
  314.8 9.3 %collective-permute-done.56 = bf16[576,384]{1,0:T(8,128)(2,1)S(1)} collective-permute-done((bf16[576,384]{1,0:T(8,128)(2,1)S(1)}, bf16[576,384]{1,0:T(8,128)(2,1)S(1)}, u32[]{:S(2)}, u32[]{:S(2)}) %collective-permute-start.56) | collective-permute-done | bytes 442400 | tf_op jit(solution)/shard_map/ppermute | solution.py:49
  (315 shorter events, 65.2 us)
Async XLA Ops:
  1.9 16.9 %collective-permute-start = (bf16[576,384]{1,0:T(8,128)(2,1)S(1)}, bf16[576,384]{1,0:T(8,128)(2,1)}, u32[]{:S(2)}, u32[]{:S(2)}) collective-permute-start(bf16[576,384]{1,0:T(8,128)(2,1)S(1)} %pad_maximum_fusion.8), channel_id=1, source_target_pairs={{0,16},{16,0},{1,17},{17,1},{2,18},{18,2},{3,19},{19,3},{4,20},{20... | collective-permute-start | bytes 1327112 | tf_op jit(solution)/shard_map/ppermute | solution.py:49
  4.9 8.8 %collective-permute-start.1 = (bf16[192,384]{1,0:T(8,128)(2,1)}, bf16[192,384]{1,0:T(8,128)(2,1)S(1)}, u32[]{:S(2)}, u32[]{:S(2)}) collective-permute-start(bf16[192,384]{1,0:T(8,128)(2,1)} %param.27), channel_id=1, source_target_pairs={{0,1},{1,2},{2,3},{3,0},{4,5},{5,6},{6,7},{7,4},{8,9},{9,10},{10,1... | collective-permute-start | bytes 442376 | tf_op jit(solution)/shard_map/ppermute | solution.py:44
  6.5 12.2 %collective-permute-start.2 = (bf16[192,384]{1,0:T(8,128)(2,1)}, bf16[192,384]{1,0:T(8,128)(2,1)S(1)}, u32[]{:S(2)}, u32[]{:S(2)}) collective-permute-start(bf16[192,384]{1,0:T(8,128)(2,1)} %param.27), channel_id=1, source_target_pairs={{0,2},{1,3},{2,0},{3,1},{4,6},{5,7},{6,4},{7,5},{8,10},{9,11},{10,... | collective-permute-start | bytes 442376 | tf_op jit(solution)/shard_map/ppermute | solution.py:44
  9.1 9.6 %collective-permute-start.3 = (bf16[192,384]{1,0:T(8,128)(2,1)}, bf16[192,384]{1,0:T(8,128)(2,1)S(1)}, u32[]{:S(2)}, u32[]{:S(2)}) collective-permute-start(bf16[192,384]{1,0:T(8,128)(2,1)} %param.27), channel_id=1, source_target_pairs={{0,3},{1,0},{2,1},{3,2},{4,7},{5,4},{6,5},{7,6},{8,11},{9,8},{10,9... | collective-permute-start | bytes 442376 | tf_op jit(solution)/shard_map/ppermute | solution.py:44
  21.9 11.0 %collective-permute-start.4 = (bf16[1,512,384]{2,1,0:T(8,128)(2,1)S(1)}, bf16[1,512,384]{2,1,0:T(8,128)(2,1)S(1)}, u32[]{:S(2)}, u32[]{:S(2)}) collective-permute-start(bf16[1,512,384]{2,1,0:T(8,128)(2,1)S(1)} %bitcast.96), channel_id=1, source_target_pairs={{0,8},{4,12},{8,0},{12,4},{1,9},{5,13},{9,1},{13,5},{2,10},{6,14},... | collective-permute-start | bytes 1179656 | tf_op jit(solution)/shard_map/ppermute | solution.py:49
  24.2 76.3 %collective-permute-start.18 = (f32[]{:T(128)}, f32[]{:T(128)}, u32[]{:S(2)}, u32[]{:S(2)}) collective-permute-start(f32[]{:T(128)} %convert_element_type.227), channel_id=1, source_target_pairs={{0,16},{16,0},{1,17},{17,1},{2,18},{18,2},{3,19},{19,3},{4,20},{20... | collective-permute-start | bytes 20 | tf_op jit(solution)/shard_map/ppermute | solution.py:49
  34.0 5.4 %collective-permute-start.5 = (bf16[2,512,384]{2,1,0:T(8,128)(2,1)}, bf16[2,512,384]{2,1,0:T(8,128)(2,1)S(1)}, u32[]{:S(2)}, u32[]{:S(2)}) collective-permute-start(bf16[2,512,384]{2,1,0:T(8,128)(2,1)} %pad_maximum_fusion.1), channel_id=1, source_target_pairs={{0,4},{4,0},{8,12},{12,8},{1,5},{5,1},{9,13},{13,9},{2,6},{6,2},{1... | collective-permute-start | bytes 2359304 | tf_op jit(solution)/shard_map/ppermute | solution.py:49
  35.0 19.5 %collective-permute-start.6 = (bf16[768,384]{1,0:T(8,128)(2,1)S(1)}, bf16[768,384]{1,0:T(8,128)(2,1)}, u32[]{:S(2)}, u32[]{:S(2)}) collective-permute-start(bf16[768,384]{1,0:T(8,128)(2,1)S(1)} %pad_maximum_fusion.6), channel_id=1, source_target_pairs={{0,16},{16,0},{1,17},{17,1},{2,18},{18,2},{3,19},{19,3},{4,20},{20... | collective-permute-start | bytes 1769480 | tf_op jit(solution)/shard_map/ppermute | solution.py:49
  55.7 16.9 %collective-permute-start.14 = (bf16[768,384]{1,0:T(8,128)(2,1)S(1)}, bf16[768,384]{1,0:T(8,128)(2,1)S(1)}, u32[]{:S(2)}, u32[]{:S(2)}) collective-permute-start(bf16[768,384]{1,0:T(8,128)(2,1)S(1)} %copy-done.20), channel_id=1, source_target_pairs={{0,16},{16,0},{1,17},{17,1},{2,18},{18,2},{3,19},{19,3},{4,20},{20... | collective-permute-start | bytes 1769480 | tf_op jit(solution)/shard_map/ppermute | solution.py:49
  57.3 7.4 %collective-permute-start.7 = (bf16[128,192]{1,0:T(8,128)(2,1)S(1)}, bf16[128,192]{1,0:T(8,128)(2,1)S(1)}, u32[]{:S(2)}, u32[]{:S(2)}) collective-permute-start(bf16[128,192]{1,0:T(8,128)(2,1)S(1)} %get-tuple-element.177), channel_id=1, source_target_pairs={{0,1},{1,2},{2,3},{3,0},{4,5},{5,6},{6,7},{7,4},{8,9},{9,10},{10,1... | collective-permute-start | bytes 147464 | tf_op jit(solution)/shard_map/ppermute | solution.py:44
  61.0 6.1 %collective-permute-start.8 = (bf16[128,192]{1,0:T(8,128)(2,1)S(1)}, bf16[128,192]{1,0:T(8,128)(2,1)S(1)}, u32[]{:S(2)}, u32[]{:S(2)}) collective-permute-start(bf16[128,192]{1,0:T(8,128)(2,1)S(1)} %get-tuple-element.176), channel_id=1, source_target_pairs={{0,2},{1,3},{2,0},{3,1},{4,6},{5,7},{6,4},{7,5},{8,10},{9,11},{10,... | collective-permute-start | bytes 147464 | tf_op jit(solution)/shard_map/ppermute | solution.py:44
  61.3 5.8 %collective-permute-start.9 = (bf16[128,192]{1,0:T(8,128)(2,1)S(1)}, bf16[128,192]{1,0:T(8,128)(2,1)S(1)}, u32[]{:S(2)}, u32[]{:S(2)}) collective-permute-start(bf16[128,192]{1,0:T(8,128)(2,1)S(1)} %get-tuple-element.175), channel_id=1, source_target_pairs={{0,3},{1,0},{2,1},{3,2},{4,7},{5,4},{6,5},{7,6},{8,11},{9,8},{10,9... | collective-permute-start | bytes 147464 | tf_op jit(solution)/shard_map/ppermute | solution.py:44
  64.7 19.2 %collective-permute-start.13 = (bf16[384,768]{1,0:T(8,128)(2,1)S(1)}, bf16[384,768]{1,0:T(8,128)(2,1)S(1)}, u32[]{:S(2)}, u32[]{:S(2)}) collective-permute-start(bf16[384,768]{1,0:T(8,128)(2,1)S(1)} %copy-done.21), channel_id=1, source_target_pairs={{0,16},{16,0},{1,17},{17,1},{2,18},{18,2},{3,19},{19,3},{4,20},{20... | collective-permute-start | bytes 1769480 | tf_op jit(solution)/shard_map/ppermute | solution.py:49
  69.3 14.6 %collective-permute-start.10 = (bf16[128,768]{1,0:T(8,128)(2,1)S(1)}, bf16[128,768]{1,0:T(8,128)(2,1)S(1)}, u32[]{:S(2)}, u32[]{:S(2)}) collective-permute-start(bf16[128,768]{1,0:T(8,128)(2,1)S(1)} %maximum_select_fusion.5), channel_id=1, source_target_pairs={{0,1},{1,2},{2,3},{3,0},{4,5},{5,6},{6,7},{7,4},{8,9},{9,10},{10,1... | collective-permute-start | bytes 589832 | tf_op jit(solution)/shard_map/ppermute | solution.py:44
  71.0 14.9 %collective-permute-start.11 = (bf16[128,768]{1,0:T(8,128)(2,1)S(1)}, bf16[128,768]{1,0:T(8,128)(2,1)S(1)}, u32[]{:S(2)}, u32[]{:S(2)}) collective-permute-start(bf16[128,768]{1,0:T(8,128)(2,1)S(1)} %maximum_select_fusion.5), channel_id=1, source_target_pairs={{0,2},{1,3},{2,0},{3,1},{4,6},{5,7},{6,4},{7,5},{8,10},{9,11},{10,... | collective-permute-start | bytes 589832 | tf_op jit(solution)/shard_map/ppermute | solution.py:44
  72.6 13.3 %collective-permute-start.12 = (bf16[128,768]{1,0:T(8,128)(2,1)S(1)}, bf16[128,768]{1,0:T(8,128)(2,1)S(1)}, u32[]{:S(2)}, u32[]{:S(2)}) collective-permute-start(bf16[128,768]{1,0:T(8,128)(2,1)S(1)} %maximum_select_fusion.5), channel_id=1, source_target_pairs={{0,3},{1,0},{2,1},{3,2},{4,7},{5,4},{6,5},{7,6},{8,11},{9,8},{10,9... | collective-permute-start | bytes 589832 | tf_op jit(solution)/shard_map/ppermute | solution.py:44
  93.6 25.9 %copy-start.46 = (f32[768]{0:T(1024)S(1)}, f32[768]{0:T(1024)}, u32[]{:S(2)}) copy-start(f32[768]{0:T(1024)} %param.34) | copy-start | bytes 9220
  94.3 10.6 %collective-permute-start.15 = (bf16[128,768]{1,0:T(8,128)(2,1)}, bf16[128,768]{1,0:T(8,128)(2,1)}, u32[]{:S(2)}, u32[]{:S(2)}) collective-permute-start(bf16[128,768]{1,0:T(8,128)(2,1)} %get-tuple-element.152), channel_id=1, source_target_pairs={{0,3},{1,0},{2,1},{3,2},{4,7},{5,4},{6,5},{7,6},{8,11},{9,8},{10,9... | collective-permute-start | bytes 589832 | tf_op jit(solution)/shard_map/ppermute | solution.py:44
  99.2 18.9 %collective-permute-start.16 = (bf16[128,768]{1,0:T(8,128)(2,1)S(1)}, bf16[128,768]{1,0:T(8,128)(2,1)}, u32[]{:S(2)}, u32[]{:S(2)}) collective-permute-start(bf16[128,768]{1,0:T(8,128)(2,1)S(1)} %get-tuple-element.154), channel_id=1, source_target_pairs={{0,2},{1,3},{2,0},{3,1},{4,6},{5,7},{6,4},{7,5},{8,10},{9,11},{10,... | collective-permute-start | bytes 589832 | tf_op jit(solution)/shard_map/ppermute | solution.py:44
  100.4 17.8 %collective-permute-start.17 = (bf16[128,768]{1,0:T(8,128)(2,1)S(1)}, bf16[128,768]{1,0:T(8,128)(2,1)}, u32[]{:S(2)}, u32[]{:S(2)}) collective-permute-start(bf16[128,768]{1,0:T(8,128)(2,1)S(1)} %get-tuple-element.153), channel_id=1, source_target_pairs={{0,1},{1,2},{2,3},{3,0},{4,5},{5,6},{6,7},{7,4},{8,9},{9,10},{10,1... | collective-permute-start | bytes 589832 | tf_op jit(solution)/shard_map/ppermute | solution.py:44
  122.5 9.7 %collective-permute-start.19 = (bf16[128,768]{1,0:T(8,128)(2,1)S(1)}, bf16[128,768]{1,0:T(8,128)(2,1)S(1)}, u32[]{:S(2)}, u32[]{:S(2)}) collective-permute-start(bf16[128,768]{1,0:T(8,128)(2,1)S(1)} %maximum_select_fusion.6), channel_id=1, source_target_pairs={{0,1},{1,2},{2,3},{3,0},{4,5},{5,6},{6,7},{7,4},{8,9},{9,10},{10,1... | collective-permute-start | bytes 589832 | tf_op jit(solution)/shard_map/ppermute | solution.py:44
  122.6 16.3 %collective-permute-start.20 = (bf16[128,768]{1,0:T(8,128)(2,1)S(1)}, bf16[128,768]{1,0:T(8,128)(2,1)S(1)}, u32[]{:S(2)}, u32[]{:S(2)}) collective-permute-start(bf16[128,768]{1,0:T(8,128)(2,1)S(1)} %maximum_select_fusion.6), channel_id=1, source_target_pairs={{0,2},{1,3},{2,0},{3,1},{4,6},{5,7},{6,4},{7,5},{8,10},{9,11},{10,... | collective-permute-start | bytes 589832 | tf_op jit(solution)/shard_map/ppermute | solution.py:44
  123.2 15.7 %collective-permute-start.21 = (bf16[128,768]{1,0:T(8,128)(2,1)S(1)}, bf16[128,768]{1,0:T(8,128)(2,1)S(1)}, u32[]{:S(2)}, u32[]{:S(2)}) collective-permute-start(bf16[128,768]{1,0:T(8,128)(2,1)S(1)} %maximum_select_fusion.6), channel_id=1, source_target_pairs={{0,3},{1,0},{2,1},{3,2},{4,7},{5,4},{6,5},{7,6},{8,11},{9,8},{10,9... | collective-permute-start | bytes 589832 | tf_op jit(solution)/shard_map/ppermute | solution.py:44
  141.1 10.2 %collective-permute-start.22 = (bf16[128,768]{1,0:T(8,128)(2,1)S(1)}, bf16[128,768]{1,0:T(8,128)(2,1)S(1)}, u32[]{:S(2)}, u32[]{:S(2)}) collective-permute-start(bf16[128,768]{1,0:T(8,128)(2,1)S(1)} %get-tuple-element.149), channel_id=1, source_target_pairs={{0,3},{1,0},{2,1},{3,2},{4,7},{5,4},{6,5},{7,6},{8,11},{9,8},{10,9... | collective-permute-start | bytes 589832 | tf_op jit(solution)/shard_map/ppermute | solution.py:44
  145.3 17.8 %collective-permute-start.23 = (bf16[128,768]{1,0:T(8,128)(2,1)S(1)}, bf16[128,768]{1,0:T(8,128)(2,1)S(1)}, u32[]{:S(2)}, u32[]{:S(2)}) collective-permute-start(bf16[128,768]{1,0:T(8,128)(2,1)S(1)} %get-tuple-element.151), channel_id=1, source_target_pairs={{0,2},{1,3},{2,0},{3,1},{4,6},{5,7},{6,4},{7,5},{8,10},{9,11},{10,... | collective-permute-start | bytes 589832 | tf_op jit(solution)/shard_map/ppermute | solution.py:44
  146.5 16.6 %collective-permute-start.24 = (bf16[128,768]{1,0:T(8,128)(2,1)S(1)}, bf16[128,768]{1,0:T(8,128)(2,1)S(1)}, u32[]{:S(2)}, u32[]{:S(2)}) collective-permute-start(bf16[128,768]{1,0:T(8,128)(2,1)S(1)} %get-tuple-element.150), channel_id=1, source_target_pairs={{0,1},{1,2},{2,3},{3,0},{4,5},{5,6},{6,7},{7,4},{8,9},{9,10},{10,1... | collective-permute-start | bytes 589832 | tf_op jit(solution)/shard_map/ppermute | solution.py:44
  148.3 42.7 %collective-permute-start.30 = (bf16[384,768]{1,0:T(8,128)(2,1)}, bf16[384,768]{1,0:T(8,128)(2,1)}, u32[]{:S(2)}, u32[]{:S(2)}) collective-permute-start(bf16[384,768]{1,0:T(8,128)(2,1)} %split.96), channel_id=1, source_target_pairs={{0,16},{16,0},{1,17},{17,1},{2,18},{18,2},{3,19},{19,3},{4,20},{20... | collective-permute-start | bytes 1769480 | tf_op jit(solution)/shard_map/ppermute | solution.py:49
  149.7 25.3 %collective-permute-start.25 = (bf16[768,384]{1,0:T(8,128)(2,1)S(1)}, bf16[768,384]{1,0:T(8,128)(2,1)S(1)}, u32[]{:S(2)}, u32[]{:S(2)}) collective-permute-start(bf16[768,384]{1,0:T(8,128)(2,1)S(1)} %split.97), channel_id=1, source_target_pairs={{0,16},{16,0},{1,17},{17,1},{2,18},{18,2},{3,19},{19,3},{4,20},{20... | collective-permute-start | bytes 1769480 | tf_op jit(solution)/shard_map/ppermute | solution.py:49
  175.1 15.8 %collective-permute-start.29 = (bf16[768,384]{1,0:T(8,128)(2,1)S(1)}, bf16[768,384]{1,0:T(8,128)(2,1)S(1)}, u32[]{:S(2)}, u32[]{:S(2)}) collective-permute-start(bf16[768,384]{1,0:T(8,128)(2,1)S(1)} %fusion.7), channel_id=1, source_target_pairs={{0,4},{4,0},{8,12},{12,8},{1,5},{5,1},{9,13},{13,9},{2,6},{6,2},{1... | collective-permute-start | bytes 1769480 | tf_op jit(solution)/shard_map/ppermute | solution.py:49
  176.0 10.7 %collective-permute-start.26 = (bf16[128,192]{1,0:T(8,128)(2,1)S(1)}, bf16[128,192]{1,0:T(8,128)(2,1)S(1)}, u32[]{:S(2)}, u32[]{:S(2)}) collective-permute-start(bf16[128,192]{1,0:T(8,128)(2,1)S(1)} %get-tuple-element.185), channel_id=1, source_target_pairs={{0,1},{1,2},{2,3},{3,0},{4,5},{5,6},{6,7},{7,4},{8,9},{9,10},{10,1... | collective-permute-start | bytes 147464 | tf_op jit(solution)/shard_map/ppermute | solution.py:44
  177.6 9.6 %collective-permute-start.27 = (bf16[128,192]{1,0:T(8,128)(2,1)S(1)}, bf16[128,192]{1,0:T(8,128)(2,1)S(1)}, u32[]{:S(2)}, u32[]{:S(2)}) collective-permute-start(bf16[128,192]{1,0:T(8,128)(2,1)S(1)} %get-tuple-element.184), channel_id=1, source_target_pairs={{0,2},{1,3},{2,0},{3,1},{4,6},{5,7},{6,4},{7,5},{8,10},{9,11},{10,... | collective-permute-start | bytes 147464 | tf_op jit(solution)/shard_map/ppermute | solution.py:44
  180.1 7.1 %collective-permute-start.28 = (bf16[128,192]{1,0:T(8,128)(2,1)S(1)}, bf16[128,192]{1,0:T(8,128)(2,1)S(1)}, u32[]{:S(2)}, u32[]{:S(2)}) collective-permute-start(bf16[128,192]{1,0:T(8,128)(2,1)S(1)} %get-tuple-element.183), channel_id=1, source_target_pairs={{0,3},{1,0},{2,1},{3,2},{4,7},{5,4},{6,5},{7,6},{8,11},{9,8},{10,9... | collective-permute-start | bytes 147464 | tf_op jit(solution)/shard_map/ppermute | solution.py:44
  186.7 4.3 %collective-permute-start.31 = (f32[12,768]{1,0:T(8,128)}, f32[12,768]{1,0:T(8,128)S(1)}, u32[]{:S(2)}, u32[]{:S(2)}) collective-permute-start(f32[12,768]{1,0:T(8,128)} %pack.1), channel_id=1, source_target_pairs={{0,16},{16,0},{1,17},{17,1},{2,18},{18,2},{3,19},{19,3},{4,20},{20... | collective-permute-start | bytes 110600 | tf_op jit(solution)/shard_map/ppermute | solution.py:49
  193.3 20.9 %collective-permute-start.33 = (bf16[384,768]{1,0:T(8,128)(2,1)S(1)}, bf16[384,768]{1,0:T(8,128)(2,1)S(1)}, u32[]{:S(2)}, u32[]{:S(2)}) collective-permute-start(bf16[384,768]{1,0:T(8,128)(2,1)S(1)} %fusion.6), channel_id=1, source_target_pairs={{0,4},{4,0},{8,12},{12,8},{1,5},{5,1},{9,13},{13,9},{2,6},{6,2},{1... | collective-permute-start | bytes 1769480 | tf_op jit(solution)/shard_map/ppermute | solution.py:49
  194.6 19.6 %collective-permute-start.32 = (bf16[768,384]{1,0:T(8,128)(2,1)S(1)}, bf16[768,384]{1,0:T(8,128)(2,1)S(1)}, u32[]{:S(2)}, u32[]{:S(2)}) collective-permute-start(bf16[768,384]{1,0:T(8,128)(2,1)S(1)} %add_convert_fusion.1), channel_id=1, source_target_pairs={{0,8},{4,12},{8,0},{12,4},{1,9},{5,13},{9,1},{13,5},{2,10},{6,14},... | collective-permute-start | bytes 1769480 | tf_op jit(solution)/shard_map/ppermute | solution.py:49
  196.2 18.0 %collective-permute-start.34 = (f32[12,768]{1,0:T(8,128)S(1)}, f32[12,768]{1,0:T(8,128)S(1)}, u32[]{:S(2)}, u32[]{:S(2)}) collective-permute-start(f32[12,768]{1,0:T(8,128)S(1)} %add.309), channel_id=1, source_target_pairs={{0,4},{4,0},{8,12},{12,8},{1,5},{5,1},{9,13},{13,9},{2,6},{6,2},{1... | collective-permute-start | bytes 110600 | tf_op jit(solution)/shard_map/ppermute | solution.py:49
  217.0 2.4 collective-permute-start.35
  220.4 12.1 %collective-permute-start.36 = (bf16[1,384,512]{2,1,0:T(8,128)(2,1)}, bf16[1,384,512]{2,1,0:T(8,128)(2,1)}, u32[]{:S(2)}, u32[]{:S(2)}) collective-permute-start(bf16[1,384,512]{2,1,0:T(8,128)(2,1)} %slice.272), channel_id=1, source_target_pairs={{0,8},{4,12},{8,0},{12,4},{1,9},{5,13},{9,1},{13,5},{2,10},{6,14},... | collective-permute-start | bytes 1179656 | tf_op jit(solution)/shard_map/ppermute | solution.py:49
  221.0 12.7 %collective-permute-start.38 = (bf16[128,768]{1,0:T(8,128)(2,1)}, bf16[128,768]{1,0:T(8,128)(2,1)}, u32[]{:S(2)}, u32[]{:S(2)}) collective-permute-start(bf16[128,768]{1,0:T(8,128)(2,1)} %copy-done.11), channel_id=1, source_target_pairs={{0,1},{1,2},{2,3},{3,0},{4,5},{5,6},{6,7},{7,4},{8,9},{9,10},{10,1... | collective-permute-start | bytes 589832 | tf_op jit(solution)/shard_map/ppermute | solution.py:44
  222.7 15.8 %collective-permute-start.39 = (bf16[128,768]{1,0:T(8,128)(2,1)}, bf16[128,768]{1,0:T(8,128)(2,1)}, u32[]{:S(2)}, u32[]{:S(2)}) collective-permute-start(bf16[128,768]{1,0:T(8,128)(2,1)} %copy-done.11), channel_id=1, source_target_pairs={{0,2},{1,3},{2,0},{3,1},{4,6},{5,7},{6,4},{7,5},{8,10},{9,11},{10,... | collective-permute-start | bytes 589832 | tf_op jit(solution)/shard_map/ppermute | solution.py:44
  223.1 15.4 %collective-permute-start.40 = (bf16[128,768]{1,0:T(8,128)(2,1)}, bf16[128,768]{1,0:T(8,128)(2,1)}, u32[]{:S(2)}, u32[]{:S(2)}) collective-permute-start(bf16[128,768]{1,0:T(8,128)(2,1)} %copy-done.11), channel_id=1, source_target_pairs={{0,3},{1,0},{2,1},{3,2},{4,7},{5,4},{6,5},{7,6},{8,11},{9,8},{10,9... | collective-permute-start | bytes 589832 | tf_op jit(solution)/shard_map/ppermute | solution.py:44
  228.3 5.4 %collective-permute-start.37 = (f32[12,768]{1,0:T(8,128)S(1)}, f32[12,768]{1,0:T(8,128)S(1)}, u32[]{:S(2)}, u32[]{:S(2)}) collective-permute-start(f32[12,768]{1,0:T(8,128)S(1)} %add.312), channel_id=1, source_target_pairs={{0,8},{4,12},{8,0},{12,4},{1,9},{5,13},{9,1},{13,5},{2,10},{6,14},... | collective-permute-start | bytes 110600 | tf_op jit(solution)/shard_map/ppermute | solution.py:49
  239.4 34.0 %collective-permute-start.48 = (f32[384]{0:T(512)S(1)}, f32[384]{0:T(512)S(1)}, u32[]{:S(2)}, u32[]{:S(2)}) collective-permute-start(f32[384]{0:T(512)S(1)} %pad_maximum_fusion.21), channel_id=1, source_target_pairs={{0,16},{16,0},{1,17},{17,1},{2,18},{18,2},{3,19},{19,3},{4,20},{20... | collective-permute-start | bytes 4616 | tf_op jit(solution)/shard_map/ppermute | solution.py:49
  240.0 37.4 %collective-permute-start.47 = (bf16[576,384]{1,0:T(8,128)(2,1)S(1)}, bf16[576,384]{1,0:T(8,128)(2,1)S(1)}, u32[]{:S(2)}, u32[]{:S(2)}) collective-permute-start(bf16[576,384]{1,0:T(8,128)(2,1)S(1)} %split.98), channel_id=1, source_target_pairs={{0,16},{16,0},{1,17},{17,1},{2,18},{18,2},{3,19},{19,3},{4,20},{20... | collective-permute-start | bytes 1327112 | tf_op jit(solution)/shard_map/ppermute | solution.py:49
  248.0 23.2 %copy-start.40 = (bf16[192,384]{1,0:T(8,128)(2,1)S(1)}, bf16[192,384]{1,0:T(8,128)(2,1)}, u32[]{:S(2)}) copy-start(bf16[192,384]{1,0:T(8,128)(2,1)} %split.99) | copy-start | bytes 442372
  248.0 9.9 %collective-permute-start.41 = (bf16[128,768]{1,0:T(8,128)(2,1)S(1)}, bf16[128,768]{1,0:T(8,128)(2,1)S(1)}, u32[]{:S(2)}, u32[]{:S(2)}) collective-permute-start(bf16[128,768]{1,0:T(8,128)(2,1)S(1)} %get-tuple-element.146), channel_id=1, source_target_pairs={{0,3},{1,0},{2,1},{3,2},{4,7},{5,4},{6,5},{7,6},{8,11},{9,8},{10,9... | collective-permute-start | bytes 589832 | tf_op jit(solution)/shard_map/ppermute | solution.py:44
  252.7 18.5 %collective-permute-start.42 = (bf16[128,768]{1,0:T(8,128)(2,1)S(1)}, bf16[128,768]{1,0:T(8,128)(2,1)S(1)}, u32[]{:S(2)}, u32[]{:S(2)}) collective-permute-start(bf16[128,768]{1,0:T(8,128)(2,1)S(1)} %get-tuple-element.148), channel_id=1, source_target_pairs={{0,2},{1,3},{2,0},{3,1},{4,6},{5,7},{6,4},{7,5},{8,10},{9,11},{10,... | collective-permute-start | bytes 589832 | tf_op jit(solution)/shard_map/ppermute | solution.py:44
  254.2 17.5 %collective-permute-start.43 = (bf16[128,768]{1,0:T(8,128)(2,1)S(1)}, bf16[128,768]{1,0:T(8,128)(2,1)S(1)}, u32[]{:S(2)}, u32[]{:S(2)}) collective-permute-start(bf16[128,768]{1,0:T(8,128)(2,1)S(1)} %get-tuple-element.147), channel_id=1, source_target_pairs={{0,1},{1,2},{2,3},{3,0},{4,5},{5,6},{6,7},{7,4},{8,9},{9,10},{10,1... | collective-permute-start | bytes 589832 | tf_op jit(solution)/shard_map/ppermute | solution.py:44
  258.0 15.6 %collective-permute-start.46 = (f32[12,768]{1,0:T(8,128)S(1)}, f32[12,768]{1,0:T(8,128)S(1)}, u32[]{:S(2)}, u32[]{:S(2)}) collective-permute-start(f32[12,768]{1,0:T(8,128)S(1)} %add.318), channel_id=1, source_target_pairs={{0,1},{1,0},{2,3},{3,2},{4,5},{5,4},{6,7},{7,6},{8,9},{9,8},{10,11... | collective-permute-start | bytes 110600 | tf_op jit(solution)/shard_map/ppermute | solution.py:49
  271.2 5.1 %collective-permute-start.45 = (bf16[192,384]{1,0:T(8,128)(2,1)S(1)}, bf16[192,384]{1,0:T(8,128)(2,1)S(1)}, u32[]{:S(2)}, u32[]{:S(2)}) collective-permute-start(bf16[192,384]{1,0:T(8,128)(2,1)S(1)} %copy-done.40), channel_id=1, source_target_pairs={{0,16},{16,0},{1,17},{17,1},{2,18},{18,2},{3,19},{19,3},{4,20},{20... | collective-permute-start | bytes 442376 | tf_op jit(solution)/shard_map/ppermute | solution.py:49
  271.7 13.5 %collective-permute-start.44 = (bf16[384,768]{1,0:T(8,128)(2,1)S(1)}, bf16[384,768]{1,0:T(8,128)(2,1)S(1)}, u32[]{:S(2)}, u32[]{:S(2)}) collective-permute-start(bf16[384,768]{1,0:T(8,128)(2,1)S(1)} %add_convert_fusion), channel_id=1, source_target_pairs={{0,8},{4,12},{8,0},{12,4},{1,9},{5,13},{9,1},{13,5},{2,10},{6,14},... | collective-permute-start | bytes 1769480 | tf_op jit(solution)/shard_map/ppermute | solution.py:49
  273.5 11.8 %collective-permute-start.49 = (bf16[128,768]{1,0:T(8,128)(2,1)S(1)}, bf16[128,768]{1,0:T(8,128)(2,1)S(1)}, u32[]{:S(2)}, u32[]{:S(2)}) collective-permute-start(bf16[128,768]{1,0:T(8,128)(2,1)S(1)} %copy-done.14), channel_id=1, source_target_pairs={{0,1},{1,2},{2,3},{3,0},{4,5},{5,6},{6,7},{7,4},{8,9},{9,10},{10,1... | collective-permute-start | bytes 589832 | tf_op jit(solution)/shard_map/ppermute | solution.py:44
  273.5 15.2 %collective-permute-start.50 = (bf16[128,768]{1,0:T(8,128)(2,1)S(1)}, bf16[128,768]{1,0:T(8,128)(2,1)S(1)}, u32[]{:S(2)}, u32[]{:S(2)}) collective-permute-start(bf16[128,768]{1,0:T(8,128)(2,1)S(1)} %copy-done.14), channel_id=1, source_target_pairs={{0,2},{1,3},{2,0},{3,1},{4,6},{5,7},{6,4},{7,5},{8,10},{9,11},{10,... | collective-permute-start | bytes 589832 | tf_op jit(solution)/shard_map/ppermute | solution.py:44
  276.3 12.4 %collective-permute-start.51 = (bf16[128,768]{1,0:T(8,128)(2,1)S(1)}, bf16[128,768]{1,0:T(8,128)(2,1)S(1)}, u32[]{:S(2)}, u32[]{:S(2)}) collective-permute-start(bf16[128,768]{1,0:T(8,128)(2,1)S(1)} %copy-done.14), channel_id=1, source_target_pairs={{0,3},{1,0},{2,1},{3,2},{4,7},{5,4},{6,5},{7,6},{8,11},{9,8},{10,9... | collective-permute-start | bytes 589832 | tf_op jit(solution)/shard_map/ppermute | solution.py:44
  288.7 25.9 %collective-permute-start.53 = (bf16[128,768]{1,0:T(8,128)(2,1)S(1)}, bf16[128,768]{1,0:T(8,128)(2,1)S(1)}, u32[]{:S(2)}, u32[]{:S(2)}) collective-permute-start(bf16[128,768]{1,0:T(8,128)(2,1)S(1)} %fusion.38), channel_id=1, source_target_pairs={{0,1},{1,2},{2,3},{3,0},{4,5},{5,6},{6,7},{7,4},{8,9},{9,10},{10,1... | collective-permute-start | bytes 589832 | tf_op jit(solution)/shard_map/ppermute | solution.py:44
  292.6 22.0 %collective-permute-start.54 = (bf16[128,768]{1,0:T(8,128)(2,1)S(1)}, bf16[128,768]{1,0:T(8,128)(2,1)S(1)}, u32[]{:S(2)}, u32[]{:S(2)}) collective-permute-start(bf16[128,768]{1,0:T(8,128)(2,1)S(1)} %fusion.38), channel_id=1, source_target_pairs={{0,2},{1,3},{2,0},{3,1},{4,6},{5,7},{6,4},{7,5},{8,10},{9,11},{10,... | collective-permute-start | bytes 589832 | tf_op jit(solution)/shard_map/ppermute | solution.py:44
  293.9 20.7 %collective-permute-start.55 = (bf16[128,768]{1,0:T(8,128)(2,1)S(1)}, bf16[128,768]{1,0:T(8,128)(2,1)S(1)}, u32[]{:S(2)}, u32[]{:S(2)}) collective-permute-start(bf16[128,768]{1,0:T(8,128)(2,1)S(1)} %fusion.38), channel_id=1, source_target_pairs={{0,3},{1,0},{2,1},{3,2},{4,7},{5,4},{6,5},{7,6},{8,11},{9,8},{10,9... | collective-permute-start | bytes 589832 | tf_op jit(solution)/shard_map/ppermute | solution.py:44
  295.0 1.8 collective-permute-start.60
  296.2 18.3 %collective-permute-start.58 = (bf16[192,384]{1,0:T(8,128)(2,1)S(1)}, bf16[192,384]{1,0:T(8,128)(2,1)S(1)}, u32[]{:S(2)}, u32[]{:S(2)}) collective-permute-start(bf16[192,384]{1,0:T(8,128)(2,1)S(1)} %fusion.45), channel_id=1, source_target_pairs={{0,8},{4,12},{8,0},{12,4},{1,9},{5,13},{9,1},{13,5},{2,10},{6,14},... | collective-permute-start | bytes 442376 | tf_op jit(solution)/shard_map/ppermute | solution.py:49
  296.8 5.7 %collective-permute-start.61 = (f32[384]{0:T(512)S(1)}, f32[384]{0:T(512)S(1)}, u32[]{:S(2)}, u32[]{:S(2)}) collective-permute-start(f32[384]{0:T(512)S(1)} %add.330), channel_id=1, source_target_pairs={{0,8},{4,12},{8,0},{12,4},{1,9},{5,13},{9,1},{13,5},{2,10},{6,14},... | collective-permute-start | bytes 4616 | tf_op jit(solution)/shard_map/ppermute | solution.py:49
  302.6 9.5 %collective-permute-start.52 = (f32[12,768]{1,0:T(8,128)S(1)}, f32[12,768]{1,0:T(8,128)S(1)}, u32[]{:S(2)}, u32[]{:S(2)}) collective-permute-start(f32[12,768]{1,0:T(8,128)S(1)} %add.319), channel_id=1, source_target_pairs={{0,2},{1,3},{2,0},{3,1},{4,6},{5,7},{6,4},{7,5},{8,10},{9,11},{10,... | collective-permute-start | bytes 110600 | tf_op jit(solution)/shard_map/ppermute | solution.py:49
  312.0 12.1 %collective-permute-start.56 = (bf16[576,384]{1,0:T(8,128)(2,1)S(1)}, bf16[576,384]{1,0:T(8,128)(2,1)S(1)}, u32[]{:S(2)}, u32[]{:S(2)}) collective-permute-start(bf16[576,384]{1,0:T(8,128)(2,1)S(1)} %fusion.8), channel_id=1, source_target_pairs={{0,8},{4,12},{8,0},{12,4},{1,9},{5,13},{9,1},{13,5},{2,10},{6,14},... | collective-permute-start | bytes 1327112 | tf_op jit(solution)/shard_map/ppermute | solution.py:49
  314.5 12.3 %collective-permute-start.59 = (bf16[192,384]{1,0:T(8,128)(2,1)S(1)}, bf16[192,384]{1,0:T(8,128)(2,1)S(1)}, u32[]{:S(2)}, u32[]{:S(2)}) collective-permute-start(bf16[192,384]{1,0:T(8,128)(2,1)S(1)} %add_convert_fusion.5), channel_id=1, source_target_pairs={{0,4},{4,0},{8,12},{12,8},{1,5},{5,1},{9,13},{13,9},{2,6},{6,2},{1... | collective-permute-start | bytes 442376 | tf_op jit(solution)/shard_map/ppermute | solution.py:49
  324.2 3.3 %collective-permute-start.57 = (bf16[576,384]{1,0:T(8,128)(2,1)S(1)}, bf16[576,384]{1,0:T(8,128)(2,1)S(1)}, u32[]{:S(2)}, u32[]{:S(2)}) collective-permute-start(bf16[576,384]{1,0:T(8,128)(2,1)S(1)} %add_convert_fusion.2), channel_id=1, source_target_pairs={{0,4},{4,0},{8,12},{12,8},{1,5},{5,1},{9,13},{13,9},{2,6},{6,2},{1... | collective-permute-start | bytes 1327112 | tf_op jit(solution)/shard_map/ppermute | solution.py:49
  (57 other events, 432.2 us)
where the time goes:
time: 331 us; the launch traced here: 330 us
  waiting for transfers between devices  130 us (39%)
  starting transfers between devices  90.5 us (27%)
  Pallas kernels  33 us (10%)
  local copies, waits for them, and re-layouts  28.1 us (8%)
  other arithmetic  25.1 us (8%)
  matrix products  17.8 us (5%)
  between operations  4.99 us (2%)
    ppermute x33, waiting for transfers between devices, shifted(): lax.ppermute(block, axis, [(i, (i + step) % size) for i in range(size)])  66.2 us
    ppermute x29, waiting for transfers between devices, flipped(): return lax.ppermute(block, axis, [(i, i ^ bit) for i in range(size)])  64 us
    ppermute x33, starting transfers between devices, shifted(): lax.ppermute(block, axis, [(i, (i + step) % size) for i in range(size)])  55.6 us
    ppermute x29, starting transfers between devices, flipped(): return lax.ppermute(block, axis, [(i, i ^ bit) for i in range(size)])  34.9 us
    dot_general x12, matrix products, dot32(): lax.dot_general(left, right, (dims, ((), ())), preferred_element_type=F32)  17.8 us
    pallas_call x1, Pallas kernels, attend_back(): pl.pallas_call(partial(attend_back_kernel, heads, scale, len(kv)), grid_s...  17.7 us
    pallas_call x1, Pallas kernels, attend(): pl.pallas_call(partial(attend_kernel, heads, len(kv)), grid_spec=pltpu.Pr...  13.1 us
    unnamed x128, local copies, waits for them, and re-layouts  8.67 us
  transfers between devices with their start and end apart: 62, of which 24 were waited for; matrix products, arithmetic and copies ran while one was open for 15% of the time, Pallas kernels for 10%

commit v1 on v0

--- a/solution.py
+++ b/solution.py
@@ -280,6 +280,8 @@
     scaled = d_mixed[...].astype(F32) * inverse[...]
     product = scaled * context[...].astype(F32)
     d_context = scaled.astype(BF16)
+    d_context_t = scaled.T.astype(BF16)
+    query_t = query[...].astype(F32).T.astype(BF16)
     for h in range(heads):
         own = slice(h * size, (h + 1) * size)
         other = slice(width + h * size, width + (h + 1) * size)
@@ -293,12 +295,8 @@
             change = (low.astype(F32) * (d_weights - mean)).astype(BF16)
             d_scores[0, h, :, span] = change
             d_head = d_head + jnp.dot(change, kv[e][:, own], preferred_element_type=F32)
-            total[e, own, :] += lax.dot_general(
-                query[:, own], change, (((0,), (0,)), ((), ())), preferred_element_type=F32
-            )
-            total[e, other, :] += lax.dot_general(
-                d_context[:, own], low, (((0,), (0,)), ((), ())), preferred_element_type=F32
-            )
+            total[e, own, :] += jnp.dot(query_t[own, :], change, preferred_element_type=F32)
+            total[e, other, :] += jnp.dot(d_context_t[own, :], low, preferred_element_type=F32)
         d_query[:, own] = scale * d_head
 
     @pl.when(step == pl.num_programs(0) - 1)
@@ -408,18 +406,16 @@
         return lax.dynamic_slice_in_dim(array, tp_place * part_rows, part_rows, 0)
 
     tokens_first = own_first(tokens)
-    projected = dot32(tokens_first, full_qkv, ((1,), (1,)))
-    query_local = (projected[:, :width_local] + bias_query).astype(BF16)
-    kv_local = jnp.concatenate(
-        [projected[:, width_local : 2 * width_local], projected[:, 2 * width_local :] + bias_value], 1
-    ).astype(BF16)
-    kv_local, output_half = tie(kv_local, output_half)
+    query_scaled = dot32(tokens_first, full_qkv[:width_local], ((1,), (1,))) + bias_query
+    query_scaled = (query_scaled.astype(BF16).astype(F32) * score_scale).astype(BF16)
+    bias_kv = jnp.concatenate([jnp.zeros_like(bias_value), bias_value])
+    kv_local = (dot32(tokens_first, full_qkv[width_local:], ((1,), (1,))) + bias_kv).astype(BF16)
+    kv_all = gather_parts(kv_local)
+    kv_all[-1], output_half = tie(kv_all[-1], output_half)
     output_moved, join_output = gather_late(output_half, 1)
-    kv_all = gather_parts(kv_local)
     starts = (ctx_place ^ jnp.asarray(ctx_order(), jnp.int32)) * row_count
     all_count = VectorSum(seq_length.astype(F32), ("dp",)).total()
 
-    query_scaled = (query_local.astype(F32) * score_scale).astype(BF16)
     logits, weights, context, inverse = attend(
         query_scaled, kv_all, starts, prev_logits, limits, heads_local
     )
@@ -466,14 +462,12 @@
         d_hidden, normed_first, spread_first, gain_first
     )
     grad_bias_output = jnp.sum(d_first, 0)
-    d_first, outer_sum.moved = tie(d_first, outer_sum.moved)
-    outer_sum.step()
     d_first_low = own_first(d_first.astype(BF16))
     d_context_mine = dot32(d_first_low, full_output, ((1,), (1,))).astype(BF16)
     d_context = jnp.concatenate(rows_exchange(jnp.split(d_context_mine, tp_size, 1)), 0)
     d_context = rows_turn(d_context)
 
-    early_sum = VectorSum(
+    packed = (
         pack(
             [
                 grad_bias_output,
@@ -487,34 +481,32 @@
             grad_bias_inner,
             tp_place,
             tp_size,
-        ),
-        ("dp", "ctx", "tp"),
-    )
-    d_context, outer_sum.moved, inner_sum.moved, early_sum.moved = tie(
-        d_context, outer_sum.moved, inner_sum.moved, early_sum.moved
+        )
+    )
+    early_sum = VectorSum(packed, ("dp", "ctx", "tp"))
+    d_context, outer_sum.moved, inner_sum.moved = tie(
+        d_context, outer_sum.moved, inner_sum.moved
     )
     outer_sum.step()
     inner_sum.step()
-    early_sum.step()
-    result_mine, d_first_low, _ = tie(result.astype(BF16), d_first_low, d_context)
-    d_first_moved = rows_moved(d_first_low)
-    result_moved = rows_moved(result_mine)
+    both_mine = jnp.concatenate([d_first_low, result.astype(BF16)], 1)
+    both_mine, _ = tie(both_mine, d_context)
+    both_moved = rows_moved(both_mine)
     d_scores, d_query, d_kv_parts = attend_back(
         weights, kv_all, starts, context, d_context, inverse, query_scaled, score_scale
     )
-    d_kv_parts, outer_sum.moved, inner_sum.moved, early_sum.moved = tie(
-        d_kv_parts, outer_sum.moved, inner_sum.moved, early_sum.moved
-    )
+    d_kv_parts, early_sum.moved = tie(d_kv_parts, early_sum.moved)
     early_sum.step()
     d_kv = scatter_parts(d_kv_parts)
     d_query_low = d_query.astype(BF16)
-    d_kv_low, inner_sum.moved, early_sum.moved = tie(
-        d_kv.astype(BF16), inner_sum.moved, early_sum.moved
+    d_kv_low, inner_sum.moved, outer_sum.moved, early_sum.moved, *both_moved = tie(
+        d_kv.astype(BF16), inner_sum.moved, outer_sum.moved, early_sum.moved, *both_moved
     )
     inner_sum.step()
+    outer_sum.step()
     early_sum.step()
-    d_kv_low, *d_first_moved = tie(d_kv_low, *d_first_moved)
-    d_first_all = jnp.concatenate([d_first_low] + d_first_moved, 0)
+    both = jnp.concatenate([both_mine] + both_moved, 0)
+    d_first_all = both[:, :model_width]
     output_sum = WeightSum(dot32(context_turned, d_first_all, ((0,), (0,))), 1, True)
     d_qkv_low = jnp.concatenate([d_query_low, d_kv_low.T], 1)
     tokens_part = rows_sum(dot32(rows_turn(d_qkv_low), full_qkv, ((1,), (0,))))
@@ -523,14 +515,13 @@
         jnp.concatenate([jnp.sum(d_query, 0), jnp.sum(d_kv[width_local:], 1)]), ("dp", "ctx")
     )
     grad_mine = (d_first + own_first(tokens_part)).astype(BF16)
-    sums = (inner_sum, output_sum, early_sum, qkv_sum, late_sum)
+    sums = (output_sum, early_sum, qkv_sum, late_sum)
     grad_mine, *moved = tie(grad_mine, *[one.moved for one in sums])
     for one, value in zip(sums, moved):
         one.moved = value
-    for one in (output_sum, early_sum, qkv_sum, late_sum):
+    for one in sums:
         one.step()
-    grad_mine, *result_moved = tie(grad_mine, *result_moved)
-    result_all = rows_turn(jnp.concatenate([result_mine] + result_moved, 0)).astype(F32)
+    result_all = rows_turn(both[:, model_width:]).astype(F32)
     grad_inputs = rows_turn(rows_gather(grad_mine)).astype(F32)
     output_shard = output_sum.total()
     shard_qkv = qkv_sum.total()

time: 331 us -> 333 us (level)
  other arithmetic: 25.1 us -> 34.6 us
  waiting for transfers between devices: 130 us -> 124 us
  local copies, waits for them, and re-layouts: 28.1 us -> 23.3 us
    ppermute x29, waiting for transfers between devices: 64 us -> 55.2 us  [flipped(): return lax.ppermute(block, axis, [(i, i ^ bit) for i in range(size)])]
    ppermute x33 -> x30, starting transfers between devices: 55.6 us -> 63.4 us  [shifted(): lax.ppermute(block, axis, [(i, (i + step) % size) for i in range(size)])]
    ppermute x29, starting transfers between devices: 34.9 us -> 30.1 us  [flipped(): return lax.ppermute(block, axis, [(i, i ^ bit) for i in range(size)])]
    unnamed x128 -> x116, local copies, waits for them, and re-layouts: 8.67 us -> 5.3 us
    ppermute x33 -> x30, waiting for transfers between devices: 66.2 us -> 68.6 us  [shifted(): lax.ppermute(block, axis, [(i, (i + step) % size) for i in range(size)])]
    dot_general x12 -> x13, matrix products: 17.8 us -> 18.7 us  [dot32(): lax.dot_general(left, right, (dims, ((), ())), preferred_element_type=F32)]
  transfers between devices with their start and end apart: 62 -> 59, of which waited for: 24 -> 24; matrix products, arithmetic and copies ran while one was open for 15% -> 17% of each run, Pallas kernels for 10% -> 10%
where the time goes in v1:
time: 333 us; the launch traced here: 332 us
  waiting for transfers between devices  124 us (37%)
  starting transfers between devices  93.6 us (28%)
  other arithmetic  34.6 us (10%)
  Pallas kernels  32.9 us (10%)
  local copies, waits for them, and re-layouts  23.3 us (7%)
  matrix products  18.7 us (6%)
  between operations  4.86 us (1%)
    ppermute x30, waiting for transfers between devices, shifted(): lax.ppermute(block, axis, [(i, (i + step) % size) for i in range(size)])  68.6 us
    ppermute x30, starting transfers between devices, shifted(): lax.ppermute(block, axis, [(i, (i + step) % size) for i in range(size)])  63.4 us
    ppermute x29, waiting for transfers between devices, flipped(): return lax.ppermute(block, axis, [(i, i ^ bit) for i in range(size)])  55.2 us
    ppermute x29, starting transfers between devices, flipped(): return lax.ppermute(block, axis, [(i, i ^ bit) for i in range(size)])  30.1 us
    dot_general x13, matrix products, dot32(): lax.dot_general(left, right, (dims, ((), ())), preferred_element_type=F32)  18.7 us
    pallas_call x1, Pallas kernels, attend_back(): pl.pallas_call(partial(attend_back_kernel, heads, scale, len(kv)), grid_s...  17.6 us
    pallas_call x1, Pallas kernels, attend(): pl.pallas_call(partial(attend_kernel, heads, len(kv)), grid_spec=pltpu.Pr...  13.2 us
  transfers between devices with their start and end apart: 59, of which 24 were waited for; matrix products, arithmetic and copies ran while one was open for 17% of the time, Pallas kernels for 10%

profile of v1, /device:TPU:0, one launch (start us, length us, event | category | flops | bytes accessed | tf_op | source)
XLA Modules:
  0.0 331.7 jit_solution(12470679458772236723)
XLA Ops:
  1.8 3.0 collective-permute-start.1
  7.1 8.0 %collective-permute-done.1 = bf16[576,384]{1,0:T(8,128)(2,1)S(1)} collective-permute-done((bf16[576,384]{1,0:T(8,128)(2,1)S(1)}, bf16[576,384]{1,0:T(8,128)(2,1)S(1)}, u32[]{:S(2)}, u32[]{:S(2)}) %collective-permute-start.1) | collective-permute-done | bytes 442400 | tf_op jit(solution)/shard_map/ppermute | solution.py:49
  16.5 1.8 collective-permute-start.2
  18.3 8.5 %collective-permute-done.2.refs_1_ = bf16[1,512,384]{2,1,0:T(8,128)(2,1)S(1)} collective-permute-done((bf16[1,512,384]{2,1,0:T(8,128)(2,1)S(1)}, bf16[1,512,384]{2,1,0:T(8,128)(2,1)S(1)}, u32[]{:S(2)}, u32[]{:S(2)}) %collective-permute-start.2) | collective-permute-done | bytes 393248 | tf_op jit(solution)/shard_map/ppermute | solution.py:49
  27.8 3.6 %collective-permute-start.6 = (bf16[192,384]{1,0:T(8,128)(2,1)S(1)}, bf16[192,384]{1,0:T(8,128)(2,1)S(1)}, u32[]{:S(2)}, u32[]{:S(2)}) collective-permute-start(bf16[192,384]{1,0:T(8,128)(2,1)S(1)} %copy-done.24), channel_id=1, source_target_pairs={{0,3},{1,0},{2,1},{3,2},{4,7},{5,4},{6,5},{7,6},{8,11},{9,8},{10,9... | collective-permute-start | bytes 442376 | tf_op jit(solution)/shard_map/ppermute | solution.py:44
  33.1 2.9 collective-permute-start
  37.1 7.6 %collective-permute-done.5 = bf16[192,384]{1,0:T(8,128)(2,1)} collective-permute-done((bf16[192,384]{1,0:T(8,128)(2,1)S(1)}, bf16[192,384]{1,0:T(8,128)(2,1)}, u32[]{:S(2)}, u32[]{:S(2)}) %collective-permute-start.5) | collective-permute-done | bytes 147488 | tf_op jit(solution)/shard_map/ppermute | solution.py:44
  44.7 1.9 pad_maximum_fusion.4
  46.6 1.5 collective-permute-start.7
  48.1 2.1 fusion.11.query
  50.2 13.2 %attend.1 = (bf16[1,3,512,2048]{3,2,1,0:T(8,128)(2,1)}, bf16[3,512,2048]{2,1,0:T(8,128)(2,1)}, bf16[512,192]{1,0:T(8,128)(2,1)}, f32[512,192]{1,0:T(8,128)}) custom-call(s32[4]{0:T(128)} %multiply_minimum_fusion.limits, s32[4]{0:T(128)} %xor_multiply_fusion.starts, bf16[512,192]{1,0:T(8,128)(2,1)} %fusion.11.query, bf16[1,3,512,2048]{3,2,1,0:T(8,128)(2,1)} %prior.1, ...), custom_call_target="tpu_custom_call" | custom-call | flops 805306368 | bytes 18874368 | tf_op jit(solution)/shard_map/attend/pallas_call | solution.py:241
  67.6 1.6 collective-permute-start.9
  69.2 1.9 collective-permute-start.8
  72.5 1.6 collective-permute-start.15
  74.0 1.3 collective-permute-done.8
  76.8 1.5 collective-permute-start.13
  78.4 3.6 %collective-permute-done.14 = bf16[384,768]{1,0:T(8,128)(2,1)S(1)} collective-permute-done((bf16[384,768]{1,0:T(8,128)(2,1)S(1)}, bf16[384,768]{1,0:T(8,128)(2,1)S(1)}, u32[]{:S(2)}, u32[]{:S(2)}) %collective-permute-start.14) | collective-permute-done | bytes 589856 | tf_op jit(solution)/shard_map/ppermute | solution.py:49
  82.8 10.1 %collective-permute-done.15 = bf16[768,384]{1,0:T(8,128)(2,1)S(1)} collective-permute-done((bf16[768,384]{1,0:T(8,128)(2,1)S(1)}, bf16[768,384]{1,0:T(8,128)(2,1)S(1)}, u32[]{:S(2)}, u32[]{:S(2)}) %collective-permute-start.15) | collective-permute-done | bytes 589856 | tf_op jit(solution)/shard_map/ppermute | solution.py:49
  93.0 2.0 collective-permute-done.12
  95.0 5.6 %multiply_convert_fusion = (bf16[512,768]{1,0:T(8,128)(2,1)S(1)}, f32[512,768]{1,0:T(8,128)}, f32[512,768]{1,0:T(8,128)}) fusion(f32[768]{0:T(1024)S(1)} %copy-done.48, bf16[768,768]{1,0:T(8,128)(2,1)S(1)} %constant_dynamic-update-slice_fusion.2, bf16[128,768]{1,0:T(8,128)(2,1)S(1)} %collective-permute-done.13, ...), kind=kOutput, calls=%fused_computation.4 | convolution fusion | flops 633077760 | bytes 5901312 | tf_op jit(solution)/shard_map/dot_general | solution.py:39
  100.7 1.9 fusion.110
  103.5 1.3 collective-permute-start.17
  104.8 2.9 collective-permute-start.16
  110.4 3.0 collective-permute-done.18
  113.4 5.9 %collective-permute-done.17 = bf16[128,768]{1,0:T(8,128)(2,1)} collective-permute-done((bf16[128,768]{1,0:T(8,128)(2,1)}, bf16[128,768]{1,0:T(8,128)(2,1)}, u32[]{:S(2)}, u32[]{:S(2)}) %collective-permute-start.17) | collective-permute-done | bytes 196640 | tf_op jit(solution)/shard_map/ppermute | solution.py:44
  124.0 6.3 %collective-permute-start.21 = (bf16[128,768]{1,0:T(8,128)(2,1)S(1)}, bf16[128,768]{1,0:T(8,128)(2,1)S(1)}, u32[]{:S(2)}, u32[]{:S(2)}) collective-permute-start(bf16[128,768]{1,0:T(8,128)(2,1)S(1)} %maximum_select_fusion.6), channel_id=1, source_target_pairs={{0,3},{1,0},{2,1},{3,2},{4,7},{5,4},{6,5},{7,6},{8,11},{9,8},{10,9... | collective-permute-start | bytes 589832 | tf_op jit(solution)/shard_map/ppermute | solution.py:44
  130.9 4.7 %collective-permute-done.21 = bf16[128,768]{1,0:T(8,128)(2,1)S(1)} collective-permute-done((bf16[128,768]{1,0:T(8,128)(2,1)S(1)}, bf16[128,768]{1,0:T(8,128)(2,1)S(1)}, u32[]{:S(2)}, u32[]{:S(2)}) %collective-permute-start.21) | collective-permute-done | bytes 196640 | tf_op jit(solution)/shard_map/ppermute | solution.py:44
  135.6 11.8 %collective-permute-done.20 = bf16[128,768]{1,0:T(8,128)(2,1)S(1)} collective-permute-done((bf16[128,768]{1,0:T(8,128)(2,1)S(1)}, bf16[128,768]{1,0:T(8,128)(2,1)S(1)}, u32[]{:S(2)}, u32[]{:S(2)}) %collective-permute-start.20) | collective-permute-done | bytes 196640 | tf_op jit(solution)/shard_map/ppermute | solution.py:44
  149.6 1.6 collective-permute-start.23
  151.2 2.9 collective-permute-start.22
  155.0 1.4 collective-permute-start.28
  159.3 6.6 %collective-permute-done.23 = bf16[128,768]{1,0:T(8,128)(2,1)S(1)} collective-permute-done((bf16[128,768]{1,0:T(8,128)(2,1)S(1)}, bf16[128,768]{1,0:T(8,128)(2,1)S(1)}, u32[]{:S(2)}, u32[]{:S(2)}) %collective-permute-start.23) | collective-permute-done | bytes 196640 | tf_op jit(solution)/shard_map/ppermute | solution.py:44
  167.2 4.9 %collective-permute-start.27 = (bf16[128,192]{1,0:T(8,128)(2,1)S(1)}, bf16[128,192]{1,0:T(8,128)(2,1)S(1)}, u32[]{:S(2)}, u32[]{:S(2)}) collective-permute-start(bf16[128,192]{1,0:T(8,128)(2,1)S(1)} %get-tuple-element.159), channel_id=1, source_target_pairs={{0,3},{1,0},{2,1},{3,2},{4,7},{5,4},{6,5},{7,6},{8,11},{9,8},{10,9... | collective-permute-start | bytes 147464 | tf_op jit(solution)/shard_map/ppermute | solution.py:44
  176.8 2.1 pack.1
  178.9 1.4 collective-permute-start.30
  182.0 17.6 %attend_back.1 = (bf16[1,3,512,2048]{3,2,1,0:T(8,128)(2,1)}, f32[512,192]{1,0:T(8,128)}, bf16[4,384,512]{2,1,0:T(8,128)(2,1)}) custom-call(s32[4]{0:T(128)} %xor_multiply_fusion.starts, bf16[3,512,2048]{2,1,0:T(8,128)(2,1)} %get-tuple-element.60.weights, bf16[512,192]{1,0:T(8,128)(2,1)} %get-tuple-element.52.context, ...), custom_call_target="tpu_custom_call" | custom-call | flops 2013265920 | bytes 18874368 | tf_op jit(solution)/shard_map/attend_back/pallas_call | solution.py:314
  201.5 1.5 fusion.13
  203.9 1.6 convert_add_fusion
  206.3 1.5 collective-permute-start.32
  211.0 1.8 copy.43
  214.0 2.1 collective-permute-start.36
  216.1 1.6 collective-permute-start.37
  218.0 3.1 collective-permute-start.38
  222.1 2.1 convert_bitcast_fusion
  224.2 3.9 %collective-permute-done.36 = bf16[128,1536]{1,0:T(8,128)(2,1)S(1)} collective-permute-done((bf16[128,1536]{1,0:T(8,128)(2,1)}, bf16[128,1536]{1,0:T(8,128)(2,1)S(1)}, u32[]{:S(2)}, u32[]{:S(2)}) %collective-permute-start.36) | collective-permute-done | bytes 393248 | tf_op jit(solution)/shard_map/ppermute | solution.py:44
  228.2 15.9 %collective-permute-done.37 = bf16[128,1536]{1,0:T(8,128)(2,1)S(1)} collective-permute-done((bf16[128,1536]{1,0:T(8,128)(2,1)}, bf16[128,1536]{1,0:T(8,128)(2,1)S(1)}, u32[]{:S(2)}, u32[]{:S(2)}) %collective-permute-start.37) | collective-permute-done | bytes 393248 | tf_op jit(solution)/shard_map/ppermute | solution.py:44
  244.2 1.9 fusion.87
  250.7 8.9 %collective-permute-start.41 = (bf16[128,768]{1,0:T(8,128)(2,1)S(1)}, bf16[128,768]{1,0:T(8,128)(2,1)S(1)}, u32[]{:S(2)}, u32[]{:S(2)}) collective-permute-start(bf16[128,768]{1,0:T(8,128)(2,1)S(1)} %get-tuple-element.119), channel_id=1, source_target_pairs={{0,1},{1,2},{2,3},{3,0},{4,5},{5,6},{6,7},{7,4},{8,9},{9,10},{10,1... | collective-permute-start | bytes 589832 | tf_op jit(solution)/shard_map/ppermute | solution.py:44
  260.5 1.6 collective-permute-start.39
  262.1 1.5 collective-permute-start.42
  268.3 4.6 %collective-permute-done.40 = bf16[128,768]{1,0:T(8,128)(2,1)S(1)} collective-permute-done((bf16[128,768]{1,0:T(8,128)(2,1)S(1)}, bf16[128,768]{1,0:T(8,128)(2,1)S(1)}, u32[]{:S(2)}, u32[]{:S(2)}) %collective-permute-start.40) | collective-permute-done | bytes 196640 | tf_op jit(solution)/shard_map/ppermute | solution.py:44
  274.5 4.2 %collective-permute-done.45 = f32[384]{0:T(512)S(1)} collective-permute-done((f32[384]{0:T(512)S(1)}, f32[384]{0:T(512)S(1)}, u32[]{:S(2)}, u32[]{:S(2)}) %collective-permute-start.45) | collective-permute-done | bytes 1568 | tf_op jit(solution)/shard_map/ppermute | solution.py:49
  278.7 1.5 collective-permute-start.56
  280.2 3.7 %collective-permute-start.50 = (bf16[128,768]{1,0:T(8,128)(2,1)S(1)}, bf16[128,768]{1,0:T(8,128)(2,1)S(1)}, u32[]{:S(2)}, u32[]{:S(2)}) collective-permute-start(bf16[128,768]{1,0:T(8,128)(2,1)S(1)} %fusion.52), channel_id=1, source_target_pairs={{0,3},{1,0},{2,1},{3,2},{4,7},{5,4},{6,5},{7,6},{8,11},{9,8},{10,9... | collective-permute-start | bytes 589832 | tf_op jit(solution)/shard_map/ppermute | solution.py:44
  285.2 1.5 collective-permute-start.58
  286.7 14.7 %collective-permute-done.58 = f32[384]{0:T(512)S(1)} collective-permute-done((f32[384]{0:T(512)S(1)}, f32[384]{0:T(512)S(1)}, u32[]{:S(2)}, u32[]{:S(2)}) %collective-permute-start.58) | collective-permute-done | bytes 1568 | tf_op jit(solution)/shard_map/ppermute | solution.py:49
  302.0 3.3 collective-permute-start.47
  305.9 1.4 collective-permute-done.47
  307.3 3.0 collective-permute-start.49
  312.2 5.5 %collective-permute-start.48 = (bf16[128,768]{1,0:T(8,128)(2,1)S(1)}, bf16[128,768]{1,0:T(8,128)(2,1)S(1)}, u32[]{:S(2)}, u32[]{:S(2)}) collective-permute-start(bf16[128,768]{1,0:T(8,128)(2,1)S(1)} %fusion.52), channel_id=1, source_target_pairs={{0,1},{1,2},{2,3},{3,0},{4,5},{5,6},{6,7},{7,4},{8,9},{9,10},{10,1... | collective-permute-start | bytes 589832 | tf_op jit(solution)/shard_map/ppermute | solution.py:44
  317.7 1.5 collective-permute-start.51
  319.2 2.2 convert_add_fusion.2
  321.4 2.2 convert_add_fusion.1
  323.8 2.2 collective-permute-done.51
  (297 shorter events, 66.6 us)
Async XLA Ops:
  1.8 13.2 %collective-permute-start.1 = (bf16[576,384]{1,0:T(8,128)(2,1)S(1)}, bf16[576,384]{1,0:T(8,128)(2,1)S(1)}, u32[]{:S(2)}, u32[]{:S(2)}) collective-permute-start(bf16[576,384]{1,0:T(8,128)(2,1)S(1)} %pad_maximum_fusion.6), channel_id=1, source_target_pairs={{0,16},{16,0},{1,17},{17,1},{2,18},{18,2},{3,19},{19,3},{4,20},{20... | collective-permute-start | bytes 1327112 | tf_op jit(solution)/shard_map/ppermute | solution.py:49
  7.1 41.0 %copy-start.5 = (bf16[512,768]{1,0:T(8,128)(2,1)}, bf16[512,768]{1,0:T(8,128)(2,1)S(1)}, u32[]{:S(2)}) copy-start(bf16[512,768]{1,0:T(8,128)(2,1)S(1)} %maximum_select_fusion) | copy-start | bytes 2359300
  16.4 33.7 %copy-start.2 = (bf16[1,512,384]{2,1,0:T(8,128)(2,1)}, bf16[1,512,384]{2,1,0:T(8,128)(2,1)S(1)}, u32[]{:S(2)}) copy-start(bf16[1,512,384]{2,1,0:T(8,128)(2,1)S(1)} %fusion.7.refs_0_) | copy-start | bytes 1179652
  16.5 31.6 %copy-start.49 = (f32[192]{0:T(256)S(1)}, f32[192]{0:T(256)}, u32[]{:S(2)}) copy-start(f32[192]{0:T(256)} %param.30) | copy-start | bytes 2308
  16.5 10.3 %collective-permute-start.2 = (bf16[1,512,384]{2,1,0:T(8,128)(2,1)S(1)}, bf16[1,512,384]{2,1,0:T(8,128)(2,1)S(1)}, u32[]{:S(2)}, u32[]{:S(2)}) collective-permute-start(bf16[1,512,384]{2,1,0:T(8,128)(2,1)S(1)} %fusion.7.refs_0_), channel_id=1, source_target_pairs={{0,8},{4,12},{8,0},{12,4},{1,9},{5,13},{9,1},{13,5},{2,10},{6,14},... | collective-permute-start | bytes 1179656 | tf_op jit(solution)/shard_map/ppermute | solution.py:49
  27.8 18.7 %collective-permute-start.3 = (bf16[2,512,384]{2,1,0:T(8,128)(2,1)}, bf16[2,512,384]{2,1,0:T(8,128)(2,1)S(1)}, u32[]{:S(2)}, u32[]{:S(2)}) collective-permute-start(bf16[2,512,384]{2,1,0:T(8,128)(2,1)} %pad_maximum_fusion), channel_id=1, source_target_pairs={{0,4},{4,0},{8,12},{12,8},{1,5},{5,1},{9,13},{13,9},{2,6},{6,2},{1... | collective-permute-start | bytes 2359304 | tf_op jit(solution)/shard_map/ppermute | solution.py:49
  27.8 9.2 %collective-permute-start.6 = (bf16[192,384]{1,0:T(8,128)(2,1)S(1)}, bf16[192,384]{1,0:T(8,128)(2,1)S(1)}, u32[]{:S(2)}, u32[]{:S(2)}) collective-permute-start(bf16[192,384]{1,0:T(8,128)(2,1)S(1)} %copy-done.24), channel_id=1, source_target_pairs={{0,3},{1,0},{2,1},{3,2},{4,7},{5,4},{6,5},{7,6},{8,11},{9,8},{10,9... | collective-permute-start | bytes 442376 | tf_op jit(solution)/shard_map/ppermute | solution.py:44
  31.4 13.3 %collective-permute-start.5 = (bf16[192,384]{1,0:T(8,128)(2,1)S(1)}, bf16[192,384]{1,0:T(8,128)(2,1)}, u32[]{:S(2)}, u32[]{:S(2)}) collective-permute-start(bf16[192,384]{1,0:T(8,128)(2,1)S(1)} %copy-done.24), channel_id=1, source_target_pairs={{0,2},{1,3},{2,0},{3,1},{4,6},{5,7},{6,4},{7,5},{8,10},{9,11},{10,... | collective-permute-start | bytes 442376 | tf_op jit(solution)/shard_map/ppermute | solution.py:44
  31.4 13.3 %collective-permute-start.4 = (bf16[192,384]{1,0:T(8,128)(2,1)S(1)}, bf16[192,384]{1,0:T(8,128)(2,1)}, u32[]{:S(2)}, u32[]{:S(2)}) collective-permute-start(bf16[192,384]{1,0:T(8,128)(2,1)S(1)} %copy-done.24), channel_id=1, source_target_pairs={{0,1},{1,2},{2,3},{3,0},{4,5},{5,6},{6,7},{7,4},{8,9},{9,10},{10,1... | collective-permute-start | bytes 442376 | tf_op jit(solution)/shard_map/ppermute | solution.py:44
  33.1 75.9 %collective-permute-start = (f32[]{:T(128)}, f32[]{:T(128)}, u32[]{:S(2)}, u32[]{:S(2)}) collective-permute-start(f32[]{:T(128)} %convert_element_type.217), channel_id=1, source_target_pairs={{0,16},{16,0},{1,17},{17,1},{2,18},{18,2},{3,19},{19,3},{4,20},{20... | collective-permute-start | bytes 20 | tf_op jit(solution)/shard_map/ppermute | solution.py:49
  46.6 19.1 %collective-permute-start.7 = (bf16[768,384]{1,0:T(8,128)(2,1)}, bf16[768,384]{1,0:T(8,128)(2,1)}, u32[]{:S(2)}, u32[]{:S(2)}) collective-permute-start(bf16[768,384]{1,0:T(8,128)(2,1)} %pad_maximum_fusion.4), channel_id=1, source_target_pairs={{0,16},{16,0},{1,17},{17,1},{2,18},{18,2},{3,19},{19,3},{4,20},{20... | collective-permute-start | bytes 1769480 | tf_op jit(solution)/shard_map/ppermute | solution.py:49
  65.7 16.3 %collective-permute-start.14 = (bf16[384,768]{1,0:T(8,128)(2,1)S(1)}, bf16[384,768]{1,0:T(8,128)(2,1)S(1)}, u32[]{:S(2)}, u32[]{:S(2)}) collective-permute-start(bf16[384,768]{1,0:T(8,128)(2,1)S(1)} %copy-done.18), channel_id=1, source_target_pairs={{0,16},{16,0},{1,17},{17,1},{2,18},{18,2},{3,19},{19,3},{4,20},{20... | collective-permute-start | bytes 1769480 | tf_op jit(solution)/shard_map/ppermute | solution.py:49
  66.4 6.1 %collective-permute-start.10 = (bf16[128,192]{1,0:T(8,128)(2,1)S(1)}, bf16[128,192]{1,0:T(8,128)(2,1)S(1)}, u32[]{:S(2)}, u32[]{:S(2)}) collective-permute-start(bf16[128,192]{1,0:T(8,128)(2,1)S(1)} %get-tuple-element.151), channel_id=1, source_target_pairs={{0,3},{1,0},{2,1},{3,2},{4,7},{5,4},{6,5},{7,6},{8,11},{9,8},{10,9... | collective-permute-start | bytes 147464 | tf_op jit(solution)/shard_map/ppermute | solution.py:44
  67.6 6.4 %collective-permute-start.9 = (bf16[128,192]{1,0:T(8,128)(2,1)S(1)}, bf16[128,192]{1,0:T(8,128)(2,1)S(1)}, u32[]{:S(2)}, u32[]{:S(2)}) collective-permute-start(bf16[128,192]{1,0:T(8,128)(2,1)S(1)} %get-tuple-element.152), channel_id=1, source_target_pairs={{0,2},{1,3},{2,0},{3,1},{4,6},{5,7},{6,4},{7,5},{8,10},{9,11},{10,... | collective-permute-start | bytes 147464 | tf_op jit(solution)/shard_map/ppermute | solution.py:44
  69.2 6.1 %collective-permute-start.8 = (bf16[128,192]{1,0:T(8,128)(2,1)S(1)}, bf16[128,192]{1,0:T(8,128)(2,1)S(1)}, u32[]{:S(2)}, u32[]{:S(2)}) collective-permute-start(bf16[128,192]{1,0:T(8,128)(2,1)S(1)} %get-tuple-element.153), channel_id=1, source_target_pairs={{0,1},{1,2},{2,3},{3,0},{4,5},{5,6},{6,7},{7,4},{8,9},{9,10},{10,1... | collective-permute-start | bytes 147464 | tf_op jit(solution)/shard_map/ppermute | solution.py:44
  72.5 20.4 %collective-permute-start.15 = (bf16[768,384]{1,0:T(8,128)(2,1)S(1)}, bf16[768,384]{1,0:T(8,128)(2,1)S(1)}, u32[]{:S(2)}, u32[]{:S(2)}) collective-permute-start(bf16[768,384]{1,0:T(8,128)(2,1)S(1)} %copy-done.19), channel_id=1, source_target_pairs={{0,16},{16,0},{1,17},{17,1},{2,18},{18,2},{3,19},{19,3},{4,20},{20... | collective-permute-start | bytes 1769480 | tf_op jit(solution)/shard_map/ppermute | solution.py:49
  76.8 16.2 %collective-permute-start.13 = (bf16[128,768]{1,0:T(8,128)(2,1)S(1)}, bf16[128,768]{1,0:T(8,128)(2,1)S(1)}, u32[]{:S(2)}, u32[]{:S(2)}) collective-permute-start(bf16[128,768]{1,0:T(8,128)(2,1)S(1)} %maximum_select_fusion.5), channel_id=1, source_target_pairs={{0,3},{1,0},{2,1},{3,2},{4,7},{5,4},{6,5},{7,6},{8,11},{9,8},{10,9... | collective-permute-start | bytes 589832 | tf_op jit(solution)/shard_map/ppermute | solution.py:44
  78.2 16.8 %collective-permute-start.12 = (bf16[128,768]{1,0:T(8,128)(2,1)S(1)}, bf16[128,768]{1,0:T(8,128)(2,1)S(1)}, u32[]{:S(2)}, u32[]{:S(2)}) collective-permute-start(bf16[128,768]{1,0:T(8,128)(2,1)S(1)} %maximum_select_fusion.5), channel_id=1, source_target_pairs={{0,2},{1,3},{2,0},{3,1},{4,6},{5,7},{6,4},{7,5},{8,10},{9,11},{10,... | collective-permute-start | bytes 589832 | tf_op jit(solution)/shard_map/ppermute | solution.py:44
  82.0 13.0 %collective-permute-start.11 = (bf16[128,768]{1,0:T(8,128)(2,1)S(1)}, bf16[128,768]{1,0:T(8,128)(2,1)S(1)}, u32[]{:S(2)}, u32[]{:S(2)}) collective-permute-start(bf16[128,768]{1,0:T(8,128)(2,1)S(1)} %maximum_select_fusion.5), channel_id=1, source_target_pairs={{0,1},{1,2},{2,3},{3,0},{4,5},{5,6},{6,7},{7,4},{8,9},{9,10},{10,1... | collective-permute-start | bytes 589832 | tf_op jit(solution)/shard_map/ppermute | solution.py:44
  103.5 9.9 %collective-permute-start.18 = (bf16[128,768]{1,0:T(8,128)(2,1)}, bf16[128,768]{1,0:T(8,128)(2,1)}, u32[]{:S(2)}, u32[]{:S(2)}) collective-permute-start(bf16[128,768]{1,0:T(8,128)(2,1)} %get-tuple-element.129), channel_id=1, source_target_pairs={{0,1},{1,2},{2,3},{3,0},{4,5},{5,6},{6,7},{7,4},{8,9},{9,10},{10,1... | collective-permute-start | bytes 589832 | tf_op jit(solution)/shard_map/ppermute | solution.py:44
  103.5 15.8 %collective-permute-start.17 = (bf16[128,768]{1,0:T(8,128)(2,1)}, bf16[128,768]{1,0:T(8,128)(2,1)}, u32[]{:S(2)}, u32[]{:S(2)}) collective-permute-start(bf16[128,768]{1,0:T(8,128)(2,1)} %get-tuple-element.130), channel_id=1, source_target_pairs={{0,2},{1,3},{2,0},{3,1},{4,6},{5,7},{6,4},{7,5},{8,10},{9,11},{10,... | collective-permute-start | bytes 589832 | tf_op jit(solution)/shard_map/ppermute | solution.py:44
  104.8 14.5 %collective-permute-start.16 = (bf16[128,768]{1,0:T(8,128)(2,1)}, bf16[128,768]{1,0:T(8,128)(2,1)}, u32[]{:S(2)}, u32[]{:S(2)}) collective-permute-start(bf16[128,768]{1,0:T(8,128)(2,1)} %get-tuple-element.128), channel_id=1, source_target_pairs={{0,3},{1,0},{2,1},{3,2},{4,7},{5,4},{6,5},{7,6},{8,11},{9,8},{10,9... | collective-permute-start | bytes 589832 | tf_op jit(solution)/shard_map/ppermute | solution.py:44
  120.6 26.8 %copy-start.52 = (f32[512,768]{1,0:T(8,128)S(1)}, f32[512,768]{1,0:T(8,128)}, u32[]{:S(2)}) copy-start(f32[512,768]{1,0:T(8,128)} %get-tuple-element.170) | copy-start | bytes 4718596
  124.0 11.6 %collective-permute-start.21 = (bf16[128,768]{1,0:T(8,128)(2,1)S(1)}, bf16[128,768]{1,0:T(8,128)(2,1)S(1)}, u32[]{:S(2)}, u32[]{:S(2)}) collective-permute-start(bf16[128,768]{1,0:T(8,128)(2,1)S(1)} %maximum_select_fusion.6), channel_id=1, source_target_pairs={{0,3},{1,0},{2,1},{3,2},{4,7},{5,4},{6,5},{7,6},{8,11},{9,8},{10,9... | collective-permute-start | bytes 589832 | tf_op jit(solution)/shard_map/ppermute | solution.py:44
  130.2 17.2 %collective-permute-start.20 = (bf16[128,768]{1,0:T(8,128)(2,1)S(1)}, bf16[128,768]{1,0:T(8,128)(2,1)S(1)}, u32[]{:S(2)}, u32[]{:S(2)}) collective-permute-start(bf16[128,768]{1,0:T(8,128)(2,1)S(1)} %maximum_select_fusion.6), channel_id=1, source_target_pairs={{0,2},{1,3},{2,0},{3,1},{4,6},{5,7},{6,4},{7,5},{8,10},{9,11},{10,... | collective-permute-start | bytes 589832 | tf_op jit(solution)/shard_map/ppermute | solution.py:44
  130.3 17.2 %collective-permute-start.19 = (bf16[128,768]{1,0:T(8,128)(2,1)S(1)}, bf16[128,768]{1,0:T(8,128)(2,1)S(1)}, u32[]{:S(2)}, u32[]{:S(2)}) collective-permute-start(bf16[128,768]{1,0:T(8,128)(2,1)S(1)} %maximum_select_fusion.6), channel_id=1, source_target_pairs={{0,1},{1,2},{2,3},{3,0},{4,5},{5,6},{6,7},{7,4},{8,9},{9,10},{10,1... | collective-permute-start | bytes 589832 | tf_op jit(solution)/shard_map/ppermute | solution.py:44
  149.5 9.7 %collective-permute-start.24 = (bf16[128,768]{1,0:T(8,128)(2,1)S(1)}, bf16[128,768]{1,0:T(8,128)(2,1)S(1)}, u32[]{:S(2)}, u32[]{:S(2)}) collective-permute-start(bf16[128,768]{1,0:T(8,128)(2,1)S(1)} %get-tuple-element.126), channel_id=1, source_target_pairs={{0,1},{1,2},{2,3},{3,0},{4,5},{5,6},{6,7},{7,4},{8,9},{9,10},{10,1... | collective-permute-start | bytes 589832 | tf_op jit(solution)/shard_map/ppermute | solution.py:44
  149.6 16.2 %collective-permute-start.23 = (bf16[128,768]{1,0:T(8,128)(2,1)S(1)}, bf16[128,768]{1,0:T(8,128)(2,1)S(1)}, u32[]{:S(2)}, u32[]{:S(2)}) collective-permute-start(bf16[128,768]{1,0:T(8,128)(2,1)S(1)} %get-tuple-element.127), channel_id=1, source_target_pairs={{0,2},{1,3},{2,0},{3,1},{4,6},{5,7},{6,4},{7,5},{8,10},{9,11},{10,... | collective-permute-start | bytes 589832 | tf_op jit(solution)/shard_map/ppermute | solution.py:44
  151.2 14.6 %collective-permute-start.22 = (bf16[128,768]{1,0:T(8,128)(2,1)S(1)}, bf16[128,768]{1,0:T(8,128)(2,1)S(1)}, u32[]{:S(2)}, u32[]{:S(2)}) collective-permute-start(bf16[128,768]{1,0:T(8,128)(2,1)S(1)} %get-tuple-element.125), channel_id=1, source_target_pairs={{0,3},{1,0},{2,1},{3,2},{4,7},{5,4},{6,5},{7,6},{8,11},{9,8},{10,9... | collective-permute-start | bytes 589832 | tf_op jit(solution)/shard_map/ppermute | solution.py:44
  155.0 26.2 %collective-permute-start.28 = (bf16[768,384]{1,0:T(8,128)(2,1)S(1)}, bf16[768,384]{1,0:T(8,128)(2,1)}, u32[]{:S(2)}, u32[]{:S(2)}) collective-permute-start(bf16[768,384]{1,0:T(8,128)(2,1)S(1)} %split.97), channel_id=1, source_target_pairs={{0,16},{16,0},{1,17},{17,1},{2,18},{18,2},{3,19},{19,3},{4,20},{20... | collective-permute-start | bytes 1769480 | tf_op jit(solution)/shard_map/ppermute | solution.py:49
  157.4 24.6 %collective-permute-start.29 = (bf16[384,768]{1,0:T(8,128)(2,1)S(1)}, bf16[384,768]{1,0:T(8,128)(2,1)}, u32[]{:S(2)}, u32[]{:S(2)}) collective-permute-start(bf16[384,768]{1,0:T(8,128)(2,1)S(1)} %split.96), channel_id=1, source_target_pairs={{0,16},{16,0},{1,17},{17,1},{2,18},{18,2},{3,19},{19,3},{4,20},{20... | collective-permute-start | bytes 1769480 | tf_op jit(solution)/shard_map/ppermute | solution.py:49
  167.2 11.7 %collective-permute-start.27 = (bf16[128,192]{1,0:T(8,128)(2,1)S(1)}, bf16[128,192]{1,0:T(8,128)(2,1)S(1)}, u32[]{:S(2)}, u32[]{:S(2)}) collective-permute-start(bf16[128,192]{1,0:T(8,128)(2,1)S(1)} %get-tuple-element.159), channel_id=1, source_target_pairs={{0,3},{1,0},{2,1},{3,2},{4,7},{5,4},{6,5},{7,6},{8,11},{9,8},{10,9... | collective-permute-start | bytes 147464 | tf_op jit(solution)/shard_map/ppermute | solution.py:44
  172.1 8.3 %collective-permute-start.26 = (bf16[128,192]{1,0:T(8,128)(2,1)S(1)}, bf16[128,192]{1,0:T(8,128)(2,1)S(1)}, u32[]{:S(2)}, u32[]{:S(2)}) collective-permute-start(bf16[128,192]{1,0:T(8,128)(2,1)S(1)} %get-tuple-element.160), channel_id=1, source_target_pairs={{0,2},{1,3},{2,0},{3,1},{4,6},{5,7},{6,4},{7,5},{8,10},{9,11},{10,... | collective-permute-start | bytes 147464 | tf_op jit(solution)/shard_map/ppermute | solution.py:44
  172.6 7.8 %collective-permute-start.25 = (bf16[128,192]{1,0:T(8,128)(2,1)S(1)}, bf16[128,192]{1,0:T(8,128)(2,1)S(1)}, u32[]{:S(2)}, u32[]{:S(2)}) collective-permute-start(bf16[128,192]{1,0:T(8,128)(2,1)S(1)} %get-tuple-element.161), channel_id=1, source_target_pairs={{0,1},{1,2},{2,3},{3,0},{4,5},{5,6},{6,7},{7,4},{8,9},{9,10},{10,1... | collective-permute-start | bytes 147464 | tf_op jit(solution)/shard_map/ppermute | solution.py:44
  178.9 20.7 %collective-permute-start.30 = (f32[12,768]{1,0:T(8,128)}, f32[12,768]{1,0:T(8,128)S(1)}, u32[]{:S(2)}, u32[]{:S(2)}) collective-permute-start(f32[12,768]{1,0:T(8,128)} %pack.1), channel_id=1, source_target_pairs={{0,16},{16,0},{1,17},{17,1},{2,18},{18,2},{3,19},{19,3},{4,20},{20... | collective-permute-start | bytes 110600 | tf_op jit(solution)/shard_map/ppermute | solution.py:49
  201.4 2.5 collective-permute-start.31
  203.0 41.1 %collective-permute-start.33 = (bf16[384,768]{1,0:T(8,128)(2,1)S(1)}, bf16[384,768]{1,0:T(8,128)(2,1)}, u32[]{:S(2)}, u32[]{:S(2)}) collective-permute-start(bf16[384,768]{1,0:T(8,128)(2,1)S(1)} %fusion.13), channel_id=1, source_target_pairs={{0,4},{4,0},{8,12},{12,8},{1,5},{5,1},{9,13},{13,9},{2,6},{6,2},{1... | collective-permute-start | bytes 1769480 | tf_op jit(solution)/shard_map/ppermute | solution.py:49
  206.3 11.7 %collective-permute-start.32 = (bf16[1,384,512]{2,1,0:T(8,128)(2,1)}, bf16[1,384,512]{2,1,0:T(8,128)(2,1)}, u32[]{:S(2)}, u32[]{:S(2)}) collective-permute-start(bf16[1,384,512]{2,1,0:T(8,128)(2,1)} %slice.275), channel_id=1, source_target_pairs={{0,8},{4,12},{8,0},{12,4},{1,9},{5,13},{9,1},{13,5},{2,10},{6,14},... | collective-permute-start | bytes 1179656 | tf_op jit(solution)/shard_map/ppermute | solution.py:49
  209.0 35.1 %collective-permute-start.34 = (bf16[768,384]{1,0:T(8,128)(2,1)S(1)}, bf16[768,384]{1,0:T(8,128)(2,1)}, u32[]{:S(2)}, u32[]{:S(2)}) collective-permute-start(bf16[768,384]{1,0:T(8,128)(2,1)S(1)} %fusion.12), channel_id=1, source_target_pairs={{0,4},{4,0},{8,12},{12,8},{1,5},{5,1},{9,13},{13,9},{2,6},{6,2},{1... | collective-permute-start | bytes 1769480 | tf_op jit(solution)/shard_map/ppermute | solution.py:49
  209.8 6.3 %collective-permute-start.35 = (f32[12,768]{1,0:T(8,128)}, f32[12,768]{1,0:T(8,128)}, u32[]{:S(2)}, u32[]{:S(2)}) collective-permute-start(f32[12,768]{1,0:T(8,128)} %add.312), channel_id=1, source_target_pairs={{0,4},{4,0},{8,12},{12,8},{1,5},{5,1},{9,13},{13,9},{2,6},{6,2},{1... | collective-permute-start | bytes 110600 | tf_op jit(solution)/shard_map/ppermute | solution.py:49
  214.0 30.2 %copy-start.12 = (bf16[512,192]{0,1:T(8,128)(2,1)S(1)}, bf16[512,192]{0,1:T(8,128)(2,1)}, u32[]{:S(2)}) copy-start(bf16[512,192]{0,1:T(8,128)(2,1)} %copy.43) | copy-start | bytes 589828
  214.0 14.2 %collective-permute-start.36 = (bf16[128,1536]{1,0:T(8,128)(2,1)}, bf16[128,1536]{1,0:T(8,128)(2,1)S(1)}, u32[]{:S(2)}, u32[]{:S(2)}) collective-permute-start(bf16[128,1536]{1,0:T(8,128)(2,1)} %pad_maximum_fusion.7), channel_id=1, source_target_pairs={{0,1},{1,2},{2,3},{3,0},{4,5},{5,6},{6,7},{7,4},{8,9},{9,10},{10,1... | collective-permute-start | bytes 1179656 | tf_op jit(solution)/shard_map/ppermute | solution.py:44
  216.1 28.0 %collective-permute-start.37 = (bf16[128,1536]{1,0:T(8,128)(2,1)}, bf16[128,1536]{1,0:T(8,128)(2,1)S(1)}, u32[]{:S(2)}, u32[]{:S(2)}) collective-permute-start(bf16[128,1536]{1,0:T(8,128)(2,1)} %pad_maximum_fusion.7), channel_id=1, source_target_pairs={{0,2},{1,3},{2,0},{3,1},{4,6},{5,7},{6,4},{7,5},{8,10},{9,11},{10,... | collective-permute-start | bytes 1179656 | tf_op jit(solution)/shard_map/ppermute | solution.py:44
  218.0 26.1 %collective-permute-start.38 = (bf16[128,1536]{1,0:T(8,128)(2,1)}, bf16[128,1536]{1,0:T(8,128)(2,1)S(1)}, u32[]{:S(2)}, u32[]{:S(2)}) collective-permute-start(bf16[128,1536]{1,0:T(8,128)(2,1)} %pad_maximum_fusion.7), channel_id=1, source_target_pairs={{0,3},{1,0},{2,1},{3,2},{4,7},{5,4},{6,5},{7,6},{8,11},{9,8},{10,9... | collective-permute-start | bytes 1179656 | tf_op jit(solution)/shard_map/ppermute | solution.py:44
  250.7 16.9 %collective-permute-start.41 = (bf16[128,768]{1,0:T(8,128)(2,1)S(1)}, bf16[128,768]{1,0:T(8,128)(2,1)S(1)}, u32[]{:S(2)}, u32[]{:S(2)}) collective-permute-start(bf16[128,768]{1,0:T(8,128)(2,1)S(1)} %get-tuple-element.119), channel_id=1, source_target_pairs={{0,1},{1,2},{2,3},{3,0},{4,5},{5,6},{6,7},{7,4},{8,9},{9,10},{10,1... | collective-permute-start | bytes 589832 | tf_op jit(solution)/shard_map/ppermute | solution.py:44
  259.6 13.3 %collective-permute-start.40 = (bf16[128,768]{1,0:T(8,128)(2,1)S(1)}, bf16[128,768]{1,0:T(8,128)(2,1)S(1)}, u32[]{:S(2)}, u32[]{:S(2)}) collective-permute-start(bf16[128,768]{1,0:T(8,128)(2,1)S(1)} %get-tuple-element.120), channel_id=1, source_target_pairs={{0,2},{1,3},{2,0},{3,1},{4,6},{5,7},{6,4},{7,5},{8,10},{9,11},{10,... | collective-permute-start | bytes 589832 | tf_op jit(solution)/shard_map/ppermute | solution.py:44
  260.5 13.3 %collective-permute-start.39 = (bf16[128,768]{1,0:T(8,128)(2,1)S(1)}, bf16[128,768]{1,0:T(8,128)(2,1)S(1)}, u32[]{:S(2)}, u32[]{:S(2)}) collective-permute-start(bf16[128,768]{1,0:T(8,128)(2,1)S(1)} %get-tuple-element.118), channel_id=1, source_target_pairs={{0,3},{1,0},{2,1},{3,2},{4,7},{5,4},{6,5},{7,6},{8,11},{9,8},{10,9... | collective-permute-start | bytes 589832 | tf_op jit(solution)/shard_map/ppermute | solution.py:44
  262.1 18.1 %collective-permute-start.42 = (bf16[192,384]{1,0:T(8,128)(2,1)S(1)}, bf16[192,384]{1,0:T(8,128)(2,1)S(1)}, u32[]{:S(2)}, u32[]{:S(2)}) collective-permute-start(bf16[192,384]{1,0:T(8,128)(2,1)S(1)} %split.99), channel_id=1, source_target_pairs={{0,16},{16,0},{1,17},{17,1},{2,18},{18,2},{3,19},{19,3},{4,20},{20... | collective-permute-start | bytes 442376 | tf_op jit(solution)/shard_map/ppermute | solution.py:49
  264.4 15.8 %collective-permute-start.43 = (f32[12,768]{1,0:T(8,128)S(1)}, f32[12,768]{1,0:T(8,128)S(1)}, u32[]{:S(2)}, u32[]{:S(2)}) collective-permute-start(f32[12,768]{1,0:T(8,128)S(1)} %add.313), channel_id=1, source_target_pairs={{0,8},{4,12},{8,0},{12,4},{1,9},{5,13},{9,1},{13,5},{2,10},{6,14},... | collective-permute-start | bytes 110600 | tf_op jit(solution)/shard_map/ppermute | solution.py:49
  267.6 12.6 %collective-permute-start.44 = (bf16[576,384]{1,0:T(8,128)(2,1)S(1)}, bf16[576,384]{1,0:T(8,128)(2,1)S(1)}, u32[]{:S(2)}, u32[]{:S(2)}) collective-permute-start(bf16[576,384]{1,0:T(8,128)(2,1)S(1)} %split.98), channel_id=1, source_target_pairs={{0,16},{16,0},{1,17},{17,1},{2,18},{18,2},{3,19},{19,3},{4,20},{20... | collective-permute-start | bytes 1327112 | tf_op jit(solution)/shard_map/ppermute | solution.py:49
  273.0 5.7 %collective-permute-start.45 = (f32[384]{0:T(512)S(1)}, f32[384]{0:T(512)S(1)}, u32[]{:S(2)}, u32[]{:S(2)}) collective-permute-start(f32[384]{0:T(512)S(1)} %pad_maximum_fusion.17), channel_id=1, source_target_pairs={{0,16},{16,0},{1,17},{17,1},{2,18},{18,2},{3,19},{19,3},{4,20},{20... | collective-permute-start | bytes 4616 | tf_op jit(solution)/shard_map/ppermute | solution.py:49
  273.8 43.9 %collective-permute-start.55 = (bf16[384,768]{1,0:T(8,128)(2,1)S(1)}, bf16[384,768]{1,0:T(8,128)(2,1)}, u32[]{:S(2)}, u32[]{:S(2)}) collective-permute-start(bf16[384,768]{1,0:T(8,128)(2,1)S(1)} %add_convert_fusion.1), channel_id=1, source_target_pairs={{0,8},{4,12},{8,0},{12,4},{1,9},{5,13},{9,1},{13,5},{2,10},{6,14},... | collective-permute-start | bytes 1769480 | tf_op jit(solution)/shard_map/ppermute | solution.py:49
  278.7 42.8 %collective-permute-start.56 = (bf16[768,384]{1,0:T(8,128)(2,1)S(1)}, bf16[768,384]{1,0:T(8,128)(2,1)}, u32[]{:S(2)}, u32[]{:S(2)}) collective-permute-start(bf16[768,384]{1,0:T(8,128)(2,1)S(1)} %add_convert_fusion), channel_id=1, source_target_pairs={{0,8},{4,12},{8,0},{12,4},{1,9},{5,13},{9,1},{13,5},{2,10},{6,14},... | collective-permute-start | bytes 1769480 | tf_op jit(solution)/shard_map/ppermute | solution.py:49
  280.2 43.5 %collective-permute-start.50 = (bf16[128,768]{1,0:T(8,128)(2,1)S(1)}, bf16[128,768]{1,0:T(8,128)(2,1)S(1)}, u32[]{:S(2)}, u32[]{:S(2)}) collective-permute-start(bf16[128,768]{1,0:T(8,128)(2,1)S(1)} %fusion.52), channel_id=1, source_target_pairs={{0,3},{1,0},{2,1},{3,2},{4,7},{5,4},{6,5},{7,6},{8,11},{9,8},{10,9... | collective-permute-start | bytes 589832 | tf_op jit(solution)/shard_map/ppermute | solution.py:44
  283.9 18.1 %collective-permute-start.46 = (f32[12,768]{1,0:T(8,128)S(1)}, f32[12,768]{1,0:T(8,128)S(1)}, u32[]{:S(2)}, u32[]{:S(2)}) collective-permute-start(f32[12,768]{1,0:T(8,128)S(1)} %add.318), channel_id=1, source_target_pairs={{0,1},{1,0},{2,3},{3,2},{4,5},{5,4},{6,7},{7,6},{8,9},{9,8},{10,11... | collective-permute-start | bytes 110600 | tf_op jit(solution)/shard_map/ppermute | solution.py:49
  284.0 1.2 collective-permute-start.57
  285.2 16.3 %collective-permute-start.58 = (f32[384]{0:T(512)S(1)}, f32[384]{0:T(512)S(1)}, u32[]{:S(2)}, u32[]{:S(2)}) collective-permute-start(f32[384]{0:T(512)S(1)} %add.332), channel_id=1, source_target_pairs={{0,8},{4,12},{8,0},{12,4},{1,9},{5,13},{9,1},{13,5},{2,10},{6,14},... | collective-permute-start | bytes 4616 | tf_op jit(solution)/shard_map/ppermute | solution.py:49
  301.4 10.7 %collective-permute-start.53 = (bf16[192,384]{1,0:T(8,128)(2,1)S(1)}, bf16[192,384]{1,0:T(8,128)(2,1)S(1)}, u32[]{:S(2)}, u32[]{:S(2)}) collective-permute-start(bf16[192,384]{1,0:T(8,128)(2,1)S(1)} %fusion.59), channel_id=1, source_target_pairs={{0,8},{4,12},{8,0},{12,4},{1,9},{5,13},{9,1},{13,5},{2,10},{6,14},... | collective-permute-start | bytes 442376 | tf_op jit(solution)/shard_map/ppermute | solution.py:49
  302.0 5.3 %collective-permute-start.47 = (f32[12,768]{1,0:T(8,128)S(1)}, f32[12,768]{1,0:T(8,128)S(1)}, u32[]{:S(2)}, u32[]{:S(2)}) collective-permute-start(f32[12,768]{1,0:T(8,128)S(1)} %add.319), channel_id=1, source_target_pairs={{0,2},{1,3},{2,0},{3,1},{4,6},{5,7},{6,4},{7,5},{8,10},{9,11},{10,... | collective-permute-start | bytes 110600 | tf_op jit(solution)/shard_map/ppermute | solution.py:49
  307.3 16.3 %collective-permute-start.49 = (bf16[128,768]{1,0:T(8,128)(2,1)S(1)}, bf16[128,768]{1,0:T(8,128)(2,1)S(1)}, u32[]{:S(2)}, u32[]{:S(2)}) collective-permute-start(bf16[128,768]{1,0:T(8,128)(2,1)S(1)} %fusion.52), channel_id=1, source_target_pairs={{0,2},{1,3},{2,0},{3,1},{4,6},{5,7},{6,4},{7,5},{8,10},{9,11},{10,... | collective-permute-start | bytes 589832 | tf_op jit(solution)/shard_map/ppermute | solution.py:44
  312.2 11.5 %collective-permute-start.48 = (bf16[128,768]{1,0:T(8,128)(2,1)S(1)}, bf16[128,768]{1,0:T(8,128)(2,1)S(1)}, u32[]{:S(2)}, u32[]{:S(2)}) collective-permute-start(bf16[128,768]{1,0:T(8,128)(2,1)S(1)} %fusion.52), channel_id=1, source_target_pairs={{0,1},{1,2},{2,3},{3,0},{4,5},{5,6},{6,7},{7,4},{8,9},{9,10},{10,1... | collective-permute-start | bytes 589832 | tf_op jit(solution)/shard_map/ppermute | solution.py:44
  317.7 8.4 %collective-permute-start.51 = (bf16[576,384]{1,0:T(8,128)(2,1)S(1)}, bf16[576,384]{1,0:T(8,128)(2,1)S(1)}, u32[]{:S(2)}, u32[]{:S(2)}) collective-permute-start(bf16[576,384]{1,0:T(8,128)(2,1)S(1)} %fusion.14), channel_id=1, source_target_pairs={{0,8},{4,12},{8,0},{12,4},{1,9},{5,13},{9,1},{13,5},{2,10},{6,14},... | collective-permute-start | bytes 1327112 | tf_op jit(solution)/shard_map/ppermute | solution.py:49
  321.4 7.3 %collective-permute-start.54 = (bf16[192,384]{1,0:T(8,128)(2,1)S(1)}, bf16[192,384]{1,0:T(8,128)(2,1)S(1)}, u32[]{:S(2)}, u32[]{:S(2)}) collective-permute-start(bf16[192,384]{1,0:T(8,128)(2,1)S(1)} %add_convert_fusion.3), channel_id=1, source_target_pairs={{0,4},{4,0},{8,12},{12,8},{1,5},{5,1},{9,13},{13,9},{2,6},{6,2},{1... | collective-permute-start | bytes 442376 | tf_op jit(solution)/shard_map/ppermute | solution.py:49
  326.2 3.3 %collective-permute-start.52 = (bf16[576,384]{1,0:T(8,128)(2,1)S(1)}, bf16[576,384]{1,0:T(8,128)(2,1)S(1)}, u32[]{:S(2)}, u32[]{:S(2)}) collective-permute-start(bf16[576,384]{1,0:T(8,128)(2,1)S(1)} %add_convert_fusion.2), channel_id=1, source_target_pairs={{0,4},{4,0},{8,12},{12,8},{1,5},{5,1},{9,13},{13,9},{2,6},{6,2},{1... | collective-permute-start | bytes 1327112 | tf_op jit(solution)/shard_map/ppermute | solution.py:49
  (48 other events, 370.3 us)

commit v2 on v1

--- a/solution.py
+++ b/solution.py
@@ -129,13 +129,15 @@
     return order
 
 
-def gather_parts(block):
+def gather_parts(block, beside):
     held, bit = [block[None]], lax.axis_size("ctx") // 2
     while bit:
         sent = held[0] if len(held) == 1 else jnp.concatenate(held, 0)
         held.append(flipped(sent, "ctx", bit))
+        if bit == lax.axis_size("ctx") // 2:
+            held[-1], beside = tie(held[-1], beside)
         bit //= 2
-    return held
+    return held, beside
 
 
 def scatter_parts(blocks):
@@ -165,7 +167,9 @@
     size = lax.axis_size("tp")
     rows = total.shape[0] // size
     low = total.astype(BF16)
-    moved = [shifted(low[e * rows : (e + 1) * rows], "tp", size - e) for e in range(1, size)]
+    moved = []
+    for e in range(1, size):
+        moved.append(shifted(low[e * rows : (e + 1) * rows], "tp", size - e))
     kept = total[:rows]
     for block in moved:
         kept = kept + block.astype(F32)
@@ -188,7 +192,7 @@
     return [blocks[0]] + [shifted(blocks[size - j], "tp", j) for j in range(1, size)]
 
 
-TILE = 128
+TILE = 256
 
 
 def blocks_of(refs):
@@ -286,6 +290,7 @@
         own = slice(h * size, (h + 1) * size)
         other = slice(width + h * size, width + (h + 1) * size)
         mean = jnp.sum(product[:, own], -1, keepdims=True)
+        changes, lows = [], []
         d_head = jnp.zeros((context.shape[0], size), F32)
         for e, span in enumerate(spans):
             d_weights = lax.dot_general(
@@ -295,13 +300,20 @@
             change = (low.astype(F32) * (d_weights - mean)).astype(BF16)
             d_scores[0, h, :, span] = change
             d_head = d_head + jnp.dot(change, kv[e][:, own], preferred_element_type=F32)
-            total[e, own, :] += jnp.dot(query_t[own, :], change, preferred_element_type=F32)
-            total[e, other, :] += jnp.dot(d_context_t[own, :], low, preferred_element_type=F32)
+            changes.append(change)
+            lows.append(low)
+        total[own, :] += jnp.dot(
+            query_t[own, :], jnp.concatenate(changes, 1), preferred_element_type=F32
+        )
+        total[other, :] += jnp.dot(
+            d_context_t[own, :], jnp.concatenate(lows, 1), preferred_element_type=F32
+        )
         d_query[:, own] = scale * d_head
 
     @pl.when(step == pl.num_programs(0) - 1)
     def _():
-        d_kv[...] = total[...].astype(BF16)
+        for e in range(len(kv)):
+            d_kv[e] = total[:, e * block : (e + 1) * block].astype(BF16)
 
 
 def attend_back(weights, kv, starts, context, d_mixed, inverse, query, scale):
@@ -324,7 +336,7 @@
                 pl.BlockSpec((TILE, width), tile),
                 pl.BlockSpec(shape, whole),
             ],
-            scratch_shapes=[pltpu.VMEM(shape, F32)],
+            scratch_shapes=[pltpu.VMEM((2 * width, keys), F32)],
         ),
         out_shape=[
             jax.ShapeDtypeStruct((1, heads, rows, keys), BF16),
@@ -410,8 +422,8 @@
     query_scaled = (query_scaled.astype(BF16).astype(F32) * score_scale).astype(BF16)
     bias_kv = jnp.concatenate([jnp.zeros_like(bias_value), bias_value])
     kv_local = (dot32(tokens_first, full_qkv[width_local:], ((1,), (1,))) + bias_kv).astype(BF16)
-    kv_all = gather_parts(kv_local)
-    kv_all[-1], output_half = tie(kv_all[-1], output_half)
+    kv_local, output_half = tie(kv_local, output_half)
+    kv_all, query_scaled = gather_parts(kv_local, query_scaled)
     output_moved, join_output = gather_late(output_half, 1)
     starts = (ctx_place ^ jnp.asarray(ctx_order(), jnp.int32)) * row_count
     all_count = VectorSum(seq_length.astype(F32), ("dp",)).total()
@@ -455,7 +467,7 @@
     grad_bias_inner = jnp.sum(d_pre, 0)
     d_pre_low = d_pre.astype(BF16)
     hidden_part = rows_sum(dot32(d_pre_low, full_inner, ((1,), (1,))))
-    outer_sum = WeightSum(dot32(act_low, d_second_low, ((0,), (0,))), 1)
+    outer_sum = WeightSum(dot32(act_low, d_second_low, ((0,), (0,))), 1, True)
     inner_sum = WeightSum(dot32(hidden_low, d_pre_low, ((0,), (0,))), 0)
     d_hidden = d_second + own_first(hidden_part)
     d_first, grad_gain_first, grad_shift_first = norm_backward(
@@ -507,13 +519,14 @@
     early_sum.step()
     both = jnp.concatenate([both_mine] + both_moved, 0)
     d_first_all = both[:, :model_width]
-    output_sum = WeightSum(dot32(context_turned, d_first_all, ((0,), (0,))), 1, True)
+    output_gradient = dot32(context_turned, d_first_all, ((0,), (0,)))
+    output_sum = WeightSum(output_gradient, 1, True)
     d_qkv_low = jnp.concatenate([d_query_low, d_kv_low.T], 1)
     tokens_part = rows_sum(dot32(rows_turn(d_qkv_low), full_qkv, ((1,), (0,))))
-    qkv_sum = WeightSum(dot32(d_qkv_low, tokens_first, ((0,), (0,))), 1, True)
-    late_sum = VectorSum(
-        jnp.concatenate([jnp.sum(d_query, 0), jnp.sum(d_kv[width_local:], 1)]), ("dp", "ctx")
-    )
+    qkv_gradient = dot32(d_qkv_low, tokens_first, ((0,), (0,)))
+    qkv_sum = WeightSum(qkv_gradient, 1, True)
+    late_vector = jnp.concatenate([jnp.sum(d_query, 0), jnp.sum(d_kv[width_local:], 1)])
+    late_sum = VectorSum(late_vector, ("dp", "ctx"))
     grad_mine = (d_first + own_first(tokens_part)).astype(BF16)
     sums = (output_sum, early_sum, qkv_sum, late_sum)
     grad_mine, *moved = tie(grad_mine, *[one.moved for one in sums])
@@ -521,8 +534,13 @@
         one.moved = value
     for one in sums:
         one.step()
+    grad_moved = rows_moved(grad_mine)
+    inner_shard, outer_shard = inner_sum.total(), outer_sum.total()
     result_all = rows_turn(both[:, model_width:]).astype(F32)
-    grad_inputs = rows_turn(rows_gather(grad_mine)).astype(F32)
+    grad_moved[-1], inner_shard, outer_shard, result_all = tie(
+        grad_moved[-1], inner_shard, outer_shard, result_all
+    )
+    grad_inputs = rows_turn(jnp.concatenate([grad_mine] + grad_moved, 0)).astype(F32)
     output_shard = output_sum.total()
     shard_qkv = qkv_sum.total()
     early = early_sum.total()
@@ -540,8 +558,8 @@
         shard_qkv[width_local : 2 * width_local].T,
         shard_qkv[2 * width_local :].T,
         output_shard,
-        inner_sum.total(),
-        outer_sum.total(),
+        inner_shard,
+        outer_shard,
         late[:width_local],
         late[width_local:],
         early[0],

time: 333 us -> 312 us (0.937)
  starting transfers between devices: 93.6 us -> 84.1 us
  other arithmetic: 34.6 us -> 29.6 us
  Pallas kernels: 32.9 us -> 28 us
    ppermute x30, starting transfers between devices: 63.4 us -> 58.1 us  [shifted(): lax.ppermute(block, axis, [(i, (i + step) % size) for i in range(size)])]
    pallas_call x1, Pallas kernels: 17.6 us -> 13.3 us  [attend_back(): pl.pallas_call(partial(attend_back_kernel, heads, scale, len(kv)), grid_s...]
    ppermute x29, starting transfers between devices: 30.1 us -> 26 us  [flipped(): return lax.ppermute(block, axis, [(i, i ^ bit) for i in range(size)])]
    unnamed x116 -> x122, local copies, waits for them, and re-layouts: 5.3 us -> 7.1 us
  transfers between devices with their start and end apart: 59 -> 59, of which waited for: 24 -> 24; matrix products, arithmetic and copies ran while one was open for 17% -> 18% of each run, Pallas kernels for 10% -> 9%
where the time goes in v2:
time: 312 us; the launch traced here: 311 us
  waiting for transfers between devices  121 us (39%)
  starting transfers between devices  84.1 us (27%)
  other arithmetic  29.6 us (9%)
  Pallas kernels  28 us (9%)
  local copies, waits for them, and re-layouts  25.6 us (8%)
  matrix products  17.7 us (6%)
  between operations  5 us (2%)
    ppermute x30, waiting for transfers between devices, shifted(): lax.ppermute(block, axis, [(i, (i + step) % size) for i in range(size)])  67.7 us
    ppermute x30, starting transfers between devices, shifted(): lax.ppermute(block, axis, [(i, (i + step) % size) for i in range(size)])  58.1 us
    ppermute x29, waiting for transfers between devices, flipped(): return lax.ppermute(block, axis, [(i, i ^ bit) for i in range(size)])  52.9 us
    ppermute x29, starting transfers between devices, flipped(): return lax.ppermute(block, axis, [(i, i ^ bit) for i in range(size)])  26 us
    dot_general x13, matrix products, dot32(): lax.dot_general(left, right, (dims, ((), ())), preferred_element_type=F32)  17.7 us
    pallas_call x1, Pallas kernels, attend_back(): pl.pallas_call(partial(attend_back_kernel, heads, scale, len(kv)), grid_s...  13.3 us
    pallas_call x1, Pallas kernels, attend(): pl.pallas_call(partial(attend_kernel, heads, len(kv)), grid_spec=pltpu.Pr...  12.5 us
    unnamed x122, local copies, waits for them, and re-layouts  7.1 us
  transfers between devices with their start and end apart: 59, of which 24 were waited for; matrix products, arithmetic and copies ran while one was open for 18% of the time, Pallas kernels for 9%

profile of v2, /device:TPU:0, one launch (start us, length us, event | category | flops | bytes accessed | tf_op | source)
XLA Modules:
  0.0 310.6 jit_solution(15487830577345011572)
XLA Ops:
  0.7 5.1 %collective-permute-start.4 = (bf16[192,384]{1,0:T(8,128)(2,1)}, bf16[192,384]{1,0:T(8,128)(2,1)S(1)}, u32[]{:S(2)}, u32[]{:S(2)}) collective-permute-start(bf16[192,384]{1,0:T(8,128)(2,1)} %param.27), channel_id=1, source_target_pairs={{0,3},{1,0},{2,1},{3,2},{4,7},{5,4},{6,5},{7,6},{8,11},{9,8},{10,9... | collective-permute-start | bytes 442376 | tf_op jit(solution)/shard_map/ppermute | solution.py:44
  7.9 1.6 collective-permute-start.1
  11.0 7.5 %collective-permute-done.3 = bf16[192,384]{1,0:T(8,128)(2,1)S(1)} collective-permute-done((bf16[192,384]{1,0:T(8,128)(2,1)}, bf16[192,384]{1,0:T(8,128)(2,1)S(1)}, u32[]{:S(2)}, u32[]{:S(2)}) %collective-permute-start.3) | collective-permute-done | bytes 147488 | tf_op jit(solution)/shard_map/ppermute | solution.py:44
  20.9 1.6 collective-permute-start.5
  23.6 7.8 %collective-permute-done.5.refs_1_ = bf16[1,512,384]{2,1,0:T(8,128)(2,1)S(1)} collective-permute-done((bf16[1,512,384]{2,1,0:T(8,128)(2,1)S(1)}, bf16[1,512,384]{2,1,0:T(8,128)(2,1)S(1)}, u32[]{:S(2)}, u32[]{:S(2)}) %collective-permute-start.5) | collective-permute-done | bytes 393248 | tf_op jit(solution)/shard_map/ppermute | solution.py:49
  33.1 2.9 collective-permute-start
  38.8 12.5 %attend.1 = (bf16[1,3,512,2048]{3,2,1,0:T(8,128)(2,1)}, bf16[3,512,2048]{2,1,0:T(8,128)(2,1)}, bf16[512,192]{1,0:T(8,128)(2,1)}, f32[512,192]{1,0:T(8,128)}) custom-call(s32[2]{0:T(128)} %multiply_minimum_fusion.limits, s32[4]{0:T(128)} %xor_multiply_fusion.starts, bf16[512,192]{1,0:T(8,128)(2,1)} %fusion.10.query, bf16[1,3,512,2048]{3,2,1,0:T(8,128)(2,1)} %prior.1, ...), custom_call_target="tpu_custom_call" | custom-call | flops 805306368 | bytes 18874368 | tf_op jit(solution)/shard_map/attend/pallas_call | solution.py:245
  53.7 1.6 collective-permute-start.14
  55.3 1.8 collective-permute-start.10
  58.1 1.9 collective-permute-start.8
  61.9 2.5 collective-permute-done.9
  65.8 1.5 collective-permute-start.13
  67.3 2.7 collective-permute-done.14
  70.9 10.2 %collective-permute-done.15 = bf16[768,384]{1,0:T(8,128)(2,1)S(1)} collective-permute-done((bf16[768,384]{1,0:T(8,128)(2,1)S(1)}, bf16[768,384]{1,0:T(8,128)(2,1)S(1)}, u32[]{:S(2)}, u32[]{:S(2)}) %collective-permute-start.15) | collective-permute-done | bytes 589856 | tf_op jit(solution)/shard_map/ppermute | solution.py:49
  81.2 3.1 collective-permute-done.12
  84.3 5.6 %multiply_convert_fusion = (bf16[512,768]{1,0:T(8,128)(2,1)S(1)}, f32[512,768]{1,0:T(8,128)}, f32[512,768]{1,0:T(8,128)}) fusion(f32[768]{0:T(1024)S(1)} %copy-done.51, bf16[768,768]{1,0:T(8,128)(2,1)S(1)} %constant_dynamic-update-slice_fusion.2, bf16[128,768]{1,0:T(8,128)(2,1)S(1)} %collective-permute-done.13, ...), kind=kOutput, calls=%fused_computation.4 | convolution fusion | flops 633077760 | bytes 5901312 | tf_op jit(solution)/shard_map/dot_general | solution.py:39
  90.0 1.9 fusion.95
  92.7 1.7 collective-permute-start.17
  94.4 2.9 collective-permute-start.16
  99.6 2.9 collective-permute-done.18
  102.5 6.3 %collective-permute-done.17 = bf16[128,768]{1,0:T(8,128)(2,1)S(1)} collective-permute-done((bf16[128,768]{1,0:T(8,128)(2,1)}, bf16[128,768]{1,0:T(8,128)(2,1)S(1)}, u32[]{:S(2)}, u32[]{:S(2)}) %collective-permute-start.17) | collective-permute-done | bytes 196640 | tf_op jit(solution)/shard_map/ppermute | solution.py:44
  113.0 6.3 %collective-permute-start.21 = (bf16[128,768]{1,0:T(8,128)(2,1)S(1)}, bf16[128,768]{1,0:T(8,128)(2,1)S(1)}, u32[]{:S(2)}, u32[]{:S(2)}) collective-permute-start(bf16[128,768]{1,0:T(8,128)(2,1)S(1)} %maximum_select_fusion.6), channel_id=1, source_target_pairs={{0,3},{1,0},{2,1},{3,2},{4,7},{5,4},{6,5},{7,6},{8,11},{9,8},{10,9... | collective-permute-start | bytes 589832 | tf_op jit(solution)/shard_map/ppermute | solution.py:44
  119.9 4.7 %collective-permute-done.21 = bf16[128,768]{1,0:T(8,128)(2,1)S(1)} collective-permute-done((bf16[128,768]{1,0:T(8,128)(2,1)S(1)}, bf16[128,768]{1,0:T(8,128)(2,1)S(1)}, u32[]{:S(2)}, u32[]{:S(2)}) %collective-permute-start.21) | collective-permute-done | bytes 196640 | tf_op jit(solution)/shard_map/ppermute | solution.py:44
  124.6 11.8 %collective-permute-done.20 = bf16[128,768]{1,0:T(8,128)(2,1)S(1)} collective-permute-done((bf16[128,768]{1,0:T(8,128)(2,1)S(1)}, bf16[128,768]{1,0:T(8,128)(2,1)S(1)}, u32[]{:S(2)}, u32[]{:S(2)}) %collective-permute-start.20) | collective-permute-done | bytes 196640 | tf_op jit(solution)/shard_map/ppermute | solution.py:44
  138.6 1.6 collective-permute-start.23
  140.2 2.9 collective-permute-start.22
  146.5 1.4 collective-permute-start.29
  148.3 6.6 %collective-permute-done.23 = bf16[128,768]{1,0:T(8,128)(2,1)S(1)} collective-permute-done((bf16[128,768]{1,0:T(8,128)(2,1)S(1)}, bf16[128,768]{1,0:T(8,128)(2,1)S(1)}, u32[]{:S(2)}, u32[]{:S(2)}) %collective-permute-start.23) | collective-permute-done | bytes 196640 | tf_op jit(solution)/shard_map/ppermute | solution.py:44
  156.2 4.9 %collective-permute-start.27 = (bf16[128,192]{1,0:T(8,128)(2,1)S(1)}, bf16[128,192]{1,0:T(8,128)(2,1)S(1)}, u32[]{:S(2)}, u32[]{:S(2)}) collective-permute-start(bf16[128,192]{1,0:T(8,128)(2,1)S(1)} %get-tuple-element.171), channel_id=1, source_target_pairs={{0,3},{1,0},{2,1},{3,2},{4,7},{5,4},{6,5},{7,6},{8,11},{9,8},{10,9... | collective-permute-start | bytes 147464 | tf_op jit(solution)/shard_map/ppermute | solution.py:44
  165.8 2.1 pack.1
  169.4 1.6 collective-permute-done.29
  171.0 13.3 %attend_back.1 = (bf16[1,3,512,2048]{3,2,1,0:T(8,128)(2,1)}, f32[512,192]{1,0:T(8,128)}, bf16[4,384,512]{2,1,0:T(8,128)(2,1)}) custom-call(s32[4]{0:T(128)} %xor_multiply_fusion.starts, bf16[3,512,2048]{2,1,0:T(8,128)(2,1)} %get-tuple-element.66.weights, bf16[512,192]{1,0:T(8,128)(2,1)} %get-tuple-element.60.context, ...), custom_call_target="tpu_custom_call" | custom-call | flops 2013265920 | bytes 18874368 | tf_op jit(solution)/shard_map/attend_back/pallas_call | solution.py:326
  185.6 1.5 fusion.12
  188.0 1.6 convert_add_fusion
  190.4 1.5 collective-permute-start.32
  196.9 1.3 collective-permute-start.36
  198.2 1.4 collective-permute-start.37
  199.6 3.1 %collective-permute-done.32 = bf16[1,384,512]{2,1,0:T(8,128)(2,1)} collective-permute-done((bf16[1,384,512]{2,1,0:T(8,128)(2,1)}, bf16[1,384,512]{2,1,0:T(8,128)(2,1)}, u32[]{:S(2)}, u32[]{:S(2)}) %collective-permute-start.32) | collective-permute-done | bytes 393248 | tf_op jit(solution)/shard_map/ppermute | solution.py:49
  202.7 2.1 collective-permute-start.38
  205.9 2.1 convert_bitcast_fusion
  208.0 3.1 collective-permute-done.36
  211.1 16.3 %collective-permute-done.37 = bf16[128,1536]{1,0:T(8,128)(2,1)S(1)} collective-permute-done((bf16[128,1536]{1,0:T(8,128)(2,1)}, bf16[128,1536]{1,0:T(8,128)(2,1)S(1)}, u32[]{:S(2)}, u32[]{:S(2)}) %collective-permute-start.37) | collective-permute-done | bytes 393248 | tf_op jit(solution)/shard_map/ppermute | solution.py:44
  227.5 1.9 fusion.72
  234.0 9.0 %collective-permute-start.41 = (bf16[128,768]{1,0:T(8,128)(2,1)S(1)}, bf16[128,768]{1,0:T(8,128)(2,1)S(1)}, u32[]{:S(2)}, u32[]{:S(2)}) collective-permute-start(bf16[128,768]{1,0:T(8,128)(2,1)S(1)} %get-tuple-element.135), channel_id=1, source_target_pairs={{0,1},{1,2},{2,3},{3,0},{4,5},{5,6},{6,7},{7,4},{8,9},{9,10},{10,1... | collective-permute-start | bytes 589832 | tf_op jit(solution)/shard_map/ppermute | solution.py:44
  243.3 2.1 collective-permute-start.39
  246.1 1.5 collective-permute-start.43
  249.0 1.3 add_convert_fusion
  250.7 1.3 maximum_convert_fusion
  251.9 1.5 collective-permute-start.44
  253.4 2.6 collective-permute-done.40
  256.0 1.5 collective-permute-start.45
  257.4 1.5 collective-permute-start.47
  259.1 3.8 %collective-permute-done.45 = f32[384]{0:T(512)S(1)} collective-permute-done((f32[384]{0:T(512)S(1)}, f32[384]{0:T(512)S(1)}, u32[]{:S(2)}, u32[]{:S(2)}) %collective-permute-start.45) | collective-permute-done | bytes 1568 | tf_op jit(solution)/shard_map/ppermute | solution.py:49
  263.0 3.8 %collective-permute-start.46 = (bf16[128,768]{1,0:T(8,128)(2,1)S(1)}, bf16[128,768]{1,0:T(8,128)(2,1)S(1)}, u32[]{:S(2)}, u32[]{:S(2)}) collective-permute-start(bf16[128,768]{1,0:T(8,128)(2,1)S(1)} %fusion.38), channel_id=1, source_target_pairs={{0,3},{1,0},{2,1},{3,2},{4,7},{5,4},{6,5},{7,6},{8,11},{9,8},{10,9... | collective-permute-start | bytes 589832 | tf_op jit(solution)/shard_map/ppermute | solution.py:44
  268.0 1.5 collective-permute-start.58
  269.6 2.8 collective-permute-done.58
  272.3 2.6 collective-permute-start.52
  276.0 9.5 %collective-permute-done.50 = f32[12,768]{1,0:T(8,128)S(1)} collective-permute-done((f32[12,768]{1,0:T(8,128)S(1)}, f32[12,768]{1,0:T(8,128)S(1)}, u32[]{:S(2)}, u32[]{:S(2)}) %collective-permute-start.50) | collective-permute-done | bytes 36896 | tf_op jit(solution)/shard_map/ppermute | solution.py:49
  288.0 1.6 slice_reduce_fusion.1
  289.6 1.5 collective-permute-start.55
  292.2 2.9 collective-permute-done.55
  295.1 1.5 collective-permute-start.53
  298.8 7.3 %collective-permute-done.53 = bf16[576,384]{1,0:T(8,128)(2,1)S(1)} collective-permute-done((bf16[576,384]{1,0:T(8,128)(2,1)S(1)}, bf16[576,384]{1,0:T(8,128)(2,1)S(1)}, u32[]{:S(2)}, u32[]{:S(2)}) %collective-permute-start.53) | collective-permute-done | bytes 442400 | tf_op jit(solution)/shard_map/ppermute | solution.py:49
  306.4 1.3 maximum_convert_fusion.1
  (304 shorter events, 64.7 us)
Async XLA Ops:
  0.7 10.3 %collective-permute-start.4 = (bf16[192,384]{1,0:T(8,128)(2,1)}, bf16[192,384]{1,0:T(8,128)(2,1)S(1)}, u32[]{:S(2)}, u32[]{:S(2)}) collective-permute-start(bf16[192,384]{1,0:T(8,128)(2,1)} %param.27), channel_id=1, source_target_pairs={{0,3},{1,0},{2,1},{3,2},{4,7},{5,4},{6,5},{7,6},{8,11},{9,8},{10,9... | collective-permute-start | bytes 442376 | tf_op jit(solution)/shard_map/ppermute | solution.py:44
  5.8 12.7 %collective-permute-start.3 = (bf16[192,384]{1,0:T(8,128)(2,1)}, bf16[192,384]{1,0:T(8,128)(2,1)S(1)}, u32[]{:S(2)}, u32[]{:S(2)}) collective-permute-start(bf16[192,384]{1,0:T(8,128)(2,1)} %param.27), channel_id=1, source_target_pairs={{0,2},{1,3},{2,0},{3,1},{4,6},{5,7},{6,4},{7,5},{8,10},{9,11},{10,... | collective-permute-start | bytes 442376 | tf_op jit(solution)/shard_map/ppermute | solution.py:44
  5.8 12.7 %collective-permute-start.2 = (bf16[192,384]{1,0:T(8,128)(2,1)}, bf16[192,384]{1,0:T(8,128)(2,1)S(1)}, u32[]{:S(2)}, u32[]{:S(2)}) collective-permute-start(bf16[192,384]{1,0:T(8,128)(2,1)} %param.27), channel_id=1, source_target_pairs={{0,1},{1,2},{2,3},{3,0},{4,5},{5,6},{6,7},{7,4},{8,9},{9,10},{10,1... | collective-permute-start | bytes 442376 | tf_op jit(solution)/shard_map/ppermute | solution.py:44
  7.9 11.5 %collective-permute-start.1 = (bf16[576,384]{1,0:T(8,128)(2,1)S(1)}, bf16[576,384]{1,0:T(8,128)(2,1)S(1)}, u32[]{:S(2)}, u32[]{:S(2)}) collective-permute-start(bf16[576,384]{1,0:T(8,128)(2,1)S(1)} %pad_maximum_fusion.7), channel_id=1, source_target_pairs={{0,16},{16,0},{1,17},{17,1},{2,18},{18,2},{3,19},{19,3},{4,20},{20... | collective-permute-start | bytes 1327112 | tf_op jit(solution)/shard_map/ppermute | solution.py:49
  20.9 10.5 %collective-permute-start.5 = (bf16[1,512,384]{2,1,0:T(8,128)(2,1)S(1)}, bf16[1,512,384]{2,1,0:T(8,128)(2,1)S(1)}, u32[]{:S(2)}, u32[]{:S(2)}) collective-permute-start(bf16[1,512,384]{2,1,0:T(8,128)(2,1)S(1)} %bitcast.102), channel_id=1, source_target_pairs={{0,8},{4,12},{8,0},{12,4},{1,9},{5,13},{9,1},{13,5},{2,10},{6,14},... | collective-permute-start | bytes 1179656 | tf_op jit(solution)/shard_map/ppermute | solution.py:49
  32.4 6.4 %collective-permute-start.6 = (bf16[2,512,384]{2,1,0:T(8,128)(2,1)}, bf16[2,512,384]{2,1,0:T(8,128)(2,1)}, u32[]{:S(2)}, u32[]{:S(2)}) collective-permute-start(bf16[2,512,384]{2,1,0:T(8,128)(2,1)} %pad_maximum_fusion.1), channel_id=1, source_target_pairs={{0,4},{4,0},{8,12},{12,8},{1,5},{5,1},{9,13},{13,9},{2,6},{6,2},{1... | collective-permute-start | bytes 2359304 | tf_op jit(solution)/shard_map/ppermute | solution.py:49
  33.1 65.0 %collective-permute-start = (f32[]{:T(128)}, f32[]{:T(128)}, u32[]{:S(2)}, u32[]{:S(2)}) collective-permute-start(f32[]{:T(128)} %convert_element_type.210), channel_id=1, source_target_pairs={{0,16},{16,0},{1,17},{17,1},{2,18},{18,2},{3,19},{19,3},{4,20},{20... | collective-permute-start | bytes 20 | tf_op jit(solution)/shard_map/ppermute | solution.py:49
  36.6 15.9 %collective-permute-start.7 = (bf16[768,384]{1,0:T(8,128)(2,1)}, bf16[768,384]{1,0:T(8,128)(2,1)}, u32[]{:S(2)}, u32[]{:S(2)}) collective-permute-start(bf16[768,384]{1,0:T(8,128)(2,1)} %pad_maximum_fusion.5), channel_id=1, source_target_pairs={{0,16},{16,0},{1,17},{17,1},{2,18},{18,2},{3,19},{19,3},{4,20},{20... | collective-permute-start | bytes 1769480 | tf_op jit(solution)/shard_map/ppermute | solution.py:49
  53.7 16.3 %collective-permute-start.14 = (bf16[384,768]{1,0:T(8,128)(2,1)S(1)}, bf16[384,768]{1,0:T(8,128)(2,1)S(1)}, u32[]{:S(2)}, u32[]{:S(2)}) collective-permute-start(bf16[384,768]{1,0:T(8,128)(2,1)S(1)} %copy-done.26), channel_id=1, source_target_pairs={{0,16},{16,0},{1,17},{17,1},{2,18},{18,2},{3,19},{19,3},{4,20},{20... | collective-permute-start | bytes 1769480 | tf_op jit(solution)/shard_map/ppermute | solution.py:49
  55.3 6.0 %collective-permute-start.10 = (bf16[128,192]{1,0:T(8,128)(2,1)S(1)}, bf16[128,192]{1,0:T(8,128)(2,1)S(1)}, u32[]{:S(2)}, u32[]{:S(2)}) collective-permute-start(bf16[128,192]{1,0:T(8,128)(2,1)S(1)} %get-tuple-element.163), channel_id=1, source_target_pairs={{0,3},{1,0},{2,1},{3,2},{4,7},{5,4},{6,5},{7,6},{8,11},{9,8},{10,9... | collective-permute-start | bytes 147464 | tf_op jit(solution)/shard_map/ppermute | solution.py:44
  57.1 7.3 %collective-permute-start.9 = (bf16[128,192]{1,0:T(8,128)(2,1)S(1)}, bf16[128,192]{1,0:T(8,128)(2,1)S(1)}, u32[]{:S(2)}, u32[]{:S(2)}) collective-permute-start(bf16[128,192]{1,0:T(8,128)(2,1)S(1)} %get-tuple-element.164), channel_id=1, source_target_pairs={{0,2},{1,3},{2,0},{3,1},{4,6},{5,7},{6,4},{7,5},{8,10},{9,11},{10,... | collective-permute-start | bytes 147464 | tf_op jit(solution)/shard_map/ppermute | solution.py:44
  58.1 6.3 %collective-permute-start.8 = (bf16[128,192]{1,0:T(8,128)(2,1)S(1)}, bf16[128,192]{1,0:T(8,128)(2,1)S(1)}, u32[]{:S(2)}, u32[]{:S(2)}) collective-permute-start(bf16[128,192]{1,0:T(8,128)(2,1)S(1)} %get-tuple-element.165), channel_id=1, source_target_pairs={{0,1},{1,2},{2,3},{3,0},{4,5},{5,6},{6,7},{7,4},{8,9},{9,10},{10,1... | collective-permute-start | bytes 147464 | tf_op jit(solution)/shard_map/ppermute | solution.py:44
  61.3 19.8 %collective-permute-start.15 = (bf16[768,384]{1,0:T(8,128)(2,1)S(1)}, bf16[768,384]{1,0:T(8,128)(2,1)S(1)}, u32[]{:S(2)}, u32[]{:S(2)}) collective-permute-start(bf16[768,384]{1,0:T(8,128)(2,1)S(1)} %copy-done.27), channel_id=1, source_target_pairs={{0,16},{16,0},{1,17},{17,1},{2,18},{18,2},{3,19},{19,3},{4,20},{20... | collective-permute-start | bytes 1769480 | tf_op jit(solution)/shard_map/ppermute | solution.py:49
  65.8 24.1 %copy-start.32 = (bf16[128,768]{1,0:T(8,128)(2,1)}, bf16[128,768]{1,0:T(8,128)(2,1)S(1)}, u32[]{:S(2)}) copy-start(bf16[128,768]{1,0:T(8,128)(2,1)S(1)} %maximum_select_fusion.5) | copy-start | bytes 589828
  65.8 15.4 %collective-permute-start.13 = (bf16[128,768]{1,0:T(8,128)(2,1)S(1)}, bf16[128,768]{1,0:T(8,128)(2,1)S(1)}, u32[]{:S(2)}, u32[]{:S(2)}) collective-permute-start(bf16[128,768]{1,0:T(8,128)(2,1)S(1)} %maximum_select_fusion.5), channel_id=1, source_target_pairs={{0,3},{1,0},{2,1},{3,2},{4,7},{5,4},{6,5},{7,6},{8,11},{9,8},{10,9... | collective-permute-start | bytes 589832 | tf_op jit(solution)/shard_map/ppermute | solution.py:44
  67.3 17.0 %collective-permute-start.12 = (bf16[128,768]{1,0:T(8,128)(2,1)S(1)}, bf16[128,768]{1,0:T(8,128)(2,1)S(1)}, u32[]{:S(2)}, u32[]{:S(2)}) collective-permute-start(bf16[128,768]{1,0:T(8,128)(2,1)S(1)} %maximum_select_fusion.5), channel_id=1, source_target_pairs={{0,2},{1,3},{2,0},{3,1},{4,6},{5,7},{6,4},{7,5},{8,10},{9,11},{10,... | collective-permute-start | bytes 589832 | tf_op jit(solution)/shard_map/ppermute | solution.py:44
  70.0 14.3 %collective-permute-start.11 = (bf16[128,768]{1,0:T(8,128)(2,1)S(1)}, bf16[128,768]{1,0:T(8,128)(2,1)S(1)}, u32[]{:S(2)}, u32[]{:S(2)}) collective-permute-start(bf16[128,768]{1,0:T(8,128)(2,1)S(1)} %maximum_select_fusion.5), channel_id=1, source_target_pairs={{0,1},{1,2},{2,3},{3,0},{4,5},{5,6},{6,7},{7,4},{8,9},{9,10},{10,1... | collective-permute-start | bytes 589832 | tf_op jit(solution)/shard_map/ppermute | solution.py:44
  92.7 9.8 %collective-permute-start.18 = (bf16[128,768]{1,0:T(8,128)(2,1)}, bf16[128,768]{1,0:T(8,128)(2,1)S(1)}, u32[]{:S(2)}, u32[]{:S(2)}) collective-permute-start(bf16[128,768]{1,0:T(8,128)(2,1)} %get-tuple-element.141), channel_id=1, source_target_pairs={{0,1},{1,2},{2,3},{3,0},{4,5},{5,6},{6,7},{7,4},{8,9},{9,10},{10,1... | collective-permute-start | bytes 589832 | tf_op jit(solution)/shard_map/ppermute | solution.py:44
  92.7 16.1 %collective-permute-start.17 = (bf16[128,768]{1,0:T(8,128)(2,1)}, bf16[128,768]{1,0:T(8,128)(2,1)S(1)}, u32[]{:S(2)}, u32[]{:S(2)}) collective-permute-start(bf16[128,768]{1,0:T(8,128)(2,1)} %get-tuple-element.142), channel_id=1, source_target_pairs={{0,2},{1,3},{2,0},{3,1},{4,6},{5,7},{6,4},{7,5},{8,10},{9,11},{10,... | collective-permute-start | bytes 589832 | tf_op jit(solution)/shard_map/ppermute | solution.py:44
  94.4 14.4 %collective-permute-start.16 = (bf16[128,768]{1,0:T(8,128)(2,1)}, bf16[128,768]{1,0:T(8,128)(2,1)S(1)}, u32[]{:S(2)}, u32[]{:S(2)}) collective-permute-start(bf16[128,768]{1,0:T(8,128)(2,1)} %get-tuple-element.140), channel_id=1, source_target_pairs={{0,3},{1,0},{2,1},{3,2},{4,7},{5,4},{6,5},{7,6},{8,11},{9,8},{10,9... | collective-permute-start | bytes 589832 | tf_op jit(solution)/shard_map/ppermute | solution.py:44
  109.9 26.5 %copy-start.55 = (f32[512,768]{1,0:T(8,128)S(1)}, f32[512,768]{1,0:T(8,128)}, u32[]{:S(2)}) copy-start(f32[512,768]{1,0:T(8,128)} %get-tuple-element.182) | copy-start | bytes 4718596
  111.9 24.5 %copy-start.7 = (bf16[768,768]{1,0:T(8,128)(2,1)S(1)}, bf16[768,768]{1,0:T(8,128)(2,1)}, u32[]{:S(2)}) copy-start(bf16[768,768]{1,0:T(8,128)(2,1)} %copy-done.6) | copy-start | bytes 3538948
  111.9 24.5 %copy-start.54 = (f32[512,768]{1,0:T(8,128)S(1)}, f32[512,768]{1,0:T(8,128)}, u32[]{:S(2)}) copy-start(f32[512,768]{1,0:T(8,128)} %get-tuple-element.120) | copy-start | bytes 4718596
  113.0 11.6 %collective-permute-start.21 = (bf16[128,768]{1,0:T(8,128)(2,1)S(1)}, bf16[128,768]{1,0:T(8,128)(2,1)S(1)}, u32[]{:S(2)}, u32[]{:S(2)}) collective-permute-start(bf16[128,768]{1,0:T(8,128)(2,1)S(1)} %maximum_select_fusion.6), channel_id=1, source_target_pairs={{0,3},{1,0},{2,1},{3,2},{4,7},{5,4},{6,5},{7,6},{8,11},{9,8},{10,9... | collective-permute-start | bytes 589832 | tf_op jit(solution)/shard_map/ppermute | solution.py:44
  119.3 17.2 %collective-permute-start.20 = (bf16[128,768]{1,0:T(8,128)(2,1)S(1)}, bf16[128,768]{1,0:T(8,128)(2,1)S(1)}, u32[]{:S(2)}, u32[]{:S(2)}) collective-permute-start(bf16[128,768]{1,0:T(8,128)(2,1)S(1)} %maximum_select_fusion.6), channel_id=1, source_target_pairs={{0,2},{1,3},{2,0},{3,1},{4,6},{5,7},{6,4},{7,5},{8,10},{9,11},{10,... | collective-permute-start | bytes 589832 | tf_op jit(solution)/shard_map/ppermute | solution.py:44
  119.3 17.2 %collective-permute-start.19 = (bf16[128,768]{1,0:T(8,128)(2,1)S(1)}, bf16[128,768]{1,0:T(8,128)(2,1)S(1)}, u32[]{:S(2)}, u32[]{:S(2)}) collective-permute-start(bf16[128,768]{1,0:T(8,128)(2,1)S(1)} %maximum_select_fusion.6), channel_id=1, source_target_pairs={{0,1},{1,2},{2,3},{3,0},{4,5},{5,6},{6,7},{7,4},{8,9},{9,10},{10,1... | collective-permute-start | bytes 589832 | tf_op jit(solution)/shard_map/ppermute | solution.py:44
  138.5 9.7 %collective-permute-start.24 = (bf16[128,768]{1,0:T(8,128)(2,1)S(1)}, bf16[128,768]{1,0:T(8,128)(2,1)S(1)}, u32[]{:S(2)}, u32[]{:S(2)}) collective-permute-start(bf16[128,768]{1,0:T(8,128)(2,1)S(1)} %get-tuple-element.138), channel_id=1, source_target_pairs={{0,1},{1,2},{2,3},{3,0},{4,5},{5,6},{6,7},{7,4},{8,9},{9,10},{10,1... | collective-permute-start | bytes 589832 | tf_op jit(solution)/shard_map/ppermute | solution.py:44
  138.6 16.2 %collective-permute-start.23 = (bf16[128,768]{1,0:T(8,128)(2,1)S(1)}, bf16[128,768]{1,0:T(8,128)(2,1)S(1)}, u32[]{:S(2)}, u32[]{:S(2)}) collective-permute-start(bf16[128,768]{1,0:T(8,128)(2,1)S(1)} %get-tuple-element.139), channel_id=1, source_target_pairs={{0,2},{1,3},{2,0},{3,1},{4,6},{5,7},{6,4},{7,5},{8,10},{9,11},{10,... | collective-permute-start | bytes 589832 | tf_op jit(solution)/shard_map/ppermute | solution.py:44
  140.2 14.6 %collective-permute-start.22 = (bf16[128,768]{1,0:T(8,128)(2,1)S(1)}, bf16[128,768]{1,0:T(8,128)(2,1)S(1)}, u32[]{:S(2)}, u32[]{:S(2)}) collective-permute-start(bf16[128,768]{1,0:T(8,128)(2,1)S(1)} %get-tuple-element.137), channel_id=1, source_target_pairs={{0,3},{1,0},{2,1},{3,2},{4,7},{5,4},{6,5},{7,6},{8,11},{9,8},{10,9... | collective-permute-start | bytes 589832 | tf_op jit(solution)/shard_map/ppermute | solution.py:44
  144.0 25.3 %collective-permute-start.28 = (bf16[768,384]{1,0:T(8,128)(2,1)S(1)}, bf16[768,384]{1,0:T(8,128)(2,1)}, u32[]{:S(2)}, u32[]{:S(2)}) collective-permute-start(bf16[768,384]{1,0:T(8,128)(2,1)S(1)} %split.97), channel_id=1, source_target_pairs={{0,16},{16,0},{1,17},{17,1},{2,18},{18,2},{3,19},{19,3},{4,20},{20... | collective-permute-start | bytes 1769480 | tf_op jit(solution)/shard_map/ppermute | solution.py:49
  146.5 24.5 %collective-permute-start.29 = (bf16[384,768]{1,0:T(8,128)(2,1)}, bf16[384,768]{1,0:T(8,128)(2,1)}, u32[]{:S(2)}, u32[]{:S(2)}) collective-permute-start(bf16[384,768]{1,0:T(8,128)(2,1)} %split.96), channel_id=1, source_target_pairs={{0,16},{16,0},{1,17},{17,1},{2,18},{18,2},{3,19},{19,3},{4,20},{20... | collective-permute-start | bytes 1769480 | tf_op jit(solution)/shard_map/ppermute | solution.py:49
  156.2 11.7 %collective-permute-start.27 = (bf16[128,192]{1,0:T(8,128)(2,1)S(1)}, bf16[128,192]{1,0:T(8,128)(2,1)S(1)}, u32[]{:S(2)}, u32[]{:S(2)}) collective-permute-start(bf16[128,192]{1,0:T(8,128)(2,1)S(1)} %get-tuple-element.171), channel_id=1, source_target_pairs={{0,3},{1,0},{2,1},{3,2},{4,7},{5,4},{6,5},{7,6},{8,11},{9,8},{10,9... | collective-permute-start | bytes 147464 | tf_op jit(solution)/shard_map/ppermute | solution.py:44
  161.1 7.4 %collective-permute-start.26 = (bf16[128,192]{1,0:T(8,128)(2,1)S(1)}, bf16[128,192]{1,0:T(8,128)(2,1)S(1)}, u32[]{:S(2)}, u32[]{:S(2)}) collective-permute-start(bf16[128,192]{1,0:T(8,128)(2,1)S(1)} %get-tuple-element.172), channel_id=1, source_target_pairs={{0,2},{1,3},{2,0},{3,1},{4,6},{5,7},{6,4},{7,5},{8,10},{9,11},{10,... | collective-permute-start | bytes 147464 | tf_op jit(solution)/shard_map/ppermute | solution.py:44
  161.6 7.0 %collective-permute-start.25 = (bf16[128,192]{1,0:T(8,128)(2,1)S(1)}, bf16[128,192]{1,0:T(8,128)(2,1)S(1)}, u32[]{:S(2)}, u32[]{:S(2)}) collective-permute-start(bf16[128,192]{1,0:T(8,128)(2,1)S(1)} %get-tuple-element.173), channel_id=1, source_target_pairs={{0,1},{1,2},{2,3},{3,0},{4,5},{5,6},{6,7},{7,4},{8,9},{9,10},{10,1... | collective-permute-start | bytes 147464 | tf_op jit(solution)/shard_map/ppermute | solution.py:44
  167.9 16.4 %collective-permute-start.30 = (f32[12,768]{1,0:T(8,128)}, f32[12,768]{1,0:T(8,128)S(1)}, u32[]{:S(2)}, u32[]{:S(2)}) collective-permute-start(f32[12,768]{1,0:T(8,128)} %pack.1), channel_id=1, source_target_pairs={{0,16},{16,0},{1,17},{17,1},{2,18},{18,2},{3,19},{19,3},{4,20},{20... | collective-permute-start | bytes 110600 | tf_op jit(solution)/shard_map/ppermute | solution.py:49
  185.5 2.5 collective-permute-start.31
  187.1 40.3 %collective-permute-start.33 = (bf16[384,768]{1,0:T(8,128)(2,1)S(1)}, bf16[384,768]{1,0:T(8,128)(2,1)}, u32[]{:S(2)}, u32[]{:S(2)}) collective-permute-start(bf16[384,768]{1,0:T(8,128)(2,1)S(1)} %fusion.12), channel_id=1, source_target_pairs={{0,4},{4,0},{8,12},{12,8},{1,5},{5,1},{9,13},{13,9},{2,6},{6,2},{1... | collective-permute-start | bytes 1769480 | tf_op jit(solution)/shard_map/ppermute | solution.py:49
  190.4 12.3 %collective-permute-start.32 = (bf16[1,384,512]{2,1,0:T(8,128)(2,1)}, bf16[1,384,512]{2,1,0:T(8,128)(2,1)}, u32[]{:S(2)}, u32[]{:S(2)}) collective-permute-start(bf16[1,384,512]{2,1,0:T(8,128)(2,1)} %slice.278), channel_id=1, source_target_pairs={{0,8},{4,12},{8,0},{12,4},{1,9},{5,13},{9,1},{13,5},{2,10},{6,14},... | collective-permute-start | bytes 1179656 | tf_op jit(solution)/shard_map/ppermute | solution.py:49
  193.2 34.3 %collective-permute-start.34 = (bf16[768,384]{1,0:T(8,128)(2,1)S(1)}, bf16[768,384]{1,0:T(8,128)(2,1)}, u32[]{:S(2)}, u32[]{:S(2)}) collective-permute-start(bf16[768,384]{1,0:T(8,128)(2,1)S(1)} %fusion.11), channel_id=1, source_target_pairs={{0,8},{4,12},{8,0},{12,4},{1,9},{5,13},{9,1},{13,5},{2,10},{6,14},... | collective-permute-start | bytes 1769480 | tf_op jit(solution)/shard_map/ppermute | solution.py:49
  193.7 4.5 %collective-permute-start.35 = (f32[12,768]{1,0:T(8,128)S(1)}, f32[12,768]{1,0:T(8,128)S(1)}, u32[]{:S(2)}, u32[]{:S(2)}) collective-permute-start(f32[12,768]{1,0:T(8,128)S(1)} %add.312), channel_id=1, source_target_pairs={{0,4},{4,0},{8,12},{12,8},{1,5},{5,1},{9,13},{13,9},{2,6},{6,2},{1... | collective-permute-start | bytes 110600 | tf_op jit(solution)/shard_map/ppermute | solution.py:49
  196.9 14.2 %collective-permute-start.36 = (bf16[128,1536]{1,0:T(8,128)(2,1)}, bf16[128,1536]{1,0:T(8,128)(2,1)S(1)}, u32[]{:S(2)}, u32[]{:S(2)}) collective-permute-start(bf16[128,1536]{1,0:T(8,128)(2,1)} %pad_maximum_fusion.8), channel_id=1, source_target_pairs={{0,1},{1,2},{2,3},{3,0},{4,5},{5,6},{6,7},{7,4},{8,9},{9,10},{10,1... | collective-permute-start | bytes 1179656 | tf_op jit(solution)/shard_map/ppermute | solution.py:44
  198.2 29.2 %collective-permute-start.37 = (bf16[128,1536]{1,0:T(8,128)(2,1)}, bf16[128,1536]{1,0:T(8,128)(2,1)S(1)}, u32[]{:S(2)}, u32[]{:S(2)}) collective-permute-start(bf16[128,1536]{1,0:T(8,128)(2,1)} %pad_maximum_fusion.8), channel_id=1, source_target_pairs={{0,2},{1,3},{2,0},{3,1},{4,6},{5,7},{6,4},{7,5},{8,10},{9,11},{10,... | collective-permute-start | bytes 1179656 | tf_op jit(solution)/shard_map/ppermute | solution.py:44
  202.7 24.7 %collective-permute-start.38 = (bf16[128,1536]{1,0:T(8,128)(2,1)}, bf16[128,1536]{1,0:T(8,128)(2,1)S(1)}, u32[]{:S(2)}, u32[]{:S(2)}) collective-permute-start(bf16[128,1536]{1,0:T(8,128)(2,1)} %pad_maximum_fusion.8), channel_id=1, source_target_pairs={{0,3},{1,0},{2,1},{3,2},{4,7},{5,4},{6,5},{7,6},{8,11},{9,8},{10,9... | collective-permute-start | bytes 1179656 | tf_op jit(solution)/shard_map/ppermute | solution.py:44
  205.9 21.6 %copy-start.5 = (bf16[512,768]{1,0:T(8,128)(2,1)S(1)}, bf16[512,768]{1,0:T(8,128)(2,1)}, u32[]{:S(2)}) copy-start(bf16[512,768]{1,0:T(8,128)(2,1)} %copy-done.4) | copy-start | bytes 2359300
  234.0 17.9 %collective-permute-start.41 = (bf16[128,768]{1,0:T(8,128)(2,1)S(1)}, bf16[128,768]{1,0:T(8,128)(2,1)S(1)}, u32[]{:S(2)}, u32[]{:S(2)}) collective-permute-start(bf16[128,768]{1,0:T(8,128)(2,1)S(1)} %get-tuple-element.135), channel_id=1, source_target_pairs={{0,1},{1,2},{2,3},{3,0},{4,5},{5,6},{6,7},{7,4},{8,9},{9,10},{10,1... | collective-permute-start | bytes 589832 | tf_op jit(solution)/shard_map/ppermute | solution.py:44
  243.0 13.0 %collective-permute-start.40 = (bf16[128,768]{1,0:T(8,128)(2,1)S(1)}, bf16[128,768]{1,0:T(8,128)(2,1)S(1)}, u32[]{:S(2)}, u32[]{:S(2)}) collective-permute-start(bf16[128,768]{1,0:T(8,128)(2,1)S(1)} %get-tuple-element.136), channel_id=1, source_target_pairs={{0,2},{1,3},{2,0},{3,1},{4,6},{5,7},{6,4},{7,5},{8,10},{9,11},{10,... | collective-permute-start | bytes 589832 | tf_op jit(solution)/shard_map/ppermute | solution.py:44
  243.3 14.1 %collective-permute-start.39 = (bf16[128,768]{1,0:T(8,128)(2,1)S(1)}, bf16[128,768]{1,0:T(8,128)(2,1)S(1)}, u32[]{:S(2)}, u32[]{:S(2)}) collective-permute-start(bf16[128,768]{1,0:T(8,128)(2,1)S(1)} %get-tuple-element.134), channel_id=1, source_target_pairs={{0,3},{1,0},{2,1},{3,2},{4,7},{5,4},{6,5},{7,6},{8,11},{9,8},{10,9... | collective-permute-start | bytes 589832 | tf_op jit(solution)/shard_map/ppermute | solution.py:44
  245.5 17.5 %collective-permute-start.42 = (bf16[192,384]{1,0:T(8,128)(2,1)S(1)}, bf16[192,384]{1,0:T(8,128)(2,1)S(1)}, u32[]{:S(2)}, u32[]{:S(2)}) collective-permute-start(bf16[192,384]{1,0:T(8,128)(2,1)S(1)} %split.99), channel_id=1, source_target_pairs={{0,16},{16,0},{1,17},{17,1},{2,18},{18,2},{3,19},{19,3},{4,20},{20... | collective-permute-start | bytes 442376 | tf_op jit(solution)/shard_map/ppermute | solution.py:49
  246.1 16.8 %collective-permute-start.43 = (f32[12,768]{1,0:T(8,128)S(1)}, f32[12,768]{1,0:T(8,128)S(1)}, u32[]{:S(2)}, u32[]{:S(2)}) collective-permute-start(f32[12,768]{1,0:T(8,128)S(1)} %add.317), channel_id=1, source_target_pairs={{0,8},{4,12},{8,0},{12,4},{1,9},{5,13},{9,1},{13,5},{2,10},{6,14},... | collective-permute-start | bytes 110600 | tf_op jit(solution)/shard_map/ppermute | solution.py:49
  251.9 11.1 %collective-permute-start.44 = (bf16[576,384]{1,0:T(8,128)(2,1)S(1)}, bf16[576,384]{1,0:T(8,128)(2,1)S(1)}, u32[]{:S(2)}, u32[]{:S(2)}) collective-permute-start(bf16[576,384]{1,0:T(8,128)(2,1)S(1)} %split.98), channel_id=1, source_target_pairs={{0,16},{16,0},{1,17},{17,1},{2,18},{18,2},{3,19},{19,3},{4,20},{20... | collective-permute-start | bytes 1327112 | tf_op jit(solution)/shard_map/ppermute | solution.py:49
  256.0 7.0 %collective-permute-start.45 = (f32[384]{0:T(512)S(1)}, f32[384]{0:T(512)S(1)}, u32[]{:S(2)}, u32[]{:S(2)}) collective-permute-start(f32[384]{0:T(512)S(1)} %pad_maximum_fusion.18), channel_id=1, source_target_pairs={{0,16},{16,0},{1,17},{17,1},{2,18},{18,2},{3,19},{19,3},{4,20},{20... | collective-permute-start | bytes 4616 | tf_op jit(solution)/shard_map/ppermute | solution.py:49
  257.4 32.2 %collective-permute-start.47 = (bf16[384,768]{1,0:T(8,128)(2,1)S(1)}, bf16[384,768]{1,0:T(8,128)(2,1)S(1)}, u32[]{:S(2)}, u32[]{:S(2)}) collective-permute-start(bf16[384,768]{1,0:T(8,128)(2,1)S(1)} %add_convert_fusion.1), channel_id=1, source_target_pairs={{0,8},{4,12},{8,0},{12,4},{1,9},{5,13},{9,1},{13,5},{2,10},{6,14},... | collective-permute-start | bytes 1769480 | tf_op jit(solution)/shard_map/ppermute | solution.py:49
  263.0 33.7 %collective-permute-start.48 = (bf16[768,384]{1,0:T(8,128)(2,1)S(1)}, bf16[768,384]{1,0:T(8,128)(2,1)S(1)}, u32[]{:S(2)}, u32[]{:S(2)}) collective-permute-start(bf16[768,384]{1,0:T(8,128)(2,1)S(1)} %add_convert_fusion), channel_id=1, source_target_pairs={{0,4},{4,0},{8,12},{12,8},{1,5},{5,1},{9,13},{13,9},{2,6},{6,2},{1... | collective-permute-start | bytes 1769480 | tf_op jit(solution)/shard_map/ppermute | solution.py:49
  263.0 34.9 %collective-permute-start.46 = (bf16[128,768]{1,0:T(8,128)(2,1)S(1)}, bf16[128,768]{1,0:T(8,128)(2,1)S(1)}, u32[]{:S(2)}, u32[]{:S(2)}) collective-permute-start(bf16[128,768]{1,0:T(8,128)(2,1)S(1)} %fusion.38), channel_id=1, source_target_pairs={{0,3},{1,0},{2,1},{3,2},{4,7},{5,4},{6,5},{7,6},{8,11},{9,8},{10,9... | collective-permute-start | bytes 589832 | tf_op jit(solution)/shard_map/ppermute | solution.py:44
  266.8 8.1 %collective-permute-start.49 = (f32[12,768]{1,0:T(8,128)S(1)}, f32[12,768]{1,0:T(8,128)S(1)}, u32[]{:S(2)}, u32[]{:S(2)}) collective-permute-start(f32[12,768]{1,0:T(8,128)S(1)} %add.322), channel_id=1, source_target_pairs={{0,1},{1,0},{2,3},{3,2},{4,5},{5,4},{6,7},{7,6},{8,9},{9,8},{10,11... | collective-permute-start | bytes 110600 | tf_op jit(solution)/shard_map/ppermute | solution.py:49
  266.9 1.2 collective-permute-start.57
  268.0 4.3 %collective-permute-start.58 = (f32[384]{0:T(512)S(1)}, f32[384]{0:T(512)S(1)}, u32[]{:S(2)}, u32[]{:S(2)}) collective-permute-start(f32[384]{0:T(512)S(1)} %add.332), channel_id=1, source_target_pairs={{0,8},{4,12},{8,0},{12,4},{1,9},{5,13},{9,1},{13,5},{2,10},{6,14},... | collective-permute-start | bytes 4616 | tf_op jit(solution)/shard_map/ppermute | solution.py:49
  272.3 25.5 %collective-permute-start.52 = (bf16[128,768]{1,0:T(8,128)(2,1)S(1)}, bf16[128,768]{1,0:T(8,128)(2,1)S(1)}, u32[]{:S(2)}, u32[]{:S(2)}) collective-permute-start(bf16[128,768]{1,0:T(8,128)(2,1)S(1)} %fusion.38), channel_id=1, source_target_pairs={{0,2},{1,3},{2,0},{3,1},{4,6},{5,7},{6,4},{7,5},{8,10},{9,11},{10,... | collective-permute-start | bytes 589832 | tf_op jit(solution)/shard_map/ppermute | solution.py:44
  274.9 10.5 %collective-permute-start.50 = (f32[12,768]{1,0:T(8,128)S(1)}, f32[12,768]{1,0:T(8,128)S(1)}, u32[]{:S(2)}, u32[]{:S(2)}) collective-permute-start(f32[12,768]{1,0:T(8,128)S(1)} %add.323), channel_id=1, source_target_pairs={{0,2},{1,3},{2,0},{3,1},{4,6},{5,7},{6,4},{7,5},{8,10},{9,11},{10,... | collective-permute-start | bytes 110600 | tf_op jit(solution)/shard_map/ppermute | solution.py:49
  285.5 12.4 %collective-permute-start.51 = (bf16[128,768]{1,0:T(8,128)(2,1)S(1)}, bf16[128,768]{1,0:T(8,128)(2,1)}, u32[]{:S(2)}, u32[]{:S(2)}) collective-permute-start(bf16[128,768]{1,0:T(8,128)(2,1)S(1)} %fusion.38), channel_id=1, source_target_pairs={{0,1},{1,2},{2,3},{3,0},{4,5},{5,6},{6,7},{7,4},{8,9},{9,10},{10,1... | collective-permute-start | bytes 589832 | tf_op jit(solution)/shard_map/ppermute | solution.py:44
  289.6 5.5 %collective-permute-start.55 = (bf16[192,384]{1,0:T(8,128)(2,1)S(1)}, bf16[192,384]{1,0:T(8,128)(2,1)S(1)}, u32[]{:S(2)}, u32[]{:S(2)}) collective-permute-start(bf16[192,384]{1,0:T(8,128)(2,1)S(1)} %fusion.45), channel_id=1, source_target_pairs={{0,8},{4,12},{8,0},{12,4},{1,9},{5,13},{9,1},{13,5},{2,10},{6,14},... | collective-permute-start | bytes 442376 | tf_op jit(solution)/shard_map/ppermute | solution.py:49
  295.1 11.1 %collective-permute-start.53 = (bf16[576,384]{1,0:T(8,128)(2,1)S(1)}, bf16[576,384]{1,0:T(8,128)(2,1)S(1)}, u32[]{:S(2)}, u32[]{:S(2)}) collective-permute-start(bf16[576,384]{1,0:T(8,128)(2,1)S(1)} %fusion.13), channel_id=1, source_target_pairs={{0,8},{4,12},{8,0},{12,4},{1,9},{5,13},{9,1},{13,5},{2,10},{6,14},... | collective-permute-start | bytes 1327112 | tf_op jit(solution)/shard_map/ppermute | solution.py:49
  296.6 11.1 %collective-permute-start.56 = (bf16[192,384]{1,0:T(8,128)(2,1)S(1)}, bf16[192,384]{1,0:T(8,128)(2,1)S(1)}, u32[]{:S(2)}, u32[]{:S(2)}) collective-permute-start(bf16[192,384]{1,0:T(8,128)(2,1)S(1)} %add_convert_fusion.3), channel_id=1, source_target_pairs={{0,4},{4,0},{8,12},{12,8},{1,5},{5,1},{9,13},{13,9},{2,6},{6,2},{1... | collective-permute-start | bytes 442376 | tf_op jit(solution)/shard_map/ppermute | solution.py:49
  306.3 2.2 collective-permute-start.54
  (51 other events, 329.4 us)

commit v3 on v2

--- a/solution.py
+++ b/solution.py
@@ -102,13 +102,15 @@
 
 
 class VectorSum:
-    def __init__(self, vector, axes):
+    def __init__(self, vector, axes, far_first=False):
         self.bits = []
         for axis in axes:
             bit = 1
             while bit < lax.axis_size(axis):
                 self.bits.append((axis, bit))
                 bit *= 2
+        if far_first:
+            self.bits.reverse()
         self.kept, self.moved = vector, flipped(vector, *self.bits.pop(0))
 
     def step(self):
@@ -140,12 +142,13 @@
     return held, beside
 
 
-def scatter_parts(blocks):
+def scatter_parts(blocks, sent):
     size, bit = lax.axis_size("ctx"), 1
     while bit < size:
+        blocks = blocks.astype(F32) + flipped(sent.astype(BF16), "ctx", bit).astype(F32)
         half = blocks.shape[0] // 2
-        moved = flipped(blocks[half:].astype(BF16), "ctx", bit)
-        blocks = blocks[:half].astype(F32) + moved.astype(F32)
+        if half:
+            blocks, sent = blocks[:half], blocks[half:]
         bit *= 2
     return blocks[0]
 
@@ -160,6 +163,23 @@
             for e in range(size)
         ],
         0,
+    )
+
+
+def rows_place(blocks):
+    size = lax.axis_size("tp")
+    place = lax.axis_index("tp")
+    return jnp.concatenate(
+        [lax.select_n(lax.rem(place - p + size, size), *blocks) for p in range(size)], 0
+    )
+
+
+def columns_turn(block):
+    size = lax.axis_size("tp")
+    place = lax.axis_index("tp")
+    blocks = jnp.split(block, size, 1)
+    return jnp.concatenate(
+        [lax.select_n(lax.rem(place - e + size, size), *blocks) for e in range(size)], 1
     )
 
 
@@ -270,7 +290,7 @@
 
 
 def attend_back_kernel(heads, scale, parts, starts, weights, context, d_mixed, inverse, query, *refs):
-    kv, (d_scores, d_query, d_kv, total) = blocks_of(refs[:parts]), refs[parts:]
+    kv, (d_scores, d_query, d_kept, d_sent, total) = blocks_of(refs[:parts]), refs[parts:]
     width = context.shape[1]
     size = width // heads
     block = kv[0].shape[0]
@@ -313,7 +333,9 @@
     @pl.when(step == pl.num_programs(0) - 1)
     def _():
         for e in range(len(kv)):
-            d_kv[e] = total[:, e * block : (e + 1) * block].astype(BF16)
+            half = d_kept.shape[0]
+            target, index = (d_kept, e) if e < half else (d_sent, e - half)
+            target[index] = total[:, e * block : (e + 1) * block].astype(BF16)
 
 
 def attend_back(weights, kv, starts, context, d_mixed, inverse, query, scale):
@@ -322,7 +344,7 @@
     block = kv[0].shape[1]
     tile = lambda i, *scalars: (i, 0)
     whole = lambda i, *scalars: (0, 0, 0)
-    shape = (keys // block, 2 * width, block)
+    shape = (keys // block // 2, 2 * width, block)
     return pl.pallas_call(
         partial(attend_back_kernel, heads, scale, len(kv)),
         grid_spec=pltpu.PrefetchScalarGridSpec(
@@ -335,12 +357,14 @@
                 pl.BlockSpec((1, heads, TILE, keys), lambda i, *scalars: (0, 0, i, 0)),
                 pl.BlockSpec((TILE, width), tile),
                 pl.BlockSpec(shape, whole),
+                pl.BlockSpec(shape, whole),
             ],
             scratch_shapes=[pltpu.VMEM((2 * width, keys), F32)],
         ),
         out_shape=[
             jax.ShapeDtypeStruct((1, heads, rows, keys), BF16),
             jax.ShapeDtypeStruct((rows, width), F32),
+            jax.ShapeDtypeStruct(shape, BF16),
             jax.ShapeDtypeStruct(shape, BF16),
         ],
         cost_estimate=pl.CostEstimate(
@@ -476,8 +500,7 @@
     grad_bias_output = jnp.sum(d_first, 0)
     d_first_low = own_first(d_first.astype(BF16))
     d_context_mine = dot32(d_first_low, full_output, ((1,), (1,))).astype(BF16)
-    d_context = jnp.concatenate(rows_exchange(jnp.split(d_context_mine, tp_size, 1)), 0)
-    d_context = rows_turn(d_context)
+    d_context = rows_place(rows_exchange(jnp.split(d_context_mine, tp_size, 1)))
 
     packed = (
         pack(
@@ -495,7 +518,7 @@
             tp_size,
         )
     )
-    early_sum = VectorSum(packed, ("dp", "ctx", "tp"))
+    early_sum = VectorSum(packed, ("dp", "ctx"))
     d_context, outer_sum.moved, inner_sum.moved = tie(
         d_context, outer_sum.moved, inner_sum.moved
     )
@@ -504,46 +527,59 @@
     both_mine = jnp.concatenate([d_first_low, result.astype(BF16)], 1)
     both_mine, _ = tie(both_mine, d_context)
     both_moved = rows_moved(both_mine)
-    d_scores, d_query, d_kv_parts = attend_back(
+    d_scores, d_query, d_kept, d_sent = attend_back(
         weights, kv_all, starts, context, d_context, inverse, query_scaled, score_scale
     )
-    d_kv_parts, early_sum.moved = tie(d_kv_parts, early_sum.moved)
+    d_sent, early_sum.moved = tie(d_sent, early_sum.moved)
     early_sum.step()
-    d_kv = scatter_parts(d_kv_parts)
+    d_kv = scatter_parts(d_kept, d_sent)
     d_query_low = d_query.astype(BF16)
-    d_kv_low, inner_sum.moved, outer_sum.moved, early_sum.moved, *both_moved = tie(
-        d_kv.astype(BF16), inner_sum.moved, outer_sum.moved, early_sum.moved, *both_moved
+    d_kv_low, inner_sum.moved, outer_sum.moved, early_sum.moved = tie(
+        d_kv.astype(BF16), inner_sum.moved, outer_sum.moved, early_sum.moved
+    )
+    tokens_part = rows_sum(
+        dot32(rows_turn(d_query_low), full_qkv[:width_local], ((1,), (0,)))
+        + dot32(columns_turn(d_kv_low), full_qkv[width_local:], ((0,), (0,))),
     )
     inner_sum.step()
     outer_sum.step()
     early_sum.step()
-    both = jnp.concatenate([both_mine] + both_moved, 0)
-    d_first_all = both[:, :model_width]
-    output_gradient = dot32(context_turned, d_first_all, ((0,), (0,)))
+    query_gradient = dot32(d_query_low, tokens_first, ((0,), (0,)))
+    kv_gradient = dot32(d_kv_low, tokens_first, ((1,), (0,)))
+    qkv_gradient = jnp.concatenate([query_gradient, kv_gradient], 0)
+    qkv_sum = WeightSum(qkv_gradient, 1, True)
+    both = [both_mine] + both_moved
+    output_gradient = sum(
+        dot32(rows, moved[:, :model_width], ((0,), (0,)))
+        for rows, moved in zip(jnp.split(context_turned, tp_size, 0), both)
+    )
     output_sum = WeightSum(output_gradient, 1, True)
-    d_qkv_low = jnp.concatenate([d_query_low, d_kv_low.T], 1)
-    tokens_part = rows_sum(dot32(rows_turn(d_qkv_low), full_qkv, ((1,), (0,))))
-    qkv_gradient = dot32(d_qkv_low, tokens_first, ((0,), (0,)))
-    qkv_sum = WeightSum(qkv_gradient, 1, True)
     late_vector = jnp.concatenate([jnp.sum(d_query, 0), jnp.sum(d_kv[width_local:], 1)])
-    late_sum = VectorSum(late_vector, ("dp", "ctx"))
+    late_sum = VectorSum(late_vector, ("dp", "ctx"), True)
     grad_mine = (d_first + own_first(tokens_part)).astype(BF16)
     sums = (output_sum, early_sum, qkv_sum, late_sum)
     grad_mine, *moved = tie(grad_mine, *[one.moved for one in sums])
     for one, value in zip(sums, moved):
         one.moved = value
-    for one in sums:
+    early = early_sum.total()
+    moved = []
+    for e in range(1, tp_size):
+        moved.append(flipped(early, "tp", e))
+    early = [early] + moved
+    while len(early) > 1:
+        early = [left + right for left, right in zip(early[::2], early[1::2])]
+    early = early[0]
+    for one in (output_sum, qkv_sum, late_sum):
         one.step()
     grad_moved = rows_moved(grad_mine)
     inner_shard, outer_shard = inner_sum.total(), outer_sum.total()
-    result_all = rows_turn(both[:, model_width:]).astype(F32)
+    result_all = rows_place([block[:, model_width:] for block in both]).astype(F32)
     grad_moved[-1], inner_shard, outer_shard, result_all = tie(
         grad_moved[-1], inner_shard, outer_shard, result_all
     )
-    grad_inputs = rows_turn(jnp.concatenate([grad_mine] + grad_moved, 0)).astype(F32)
+    grad_inputs = rows_place([grad_mine] + grad_moved).astype(F32)
     output_shard = output_sum.total()
     shard_qkv = qkv_sum.total()
-    early = early_sum.total()
     loss_value = early[6, 0] / (all_count * model_width)
     inner_rows = grad_bias_inner.shape[0] // model_width
     sum_bias_inner = lax.dynamic_slice_in_dim(early, 8 + tp_place * inner_rows, inner_rows, 0).reshape(-1)

time: 312 us -> 285 us (0.913)
  waiting for transfers between devices: 121 us -> 97.6 us
  local copies, waits for them, and re-layouts: 25.6 us -> 20.2 us
  matrix products: 17.7 us -> 22 us
    ppermute x29 -> x30, waiting for transfers between devices: 52.9 us -> 41.3 us  [flipped(): return lax.ppermute(block, axis, [(i, i ^ bit) for i in range(size)])]
    ppermute x30, waiting for transfers between devices: 67.7 us -> 56.3 us  [shifted(): lax.ppermute(block, axis, [(i, (i + step) % size) for i in range(size)])]
    ppermute x30, starting transfers between devices: 58.1 us -> 51.5 us  [shifted(): lax.ppermute(block, axis, [(i, (i + step) % size) for i in range(size)])]
    ppermute x29 -> x30, starting transfers between devices: 26 us -> 31.6 us  [flipped(): return lax.ppermute(block, axis, [(i, i ^ bit) for i in range(size)])]
    dot_general x13 -> x18, matrix products: 17.7 us -> 22 us  [dot32(): lax.dot_general(left, right, (dims, ((), ())), preferred_element_type=F32)]
    unnamed x122 -> x121, local copies, waits for them, and re-layouts: 7.1 us -> 4.47 us
  transfers between devices with their start and end apart: 59 -> 60, of which waited for: 24 -> 23; matrix products, arithmetic and copies ran while one was open for 18% -> 20% of each run, Pallas kernels for 9% -> 10%
where the time goes in v3:
time: 285 us
  waiting for transfers between devices  97.6 us (34%)
  starting transfers between devices  83.1 us (29%)
  other arithmetic  28.5 us (10%)
  Pallas kernels  28 us (10%)
  matrix products  22 us (8%)
  local copies, waits for them, and re-layouts  20.2 us (7%)
  between operations  5.15 us (2%)
    ppermute x30, waiting for transfers between devices, shifted(): lax.ppermute(block, axis, [(i, (i + step) % size) for i in range(size)])  56.3 us
    ppermute x30, starting transfers between devices, shifted(): lax.ppermute(block, axis, [(i, (i + step) % size) for i in range(size)])  51.5 us
    ppermute x30, waiting for transfers between devices, flipped(): return lax.ppermute(block, axis, [(i, i ^ bit) for i in range(size)])  41.3 us
    ppermute x30, starting transfers between devices, flipped(): return lax.ppermute(block, axis, [(i, i ^ bit) for i in range(size)])  31.6 us
    dot_general x18, matrix products, dot32(): lax.dot_general(left, right, (dims, ((), ())), preferred_element_type=F32)  22 us
    pallas_call x1, Pallas kernels, attend_back(): pl.pallas_call(partial(attend_back_kernel, heads, scale, len(kv)), grid_s...  13.3 us
    pallas_call x1, Pallas kernels, attend(): pl.pallas_call(partial(attend_kernel, heads, len(kv)), grid_spec=pltpu.Pr...  12.6 us
  transfers between devices with their start and end apart: 60, of which 23 were waited for; matrix products, arithmetic and copies ran while one was open for 20% of the time, Pallas kernels for 10%

profile of v3, /device:TPU:0, one launch (start us, length us, event | category | flops | bytes accessed | tf_op | source)
XLA Modules:
  0.0 284.6 jit_solution(910676936776447299)
XLA Ops:
  0.7 5.1 %collective-permute-start.4 = (bf16[192,384]{1,0:T(8,128)(2,1)}, bf16[192,384]{1,0:T(8,128)(2,1)}, u32[]{:S(2)}, u32[]{:S(2)}) collective-permute-start(bf16[192,384]{1,0:T(8,128)(2,1)} %param.27), channel_id=1, source_target_pairs={{0,3},{1,0},{2,1},{3,2},{4,7},{5,4},{6,5},{7,6},{8,11},{9,8},{10,9... | collective-permute-start | bytes 442376 | tf_op jit(solution)/shard_map/ppermute | solution.py:44
  6.8 1.9 pad_maximum_fusion.6
  8.7 1.5 collective-permute-start.1
  11.7 6.9 %collective-permute-done.3 = bf16[192,384]{1,0:T(8,128)(2,1)} collective-permute-done((bf16[192,384]{1,0:T(8,128)(2,1)}, bf16[192,384]{1,0:T(8,128)(2,1)}, u32[]{:S(2)}, u32[]{:S(2)}) %collective-permute-start.3) | collective-permute-done | bytes 147488 | tf_op jit(solution)/shard_map/ppermute | solution.py:44
  18.6 1.9 pad_maximum_fusion.5
  21.3 1.6 collective-permute-start.5
  24.0 7.8 %collective-permute-done.5.refs_1_ = bf16[1,512,384]{2,1,0:T(8,128)(2,1)S(1)} collective-permute-done((bf16[1,512,384]{2,1,0:T(8,128)(2,1)S(1)}, bf16[1,512,384]{2,1,0:T(8,128)(2,1)S(1)}, u32[]{:S(2)}, u32[]{:S(2)}) %collective-permute-start.5) | collective-permute-done | bytes 393248 | tf_op jit(solution)/shard_map/ppermute | solution.py:49
  33.5 2.8 %collective-permute-start = (f32[]{:T(128)}, f32[]{:T(128)}, u32[]{:S(2)}, u32[]{:S(2)}) collective-permute-start(f32[]{:T(128)} %convert_element_type.210), channel_id=1, source_target_pairs={{0,16},{16,0},{1,17},{17,1},{2,18},{18,2},{3,19},{19,3},{4,20},{20... | collective-permute-start | bytes 20 | tf_op jit(solution)/shard_map/ppermute | solution.py:49
  39.2 12.6 %attend.1 = (bf16[1,3,512,2048]{3,2,1,0:T(8,128)(2,1)}, bf16[3,512,2048]{2,1,0:T(8,128)(2,1)}, bf16[512,192]{1,0:T(8,128)(2,1)}, f32[512,192]{1,0:T(8,128)}) custom-call(s32[2]{0:T(128)} %multiply_minimum_fusion.limits, s32[4]{0:T(128)} %xor_multiply_fusion.starts, bf16[512,192]{1,0:T(8,128)(2,1)} %fusion.11.query, bf16[1,3,512,2048]{3,2,1,0:T(8,128)(2,1)} %prior.1, ...), custom_call_target="tpu_custom_call" | custom-call | flops 805306368 | bytes 18874368 | tf_op jit(solution)/shard_map/attend/pallas_call | solution.py:265
  54.1 1.5 collective-permute-start.14
  55.6 1.5 collective-permute-start.10
  58.4 1.9 collective-permute-start.8
  62.2 1.5 collective-permute-done.9
  65.9 1.7 collective-permute-start.13
  67.6 2.7 collective-permute-done.14
  71.1 10.3 %collective-permute-done.15 = bf16[768,384]{1,0:T(8,128)(2,1)S(1)} collective-permute-done((bf16[768,384]{1,0:T(8,128)(2,1)S(1)}, bf16[768,384]{1,0:T(8,128)(2,1)S(1)}, u32[]{:S(2)}, u32[]{:S(2)}) %collective-permute-start.15) | collective-permute-done | bytes 589856 | tf_op jit(solution)/shard_map/ppermute | solution.py:49
  81.5 3.0 %collective-permute-done.12 = bf16[128,768]{1,0:T(8,128)(2,1)S(1)} collective-permute-done((bf16[128,768]{1,0:T(8,128)(2,1)S(1)}, bf16[128,768]{1,0:T(8,128)(2,1)S(1)}, u32[]{:S(2)}, u32[]{:S(2)}) %collective-permute-start.12) | collective-permute-done | bytes 196640 | tf_op jit(solution)/shard_map/ppermute | solution.py:44
  84.6 5.6 %multiply_convert_fusion = (bf16[512,768]{1,0:T(8,128)(2,1)S(1)}, f32[512,768]{1,0:T(8,128)}, f32[512,768]{1,0:T(8,128)}) fusion(f32[768]{0:T(1024)S(1)} %copy-done.56, bf16[768,768]{1,0:T(8,128)(2,1)S(1)} %constant_dynamic-update-slice_fusion.2, bf16[128,768]{1,0:T(8,128)(2,1)S(1)} %collective-permute-done.13, ...), kind=kOutput, calls=%fused_computation.6 | convolution fusion | flops 633077760 | bytes 5901312 | tf_op jit(solution)/shard_map/dot_general | solution.py:39
  90.3 1.9 fusion.107
  93.2 1.9 collective-permute-start.17
  95.1 2.9 %collective-permute-start.16 = (bf16[128,768]{1,0:T(8,128)(2,1)}, bf16[128,768]{1,0:T(8,128)(2,1)S(1)}, u32[]{:S(2)}, u32[]{:S(2)}) collective-permute-start(bf16[128,768]{1,0:T(8,128)(2,1)} %get-tuple-element.136), channel_id=1, source_target_pairs={{0,3},{1,0},{2,1},{3,2},{4,7},{5,4},{6,5},{7,6},{8,11},{9,8},{10,9... | collective-permute-start | bytes 589832 | tf_op jit(solution)/shard_map/ppermute | solution.py:44
  100.8 2.0 collective-permute-done.18
  102.8 6.3 %collective-permute-done.17 = bf16[128,768]{1,0:T(8,128)(2,1)S(1)} collective-permute-done((bf16[128,768]{1,0:T(8,128)(2,1)}, bf16[128,768]{1,0:T(8,128)(2,1)S(1)}, u32[]{:S(2)}, u32[]{:S(2)}) %collective-permute-start.17) | collective-permute-done | bytes 196640 | tf_op jit(solution)/shard_map/ppermute | solution.py:44
  113.2 1.5 fusion.84
  114.8 6.7 %collective-permute-start.21 = (bf16[128,768]{1,0:T(8,128)(2,1)S(1)}, bf16[128,768]{1,0:T(8,128)(2,1)S(1)}, u32[]{:S(2)}, u32[]{:S(2)}) collective-permute-start(bf16[128,768]{1,0:T(8,128)(2,1)S(1)} %maximum_select_fusion.6), channel_id=1, source_target_pairs={{0,3},{1,0},{2,1},{3,2},{4,7},{5,4},{6,5},{7,6},{8,11},{9,8},{10,9... | collective-permute-start | bytes 589832 | tf_op jit(solution)/shard_map/ppermute | solution.py:44
  122.2 1.3 reshape.196.refs_1_
  123.4 1.3 reshape.199.refs_4_
  126.9 11.7 %collective-permute-done.20 = bf16[128,768]{1,0:T(8,128)(2,1)} collective-permute-done((bf16[128,768]{1,0:T(8,128)(2,1)S(1)}, bf16[128,768]{1,0:T(8,128)(2,1)}, u32[]{:S(2)}, u32[]{:S(2)}) %collective-permute-start.20) | collective-permute-done | bytes 196640 | tf_op jit(solution)/shard_map/ppermute | solution.py:44
  138.6 3.7 %fusion.109 = (f32[768]{0:T(1024)S(1)}, bf16[512,768]{1,0:T(8,128)(2,1)S(1)}) fusion(f32[512,768]{1,0:T(8,128)} %get-tuple-element.116, f32[512,768]{1,0:T(8,128)} %get-tuple-element.183, bf16[768,768]{1,0:T(8,128)(2,1)} %copy-done.5, bf16[128,768]{1,0:T(8,128)(2,1)S(1)} %collective-permute-done.21, bf16[128,768]{1,0:T(8,128)(2,1)} %collective-permute-done.20, ...), kind=kOutput, calls=%fused_computation.244 | convolution fusion | flops 613022976 | bytes 5901312 | tf_op jit(solution)/shard_map/dot_general | solution.py:39
  143.3 1.8 collective-permute-start.23
  145.1 2.9 %collective-permute-start.22 = (bf16[128,768]{1,0:T(8,128)(2,1)S(1)}, bf16[128,768]{1,0:T(8,128)(2,1)S(1)}, u32[]{:S(2)}, u32[]{:S(2)}) collective-permute-start(bf16[128,768]{1,0:T(8,128)(2,1)S(1)} %get-tuple-element.133), channel_id=1, source_target_pairs={{0,3},{1,0},{2,1},{3,2},{4,7},{5,4},{6,5},{7,6},{8,11},{9,8},{10,9... | collective-permute-start | bytes 589832 | tf_op jit(solution)/shard_map/ppermute | solution.py:44
  148.0 1.8 fusion.70
  153.2 1.5 collective-permute-start.29
  155.3 4.3 %collective-permute-done.23 = bf16[128,768]{1,0:T(8,128)(2,1)S(1)} collective-permute-done((bf16[128,768]{1,0:T(8,128)(2,1)S(1)}, bf16[128,768]{1,0:T(8,128)(2,1)S(1)}, u32[]{:S(2)}, u32[]{:S(2)}) %collective-permute-start.23) | collective-permute-done | bytes 196640 | tf_op jit(solution)/shard_map/ppermute | solution.py:44
  161.0 2.9 %collective-permute-start.26 = (bf16[128,192]{1,0:T(8,128)(2,1)S(1)}, bf16[128,192]{1,0:T(8,128)(2,1)S(1)}, u32[]{:S(2)}, u32[]{:S(2)}) collective-permute-start(bf16[128,192]{1,0:T(8,128)(2,1)S(1)} %get-tuple-element.174), channel_id=1, source_target_pairs={{0,2},{1,3},{2,0},{3,1},{4,6},{5,7},{6,4},{7,5},{8,10},{9,11},{10,... | collective-permute-start | bytes 147464 | tf_op jit(solution)/shard_map/ppermute | solution.py:44
  163.9 3.4 %collective-permute-start.27 = (bf16[128,192]{1,0:T(8,128)(2,1)S(1)}, bf16[128,192]{1,0:T(8,128)(2,1)S(1)}, u32[]{:S(2)}, u32[]{:S(2)}) collective-permute-start(bf16[128,192]{1,0:T(8,128)(2,1)S(1)} %get-tuple-element.173), channel_id=1, source_target_pairs={{0,3},{1,0},{2,1},{3,2},{4,7},{5,4},{6,5},{7,6},{8,11},{9,8},{10,9... | collective-permute-start | bytes 147464 | tf_op jit(solution)/shard_map/ppermute | solution.py:44
  169.0 2.1 pack.1
  171.7 1.6 collective-permute-done.25
  174.1 3.8 %collective-permute-done.29 = bf16[384,768]{1,0:T(8,128)(2,1)} collective-permute-done((bf16[384,768]{1,0:T(8,128)(2,1)}, bf16[384,768]{1,0:T(8,128)(2,1)}, u32[]{:S(2)}, u32[]{:S(2)}) %collective-permute-start.29) | collective-permute-done | bytes 589856 | tf_op jit(solution)/shard_map/ppermute | solution.py:49
  178.3 1.6 collective-permute-start.39
  181.0 13.3 %attend_back.1 = (bf16[1,3,512,2048]{3,2,1,0:T(8,128)(2,1)}, f32[512,192]{1,0:T(8,128)}, bf16[2,384,512]{2,1,0:T(8,128)(2,1)}, bf16[2,384,512]{2,1,0:T(8,128)(2,1)}) custom-call(s32[4]{0:T(128)} %xor_multiply_fusion.starts, bf16[3,512,2048]{2,1,0:T(8,128)(2,1)} %get-tuple-element.64.weights, bf16[512,192]{1,0:T(8,128)(2,1)} %get-tuple-element.58.context, ...), custom_call_target="tpu_custom_call" | custom-call | flops 2013265920 | bytes 18874368 | tf_op jit(solution)/shard_map/attend_back/pallas_call | solution.py:348
  194.5 1.7 fusion.13
  198.6 1.6 collective-permute-start.34
  202.1 9.0 %collective-permute-done.40 = bf16[128,1536]{1,0:T(8,128)(2,1)} collective-permute-done((bf16[128,1536]{1,0:T(8,128)(2,1)S(1)}, bf16[128,1536]{1,0:T(8,128)(2,1)}, u32[]{:S(2)}, u32[]{:S(2)}) %collective-permute-start.40) | collective-permute-done | bytes 393248 | tf_op jit(solution)/shard_map/ppermute | solution.py:44
  214.3 1.6 collective-permute-start.32
  218.3 4.2 %collective-permute-done.32 = bf16[1,384,512]{2,1,0:T(8,128)(2,1)S(1)} collective-permute-done((bf16[1,384,512]{2,1,0:T(8,128)(2,1)S(1)}, bf16[1,384,512]{2,1,0:T(8,128)(2,1)S(1)}, u32[]{:S(2)}, u32[]{:S(2)}) %collective-permute-start.32) | collective-permute-done | bytes 393248 | tf_op jit(solution)/shard_map/ppermute | solution.py:49
  224.9 2.7 collective-permute-start.38
  227.7 3.2 %collective-permute-start.37 = (bf16[128,768]{1,0:T(8,128)(2,1)S(1)}, bf16[128,768]{1,0:T(8,128)(2,1)S(1)}, u32[]{:S(2)}, u32[]{:S(2)}) collective-permute-start(bf16[128,768]{1,0:T(8,128)(2,1)S(1)} %get-tuple-element.132), channel_id=1, source_target_pairs={{0,2},{1,3},{2,0},{3,1},{4,6},{5,7},{6,4},{7,5},{8,10},{9,11},{10,... | collective-permute-start | bytes 589832 | tf_op jit(solution)/shard_map/ppermute | solution.py:44
  230.8 1.6 collective-permute-start.43
  233.0 3.1 %collective-permute-done.38 = bf16[128,768]{1,0:T(8,128)(2,1)S(1)} collective-permute-done((bf16[128,768]{1,0:T(8,128)(2,1)S(1)}, bf16[128,768]{1,0:T(8,128)(2,1)S(1)}, u32[]{:S(2)}, u32[]{:S(2)}) %collective-permute-start.38) | collective-permute-done | bytes 196640 | tf_op jit(solution)/shard_map/ppermute | solution.py:44
  236.1 1.4 collective-permute-start.44
  237.5 5.2 %collective-permute-done.37 = bf16[128,768]{1,0:T(8,128)(2,1)S(1)} collective-permute-done((bf16[128,768]{1,0:T(8,128)(2,1)S(1)}, bf16[128,768]{1,0:T(8,128)(2,1)S(1)}, u32[]{:S(2)}, u32[]{:S(2)}) %collective-permute-start.37) | collective-permute-done | bytes 196640 | tf_op jit(solution)/shard_map/ppermute | solution.py:44
  242.7 1.5 collective-permute-start.45
  245.0 1.3 collective-permute-done.45
  246.3 5.4 %collective-permute-start.50 = (f32[12,768]{1,0:T(8,128)S(1)}, f32[12,768]{1,0:T(8,128)S(1)}, u32[]{:S(2)}, u32[]{:S(2)}) collective-permute-start(f32[12,768]{1,0:T(8,128)S(1)} %add.331), channel_id=1, source_target_pairs={{0,2},{1,3},{2,0},{3,1},{4,6},{5,7},{6,4},{7,5},{8,10},{9,11},{10,... | collective-permute-start | bytes 110600 | tf_op jit(solution)/shard_map/ppermute | solution.py:49
  252.9 1.5 collective-permute-start.59
  254.5 2.1 collective-permute-done.59
  257.8 3.2 %collective-permute-start.46 = (bf16[128,768]{1,0:T(8,128)(2,1)S(1)}, bf16[128,768]{1,0:T(8,128)(2,1)S(1)}, u32[]{:S(2)}, u32[]{:S(2)}) collective-permute-start(bf16[128,768]{1,0:T(8,128)(2,1)S(1)} %fusion.41), channel_id=1, source_target_pairs={{0,3},{1,0},{2,1},{3,2},{4,7},{5,4},{6,5},{7,6},{8,11},{9,8},{10,9... | collective-permute-start | bytes 589832 | tf_op jit(solution)/shard_map/ppermute | solution.py:44
  261.6 2.0 collective-permute-start.52
  265.4 1.6 collective-permute-start.56
  268.1 2.8 collective-permute-done.56
  270.9 1.6 collective-permute-start.54
  272.6 2.2 convert_add_fusion.1
  274.8 5.2 %collective-permute-done.54 = bf16[576,384]{1,0:T(8,128)(2,1)S(1)} collective-permute-done((bf16[576,384]{1,0:T(8,128)(2,1)S(1)}, bf16[576,384]{1,0:T(8,128)(2,1)S(1)}, u32[]{:S(2)}, u32[]{:S(2)}) %collective-permute-start.54) | collective-permute-done | bytes 442400 | tf_op jit(solution)/shard_map/ppermute | solution.py:49
  (304 shorter events, 59.6 us)
Async XLA Ops:
  0.7 11.0 %collective-permute-start.4 = (bf16[192,384]{1,0:T(8,128)(2,1)}, bf16[192,384]{1,0:T(8,128)(2,1)}, u32[]{:S(2)}, u32[]{:S(2)}) collective-permute-start(bf16[192,384]{1,0:T(8,128)(2,1)} %param.27), channel_id=1, source_target_pairs={{0,3},{1,0},{2,1},{3,2},{4,7},{5,4},{6,5},{7,6},{8,11},{9,8},{10,9... | collective-permute-start | bytes 442376 | tf_op jit(solution)/shard_map/ppermute | solution.py:44
  5.8 12.8 %collective-permute-start.3 = (bf16[192,384]{1,0:T(8,128)(2,1)}, bf16[192,384]{1,0:T(8,128)(2,1)}, u32[]{:S(2)}, u32[]{:S(2)}) collective-permute-start(bf16[192,384]{1,0:T(8,128)(2,1)} %param.27), channel_id=1, source_target_pairs={{0,2},{1,3},{2,0},{3,1},{4,6},{5,7},{6,4},{7,5},{8,10},{9,11},{10,... | collective-permute-start | bytes 442376 | tf_op jit(solution)/shard_map/ppermute | solution.py:44
  5.8 12.8 %collective-permute-start.2 = (bf16[192,384]{1,0:T(8,128)(2,1)}, bf16[192,384]{1,0:T(8,128)(2,1)}, u32[]{:S(2)}, u32[]{:S(2)}) collective-permute-start(bf16[192,384]{1,0:T(8,128)(2,1)} %param.27), channel_id=1, source_target_pairs={{0,1},{1,2},{2,3},{3,0},{4,5},{5,6},{6,7},{7,4},{8,9},{9,10},{10,1... | collective-permute-start | bytes 442376 | tf_op jit(solution)/shard_map/ppermute | solution.py:44
  8.7 11.9 %collective-permute-start.1 = (bf16[576,384]{1,0:T(8,128)(2,1)}, bf16[576,384]{1,0:T(8,128)(2,1)S(1)}, u32[]{:S(2)}, u32[]{:S(2)}) collective-permute-start(bf16[576,384]{1,0:T(8,128)(2,1)} %pad_maximum_fusion.6), channel_id=1, source_target_pairs={{0,16},{16,0},{1,17},{17,1},{2,18},{18,2},{3,19},{19,3},{4,20},{20... | collective-permute-start | bytes 1327112 | tf_op jit(solution)/shard_map/ppermute | solution.py:49
  21.3 10.5 %collective-permute-start.5 = (bf16[1,512,384]{2,1,0:T(8,128)(2,1)S(1)}, bf16[1,512,384]{2,1,0:T(8,128)(2,1)S(1)}, u32[]{:S(2)}, u32[]{:S(2)}) collective-permute-start(bf16[1,512,384]{2,1,0:T(8,128)(2,1)S(1)} %bitcast.87), channel_id=1, source_target_pairs={{0,8},{4,12},{8,0},{12,4},{1,9},{5,13},{9,1},{13,5},{2,10},{6,14},... | collective-permute-start | bytes 1179656 | tf_op jit(solution)/shard_map/ppermute | solution.py:49
  32.8 6.4 %collective-permute-start.6 = (bf16[2,512,384]{2,1,0:T(8,128)(2,1)}, bf16[2,512,384]{2,1,0:T(8,128)(2,1)}, u32[]{:S(2)}, u32[]{:S(2)}) collective-permute-start(bf16[2,512,384]{2,1,0:T(8,128)(2,1)} %pad_maximum_fusion.2), channel_id=1, source_target_pairs={{0,4},{4,0},{8,12},{12,8},{1,5},{5,1},{9,13},{13,9},{2,6},{6,2},{1... | collective-permute-start | bytes 2359304 | tf_op jit(solution)/shard_map/ppermute | solution.py:49
  33.5 65.8 %collective-permute-start = (f32[]{:T(128)}, f32[]{:T(128)}, u32[]{:S(2)}, u32[]{:S(2)}) collective-permute-start(f32[]{:T(128)} %convert_element_type.210), channel_id=1, source_target_pairs={{0,16},{16,0},{1,17},{17,1},{2,18},{18,2},{3,19},{19,3},{4,20},{20... | collective-permute-start | bytes 20 | tf_op jit(solution)/shard_map/ppermute | solution.py:49
  37.0 15.9 %collective-permute-start.7 = (bf16[768,384]{1,0:T(8,128)(2,1)}, bf16[768,384]{1,0:T(8,128)(2,1)}, u32[]{:S(2)}, u32[]{:S(2)}) collective-permute-start(bf16[768,384]{1,0:T(8,128)(2,1)} %pad_maximum_fusion.5), channel_id=1, source_target_pairs={{0,16},{16,0},{1,17},{17,1},{2,18},{18,2},{3,19},{19,3},{4,20},{20... | collective-permute-start | bytes 1769480 | tf_op jit(solution)/shard_map/ppermute | solution.py:49
  54.1 16.3 %collective-permute-start.14 = (bf16[384,768]{1,0:T(8,128)(2,1)S(1)}, bf16[384,768]{1,0:T(8,128)(2,1)S(1)}, u32[]{:S(2)}, u32[]{:S(2)}) collective-permute-start(bf16[384,768]{1,0:T(8,128)(2,1)S(1)} %copy-done.24), channel_id=1, source_target_pairs={{0,16},{16,0},{1,17},{17,1},{2,18},{18,2},{3,19},{19,3},{4,20},{20... | collective-permute-start | bytes 1769480 | tf_op jit(solution)/shard_map/ppermute | solution.py:49
  55.6 6.0 %collective-permute-start.10 = (bf16[128,192]{1,0:T(8,128)(2,1)S(1)}, bf16[128,192]{1,0:T(8,128)(2,1)S(1)}, u32[]{:S(2)}, u32[]{:S(2)}) collective-permute-start(bf16[128,192]{1,0:T(8,128)(2,1)S(1)} %get-tuple-element.165), channel_id=1, source_target_pairs={{0,3},{1,0},{2,1},{3,2},{4,7},{5,4},{6,5},{7,6},{8,11},{9,8},{10,9... | collective-permute-start | bytes 147464 | tf_op jit(solution)/shard_map/ppermute | solution.py:44
  57.2 6.6 %collective-permute-start.9 = (bf16[128,192]{1,0:T(8,128)(2,1)S(1)}, bf16[128,192]{1,0:T(8,128)(2,1)S(1)}, u32[]{:S(2)}, u32[]{:S(2)}) collective-permute-start(bf16[128,192]{1,0:T(8,128)(2,1)S(1)} %get-tuple-element.166), channel_id=1, source_target_pairs={{0,2},{1,3},{2,0},{3,1},{4,6},{5,7},{6,4},{7,5},{8,10},{9,11},{10,... | collective-permute-start | bytes 147464 | tf_op jit(solution)/shard_map/ppermute | solution.py:44
  58.4 6.1 %collective-permute-start.8 = (bf16[128,192]{1,0:T(8,128)(2,1)S(1)}, bf16[128,192]{1,0:T(8,128)(2,1)S(1)}, u32[]{:S(2)}, u32[]{:S(2)}) collective-permute-start(bf16[128,192]{1,0:T(8,128)(2,1)S(1)} %get-tuple-element.167), channel_id=1, source_target_pairs={{0,1},{1,2},{2,3},{3,0},{4,5},{5,6},{6,7},{7,4},{8,9},{9,10},{10,1... | collective-permute-start | bytes 147464 | tf_op jit(solution)/shard_map/ppermute | solution.py:44
  61.6 19.8 %collective-permute-start.15 = (bf16[768,384]{1,0:T(8,128)(2,1)S(1)}, bf16[768,384]{1,0:T(8,128)(2,1)S(1)}, u32[]{:S(2)}, u32[]{:S(2)}) collective-permute-start(bf16[768,384]{1,0:T(8,128)(2,1)S(1)} %copy-done.25), channel_id=1, source_target_pairs={{0,16},{16,0},{1,17},{17,1},{2,18},{18,2},{3,19},{19,3},{4,20},{20... | collective-permute-start | bytes 1769480 | tf_op jit(solution)/shard_map/ppermute | solution.py:49
  65.7 18.8 %copy-start.56 = (f32[768]{0:T(1024)S(1)}, f32[768]{0:T(1024)}, u32[]{:S(2)}) copy-start(f32[768]{0:T(1024)} %param.33) | copy-start | bytes 9220
  65.9 24.3 %copy-start.28 = (bf16[128,768]{1,0:T(8,128)(2,1)}, bf16[128,768]{1,0:T(8,128)(2,1)S(1)}, u32[]{:S(2)}) copy-start(bf16[128,768]{1,0:T(8,128)(2,1)S(1)} %maximum_select_fusion.5) | copy-start | bytes 589828
  65.9 15.6 %collective-permute-start.13 = (bf16[128,768]{1,0:T(8,128)(2,1)S(1)}, bf16[128,768]{1,0:T(8,128)(2,1)S(1)}, u32[]{:S(2)}, u32[]{:S(2)}) collective-permute-start(bf16[128,768]{1,0:T(8,128)(2,1)S(1)} %maximum_select_fusion.5), channel_id=1, source_target_pairs={{0,3},{1,0},{2,1},{3,2},{4,7},{5,4},{6,5},{7,6},{8,11},{9,8},{10,9... | collective-permute-start | bytes 589832 | tf_op jit(solution)/shard_map/ppermute | solution.py:44
  67.6 16.9 %collective-permute-start.12 = (bf16[128,768]{1,0:T(8,128)(2,1)S(1)}, bf16[128,768]{1,0:T(8,128)(2,1)S(1)}, u32[]{:S(2)}, u32[]{:S(2)}) collective-permute-start(bf16[128,768]{1,0:T(8,128)(2,1)S(1)} %maximum_select_fusion.5), channel_id=1, source_target_pairs={{0,2},{1,3},{2,0},{3,1},{4,6},{5,7},{6,4},{7,5},{8,10},{9,11},{10,... | collective-permute-start | bytes 589832 | tf_op jit(solution)/shard_map/ppermute | solution.py:44
  70.3 14.3 %collective-permute-start.11 = (bf16[128,768]{1,0:T(8,128)(2,1)S(1)}, bf16[128,768]{1,0:T(8,128)(2,1)S(1)}, u32[]{:S(2)}, u32[]{:S(2)}) collective-permute-start(bf16[128,768]{1,0:T(8,128)(2,1)S(1)} %maximum_select_fusion.5), channel_id=1, source_target_pairs={{0,1},{1,2},{2,3},{3,0},{4,5},{5,6},{6,7},{7,4},{8,9},{9,10},{10,1... | collective-permute-start | bytes 589832 | tf_op jit(solution)/shard_map/ppermute | solution.py:44
  71.1 19.1 %copy-start.3 = (bf16[768,768]{1,0:T(8,128)(2,1)}, bf16[768,768]{1,0:T(8,128)(2,1)S(1)}, u32[]{:S(2)}) copy-start(bf16[768,768]{1,0:T(8,128)(2,1)S(1)} %constant_dynamic-update-slice_fusion.2) | copy-start | bytes 3538948
  93.0 9.8 %collective-permute-start.18 = (bf16[128,768]{1,0:T(8,128)(2,1)}, bf16[128,768]{1,0:T(8,128)(2,1)S(1)}, u32[]{:S(2)}, u32[]{:S(2)}) collective-permute-start(bf16[128,768]{1,0:T(8,128)(2,1)} %get-tuple-element.137), channel_id=1, source_target_pairs={{0,1},{1,2},{2,3},{3,0},{4,5},{5,6},{6,7},{7,4},{8,9},{9,10},{10,1... | collective-permute-start | bytes 589832 | tf_op jit(solution)/shard_map/ppermute | solution.py:44
  93.2 15.9 %collective-permute-start.17 = (bf16[128,768]{1,0:T(8,128)(2,1)}, bf16[128,768]{1,0:T(8,128)(2,1)S(1)}, u32[]{:S(2)}, u32[]{:S(2)}) collective-permute-start(bf16[128,768]{1,0:T(8,128)(2,1)} %get-tuple-element.138), channel_id=1, source_target_pairs={{0,2},{1,3},{2,0},{3,1},{4,6},{5,7},{6,4},{7,5},{8,10},{9,11},{10,... | collective-permute-start | bytes 589832 | tf_op jit(solution)/shard_map/ppermute | solution.py:44
  95.1 14.0 %collective-permute-start.16 = (bf16[128,768]{1,0:T(8,128)(2,1)}, bf16[128,768]{1,0:T(8,128)(2,1)S(1)}, u32[]{:S(2)}, u32[]{:S(2)}) collective-permute-start(bf16[128,768]{1,0:T(8,128)(2,1)} %get-tuple-element.136), channel_id=1, source_target_pairs={{0,3},{1,0},{2,1},{3,2},{4,7},{5,4},{6,5},{7,6},{8,11},{9,8},{10,9... | collective-permute-start | bytes 589832 | tf_op jit(solution)/shard_map/ppermute | solution.py:44
  114.8 27.4 %copy-start.30 = (bf16[128,768]{1,0:T(8,128)(2,1)}, bf16[128,768]{1,0:T(8,128)(2,1)S(1)}, u32[]{:S(2)}) copy-start(bf16[128,768]{1,0:T(8,128)(2,1)S(1)} %maximum_select_fusion.6) | copy-start | bytes 589828
  114.8 12.0 %collective-permute-start.21 = (bf16[128,768]{1,0:T(8,128)(2,1)S(1)}, bf16[128,768]{1,0:T(8,128)(2,1)S(1)}, u32[]{:S(2)}, u32[]{:S(2)}) collective-permute-start(bf16[128,768]{1,0:T(8,128)(2,1)S(1)} %maximum_select_fusion.6), channel_id=1, source_target_pairs={{0,3},{1,0},{2,1},{3,2},{4,7},{5,4},{6,5},{7,6},{8,11},{9,8},{10,9... | collective-permute-start | bytes 589832 | tf_op jit(solution)/shard_map/ppermute | solution.py:44
  121.5 17.1 %collective-permute-start.20 = (bf16[128,768]{1,0:T(8,128)(2,1)S(1)}, bf16[128,768]{1,0:T(8,128)(2,1)}, u32[]{:S(2)}, u32[]{:S(2)}) collective-permute-start(bf16[128,768]{1,0:T(8,128)(2,1)S(1)} %maximum_select_fusion.6), channel_id=1, source_target_pairs={{0,2},{1,3},{2,0},{3,1},{4,6},{5,7},{6,4},{7,5},{8,10},{9,11},{10,... | collective-permute-start | bytes 589832 | tf_op jit(solution)/shard_map/ppermute | solution.py:44
  121.5 17.1 %collective-permute-start.19 = (bf16[128,768]{1,0:T(8,128)(2,1)S(1)}, bf16[128,768]{1,0:T(8,128)(2,1)}, u32[]{:S(2)}, u32[]{:S(2)}) collective-permute-start(bf16[128,768]{1,0:T(8,128)(2,1)S(1)} %maximum_select_fusion.6), channel_id=1, source_target_pairs={{0,1},{1,2},{2,3},{3,0},{4,5},{5,6},{6,7},{7,4},{8,9},{9,10},{10,1... | collective-permute-start | bytes 589832 | tf_op jit(solution)/shard_map/ppermute | solution.py:44
  143.2 12.1 %collective-permute-start.24 = (bf16[128,768]{1,0:T(8,128)(2,1)S(1)}, bf16[128,768]{1,0:T(8,128)(2,1)S(1)}, u32[]{:S(2)}, u32[]{:S(2)}) collective-permute-start(bf16[128,768]{1,0:T(8,128)(2,1)S(1)} %get-tuple-element.134), channel_id=1, source_target_pairs={{0,1},{1,2},{2,3},{3,0},{4,5},{5,6},{6,7},{7,4},{8,9},{9,10},{10,1... | collective-permute-start | bytes 589832 | tf_op jit(solution)/shard_map/ppermute | solution.py:44
  143.3 16.3 %collective-permute-start.23 = (bf16[128,768]{1,0:T(8,128)(2,1)S(1)}, bf16[128,768]{1,0:T(8,128)(2,1)S(1)}, u32[]{:S(2)}, u32[]{:S(2)}) collective-permute-start(bf16[128,768]{1,0:T(8,128)(2,1)S(1)} %get-tuple-element.135), channel_id=1, source_target_pairs={{0,2},{1,3},{2,0},{3,1},{4,6},{5,7},{6,4},{7,5},{8,10},{9,11},{10,... | collective-permute-start | bytes 589832 | tf_op jit(solution)/shard_map/ppermute | solution.py:44
  145.1 14.5 %collective-permute-start.22 = (bf16[128,768]{1,0:T(8,128)(2,1)S(1)}, bf16[128,768]{1,0:T(8,128)(2,1)S(1)}, u32[]{:S(2)}, u32[]{:S(2)}) collective-permute-start(bf16[128,768]{1,0:T(8,128)(2,1)S(1)} %get-tuple-element.133), channel_id=1, source_target_pairs={{0,3},{1,0},{2,1},{3,2},{4,7},{5,4},{6,5},{7,6},{8,11},{9,8},{10,9... | collective-permute-start | bytes 589832 | tf_op jit(solution)/shard_map/ppermute | solution.py:44
  150.8 23.3 %collective-permute-start.28 = (bf16[768,384]{1,0:T(8,128)(2,1)}, bf16[768,384]{1,0:T(8,128)(2,1)}, u32[]{:S(2)}, u32[]{:S(2)}) collective-permute-start(bf16[768,384]{1,0:T(8,128)(2,1)} %split.149), channel_id=1, source_target_pairs={{0,16},{16,0},{1,17},{17,1},{2,18},{18,2},{3,19},{19,3},{4,20},{20... | collective-permute-start | bytes 1769480 | tf_op jit(solution)/shard_map/ppermute | solution.py:49
  153.2 24.7 %collective-permute-start.29 = (bf16[384,768]{1,0:T(8,128)(2,1)}, bf16[384,768]{1,0:T(8,128)(2,1)}, u32[]{:S(2)}, u32[]{:S(2)}) collective-permute-start(bf16[384,768]{1,0:T(8,128)(2,1)} %split.148), channel_id=1, source_target_pairs={{0,16},{16,0},{1,17},{17,1},{2,18},{18,2},{3,19},{19,3},{4,20},{20... | collective-permute-start | bytes 1769480 | tf_op jit(solution)/shard_map/ppermute | solution.py:49
  161.0 10.2 %collective-permute-start.26 = (bf16[128,192]{1,0:T(8,128)(2,1)S(1)}, bf16[128,192]{1,0:T(8,128)(2,1)S(1)}, u32[]{:S(2)}, u32[]{:S(2)}) collective-permute-start(bf16[128,192]{1,0:T(8,128)(2,1)S(1)} %get-tuple-element.174), channel_id=1, source_target_pairs={{0,2},{1,3},{2,0},{3,1},{4,6},{5,7},{6,4},{7,5},{8,10},{9,11},{10,... | collective-permute-start | bytes 147464 | tf_op jit(solution)/shard_map/ppermute | solution.py:44
  163.9 7.9 %collective-permute-start.27 = (bf16[128,192]{1,0:T(8,128)(2,1)S(1)}, bf16[128,192]{1,0:T(8,128)(2,1)S(1)}, u32[]{:S(2)}, u32[]{:S(2)}) collective-permute-start(bf16[128,192]{1,0:T(8,128)(2,1)S(1)} %get-tuple-element.173), channel_id=1, source_target_pairs={{0,3},{1,0},{2,1},{3,2},{4,7},{5,4},{6,5},{7,6},{8,11},{9,8},{10,9... | collective-permute-start | bytes 147464 | tf_op jit(solution)/shard_map/ppermute | solution.py:44
  167.2 6.1 %collective-permute-start.25 = (bf16[128,192]{1,0:T(8,128)(2,1)S(1)}, bf16[128,192]{1,0:T(8,128)(2,1)S(1)}, u32[]{:S(2)}, u32[]{:S(2)}) collective-permute-start(bf16[128,192]{1,0:T(8,128)(2,1)S(1)} %get-tuple-element.172), channel_id=1, source_target_pairs={{0,1},{1,2},{2,3},{3,0},{4,5},{5,6},{6,7},{7,4},{8,9},{9,10},{10,1... | collective-permute-start | bytes 147464 | tf_op jit(solution)/shard_map/ppermute | solution.py:44
  171.1 23.2 %collective-permute-start.30 = (f32[12,768]{1,0:T(8,128)}, f32[12,768]{1,0:T(8,128)S(1)}, u32[]{:S(2)}, u32[]{:S(2)}) collective-permute-start(f32[12,768]{1,0:T(8,128)} %pack.1), channel_id=1, source_target_pairs={{0,16},{16,0},{1,17},{17,1},{2,18},{18,2},{3,19},{19,3},{4,20},{20... | collective-permute-start | bytes 110600 | tf_op jit(solution)/shard_map/ppermute | solution.py:49
  177.9 20.7 %collective-permute-start.41 = (bf16[128,1536]{1,0:T(8,128)(2,1)S(1)}, bf16[128,1536]{1,0:T(8,128)(2,1)S(1)}, u32[]{:S(2)}, u32[]{:S(2)}) collective-permute-start(bf16[128,1536]{1,0:T(8,128)(2,1)S(1)} %pad_maximum_fusion.7), channel_id=1, source_target_pairs={{0,3},{1,0},{2,1},{3,2},{4,7},{5,4},{6,5},{7,6},{8,11},{9,8},{10,9... | collective-permute-start | bytes 1179656 | tf_op jit(solution)/shard_map/ppermute | solution.py:44
  178.3 22.2 %collective-permute-start.39 = (bf16[128,1536]{1,0:T(8,128)(2,1)S(1)}, bf16[128,1536]{1,0:T(8,128)(2,1)}, u32[]{:S(2)}, u32[]{:S(2)}) collective-permute-start(bf16[128,1536]{1,0:T(8,128)(2,1)S(1)} %pad_maximum_fusion.7), channel_id=1, source_target_pairs={{0,1},{1,2},{2,3},{3,0},{4,5},{5,6},{6,7},{7,4},{8,9},{9,10},{10,1... | collective-permute-start | bytes 1179656 | tf_op jit(solution)/shard_map/ppermute | solution.py:44
  179.9 31.2 %collective-permute-start.40 = (bf16[128,1536]{1,0:T(8,128)(2,1)S(1)}, bf16[128,1536]{1,0:T(8,128)(2,1)}, u32[]{:S(2)}, u32[]{:S(2)}) collective-permute-start(bf16[128,1536]{1,0:T(8,128)(2,1)S(1)} %pad_maximum_fusion.7), channel_id=1, source_target_pairs={{0,2},{1,3},{2,0},{3,1},{4,6},{5,7},{6,4},{7,5},{8,10},{9,11},{10,... | collective-permute-start | bytes 1179656 | tf_op jit(solution)/shard_map/ppermute | solution.py:44
  194.4 19.6 %collective-permute-start.31 = (bf16[2,384,512]{2,1,0:T(8,128)(2,1)}, bf16[2,384,512]{2,1,0:T(8,128)(2,1)S(1)}, u32[]{:S(2)}, u32[]{:S(2)}) collective-permute-start(bf16[2,384,512]{2,1,0:T(8,128)(2,1)} %get-tuple-element.70), channel_id=1, source_target_pairs={{0,4},{4,0},{8,12},{12,8},{1,5},{5,1},{9,13},{13,9},{2,6},{6,2},{1... | collective-permute-start | bytes 2359304 | tf_op jit(solution)/shard_map/ppermute | solution.py:49
  196.2 26.5 %collective-permute-start.33 = (bf16[384,768]{1,0:T(8,128)(2,1)S(1)}, bf16[384,768]{1,0:T(8,128)(2,1)S(1)}, u32[]{:S(2)}, u32[]{:S(2)}) collective-permute-start(bf16[384,768]{1,0:T(8,128)(2,1)S(1)} %fusion.13), channel_id=1, source_target_pairs={{0,4},{4,0},{8,12},{12,8},{1,5},{5,1},{9,13},{13,9},{2,6},{6,2},{1... | collective-permute-start | bytes 1769480 | tf_op jit(solution)/shard_map/ppermute | solution.py:49
  198.6 24.1 %collective-permute-start.34 = (bf16[768,384]{1,0:T(8,128)(2,1)S(1)}, bf16[768,384]{1,0:T(8,128)(2,1)S(1)}, u32[]{:S(2)}, u32[]{:S(2)}) collective-permute-start(bf16[768,384]{1,0:T(8,128)(2,1)S(1)} %fusion.12), channel_id=1, source_target_pairs={{0,8},{4,12},{8,0},{12,4},{1,9},{5,13},{9,1},{13,5},{2,10},{6,14},... | collective-permute-start | bytes 1769480 | tf_op jit(solution)/shard_map/ppermute | solution.py:49
  200.6 22.1 %collective-permute-start.35 = (f32[12,768]{1,0:T(8,128)S(1)}, f32[12,768]{1,0:T(8,128)S(1)}, u32[]{:S(2)}, u32[]{:S(2)}) collective-permute-start(f32[12,768]{1,0:T(8,128)S(1)} %add.317), channel_id=1, source_target_pairs={{0,4},{4,0},{8,12},{12,8},{1,5},{5,1},{9,13},{13,9},{2,6},{6,2},{1... | collective-permute-start | bytes 110600 | tf_op jit(solution)/shard_map/ppermute | solution.py:49
  212.3 32.6 %collective-permute-start.42 = (bf16[192,384]{1,0:T(8,128)(2,1)S(1)}, bf16[192,384]{1,0:T(8,128)(2,1)S(1)}, u32[]{:S(2)}, u32[]{:S(2)}) collective-permute-start(bf16[192,384]{1,0:T(8,128)(2,1)S(1)} %split.150), channel_id=1, source_target_pairs={{0,16},{16,0},{1,17},{17,1},{2,18},{18,2},{3,19},{19,3},{4,20},{20... | collective-permute-start | bytes 442376 | tf_op jit(solution)/shard_map/ppermute | solution.py:49
  214.3 8.2 %collective-permute-start.32 = (bf16[1,384,512]{2,1,0:T(8,128)(2,1)S(1)}, bf16[1,384,512]{2,1,0:T(8,128)(2,1)S(1)}, u32[]{:S(2)}, u32[]{:S(2)}) collective-permute-start(bf16[1,384,512]{2,1,0:T(8,128)(2,1)S(1)} %slice.323), channel_id=1, source_target_pairs={{0,8},{4,12},{8,0},{12,4},{1,9},{5,13},{9,1},{13,5},{2,10},{6,14},... | collective-permute-start | bytes 1179656 | tf_op jit(solution)/shard_map/ppermute | solution.py:49
  224.9 11.2 %collective-permute-start.38 = (bf16[128,768]{1,0:T(8,128)(2,1)S(1)}, bf16[128,768]{1,0:T(8,128)(2,1)S(1)}, u32[]{:S(2)}, u32[]{:S(2)}) collective-permute-start(bf16[128,768]{1,0:T(8,128)(2,1)S(1)} %get-tuple-element.131), channel_id=1, source_target_pairs={{0,1},{1,2},{2,3},{3,0},{4,5},{5,6},{6,7},{7,4},{8,9},{9,10},{10,1... | collective-permute-start | bytes 589832 | tf_op jit(solution)/shard_map/ppermute | solution.py:44
  227.7 15.0 %collective-permute-start.37 = (bf16[128,768]{1,0:T(8,128)(2,1)S(1)}, bf16[128,768]{1,0:T(8,128)(2,1)S(1)}, u32[]{:S(2)}, u32[]{:S(2)}) collective-permute-start(bf16[128,768]{1,0:T(8,128)(2,1)S(1)} %get-tuple-element.132), channel_id=1, source_target_pairs={{0,2},{1,3},{2,0},{3,1},{4,6},{5,7},{6,4},{7,5},{8,10},{9,11},{10,... | collective-permute-start | bytes 589832 | tf_op jit(solution)/shard_map/ppermute | solution.py:44
  230.8 13.4 %collective-permute-start.36 = (bf16[128,768]{1,0:T(8,128)(2,1)S(1)}, bf16[128,768]{1,0:T(8,128)(2,1)S(1)}, u32[]{:S(2)}, u32[]{:S(2)}) collective-permute-start(bf16[128,768]{1,0:T(8,128)(2,1)S(1)} %get-tuple-element.130), channel_id=1, source_target_pairs={{0,3},{1,0},{2,1},{3,2},{4,7},{5,4},{6,5},{7,6},{8,11},{9,8},{10,9... | collective-permute-start | bytes 589832 | tf_op jit(solution)/shard_map/ppermute | solution.py:44
  230.8 15.4 %collective-permute-start.43 = (f32[12,768]{1,0:T(8,128)S(1)}, f32[12,768]{1,0:T(8,128)S(1)}, u32[]{:S(2)}, u32[]{:S(2)}) collective-permute-start(f32[12,768]{1,0:T(8,128)S(1)} %add.326), channel_id=1, source_target_pairs={{0,8},{4,12},{8,0},{12,4},{1,9},{5,13},{9,1},{13,5},{2,10},{6,14},... | collective-permute-start | bytes 110600 | tf_op jit(solution)/shard_map/ppermute | solution.py:49
  236.1 10.2 %collective-permute-start.44 = (bf16[576,384]{1,0:T(8,128)(2,1)S(1)}, bf16[576,384]{1,0:T(8,128)(2,1)S(1)}, u32[]{:S(2)}, u32[]{:S(2)}) collective-permute-start(bf16[576,384]{1,0:T(8,128)(2,1)S(1)} %fusion.15), channel_id=1, source_target_pairs={{0,16},{16,0},{1,17},{17,1},{2,18},{18,2},{3,19},{19,3},{4,20},{20... | collective-permute-start | bytes 1327112 | tf_op jit(solution)/shard_map/ppermute | solution.py:49
  242.7 3.6 %collective-permute-start.45 = (f32[384]{0:T(512)S(1)}, f32[384]{0:T(512)S(1)}, u32[]{:S(2)}, u32[]{:S(2)}) collective-permute-start(f32[384]{0:T(512)S(1)} %pad_maximum_fusion.17), channel_id=1, source_target_pairs={{0,8},{4,12},{8,0},{12,4},{1,9},{5,13},{9,1},{13,5},{2,10},{6,14},... | collective-permute-start | bytes 4616 | tf_op jit(solution)/shard_map/ppermute | solution.py:49
  244.2 21.2 %collective-permute-start.47 = (bf16[384,768]{1,0:T(8,128)(2,1)S(1)}, bf16[384,768]{1,0:T(8,128)(2,1)S(1)}, u32[]{:S(2)}, u32[]{:S(2)}) collective-permute-start(bf16[384,768]{1,0:T(8,128)(2,1)S(1)} %add_convert_fusion.1), channel_id=1, source_target_pairs={{0,8},{4,12},{8,0},{12,4},{1,9},{5,13},{9,1},{13,5},{2,10},{6,14},... | collective-permute-start | bytes 1769480 | tf_op jit(solution)/shard_map/ppermute | solution.py:49
  244.9 27.6 %collective-permute-start.48 = (bf16[768,384]{1,0:T(8,128)(2,1)S(1)}, bf16[768,384]{1,0:T(8,128)(2,1)}, u32[]{:S(2)}, u32[]{:S(2)}) collective-permute-start(bf16[768,384]{1,0:T(8,128)(2,1)S(1)} %add_convert_fusion), channel_id=1, source_target_pairs={{0,4},{4,0},{8,12},{12,8},{1,5},{5,1},{9,13},{13,9},{2,6},{6,2},{1... | collective-permute-start | bytes 1769480 | tf_op jit(solution)/shard_map/ppermute | solution.py:49
  246.3 11.5 %collective-permute-start.50 = (f32[12,768]{1,0:T(8,128)S(1)}, f32[12,768]{1,0:T(8,128)S(1)}, u32[]{:S(2)}, u32[]{:S(2)}) collective-permute-start(f32[12,768]{1,0:T(8,128)S(1)} %add.331), channel_id=1, source_target_pairs={{0,2},{1,3},{2,0},{3,1},{4,6},{5,7},{6,4},{7,5},{8,10},{9,11},{10,... | collective-permute-start | bytes 110600 | tf_op jit(solution)/shard_map/ppermute | solution.py:49
  251.7 9.3 %collective-permute-start.51 = (f32[12,768]{1,0:T(8,128)S(1)}, f32[12,768]{1,0:T(8,128)S(1)}, u32[]{:S(2)}, u32[]{:S(2)}) collective-permute-start(f32[12,768]{1,0:T(8,128)S(1)} %add.331), channel_id=1, source_target_pairs={{0,3},{1,2},{2,1},{3,0},{4,7},{5,6},{6,5},{7,4},{8,11},{9,10},{10,... | collective-permute-start | bytes 110600 | tf_op jit(solution)/shard_map/ppermute | solution.py:49
  251.8 1.2 collective-permute-start.58
  252.9 3.6 %collective-permute-start.59 = (f32[384]{0:T(512)S(1)}, f32[384]{0:T(512)S(1)}, u32[]{:S(2)}, u32[]{:S(2)}) collective-permute-start(f32[384]{0:T(512)S(1)} %add.342), channel_id=1, source_target_pairs={{0,16},{16,0},{1,17},{17,1},{2,18},{18,2},{3,19},{19,3},{4,20},{20... | collective-permute-start | bytes 4616 | tf_op jit(solution)/shard_map/ppermute | solution.py:49
  256.5 5.1 %collective-permute-start.49 = (f32[12,768]{1,0:T(8,128)S(1)}, f32[12,768]{1,0:T(8,128)S(1)}, u32[]{:S(2)}, u32[]{:S(2)}) collective-permute-start(f32[12,768]{1,0:T(8,128)S(1)} %add.331), channel_id=1, source_target_pairs={{0,1},{1,0},{2,3},{3,2},{4,5},{5,4},{6,7},{7,6},{8,9},{9,8},{10,11... | collective-permute-start | bytes 110600 | tf_op jit(solution)/shard_map/ppermute | solution.py:49
  257.8 17.0 %collective-permute-start.46 = (bf16[128,768]{1,0:T(8,128)(2,1)S(1)}, bf16[128,768]{1,0:T(8,128)(2,1)S(1)}, u32[]{:S(2)}, u32[]{:S(2)}) collective-permute-start(bf16[128,768]{1,0:T(8,128)(2,1)S(1)} %fusion.41), channel_id=1, source_target_pairs={{0,3},{1,0},{2,1},{3,2},{4,7},{5,4},{6,5},{7,6},{8,11},{9,8},{10,9... | collective-permute-start | bytes 589832 | tf_op jit(solution)/shard_map/ppermute | solution.py:44
  261.0 19.3 %collective-permute-start.53 = (bf16[128,768]{1,0:T(8,128)(2,1)S(1)}, bf16[128,768]{1,0:T(8,128)(2,1)S(1)}, u32[]{:S(2)}, u32[]{:S(2)}) collective-permute-start(bf16[128,768]{1,0:T(8,128)(2,1)S(1)} %fusion.41), channel_id=1, source_target_pairs={{0,2},{1,3},{2,0},{3,1},{4,6},{5,7},{6,4},{7,5},{8,10},{9,11},{10,... | collective-permute-start | bytes 589832 | tf_op jit(solution)/shard_map/ppermute | solution.py:44
  261.6 18.6 %collective-permute-start.52 = (bf16[128,768]{1,0:T(8,128)(2,1)S(1)}, bf16[128,768]{1,0:T(8,128)(2,1)S(1)}, u32[]{:S(2)}, u32[]{:S(2)}) collective-permute-start(bf16[128,768]{1,0:T(8,128)(2,1)S(1)} %fusion.41), channel_id=1, source_target_pairs={{0,1},{1,2},{2,3},{3,0},{4,5},{5,6},{6,7},{7,4},{8,9},{9,10},{10,1... | collective-permute-start | bytes 589832 | tf_op jit(solution)/shard_map/ppermute | solution.py:44
  265.4 5.5 %collective-permute-start.56 = (bf16[192,384]{1,0:T(8,128)(2,1)S(1)}, bf16[192,384]{1,0:T(8,128)(2,1)S(1)}, u32[]{:S(2)}, u32[]{:S(2)}) collective-permute-start(bf16[192,384]{1,0:T(8,128)(2,1)S(1)} %fusion.48), channel_id=1, source_target_pairs={{0,8},{4,12},{8,0},{12,4},{1,9},{5,13},{9,1},{13,5},{2,10},{6,14},... | collective-permute-start | bytes 442376 | tf_op jit(solution)/shard_map/ppermute | solution.py:49
  270.9 9.1 %collective-permute-start.54 = (bf16[576,384]{1,0:T(8,128)(2,1)S(1)}, bf16[576,384]{1,0:T(8,128)(2,1)S(1)}, u32[]{:S(2)}, u32[]{:S(2)}) collective-permute-start(bf16[576,384]{1,0:T(8,128)(2,1)S(1)} %fusion.17), channel_id=1, source_target_pairs={{0,8},{4,12},{8,0},{12,4},{1,9},{5,13},{9,1},{13,5},{2,10},{6,14},... | collective-permute-start | bytes 1327112 | tf_op jit(solution)/shard_map/ppermute | solution.py:49
  272.6 9.1 %collective-permute-start.57 = (bf16[192,384]{1,0:T(8,128)(2,1)S(1)}, bf16[192,384]{1,0:T(8,128)(2,1)S(1)}, u32[]{:S(2)}, u32[]{:S(2)}) collective-permute-start(bf16[192,384]{1,0:T(8,128)(2,1)S(1)} %add_convert_fusion.3), channel_id=1, source_target_pairs={{0,4},{4,0},{8,12},{12,8},{1,5},{5,1},{9,13},{13,9},{2,6},{6,2},{1... | collective-permute-start | bytes 442376 | tf_op jit(solution)/shard_map/ppermute | solution.py:49
  280.2 2.2 collective-permute-start.55
  (55 other events, 324.1 us)

commit v4 on v3

--- a/solution.py
+++ b/solution.py
@@ -534,8 +534,8 @@
     early_sum.step()
     d_kv = scatter_parts(d_kept, d_sent)
     d_query_low = d_query.astype(BF16)
-    d_kv_low, inner_sum.moved, outer_sum.moved, early_sum.moved = tie(
-        d_kv.astype(BF16), inner_sum.moved, outer_sum.moved, early_sum.moved
+    d_kv_low, inner_sum.moved, outer_sum.moved, early_sum.moved, *both_moved = tie(
+        d_kv.astype(BF16), inner_sum.moved, outer_sum.moved, early_sum.moved, *both_moved
     )
     tokens_part = rows_sum(
         dot32(rows_turn(d_query_low), full_qkv[:width_local], ((1,), (0,)))
@@ -557,7 +557,7 @@
     late_vector = jnp.concatenate([jnp.sum(d_query, 0), jnp.sum(d_kv[width_local:], 1)])
     late_sum = VectorSum(late_vector, ("dp", "ctx"), True)
     grad_mine = (d_first + own_first(tokens_part)).astype(BF16)
-    sums = (output_sum, early_sum, qkv_sum, late_sum)
+    sums = (early_sum, late_sum)
     grad_mine, *moved = tie(grad_mine, *[one.moved for one in sums])
     for one, value in zip(sums, moved):
         one.moved = value
@@ -569,8 +569,9 @@
     while len(early) > 1:
         early = [left + right for left, right in zip(early[::2], early[1::2])]
     early = early[0]
-    for one in (output_sum, qkv_sum, late_sum):
-        one.step()
+    qkv_sum.step()
+    output_sum.step()
+    late_sum.step()
     grad_moved = rows_moved(grad_mine)
     inner_shard, outer_shard = inner_sum.total(), outer_sum.total()
     result_all = rows_place([block[:, model_width:] for block in both]).astype(F32)

time: 285 us -> 287 us (level)
  starting transfers between devices: 83.1 us -> 88.3 us
  matrix products: 22 us -> 17.2 us
  local copies, waits for them, and re-layouts: 20.2 us -> 16.5 us
  other arithmetic: 28.5 us -> 31.9 us
    dot_general x18, matrix products: 22 us -> 17.2 us  [dot32(): lax.dot_general(left, right, (dims, ((), ())), preferred_element_type=F32)]
    ppermute x30, starting transfers between devices: 51.5 us -> 55.9 us  [shifted(): lax.ppermute(block, axis, [(i, (i + step) % size) for i in range(size)])]
  transfers between devices with their start and end apart: 60 -> 60, of which waited for: 23 -> 22; matrix products, arithmetic and copies ran while one was open for 20% -> 18% of each run, Pallas kernels for 10% -> 10%
where the time goes in v4:
time: 287 us
  waiting for transfers between devices  99.7 us (35%)
  starting transfers between devices  88.3 us (31%)
  other arithmetic  31.9 us (11%)
  Pallas kernels  28.1 us (10%)
  matrix products  17.2 us (6%)
  local copies, waits for them, and re-layouts  16.5 us (6%)
  between operations  4.93 us (2%)
    ppermute x30, waiting for transfers between devices, shifted(): lax.ppermute(block, axis, [(i, (i + step) % size) for i in range(size)])  56.5 us
    ppermute x30, starting transfers between devices, shifted(): lax.ppermute(block, axis, [(i, (i + step) % size) for i in range(size)])  55.9 us
    ppermute x30, waiting for transfers between devices, flipped(): return lax.ppermute(block, axis, [(i, i ^ bit) for i in range(size)])  43.2 us
    ppermute x30, starting transfers between devices, flipped(): return lax.ppermute(block, axis, [(i, i ^ bit) for i in range(size)])  32.4 us
    dot_general x18, matrix products, dot32(): lax.dot_general(left, right, (dims, ((), ())), preferred_element_type=F32)  17.2 us
    pallas_call x1, Pallas kernels, attend_back(): pl.pallas_call(partial(attend_back_kernel, heads, scale, len(kv)), grid_s...  13.5 us
    pallas_call x1, Pallas kernels, attend(): pl.pallas_call(partial(attend_kernel, heads, len(kv)), grid_spec=pltpu.Pr...  12.6 us
    convert_element_type x8, other arithmetic, step(): low = (self.kept.astype(F32) + self.moved.astype(F32)).astype(BF16)  6 us
  transfers between devices with their start and end apart: 60, of which 22 were waited for; matrix products, arithmetic and copies ran while one was open for 18% of the time, Pallas kernels for 10%

profile of v4, /device:TPU:0, one launch (start us, length us, event | category | flops | bytes accessed | tf_op | source)
XLA Modules:
  0.0 286.7 jit_solution(826570474849767231)
XLA Ops:
  0.7 5.1 %collective-permute-start.4 = (bf16[192,384]{1,0:T(8,128)(2,1)}, bf16[192,384]{1,0:T(8,128)(2,1)S(1)}, u32[]{:S(2)}, u32[]{:S(2)}) collective-permute-start(bf16[192,384]{1,0:T(8,128)(2,1)} %param.27), channel_id=1, source_target_pairs={{0,3},{1,0},{2,1},{3,2},{4,7},{5,4},{6,5},{7,6},{8,11},{9,8},{10,9... | collective-permute-start | bytes 442376 | tf_op jit(solution)/shard_map/ppermute | solution.py:44
  6.8 1.9 pad_maximum_fusion.6
  8.7 1.5 collective-permute-start.1
  10.2 1.2 fusion.93
  11.7 6.9 %collective-permute-done.3 = bf16[192,384]{1,0:T(8,128)(2,1)} collective-permute-done((bf16[192,384]{1,0:T(8,128)(2,1)}, bf16[192,384]{1,0:T(8,128)(2,1)}, u32[]{:S(2)}, u32[]{:S(2)}) %collective-permute-start.3) | collective-permute-done | bytes 147488 | tf_op jit(solution)/shard_map/ppermute | solution.py:44
  18.6 1.9 pad_maximum_fusion.5
  21.2 1.6 collective-permute-start.5
  23.9 7.8 %collective-permute-done.5.refs_1_ = bf16[1,512,384]{2,1,0:T(8,128)(2,1)S(1)} collective-permute-done((bf16[1,512,384]{2,1,0:T(8,128)(2,1)S(1)}, bf16[1,512,384]{2,1,0:T(8,128)(2,1)S(1)}, u32[]{:S(2)}, u32[]{:S(2)}) %collective-permute-start.5) | collective-permute-done | bytes 393248 | tf_op jit(solution)/shard_map/ppermute | solution.py:49
  33.4 2.9 collective-permute-start
  39.2 12.6 %attend.1 = (bf16[1,3,512,2048]{3,2,1,0:T(8,128)(2,1)}, bf16[3,512,2048]{2,1,0:T(8,128)(2,1)}, bf16[512,192]{1,0:T(8,128)(2,1)}, f32[512,192]{1,0:T(8,128)}) custom-call(s32[2]{0:T(128)} %multiply_minimum_fusion.limits, s32[4]{0:T(128)} %xor_multiply_fusion.starts, bf16[512,192]{1,0:T(8,128)(2,1)} %fusion.10.query, bf16[1,3,512,2048]{3,2,1,0:T(8,128)(2,1)} %prior.1, ...), custom_call_target="tpu_custom_call" | custom-call | flops 805306368 | bytes 18874368 | tf_op jit(solution)/shard_map/attend/pallas_call | solution.py:265
  52.9 1.2 constant_dynamic-update-slice_fusion.3
  54.1 1.6 collective-permute-start.14
  55.7 1.6 collective-permute-start.10
  58.4 1.9 collective-permute-start.8
  62.2 2.3 collective-permute-done.9
  66.0 1.7 collective-permute-start.13
  67.7 2.7 collective-permute-done.14
  71.1 10.3 %collective-permute-done.15 = bf16[768,384]{1,0:T(8,128)(2,1)S(1)} collective-permute-done((bf16[768,384]{1,0:T(8,128)(2,1)S(1)}, bf16[768,384]{1,0:T(8,128)(2,1)S(1)}, u32[]{:S(2)}, u32[]{:S(2)}) %collective-permute-start.15) | collective-permute-done | bytes 589856 | tf_op jit(solution)/shard_map/ppermute | solution.py:49
  81.6 3.1 %collective-permute-done.12 = bf16[128,768]{1,0:T(8,128)(2,1)S(1)} collective-permute-done((bf16[128,768]{1,0:T(8,128)(2,1)S(1)}, bf16[128,768]{1,0:T(8,128)(2,1)S(1)}, u32[]{:S(2)}, u32[]{:S(2)}) %collective-permute-start.12) | collective-permute-done | bytes 196640 | tf_op jit(solution)/shard_map/ppermute | solution.py:44
  84.6 5.6 %multiply_convert_fusion = (bf16[512,768]{1,0:T(8,128)(2,1)S(1)}, f32[512,768]{1,0:T(8,128)}, f32[512,768]{1,0:T(8,128)}) fusion(f32[768]{0:T(1024)S(1)} %copy-done.55, bf16[768,768]{1,0:T(8,128)(2,1)S(1)} %constant_dynamic-update-slice_fusion.2, bf16[128,768]{1,0:T(8,128)(2,1)S(1)} %collective-permute-done.13, ...), kind=kOutput, calls=%fused_computation.6 | convolution fusion | flops 633077760 | bytes 5901312 | tf_op jit(solution)/shard_map/dot_general | solution.py:39
  90.3 1.9 fusion.105
  92.5 2.0 collective-permute-start.17
  94.5 2.8 collective-permute-start.16
  97.4 1.3 compare_convert_fusion
  100.0 1.9 collective-permute-done.18
  101.9 6.3 %collective-permute-done.17 = bf16[128,768]{1,0:T(8,128)(2,1)S(1)} collective-permute-done((bf16[128,768]{1,0:T(8,128)(2,1)S(1)}, bf16[128,768]{1,0:T(8,128)(2,1)S(1)}, u32[]{:S(2)}, u32[]{:S(2)}) %collective-permute-start.17) | collective-permute-done | bytes 196640 | tf_op jit(solution)/shard_map/ppermute | solution.py:44
  111.7 1.5 fusion.82
  113.3 6.6 %collective-permute-start.21 = (bf16[128,768]{1,0:T(8,128)(2,1)S(1)}, bf16[128,768]{1,0:T(8,128)(2,1)S(1)}, u32[]{:S(2)}, u32[]{:S(2)}) collective-permute-start(bf16[128,768]{1,0:T(8,128)(2,1)S(1)} %maximum_select_fusion.6), channel_id=1, source_target_pairs={{0,3},{1,0},{2,1},{3,2},{4,7},{5,4},{6,5},{7,6},{8,11},{9,8},{10,9... | collective-permute-start | bytes 589832 | tf_op jit(solution)/shard_map/ppermute | solution.py:44
  120.6 4.7 %collective-permute-done.21 = bf16[128,768]{1,0:T(8,128)(2,1)S(1)} collective-permute-done((bf16[128,768]{1,0:T(8,128)(2,1)S(1)}, bf16[128,768]{1,0:T(8,128)(2,1)S(1)}, u32[]{:S(2)}, u32[]{:S(2)}) %collective-permute-start.21) | collective-permute-done | bytes 196640 | tf_op jit(solution)/shard_map/ppermute | solution.py:44
  125.3 11.7 %collective-permute-done.20 = bf16[128,768]{1,0:T(8,128)(2,1)S(1)} collective-permute-done((bf16[128,768]{1,0:T(8,128)(2,1)S(1)}, bf16[128,768]{1,0:T(8,128)(2,1)S(1)}, u32[]{:S(2)}, u32[]{:S(2)}) %collective-permute-start.20) | collective-permute-done | bytes 196640 | tf_op jit(solution)/shard_map/ppermute | solution.py:44
  137.0 1.8 fusion.107
  139.7 1.8 collective-permute-start.23
  141.5 2.9 %collective-permute-start.22 = (bf16[128,768]{1,0:T(8,128)(2,1)S(1)}, bf16[128,768]{1,0:T(8,128)(2,1)S(1)}, u32[]{:S(2)}, u32[]{:S(2)}) collective-permute-start(bf16[128,768]{1,0:T(8,128)(2,1)S(1)} %get-tuple-element.135), channel_id=1, source_target_pairs={{0,3},{1,0},{2,1},{3,2},{4,7},{5,4},{6,5},{7,6},{8,11},{9,8},{10,9... | collective-permute-start | bytes 589832 | tf_op jit(solution)/shard_map/ppermute | solution.py:44
  148.5 1.5 collective-permute-start.29
  150.0 6.0 %collective-permute-done.23 = bf16[128,768]{1,0:T(8,128)(2,1)S(1)} collective-permute-done((bf16[128,768]{1,0:T(8,128)(2,1)S(1)}, bf16[128,768]{1,0:T(8,128)(2,1)S(1)}, u32[]{:S(2)}, u32[]{:S(2)}) %collective-permute-start.23) | collective-permute-done | bytes 196640 | tf_op jit(solution)/shard_map/ppermute | solution.py:44
  158.6 2.9 %collective-permute-start.26 = (bf16[128,192]{1,0:T(8,128)(2,1)S(1)}, bf16[128,192]{1,0:T(8,128)(2,1)S(1)}, u32[]{:S(2)}, u32[]{:S(2)}) collective-permute-start(bf16[128,192]{1,0:T(8,128)(2,1)S(1)} %get-tuple-element.176), channel_id=1, source_target_pairs={{0,2},{1,3},{2,0},{3,1},{4,6},{5,7},{6,4},{7,5},{8,10},{9,11},{10,... | collective-permute-start | bytes 147464 | tf_op jit(solution)/shard_map/ppermute | solution.py:44
  161.5 3.4 %collective-permute-start.27 = (bf16[128,192]{1,0:T(8,128)(2,1)S(1)}, bf16[128,192]{1,0:T(8,128)(2,1)S(1)}, u32[]{:S(2)}, u32[]{:S(2)}) collective-permute-start(bf16[128,192]{1,0:T(8,128)(2,1)S(1)} %get-tuple-element.175), channel_id=1, source_target_pairs={{0,3},{1,0},{2,1},{3,2},{4,7},{5,4},{6,5},{7,6},{8,11},{9,8},{10,9... | collective-permute-start | bytes 147464 | tf_op jit(solution)/shard_map/ppermute | solution.py:44
  168.9 2.1 pack.1
  172.8 13.5 %attend_back.1 = (bf16[1,3,512,2048]{3,2,1,0:T(8,128)(2,1)}, f32[512,192]{1,0:T(8,128)}, bf16[2,384,512]{2,1,0:T(8,128)(2,1)}, bf16[2,384,512]{2,1,0:T(8,128)(2,1)}) custom-call(s32[4]{0:T(128)} %xor_multiply_fusion.starts, bf16[3,512,2048]{2,1,0:T(8,128)(2,1)} %get-tuple-element.65.weights, bf16[512,192]{1,0:T(8,128)(2,1)} %get-tuple-element.59.context, ...), custom_call_target="tpu_custom_call" | custom-call | flops 2013265920 | bytes 18874368 | tf_op jit(solution)/shard_map/attend_back/pallas_call | solution.py:348
  187.3 3.1 %collective-permute-start.37 = (bf16[128,1536]{1,0:T(8,128)(2,1)S(1)}, bf16[128,1536]{1,0:T(8,128)(2,1)S(1)}, u32[]{:S(2)}, u32[]{:S(2)}) collective-permute-start(bf16[128,1536]{1,0:T(8,128)(2,1)S(1)} %pad_maximum_fusion.7), channel_id=1, source_target_pairs={{0,2},{1,3},{2,0},{3,1},{4,6},{5,7},{6,4},{7,5},{8,10},{9,11},{10,... | collective-permute-start | bytes 1179656 | tf_op jit(solution)/shard_map/ppermute | solution.py:44
  191.1 1.5 fusion.12
  193.0 1.6 collective-permute-start.32
  194.6 1.2 fusion.11
  196.2 8.4 %collective-permute-done.32 = bf16[1,384,512]{2,1,0:T(8,128)(2,1)S(1)} collective-permute-done((bf16[1,384,512]{2,1,0:T(8,128)(2,1)S(1)}, bf16[1,384,512]{2,1,0:T(8,128)(2,1)S(1)}, u32[]{:S(2)}, u32[]{:S(2)}) %collective-permute-start.32) | collective-permute-done | bytes 393248 | tf_op jit(solution)/shard_map/ppermute | solution.py:49
  204.6 1.5 collective-permute-start.34
  206.6 10.1 %collective-permute-done.37 = bf16[128,1536]{1,0:T(8,128)(2,1)S(1)} collective-permute-done((bf16[128,1536]{1,0:T(8,128)(2,1)S(1)}, bf16[128,1536]{1,0:T(8,128)(2,1)S(1)}, u32[]{:S(2)}, u32[]{:S(2)}) %collective-permute-start.37) | collective-permute-done | bytes 393248 | tf_op jit(solution)/shard_map/ppermute | solution.py:44
  216.7 2.8 collective-permute-done.34
  221.7 6.2 %collective-permute-start.41 = (bf16[128,768]{1,0:T(8,128)(2,1)S(1)}, bf16[128,768]{1,0:T(8,128)(2,1)S(1)}, u32[]{:S(2)}, u32[]{:S(2)}) collective-permute-start(bf16[128,768]{1,0:T(8,128)(2,1)S(1)} %get-tuple-element.133), channel_id=1, source_target_pairs={{0,1},{1,2},{2,3},{3,0},{4,5},{5,6},{6,7},{7,4},{8,9},{9,10},{10,1... | collective-permute-start | bytes 589832 | tf_op jit(solution)/shard_map/ppermute | solution.py:44
  228.7 1.7 collective-permute-start.39
  230.4 1.6 collective-permute-start.42
  235.0 1.3 maximum_convert_fusion
  236.2 1.6 collective-permute-start.45
  237.8 3.5 %collective-permute-done.40 = bf16[128,768]{1,0:T(8,128)(2,1)S(1)} collective-permute-done((bf16[128,768]{1,0:T(8,128)(2,1)S(1)}, bf16[128,768]{1,0:T(8,128)(2,1)S(1)}, u32[]{:S(2)}, u32[]{:S(2)}) %collective-permute-start.40) | collective-permute-done | bytes 196640 | tf_op jit(solution)/shard_map/ppermute | solution.py:44
  244.8 2.8 collective-permute-done.55
  247.7 3.2 %collective-permute-start.48 = (f32[12,768]{1,0:T(8,128)S(1)}, f32[12,768]{1,0:T(8,128)S(1)}, u32[]{:S(2)}, u32[]{:S(2)}) collective-permute-start(f32[12,768]{1,0:T(8,128)S(1)} %add.328), channel_id=1, source_target_pairs={{0,2},{1,3},{2,0},{3,1},{4,6},{5,7},{6,4},{7,5},{8,10},{9,11},{10,... | collective-permute-start | bytes 110600 | tf_op jit(solution)/shard_map/ppermute | solution.py:49
  250.9 3.7 %collective-permute-start.49 = (f32[12,768]{1,0:T(8,128)S(1)}, f32[12,768]{1,0:T(8,128)S(1)}, u32[]{:S(2)}, u32[]{:S(2)}) collective-permute-start(f32[12,768]{1,0:T(8,128)S(1)} %add.328), channel_id=1, source_target_pairs={{0,3},{1,2},{2,1},{3,0},{4,7},{5,6},{6,5},{7,4},{8,11},{9,10},{10,... | collective-permute-start | bytes 110600 | tf_op jit(solution)/shard_map/ppermute | solution.py:49
  255.7 1.4 collective-permute-start.52
  257.2 1.6 collective-permute-start.56
  258.8 3.8 %collective-permute-start.44 = (bf16[128,768]{1,0:T(8,128)(2,1)S(1)}, bf16[128,768]{1,0:T(8,128)(2,1)}, u32[]{:S(2)}, u32[]{:S(2)}) collective-permute-start(bf16[128,768]{1,0:T(8,128)(2,1)S(1)} %fusion.40), channel_id=1, source_target_pairs={{0,3},{1,0},{2,1},{3,2},{4,7},{5,4},{6,5},{7,6},{8,11},{9,8},{10,9... | collective-permute-start | bytes 589832 | tf_op jit(solution)/shard_map/ppermute | solution.py:44
  268.5 1.6 collective-permute-start.53
  270.8 1.5 collective-permute-start.50
  272.4 2.4 convert_add_fusion.2
  274.8 6.2 %collective-permute-done.53 = bf16[576,384]{1,0:T(8,128)(2,1)S(1)} collective-permute-done((bf16[576,384]{1,0:T(8,128)(2,1)S(1)}, bf16[576,384]{1,0:T(8,128)(2,1)S(1)}, u32[]{:S(2)}, u32[]{:S(2)}) %collective-permute-start.53) | collective-permute-done | bytes 442400 | tf_op jit(solution)/shard_map/ppermute | solution.py:49
  283.3 1.3 maximum_convert_fusion.1
  (306 shorter events, 54.6 us)
Async XLA Ops:
  0.7 11.0 %collective-permute-start.4 = (bf16[192,384]{1,0:T(8,128)(2,1)}, bf16[192,384]{1,0:T(8,128)(2,1)S(1)}, u32[]{:S(2)}, u32[]{:S(2)}) collective-permute-start(bf16[192,384]{1,0:T(8,128)(2,1)} %param.27), channel_id=1, source_target_pairs={{0,3},{1,0},{2,1},{3,2},{4,7},{5,4},{6,5},{7,6},{8,11},{9,8},{10,9... | collective-permute-start | bytes 442376 | tf_op jit(solution)/shard_map/ppermute | solution.py:44
  5.8 12.8 %collective-permute-start.3 = (bf16[192,384]{1,0:T(8,128)(2,1)}, bf16[192,384]{1,0:T(8,128)(2,1)}, u32[]{:S(2)}, u32[]{:S(2)}) collective-permute-start(bf16[192,384]{1,0:T(8,128)(2,1)} %param.27), channel_id=1, source_target_pairs={{0,2},{1,3},{2,0},{3,1},{4,6},{5,7},{6,4},{7,5},{8,10},{9,11},{10,... | collective-permute-start | bytes 442376 | tf_op jit(solution)/shard_map/ppermute | solution.py:44
  5.8 12.8 %collective-permute-start.2 = (bf16[192,384]{1,0:T(8,128)(2,1)}, bf16[192,384]{1,0:T(8,128)(2,1)}, u32[]{:S(2)}, u32[]{:S(2)}) collective-permute-start(bf16[192,384]{1,0:T(8,128)(2,1)} %param.27), channel_id=1, source_target_pairs={{0,1},{1,2},{2,3},{3,0},{4,5},{5,6},{6,7},{7,4},{8,9},{9,10},{10,1... | collective-permute-start | bytes 442376 | tf_op jit(solution)/shard_map/ppermute | solution.py:44
  8.7 11.8 %collective-permute-start.1 = (bf16[576,384]{1,0:T(8,128)(2,1)}, bf16[576,384]{1,0:T(8,128)(2,1)S(1)}, u32[]{:S(2)}, u32[]{:S(2)}) collective-permute-start(bf16[576,384]{1,0:T(8,128)(2,1)} %pad_maximum_fusion.6), channel_id=1, source_target_pairs={{0,16},{16,0},{1,17},{17,1},{2,18},{18,2},{3,19},{19,3},{4,20},{20... | collective-permute-start | bytes 1327112 | tf_op jit(solution)/shard_map/ppermute | solution.py:49
  21.2 10.5 %collective-permute-start.5 = (bf16[1,512,384]{2,1,0:T(8,128)(2,1)S(1)}, bf16[1,512,384]{2,1,0:T(8,128)(2,1)S(1)}, u32[]{:S(2)}, u32[]{:S(2)}) collective-permute-start(bf16[1,512,384]{2,1,0:T(8,128)(2,1)S(1)} %bitcast.87), channel_id=1, source_target_pairs={{0,8},{4,12},{8,0},{12,4},{1,9},{5,13},{9,1},{13,5},{2,10},{6,14},... | collective-permute-start | bytes 1179656 | tf_op jit(solution)/shard_map/ppermute | solution.py:49
  32.8 6.4 %collective-permute-start.6 = (bf16[2,512,384]{2,1,0:T(8,128)(2,1)}, bf16[2,512,384]{2,1,0:T(8,128)(2,1)}, u32[]{:S(2)}, u32[]{:S(2)}) collective-permute-start(bf16[2,512,384]{2,1,0:T(8,128)(2,1)} %pad_maximum_fusion.2), channel_id=1, source_target_pairs={{0,4},{4,0},{8,12},{12,8},{1,5},{5,1},{9,13},{13,9},{2,6},{6,2},{1... | collective-permute-start | bytes 2359304 | tf_op jit(solution)/shard_map/ppermute | solution.py:49
  33.4 65.2 %collective-permute-start = (f32[]{:T(128)}, f32[]{:T(128)}, u32[]{:S(2)}, u32[]{:S(2)}) collective-permute-start(f32[]{:T(128)} %convert_element_type.210), channel_id=1, source_target_pairs={{0,16},{16,0},{1,17},{17,1},{2,18},{18,2},{3,19},{19,3},{4,20},{20... | collective-permute-start | bytes 20 | tf_op jit(solution)/shard_map/ppermute | solution.py:49
  37.0 15.9 %collective-permute-start.7 = (bf16[768,384]{1,0:T(8,128)(2,1)}, bf16[768,384]{1,0:T(8,128)(2,1)}, u32[]{:S(2)}, u32[]{:S(2)}) collective-permute-start(bf16[768,384]{1,0:T(8,128)(2,1)} %pad_maximum_fusion.5), channel_id=1, source_target_pairs={{0,16},{16,0},{1,17},{17,1},{2,18},{18,2},{3,19},{19,3},{4,20},{20... | collective-permute-start | bytes 1769480 | tf_op jit(solution)/shard_map/ppermute | solution.py:49
  54.1 16.3 %collective-permute-start.14 = (bf16[384,768]{1,0:T(8,128)(2,1)S(1)}, bf16[384,768]{1,0:T(8,128)(2,1)S(1)}, u32[]{:S(2)}, u32[]{:S(2)}) collective-permute-start(bf16[384,768]{1,0:T(8,128)(2,1)S(1)} %copy-done.26), channel_id=1, source_target_pairs={{0,16},{16,0},{1,17},{17,1},{2,18},{18,2},{3,19},{19,3},{4,20},{20... | collective-permute-start | bytes 1769480 | tf_op jit(solution)/shard_map/ppermute | solution.py:49
  55.7 6.0 %collective-permute-start.10 = (bf16[128,192]{1,0:T(8,128)(2,1)S(1)}, bf16[128,192]{1,0:T(8,128)(2,1)S(1)}, u32[]{:S(2)}, u32[]{:S(2)}) collective-permute-start(bf16[128,192]{1,0:T(8,128)(2,1)S(1)} %get-tuple-element.167), channel_id=1, source_target_pairs={{0,3},{1,0},{2,1},{3,2},{4,7},{5,4},{6,5},{7,6},{8,11},{9,8},{10,9... | collective-permute-start | bytes 147464 | tf_op jit(solution)/shard_map/ppermute | solution.py:44
  57.3 7.3 %collective-permute-start.9 = (bf16[128,192]{1,0:T(8,128)(2,1)S(1)}, bf16[128,192]{1,0:T(8,128)(2,1)S(1)}, u32[]{:S(2)}, u32[]{:S(2)}) collective-permute-start(bf16[128,192]{1,0:T(8,128)(2,1)S(1)} %get-tuple-element.168), channel_id=1, source_target_pairs={{0,2},{1,3},{2,0},{3,1},{4,6},{5,7},{6,4},{7,5},{8,10},{9,11},{10,... | collective-permute-start | bytes 147464 | tf_op jit(solution)/shard_map/ppermute | solution.py:44
  58.4 6.1 %collective-permute-start.8 = (bf16[128,192]{1,0:T(8,128)(2,1)S(1)}, bf16[128,192]{1,0:T(8,128)(2,1)S(1)}, u32[]{:S(2)}, u32[]{:S(2)}) collective-permute-start(bf16[128,192]{1,0:T(8,128)(2,1)S(1)} %get-tuple-element.169), channel_id=1, source_target_pairs={{0,1},{1,2},{2,3},{3,0},{4,5},{5,6},{6,7},{7,4},{8,9},{9,10},{10,1... | collective-permute-start | bytes 147464 | tf_op jit(solution)/shard_map/ppermute | solution.py:44
  61.6 19.8 %collective-permute-start.15 = (bf16[768,384]{1,0:T(8,128)(2,1)S(1)}, bf16[768,384]{1,0:T(8,128)(2,1)S(1)}, u32[]{:S(2)}, u32[]{:S(2)}) collective-permute-start(bf16[768,384]{1,0:T(8,128)(2,1)S(1)} %copy-done.27), channel_id=1, source_target_pairs={{0,16},{16,0},{1,17},{17,1},{2,18},{18,2},{3,19},{19,3},{4,20},{20... | collective-permute-start | bytes 1769480 | tf_op jit(solution)/shard_map/ppermute | solution.py:49
  65.6 43.8 %copy-start.42 = (f32[128]{0:T(128)}, f32[128]{0:T(128)S(1)}, u32[]{:S(2)}) copy-start(f32[128]{0:T(128)S(1)} %add_rsqrt_fusion.1) | copy-start | bytes 1540
  66.0 15.6 %collective-permute-start.13 = (bf16[128,768]{1,0:T(8,128)(2,1)S(1)}, bf16[128,768]{1,0:T(8,128)(2,1)S(1)}, u32[]{:S(2)}, u32[]{:S(2)}) collective-permute-start(bf16[128,768]{1,0:T(8,128)(2,1)S(1)} %maximum_select_fusion.5), channel_id=1, source_target_pairs={{0,3},{1,0},{2,1},{3,2},{4,7},{5,4},{6,5},{7,6},{8,11},{9,8},{10,9... | collective-permute-start | bytes 589832 | tf_op jit(solution)/shard_map/ppermute | solution.py:44
  67.6 17.0 %collective-permute-start.12 = (bf16[128,768]{1,0:T(8,128)(2,1)S(1)}, bf16[128,768]{1,0:T(8,128)(2,1)S(1)}, u32[]{:S(2)}, u32[]{:S(2)}) collective-permute-start(bf16[128,768]{1,0:T(8,128)(2,1)S(1)} %maximum_select_fusion.5), channel_id=1, source_target_pairs={{0,2},{1,3},{2,0},{3,1},{4,6},{5,7},{6,4},{7,5},{8,10},{9,11},{10,... | collective-permute-start | bytes 589832 | tf_op jit(solution)/shard_map/ppermute | solution.py:44
  70.3 14.3 %collective-permute-start.11 = (bf16[128,768]{1,0:T(8,128)(2,1)S(1)}, bf16[128,768]{1,0:T(8,128)(2,1)S(1)}, u32[]{:S(2)}, u32[]{:S(2)}) collective-permute-start(bf16[128,768]{1,0:T(8,128)(2,1)S(1)} %maximum_select_fusion.5), channel_id=1, source_target_pairs={{0,1},{1,2},{2,3},{3,0},{4,5},{5,6},{6,7},{7,4},{8,9},{9,10},{10,1... | collective-permute-start | bytes 589832 | tf_op jit(solution)/shard_map/ppermute | solution.py:44
  92.3 9.6 %collective-permute-start.18 = (bf16[128,768]{1,0:T(8,128)(2,1)S(1)}, bf16[128,768]{1,0:T(8,128)(2,1)S(1)}, u32[]{:S(2)}, u32[]{:S(2)}) collective-permute-start(bf16[128,768]{1,0:T(8,128)(2,1)S(1)} %get-tuple-element.139), channel_id=1, source_target_pairs={{0,1},{1,2},{2,3},{3,0},{4,5},{5,6},{6,7},{7,4},{8,9},{9,10},{10,1... | collective-permute-start | bytes 589832 | tf_op jit(solution)/shard_map/ppermute | solution.py:44
  92.5 15.7 %collective-permute-start.17 = (bf16[128,768]{1,0:T(8,128)(2,1)S(1)}, bf16[128,768]{1,0:T(8,128)(2,1)S(1)}, u32[]{:S(2)}, u32[]{:S(2)}) collective-permute-start(bf16[128,768]{1,0:T(8,128)(2,1)S(1)} %get-tuple-element.140), channel_id=1, source_target_pairs={{0,2},{1,3},{2,0},{3,1},{4,6},{5,7},{6,4},{7,5},{8,10},{9,11},{10,... | collective-permute-start | bytes 589832 | tf_op jit(solution)/shard_map/ppermute | solution.py:44
  94.5 13.7 %collective-permute-start.16 = (bf16[128,768]{1,0:T(8,128)(2,1)S(1)}, bf16[128,768]{1,0:T(8,128)(2,1)S(1)}, u32[]{:S(2)}, u32[]{:S(2)}) collective-permute-start(bf16[128,768]{1,0:T(8,128)(2,1)S(1)} %get-tuple-element.138), channel_id=1, source_target_pairs={{0,3},{1,0},{2,1},{3,2},{4,7},{5,4},{6,5},{7,6},{8,11},{9,8},{10,9... | collective-permute-start | bytes 589832 | tf_op jit(solution)/shard_map/ppermute | solution.py:44
  109.4 27.6 %copy-start.59 = (f32[512,768]{1,0:T(8,128)S(1)}, f32[512,768]{1,0:T(8,128)}, u32[]{:S(2)}) copy-start(f32[512,768]{1,0:T(8,128)} %get-tuple-element.185) | copy-start | bytes 4718596
  111.7 25.3 %copy-start.6 = (bf16[768,768]{1,0:T(8,128)(2,1)S(1)}, bf16[768,768]{1,0:T(8,128)(2,1)}, u32[]{:S(2)}) copy-start(bf16[768,768]{1,0:T(8,128)(2,1)} %copy-done.5) | copy-start | bytes 3538948
  111.7 25.3 %copy-start.58 = (f32[512,768]{1,0:T(8,128)S(1)}, f32[512,768]{1,0:T(8,128)}, u32[]{:S(2)}) copy-start(f32[512,768]{1,0:T(8,128)} %get-tuple-element.118) | copy-start | bytes 4718596
  113.3 12.0 %collective-permute-start.21 = (bf16[128,768]{1,0:T(8,128)(2,1)S(1)}, bf16[128,768]{1,0:T(8,128)(2,1)S(1)}, u32[]{:S(2)}, u32[]{:S(2)}) collective-permute-start(bf16[128,768]{1,0:T(8,128)(2,1)S(1)} %maximum_select_fusion.6), channel_id=1, source_target_pairs={{0,3},{1,0},{2,1},{3,2},{4,7},{5,4},{6,5},{7,6},{8,11},{9,8},{10,9... | collective-permute-start | bytes 589832 | tf_op jit(solution)/shard_map/ppermute | solution.py:44
  120.0 17.0 %collective-permute-start.20 = (bf16[128,768]{1,0:T(8,128)(2,1)S(1)}, bf16[128,768]{1,0:T(8,128)(2,1)S(1)}, u32[]{:S(2)}, u32[]{:S(2)}) collective-permute-start(bf16[128,768]{1,0:T(8,128)(2,1)S(1)} %maximum_select_fusion.6), channel_id=1, source_target_pairs={{0,2},{1,3},{2,0},{3,1},{4,6},{5,7},{6,4},{7,5},{8,10},{9,11},{10,... | collective-permute-start | bytes 589832 | tf_op jit(solution)/shard_map/ppermute | solution.py:44
  120.0 17.0 %collective-permute-start.19 = (bf16[128,768]{1,0:T(8,128)(2,1)S(1)}, bf16[128,768]{1,0:T(8,128)(2,1)S(1)}, u32[]{:S(2)}, u32[]{:S(2)}) collective-permute-start(bf16[128,768]{1,0:T(8,128)(2,1)S(1)} %maximum_select_fusion.6), channel_id=1, source_target_pairs={{0,1},{1,2},{2,3},{3,0},{4,5},{5,6},{6,7},{7,4},{8,9},{9,10},{10,1... | collective-permute-start | bytes 589832 | tf_op jit(solution)/shard_map/ppermute | solution.py:44
  139.7 10.4 %collective-permute-start.24 = (bf16[128,768]{1,0:T(8,128)(2,1)S(1)}, bf16[128,768]{1,0:T(8,128)(2,1)S(1)}, u32[]{:S(2)}, u32[]{:S(2)}) collective-permute-start(bf16[128,768]{1,0:T(8,128)(2,1)S(1)} %get-tuple-element.136), channel_id=1, source_target_pairs={{0,1},{1,2},{2,3},{3,0},{4,5},{5,6},{6,7},{7,4},{8,9},{9,10},{10,1... | collective-permute-start | bytes 589832 | tf_op jit(solution)/shard_map/ppermute | solution.py:44
  139.7 16.3 %collective-permute-start.23 = (bf16[128,768]{1,0:T(8,128)(2,1)S(1)}, bf16[128,768]{1,0:T(8,128)(2,1)S(1)}, u32[]{:S(2)}, u32[]{:S(2)}) collective-permute-start(bf16[128,768]{1,0:T(8,128)(2,1)S(1)} %get-tuple-element.137), channel_id=1, source_target_pairs={{0,2},{1,3},{2,0},{3,1},{4,6},{5,7},{6,4},{7,5},{8,10},{9,11},{10,... | collective-permute-start | bytes 589832 | tf_op jit(solution)/shard_map/ppermute | solution.py:44
  141.5 14.5 %collective-permute-start.22 = (bf16[128,768]{1,0:T(8,128)(2,1)S(1)}, bf16[128,768]{1,0:T(8,128)(2,1)S(1)}, u32[]{:S(2)}, u32[]{:S(2)}) collective-permute-start(bf16[128,768]{1,0:T(8,128)(2,1)S(1)} %get-tuple-element.135), channel_id=1, source_target_pairs={{0,3},{1,0},{2,1},{3,2},{4,7},{5,4},{6,5},{7,6},{8,11},{9,8},{10,9... | collective-permute-start | bytes 589832 | tf_op jit(solution)/shard_map/ppermute | solution.py:44
  146.2 26.2 %collective-permute-start.28 = (bf16[768,384]{1,0:T(8,128)(2,1)}, bf16[768,384]{1,0:T(8,128)(2,1)}, u32[]{:S(2)}, u32[]{:S(2)}) collective-permute-start(bf16[768,384]{1,0:T(8,128)(2,1)} %split.151), channel_id=1, source_target_pairs={{0,16},{16,0},{1,17},{17,1},{2,18},{18,2},{3,19},{19,3},{4,20},{20... | collective-permute-start | bytes 1769480 | tf_op jit(solution)/shard_map/ppermute | solution.py:49
  148.5 24.2 %collective-permute-start.29 = (bf16[384,768]{1,0:T(8,128)(2,1)}, bf16[384,768]{1,0:T(8,128)(2,1)}, u32[]{:S(2)}, u32[]{:S(2)}) collective-permute-start(bf16[384,768]{1,0:T(8,128)(2,1)} %split.150), channel_id=1, source_target_pairs={{0,16},{16,0},{1,17},{17,1},{2,18},{18,2},{3,19},{19,3},{4,20},{20... | collective-permute-start | bytes 1769480 | tf_op jit(solution)/shard_map/ppermute | solution.py:49
  158.6 12.5 %collective-permute-start.26 = (bf16[128,192]{1,0:T(8,128)(2,1)S(1)}, bf16[128,192]{1,0:T(8,128)(2,1)S(1)}, u32[]{:S(2)}, u32[]{:S(2)}) collective-permute-start(bf16[128,192]{1,0:T(8,128)(2,1)S(1)} %get-tuple-element.176), channel_id=1, source_target_pairs={{0,2},{1,3},{2,0},{3,1},{4,6},{5,7},{6,4},{7,5},{8,10},{9,11},{10,... | collective-permute-start | bytes 147464 | tf_op jit(solution)/shard_map/ppermute | solution.py:44
  161.5 10.1 %collective-permute-start.27 = (bf16[128,192]{1,0:T(8,128)(2,1)S(1)}, bf16[128,192]{1,0:T(8,128)(2,1)S(1)}, u32[]{:S(2)}, u32[]{:S(2)}) collective-permute-start(bf16[128,192]{1,0:T(8,128)(2,1)S(1)} %get-tuple-element.175), channel_id=1, source_target_pairs={{0,3},{1,0},{2,1},{3,2},{4,7},{5,4},{6,5},{7,6},{8,11},{9,8},{10,9... | collective-permute-start | bytes 147464 | tf_op jit(solution)/shard_map/ppermute | solution.py:44
  164.8 6.7 %collective-permute-start.25 = (bf16[128,192]{1,0:T(8,128)(2,1)S(1)}, bf16[128,192]{1,0:T(8,128)(2,1)S(1)}, u32[]{:S(2)}, u32[]{:S(2)}) collective-permute-start(bf16[128,192]{1,0:T(8,128)(2,1)S(1)} %get-tuple-element.174), channel_id=1, source_target_pairs={{0,1},{1,2},{2,3},{3,0},{4,5},{5,6},{6,7},{7,4},{8,9},{9,10},{10,1... | collective-permute-start | bytes 147464 | tf_op jit(solution)/shard_map/ppermute | solution.py:44
  171.0 15.2 %collective-permute-start.30 = (f32[12,768]{1,0:T(8,128)}, f32[12,768]{1,0:T(8,128)S(1)}, u32[]{:S(2)}, u32[]{:S(2)}) collective-permute-start(f32[12,768]{1,0:T(8,128)} %pack.1), channel_id=1, source_target_pairs={{0,16},{16,0},{1,17},{17,1},{2,18},{18,2},{3,19},{19,3},{4,20},{20... | collective-permute-start | bytes 110600 | tf_op jit(solution)/shard_map/ppermute | solution.py:49
  186.3 6.4 %collective-permute-start.31 = (bf16[2,384,512]{2,1,0:T(8,128)(2,1)}, bf16[2,384,512]{2,1,0:T(8,128)(2,1)S(1)}, u32[]{:S(2)}, u32[]{:S(2)}) collective-permute-start(bf16[2,384,512]{2,1,0:T(8,128)(2,1)} %get-tuple-element.71), channel_id=1, source_target_pairs={{0,4},{4,0},{8,12},{12,8},{1,5},{5,1},{9,13},{13,9},{2,6},{6,2},{1... | collective-permute-start | bytes 2359304 | tf_op jit(solution)/shard_map/ppermute | solution.py:49
  186.4 20.2 %collective-permute-start.36 = (bf16[128,1536]{1,0:T(8,128)(2,1)S(1)}, bf16[128,1536]{1,0:T(8,128)(2,1)S(1)}, u32[]{:S(2)}, u32[]{:S(2)}) collective-permute-start(bf16[128,1536]{1,0:T(8,128)(2,1)S(1)} %pad_maximum_fusion.7), channel_id=1, source_target_pairs={{0,1},{1,2},{2,3},{3,0},{4,5},{5,6},{6,7},{7,4},{8,9},{9,10},{10,1... | collective-permute-start | bytes 1179656 | tf_op jit(solution)/shard_map/ppermute | solution.py:44
  187.3 29.3 %collective-permute-start.37 = (bf16[128,1536]{1,0:T(8,128)(2,1)S(1)}, bf16[128,1536]{1,0:T(8,128)(2,1)S(1)}, u32[]{:S(2)}, u32[]{:S(2)}) collective-permute-start(bf16[128,1536]{1,0:T(8,128)(2,1)S(1)} %pad_maximum_fusion.7), channel_id=1, source_target_pairs={{0,2},{1,3},{2,0},{3,1},{4,6},{5,7},{6,4},{7,5},{8,10},{9,11},{10,... | collective-permute-start | bytes 1179656 | tf_op jit(solution)/shard_map/ppermute | solution.py:44
  190.4 26.3 %collective-permute-start.38 = (bf16[128,1536]{1,0:T(8,128)(2,1)S(1)}, bf16[128,1536]{1,0:T(8,128)(2,1)S(1)}, u32[]{:S(2)}, u32[]{:S(2)}) collective-permute-start(bf16[128,1536]{1,0:T(8,128)(2,1)S(1)} %pad_maximum_fusion.7), channel_id=1, source_target_pairs={{0,3},{1,0},{2,1},{3,2},{4,7},{5,4},{6,5},{7,6},{8,11},{9,8},{10,9... | collective-permute-start | bytes 1179656 | tf_op jit(solution)/shard_map/ppermute | solution.py:44
  191.1 4.8 %collective-permute-start.35 = (f32[12,768]{1,0:T(8,128)S(1)}, f32[12,768]{1,0:T(8,128)S(1)}, u32[]{:S(2)}, u32[]{:S(2)}) collective-permute-start(f32[12,768]{1,0:T(8,128)S(1)} %add.317), channel_id=1, source_target_pairs={{0,4},{4,0},{8,12},{12,8},{1,5},{5,1},{9,13},{13,9},{2,6},{6,2},{1... | collective-permute-start | bytes 110600 | tf_op jit(solution)/shard_map/ppermute | solution.py:49
  193.0 11.6 %collective-permute-start.32 = (bf16[1,384,512]{2,1,0:T(8,128)(2,1)S(1)}, bf16[1,384,512]{2,1,0:T(8,128)(2,1)S(1)}, u32[]{:S(2)}, u32[]{:S(2)}) collective-permute-start(bf16[1,384,512]{2,1,0:T(8,128)(2,1)S(1)} %slice.317), channel_id=1, source_target_pairs={{0,8},{4,12},{8,0},{12,4},{1,9},{5,13},{9,1},{13,5},{2,10},{6,14},... | collective-permute-start | bytes 1179656 | tf_op jit(solution)/shard_map/ppermute | solution.py:49
  195.9 20.8 %collective-permute-start.33 = (bf16[384,768]{1,0:T(8,128)(2,1)S(1)}, bf16[384,768]{1,0:T(8,128)(2,1)S(1)}, u32[]{:S(2)}, u32[]{:S(2)}) collective-permute-start(bf16[384,768]{1,0:T(8,128)(2,1)S(1)} %fusion.12), channel_id=1, source_target_pairs={{0,4},{4,0},{8,12},{12,8},{1,5},{5,1},{9,13},{13,9},{2,6},{6,2},{1... | collective-permute-start | bytes 1769480 | tf_op jit(solution)/shard_map/ppermute | solution.py:49
  204.6 14.9 %collective-permute-start.34 = (bf16[768,384]{1,0:T(8,128)(2,1)S(1)}, bf16[768,384]{1,0:T(8,128)(2,1)S(1)}, u32[]{:S(2)}, u32[]{:S(2)}) collective-permute-start(bf16[768,384]{1,0:T(8,128)(2,1)S(1)} %fusion.11), channel_id=1, source_target_pairs={{0,8},{4,12},{8,0},{12,4},{1,9},{5,13},{9,1},{13,5},{2,10},{6,14},... | collective-permute-start | bytes 1769480 | tf_op jit(solution)/shard_map/ppermute | solution.py:49
  221.7 14.5 %collective-permute-start.41 = (bf16[128,768]{1,0:T(8,128)(2,1)S(1)}, bf16[128,768]{1,0:T(8,128)(2,1)S(1)}, u32[]{:S(2)}, u32[]{:S(2)}) collective-permute-start(bf16[128,768]{1,0:T(8,128)(2,1)S(1)} %get-tuple-element.133), channel_id=1, source_target_pairs={{0,1},{1,2},{2,3},{3,0},{4,5},{5,6},{6,7},{7,4},{8,9},{9,10},{10,1... | collective-permute-start | bytes 589832 | tf_op jit(solution)/shard_map/ppermute | solution.py:44
  227.9 13.4 %collective-permute-start.40 = (bf16[128,768]{1,0:T(8,128)(2,1)S(1)}, bf16[128,768]{1,0:T(8,128)(2,1)S(1)}, u32[]{:S(2)}, u32[]{:S(2)}) collective-permute-start(bf16[128,768]{1,0:T(8,128)(2,1)S(1)} %get-tuple-element.134), channel_id=1, source_target_pairs={{0,2},{1,3},{2,0},{3,1},{4,6},{5,7},{6,4},{7,5},{8,10},{9,11},{10,... | collective-permute-start | bytes 589832 | tf_op jit(solution)/shard_map/ppermute | solution.py:44
  228.7 12.6 %collective-permute-start.39 = (bf16[128,768]{1,0:T(8,128)(2,1)S(1)}, bf16[128,768]{1,0:T(8,128)(2,1)S(1)}, u32[]{:S(2)}, u32[]{:S(2)}) collective-permute-start(bf16[128,768]{1,0:T(8,128)(2,1)S(1)} %get-tuple-element.132), channel_id=1, source_target_pairs={{0,3},{1,0},{2,1},{3,2},{4,7},{5,4},{6,5},{7,6},{8,11},{9,8},{10,9... | collective-permute-start | bytes 589832 | tf_op jit(solution)/shard_map/ppermute | solution.py:44
  230.4 12.0 %collective-permute-start.42 = (f32[12,768]{1,0:T(8,128)S(1)}, f32[12,768]{1,0:T(8,128)S(1)}, u32[]{:S(2)}, u32[]{:S(2)}) collective-permute-start(f32[12,768]{1,0:T(8,128)S(1)} %add.323), channel_id=1, source_target_pairs={{0,8},{4,12},{8,0},{12,4},{1,9},{5,13},{9,1},{13,5},{2,10},{6,14},... | collective-permute-start | bytes 110600 | tf_op jit(solution)/shard_map/ppermute | solution.py:49
  232.2 10.2 %collective-permute-start.43 = (f32[384]{0:T(512)S(1)}, f32[384]{0:T(512)S(1)}, u32[]{:S(2)}, u32[]{:S(2)}) collective-permute-start(f32[384]{0:T(512)S(1)} %pad_maximum_fusion.17), channel_id=1, source_target_pairs={{0,8},{4,12},{8,0},{12,4},{1,9},{5,13},{9,1},{13,5},{2,10},{6,14},... | collective-permute-start | bytes 4616 | tf_op jit(solution)/shard_map/ppermute | solution.py:49
  236.2 34.6 %collective-permute-start.45 = (bf16[384,768]{1,0:T(8,128)(2,1)}, bf16[384,768]{1,0:T(8,128)(2,1)}, u32[]{:S(2)}, u32[]{:S(2)}) collective-permute-start(bf16[384,768]{1,0:T(8,128)(2,1)} %add_convert_fusion.1), channel_id=1, source_target_pairs={{0,8},{4,12},{8,0},{12,4},{1,9},{5,13},{9,1},{13,5},{2,10},{6,14},... | collective-permute-start | bytes 1769480 | tf_op jit(solution)/shard_map/ppermute | solution.py:49
  241.3 39.8 %collective-permute-start.46 = (bf16[768,384]{1,0:T(8,128)(2,1)S(1)}, bf16[768,384]{1,0:T(8,128)(2,1)S(1)}, u32[]{:S(2)}, u32[]{:S(2)}) collective-permute-start(bf16[768,384]{1,0:T(8,128)(2,1)S(1)} %add_convert_fusion), channel_id=1, source_target_pairs={{0,4},{4,0},{8,12},{12,8},{1,5},{5,1},{9,13},{13,9},{2,6},{6,2},{1... | collective-permute-start | bytes 1769480 | tf_op jit(solution)/shard_map/ppermute | solution.py:49
  241.3 6.3 %collective-permute-start.55 = (bf16[192,384]{1,0:T(8,128)(2,1)S(1)}, bf16[192,384]{1,0:T(8,128)(2,1)S(1)}, u32[]{:S(2)}, u32[]{:S(2)}) collective-permute-start(bf16[192,384]{1,0:T(8,128)(2,1)S(1)} %split.152), channel_id=1, source_target_pairs={{0,16},{16,0},{1,17},{17,1},{2,18},{18,2},{3,19},{19,3},{4,20},{20... | collective-permute-start | bytes 442376 | tf_op jit(solution)/shard_map/ppermute | solution.py:49
  242.5 1.2 collective-permute-start.58
  243.7 10.9 %collective-permute-start.59 = (f32[384]{0:T(512)S(1)}, f32[384]{0:T(512)S(1)}, u32[]{:S(2)}, u32[]{:S(2)}) collective-permute-start(f32[384]{0:T(512)S(1)} %add.342), channel_id=1, source_target_pairs={{0,16},{16,0},{1,17},{17,1},{2,18},{18,2},{3,19},{19,3},{4,20},{20... | collective-permute-start | bytes 4616 | tf_op jit(solution)/shard_map/ppermute | solution.py:49
  247.7 8.0 %collective-permute-start.48 = (f32[12,768]{1,0:T(8,128)S(1)}, f32[12,768]{1,0:T(8,128)S(1)}, u32[]{:S(2)}, u32[]{:S(2)}) collective-permute-start(f32[12,768]{1,0:T(8,128)S(1)} %add.328), channel_id=1, source_target_pairs={{0,2},{1,3},{2,0},{3,1},{4,6},{5,7},{6,4},{7,5},{8,10},{9,11},{10,... | collective-permute-start | bytes 110600 | tf_op jit(solution)/shard_map/ppermute | solution.py:49
  250.9 6.3 %collective-permute-start.49 = (f32[12,768]{1,0:T(8,128)S(1)}, f32[12,768]{1,0:T(8,128)S(1)}, u32[]{:S(2)}, u32[]{:S(2)}) collective-permute-start(f32[12,768]{1,0:T(8,128)S(1)} %add.328), channel_id=1, source_target_pairs={{0,3},{1,2},{2,1},{3,0},{4,7},{5,6},{6,5},{7,4},{8,11},{9,10},{10,... | collective-permute-start | bytes 110600 | tf_op jit(solution)/shard_map/ppermute | solution.py:49
  254.6 4.2 %collective-permute-start.47 = (f32[12,768]{1,0:T(8,128)S(1)}, f32[12,768]{1,0:T(8,128)S(1)}, u32[]{:S(2)}, u32[]{:S(2)}) collective-permute-start(f32[12,768]{1,0:T(8,128)S(1)} %add.328), channel_id=1, source_target_pairs={{0,1},{1,0},{2,3},{3,2},{4,5},{5,4},{6,7},{7,6},{8,9},{9,8},{10,11... | collective-permute-start | bytes 110600 | tf_op jit(solution)/shard_map/ppermute | solution.py:49
  255.7 11.5 %collective-permute-start.52 = (bf16[576,384]{1,0:T(8,128)(2,1)}, bf16[576,384]{1,0:T(8,128)(2,1)}, u32[]{:S(2)}, u32[]{:S(2)}) collective-permute-start(bf16[576,384]{1,0:T(8,128)(2,1)} %fusion.16), channel_id=1, source_target_pairs={{0,16},{16,0},{1,17},{17,1},{2,18},{18,2},{3,19},{19,3},{4,20},{20... | collective-permute-start | bytes 1327112 | tf_op jit(solution)/shard_map/ppermute | solution.py:49
  257.2 7.3 %collective-permute-start.56 = (bf16[192,384]{1,0:T(8,128)(2,1)S(1)}, bf16[192,384]{1,0:T(8,128)(2,1)}, u32[]{:S(2)}, u32[]{:S(2)}) collective-permute-start(bf16[192,384]{1,0:T(8,128)(2,1)S(1)} %fusion.47), channel_id=1, source_target_pairs={{0,8},{4,12},{8,0},{12,4},{1,9},{5,13},{9,1},{13,5},{2,10},{6,14},... | collective-permute-start | bytes 442376 | tf_op jit(solution)/shard_map/ppermute | solution.py:49
  258.8 23.5 %collective-permute-start.44 = (bf16[128,768]{1,0:T(8,128)(2,1)S(1)}, bf16[128,768]{1,0:T(8,128)(2,1)}, u32[]{:S(2)}, u32[]{:S(2)}) collective-permute-start(bf16[128,768]{1,0:T(8,128)(2,1)S(1)} %fusion.40), channel_id=1, source_target_pairs={{0,3},{1,0},{2,1},{3,2},{4,7},{5,4},{6,5},{7,6},{8,11},{9,8},{10,9... | collective-permute-start | bytes 589832 | tf_op jit(solution)/shard_map/ppermute | solution.py:44
  264.4 17.8 %collective-permute-start.51 = (bf16[128,768]{1,0:T(8,128)(2,1)S(1)}, bf16[128,768]{1,0:T(8,128)(2,1)S(1)}, u32[]{:S(2)}, u32[]{:S(2)}) collective-permute-start(bf16[128,768]{1,0:T(8,128)(2,1)S(1)} %fusion.40), channel_id=1, source_target_pairs={{0,2},{1,3},{2,0},{3,1},{4,6},{5,7},{6,4},{7,5},{8,10},{9,11},{10,... | collective-permute-start | bytes 589832 | tf_op jit(solution)/shard_map/ppermute | solution.py:44
  267.2 1.4 collective-permute-start.57
  268.5 12.4 %collective-permute-start.53 = (bf16[576,384]{1,0:T(8,128)(2,1)S(1)}, bf16[576,384]{1,0:T(8,128)(2,1)S(1)}, u32[]{:S(2)}, u32[]{:S(2)}) collective-permute-start(bf16[576,384]{1,0:T(8,128)(2,1)S(1)} %fusion.15), channel_id=1, source_target_pairs={{0,8},{4,12},{8,0},{12,4},{1,9},{5,13},{9,1},{13,5},{2,10},{6,14},... | collective-permute-start | bytes 1327112 | tf_op jit(solution)/shard_map/ppermute | solution.py:49
  270.8 11.4 %collective-permute-start.50 = (bf16[128,768]{1,0:T(8,128)(2,1)S(1)}, bf16[128,768]{1,0:T(8,128)(2,1)S(1)}, u32[]{:S(2)}, u32[]{:S(2)}) collective-permute-start(bf16[128,768]{1,0:T(8,128)(2,1)S(1)} %fusion.40), channel_id=1, source_target_pairs={{0,1},{1,2},{2,3},{3,0},{4,5},{5,6},{6,7},{7,4},{8,9},{9,10},{10,1... | collective-permute-start | bytes 589832 | tf_op jit(solution)/shard_map/ppermute | solution.py:44
  281.0 3.5 %collective-permute-start.54 = (bf16[576,384]{1,0:T(8,128)(2,1)S(1)}, bf16[576,384]{1,0:T(8,128)(2,1)S(1)}, u32[]{:S(2)}, u32[]{:S(2)}) collective-permute-start(bf16[576,384]{1,0:T(8,128)(2,1)S(1)} %add_convert_fusion.2), channel_id=1, source_target_pairs={{0,4},{4,0},{8,12},{12,8},{1,5},{5,1},{9,13},{13,9},{2,6},{6,2},{1... | collective-permute-start | bytes 1327112 | tf_op jit(solution)/shard_map/ppermute | solution.py:49
  (56 other events, 366.5 us)

commit v5 on v4

--- a/solution.py
+++ b/solution.py
@@ -171,15 +171,6 @@
     place = lax.axis_index("tp")
     return jnp.concatenate(
         [lax.select_n(lax.rem(place - p + size, size), *blocks) for p in range(size)], 0
-    )
-
-
-def columns_turn(block):
-    size = lax.axis_size("tp")
-    place = lax.axis_index("tp")
-    blocks = jnp.split(block, size, 1)
-    return jnp.concatenate(
-        [lax.select_n(lax.rem(place - e + size, size), *blocks) for e in range(size)], 1
     )
 
 
@@ -500,7 +491,8 @@
     grad_bias_output = jnp.sum(d_first, 0)
     d_first_low = own_first(d_first.astype(BF16))
     d_context_mine = dot32(d_first_low, full_output, ((1,), (1,))).astype(BF16)
-    d_context = rows_place(rows_exchange(jnp.split(d_context_mine, tp_size, 1)))
+    d_context = jnp.concatenate(rows_exchange(jnp.split(d_context_mine, tp_size, 1)), 0)
+    d_context = rows_turn(d_context)
 
     packed = (
         pack(
@@ -537,27 +529,21 @@
     d_kv_low, inner_sum.moved, outer_sum.moved, early_sum.moved, *both_moved = tie(
         d_kv.astype(BF16), inner_sum.moved, outer_sum.moved, early_sum.moved, *both_moved
     )
-    tokens_part = rows_sum(
-        dot32(rows_turn(d_query_low), full_qkv[:width_local], ((1,), (0,)))
-        + dot32(columns_turn(d_kv_low), full_qkv[width_local:], ((0,), (0,))),
-    )
+    d_qkv_low = jnp.concatenate([d_query_low, d_kv_low.T], 1)
+    tokens_part = rows_sum(dot32(rows_turn(d_qkv_low), full_qkv, ((1,), (0,))))
     inner_sum.step()
     outer_sum.step()
     early_sum.step()
-    query_gradient = dot32(d_query_low, tokens_first, ((0,), (0,)))
-    kv_gradient = dot32(d_kv_low, tokens_first, ((1,), (0,)))
-    qkv_gradient = jnp.concatenate([query_gradient, kv_gradient], 0)
+    qkv_gradient = dot32(d_qkv_low, tokens_first, ((0,), (0,)))
     qkv_sum = WeightSum(qkv_gradient, 1, True)
     both = [both_mine] + both_moved
-    output_gradient = sum(
-        dot32(rows, moved[:, :model_width], ((0,), (0,)))
-        for rows, moved in zip(jnp.split(context_turned, tp_size, 0), both)
-    )
+    d_first_all = jnp.concatenate([block[:, :model_width] for block in both], 0)
+    output_gradient = dot32(context_turned, d_first_all, ((0,), (0,)))
     output_sum = WeightSum(output_gradient, 1, True)
     late_vector = jnp.concatenate([jnp.sum(d_query, 0), jnp.sum(d_kv[width_local:], 1)])
     late_sum = VectorSum(late_vector, ("dp", "ctx"), True)
     grad_mine = (d_first + own_first(tokens_part)).astype(BF16)
-    sums = (early_sum, late_sum)
+    sums = (early_sum,)
     grad_mine, *moved = tie(grad_mine, *[one.moved for one in sums])
     for one, value in zip(sums, moved):
         one.moved = value
@@ -572,6 +558,8 @@
     qkv_sum.step()
     output_sum.step()
     late_sum.step()
+    output_sum.step()
+    qkv_sum.step()
     grad_moved = rows_moved(grad_mine)
     inner_shard, outer_shard = inner_sum.total(), outer_sum.total()
     result_all = rows_place([block[:, model_width:] for block in both]).astype(F32)

time: 287 us -> 292 us (1.017)
  starting transfers between devices: 88.3 us -> 78.5 us
  waiting for transfers between devices: 99.7 us -> 108 us
  local copies, waits for them, and re-layouts: 16.5 us -> 21.4 us
  other arithmetic: 31.9 us -> 36.4 us
    ppermute x30, starting transfers between devices: 32.4 us -> 25.4 us  [flipped(): return lax.ppermute(block, axis, [(i, i ^ bit) for i in range(size)])]
    ppermute x30, waiting for transfers between devices: 56.5 us -> 62.7 us  [shifted(): lax.ppermute(block, axis, [(i, (i + step) % size) for i in range(size)])]
    convert_element_type x8, other arithmetic: 6 us -> 9.17 us  [step(): low = (self.kept.astype(F32) + self.moved.astype(F32)).astype(BF16)]
    dot_general x18 -> x13, matrix products: 17.2 us -> 14.4 us  [dot32(): lax.dot_general(left, right, (dims, ((), ())), preferred_element_type=F32)]
  transfers between devices with their start and end apart: 60 -> 60, of which waited for: 22 -> 26; matrix products, arithmetic and copies ran while one was open for 18% -> 20% of each run, Pallas kernels for 10% -> 10%
where the time goes in v5:
time: 292 us; the launch traced here: 291 us
  waiting for transfers between devices  108 us (37%)
  starting transfers between devices  78.5 us (27%)
  other arithmetic  36.4 us (12%)
  Pallas kernels  28 us (10%)
  local copies, waits for them, and re-layouts  21.4 us (7%)
  matrix products  14.4 us (5%)
  between operations  4.94 us (2%)
    ppermute x30, waiting for transfers between devices, shifted(): lax.ppermute(block, axis, [(i, (i + step) % size) for i in range(size)])  62.7 us
    ppermute x30, starting transfers between devices, shifted(): lax.ppermute(block, axis, [(i, (i + step) % size) for i in range(size)])  53.1 us
    ppermute x30, waiting for transfers between devices, flipped(): return lax.ppermute(block, axis, [(i, i ^ bit) for i in range(size)])  45 us
    ppermute x30, starting transfers between devices, flipped(): return lax.ppermute(block, axis, [(i, i ^ bit) for i in range(size)])  25.4 us
    dot_general x13, matrix products, dot32(): lax.dot_general(left, right, (dims, ((), ())), preferred_element_type=F32)  14.4 us
    pallas_call x1, Pallas kernels, attend_back(): pl.pallas_call(partial(attend_back_kernel, heads, scale, len(kv)), grid_s...  13.3 us
    pallas_call x1, Pallas kernels, attend(): pl.pallas_call(partial(attend_kernel, heads, len(kv)), grid_spec=pltpu.Pr...  12.6 us
    convert_element_type x8, other arithmetic, step(): low = (self.kept.astype(F32) + self.moved.astype(F32)).astype(BF16)  9.17 us
  transfers between devices with their start and end apart: 60, of which 26 were waited for; matrix products, arithmetic and copies ran while one was open for 20% of the time, Pallas kernels for 10%

profile of v5, /device:TPU:0, one launch (start us, length us, event | category | flops | bytes accessed | tf_op | source)
XLA Modules:
  0.0 291.3 jit_solution(6537135933508962774)
XLA Ops:
  0.7 5.1 %collective-permute-start.4 = (bf16[192,384]{1,0:T(8,128)(2,1)}, bf16[192,384]{1,0:T(8,128)(2,1)S(1)}, u32[]{:S(2)}, u32[]{:S(2)}) collective-permute-start(bf16[192,384]{1,0:T(8,128)(2,1)} %param.27), channel_id=1, source_target_pairs={{0,3},{1,0},{2,1},{3,2},{4,7},{5,4},{6,5},{7,6},{8,11},{9,8},{10,9... | collective-permute-start | bytes 442376 | tf_op jit(solution)/shard_map/ppermute | solution.py:44
  7.9 1.6 collective-permute-start.1
  9.5 1.2 fusion.91
  11.0 7.5 %collective-permute-done.3 = bf16[192,384]{1,0:T(8,128)(2,1)S(1)} collective-permute-done((bf16[192,384]{1,0:T(8,128)(2,1)}, bf16[192,384]{1,0:T(8,128)(2,1)S(1)}, u32[]{:S(2)}, u32[]{:S(2)}) %collective-permute-start.3) | collective-permute-done | bytes 147488 | tf_op jit(solution)/shard_map/ppermute | solution.py:44
  20.1 1.6 collective-permute-start.5
  22.8 7.8 %collective-permute-done.5.refs_1_ = bf16[1,512,384]{2,1,0:T(8,128)(2,1)S(1)} collective-permute-done((bf16[1,512,384]{2,1,0:T(8,128)(2,1)S(1)}, bf16[1,512,384]{2,1,0:T(8,128)(2,1)S(1)}, u32[]{:S(2)}, u32[]{:S(2)}) %collective-permute-start.5) | collective-permute-done | bytes 393248 | tf_op jit(solution)/shard_map/ppermute | solution.py:49
  32.3 2.9 collective-permute-start
  38.0 12.6 %attend.1 = (bf16[1,3,512,2048]{3,2,1,0:T(8,128)(2,1)}, bf16[3,512,2048]{2,1,0:T(8,128)(2,1)}, bf16[512,192]{1,0:T(8,128)(2,1)}, f32[512,192]{1,0:T(8,128)}) custom-call(s32[2]{0:T(128)} %multiply_minimum_fusion.limits, s32[4]{0:T(128)} %xor_multiply_fusion.starts, bf16[512,192]{1,0:T(8,128)(2,1)} %fusion.10.query, bf16[1,3,512,2048]{3,2,1,0:T(8,128)(2,1)} %prior.1, ...), custom_call_target="tpu_custom_call" | custom-call | flops 805306368 | bytes 18874368 | tf_op jit(solution)/shard_map/attend/pallas_call | solution.py:256
  51.8 1.2 constant_dynamic-update-slice_fusion.3
  53.0 1.6 collective-permute-start.14
  54.5 1.8 collective-permute-start.10
  57.3 1.9 collective-permute-start.8
  61.1 2.5 collective-permute-done.9
  65.0 1.5 collective-permute-start.13
  66.5 2.7 collective-permute-done.14
  70.1 10.2 %collective-permute-done.15 = bf16[768,384]{1,0:T(8,128)(2,1)S(1)} collective-permute-done((bf16[768,384]{1,0:T(8,128)(2,1)S(1)}, bf16[768,384]{1,0:T(8,128)(2,1)S(1)}, u32[]{:S(2)}, u32[]{:S(2)}) %collective-permute-start.15) | collective-permute-done | bytes 589856 | tf_op jit(solution)/shard_map/ppermute | solution.py:49
  80.4 3.1 %collective-permute-done.12 = bf16[128,768]{1,0:T(8,128)(2,1)S(1)} collective-permute-done((bf16[128,768]{1,0:T(8,128)(2,1)S(1)}, bf16[128,768]{1,0:T(8,128)(2,1)S(1)}, u32[]{:S(2)}, u32[]{:S(2)}) %collective-permute-start.12) | collective-permute-done | bytes 196640 | tf_op jit(solution)/shard_map/ppermute | solution.py:44
  83.5 5.6 %multiply_convert_fusion = (bf16[512,768]{1,0:T(8,128)(2,1)S(1)}, f32[512,768]{1,0:T(8,128)}, f32[512,768]{1,0:T(8,128)}) fusion(f32[768]{0:T(1024)S(1)} %copy-done.54, bf16[768,768]{1,0:T(8,128)(2,1)S(1)} %constant_dynamic-update-slice_fusion.2, bf16[128,768]{1,0:T(8,128)(2,1)S(1)} %collective-permute-done.13, ...), kind=kOutput, calls=%fused_computation.4 | convolution fusion | flops 633077760 | bytes 5901312 | tf_op jit(solution)/shard_map/dot_general | solution.py:39
  90.8 1.7 collective-permute-start.17
  92.5 2.9 %collective-permute-start.16 = (bf16[128,768]{1,0:T(8,128)(2,1)S(1)}, bf16[128,768]{1,0:T(8,128)(2,1)}, u32[]{:S(2)}, u32[]{:S(2)}) collective-permute-start(bf16[128,768]{1,0:T(8,128)(2,1)S(1)} %get-tuple-element.136), channel_id=1, source_target_pairs={{0,3},{1,0},{2,1},{3,2},{4,7},{5,4},{6,5},{7,6},{8,11},{9,8},{10,9... | collective-permute-start | bytes 589832 | tf_op jit(solution)/shard_map/ppermute | solution.py:44
  95.4 1.3 compare_convert_fusion
  98.1 2.6 collective-permute-done.18
  100.7 6.3 %collective-permute-done.17 = bf16[128,768]{1,0:T(8,128)(2,1)} collective-permute-done((bf16[128,768]{1,0:T(8,128)(2,1)S(1)}, bf16[128,768]{1,0:T(8,128)(2,1)}, u32[]{:S(2)}, u32[]{:S(2)}) %collective-permute-start.17) | collective-permute-done | bytes 196640 | tf_op jit(solution)/shard_map/ppermute | solution.py:44
  107.0 1.2 fusion.37
  110.9 6.3 %collective-permute-start.21 = (bf16[128,768]{1,0:T(8,128)(2,1)S(1)}, bf16[128,768]{1,0:T(8,128)(2,1)S(1)}, u32[]{:S(2)}, u32[]{:S(2)}) collective-permute-start(bf16[128,768]{1,0:T(8,128)(2,1)S(1)} %maximum_select_fusion.6), channel_id=1, source_target_pairs={{0,3},{1,0},{2,1},{3,2},{4,7},{5,4},{6,5},{7,6},{8,11},{9,8},{10,9... | collective-permute-start | bytes 589832 | tf_op jit(solution)/shard_map/ppermute | solution.py:44
  117.8 4.7 %collective-permute-done.21 = bf16[128,768]{1,0:T(8,128)(2,1)S(1)} collective-permute-done((bf16[128,768]{1,0:T(8,128)(2,1)S(1)}, bf16[128,768]{1,0:T(8,128)(2,1)S(1)}, u32[]{:S(2)}, u32[]{:S(2)}) %collective-permute-start.21) | collective-permute-done | bytes 196640 | tf_op jit(solution)/shard_map/ppermute | solution.py:44
  122.5 11.4 %collective-permute-done.20 = bf16[128,768]{1,0:T(8,128)(2,1)S(1)} collective-permute-done((bf16[128,768]{1,0:T(8,128)(2,1)S(1)}, bf16[128,768]{1,0:T(8,128)(2,1)S(1)}, u32[]{:S(2)}, u32[]{:S(2)}) %collective-permute-start.20) | collective-permute-done | bytes 196640 | tf_op jit(solution)/shard_map/ppermute | solution.py:44
  134.0 1.2 fusion.104
  136.2 2.0 collective-permute-start.23
  138.2 2.9 collective-permute-start.22
  144.4 1.5 collective-permute-start.29
  145.9 6.2 %collective-permute-done.23 = bf16[128,768]{1,0:T(8,128)(2,1)S(1)} collective-permute-done((bf16[128,768]{1,0:T(8,128)(2,1)S(1)}, bf16[128,768]{1,0:T(8,128)(2,1)S(1)}, u32[]{:S(2)}, u32[]{:S(2)}) %collective-permute-start.23) | collective-permute-done | bytes 196640 | tf_op jit(solution)/shard_map/ppermute | solution.py:44
  153.5 5.6 %collective-permute-start.27 = (bf16[128,192]{1,0:T(8,128)(2,1)S(1)}, bf16[128,192]{1,0:T(8,128)(2,1)S(1)}, u32[]{:S(2)}, u32[]{:S(2)}) collective-permute-start(bf16[128,192]{1,0:T(8,128)(2,1)S(1)} %get-tuple-element.171), channel_id=1, source_target_pairs={{0,3},{1,0},{2,1},{3,2},{4,7},{5,4},{6,5},{7,6},{8,11},{9,8},{10,9... | collective-permute-start | bytes 147464 | tf_op jit(solution)/shard_map/ppermute | solution.py:44
  163.8 2.1 pack.1
  167.3 2.7 collective-permute-done.29
  170.0 13.3 %attend_back.1 = (bf16[1,3,512,2048]{3,2,1,0:T(8,128)(2,1)}, f32[512,192]{1,0:T(8,128)}, bf16[2,384,512]{2,1,0:T(8,128)(2,1)}, bf16[2,384,512]{2,1,0:T(8,128)(2,1)}) custom-call(s32[4]{0:T(128)} %xor_multiply_fusion.starts, bf16[3,512,2048]{2,1,0:T(8,128)(2,1)} %get-tuple-element.64.weights, bf16[512,192]{1,0:T(8,128)(2,1)} %get-tuple-element.58.context, ...), custom_call_target="tpu_custom_call" | custom-call | flops 2013265920 | bytes 18874368 | tf_op jit(solution)/shard_map/attend_back/pallas_call | solution.py:339
  183.4 1.6 fusion.12
  186.2 1.6 collective-permute-start.32
  187.8 2.0 fusion.11
  189.8 1.3 collective-permute-start.34
  193.0 5.4 %collective-permute-done.32 = bf16[1,384,512]{2,1,0:T(8,128)(2,1)} collective-permute-done((bf16[1,384,512]{2,1,0:T(8,128)(2,1)S(1)}, bf16[1,384,512]{2,1,0:T(8,128)(2,1)}, u32[]{:S(2)}, u32[]{:S(2)}) %collective-permute-start.32) | collective-permute-done | bytes 393248 | tf_op jit(solution)/shard_map/ppermute | solution.py:49
  201.2 2.1 convert_bitcast_fusion
  203.3 2.0 collective-permute-done.36
  205.2 16.5 %collective-permute-done.37 = bf16[128,1536]{1,0:T(8,128)(2,1)} collective-permute-done((bf16[128,1536]{1,0:T(8,128)(2,1)S(1)}, bf16[128,1536]{1,0:T(8,128)(2,1)}, u32[]{:S(2)}, u32[]{:S(2)}) %collective-permute-start.37) | collective-permute-done | bytes 393248 | tf_op jit(solution)/shard_map/ppermute | solution.py:44
  223.2 1.6 reshape.205
  224.8 1.2 constant_dynamic-slice_fusion.4
  227.2 8.8 %collective-permute-start.41 = (bf16[128,768]{1,0:T(8,128)(2,1)S(1)}, bf16[128,768]{1,0:T(8,128)(2,1)S(1)}, u32[]{:S(2)}, u32[]{:S(2)}) collective-permute-start(bf16[128,768]{1,0:T(8,128)(2,1)S(1)} %get-tuple-element.131), channel_id=1, source_target_pairs={{0,1},{1,2},{2,3},{3,0},{4,5},{5,6},{6,7},{7,4},{8,9},{9,10},{10,1... | collective-permute-start | bytes 589832 | tf_op jit(solution)/shard_map/ppermute | solution.py:44
  236.0 2.4 collective-permute-start.39
  239.3 2.0 add_convert_fusion.1
  241.3 1.4 add_convert_fusion
  242.9 1.3 collective-permute-start.57
  244.2 1.3 select_select_fusion.1
  248.4 1.3 maximum_convert_fusion
  251.4 1.2 collective-permute-start.44
  254.7 2.2 collective-permute-start.48
  256.9 2.6 collective-permute-done.54
  259.6 1.5 collective-permute-done.47
  261.0 1.4 collective-permute-start.51
  263.6 1.9 collective-permute-start.43
  267.4 1.7 collective-permute-done.55
  274.7 2.2 collective-permute-start.49
  276.8 2.4 convert_add_fusion.2
  279.2 6.3 %collective-permute-done.52 = bf16[576,384]{1,0:T(8,128)(2,1)S(1)} collective-permute-done((bf16[576,384]{1,0:T(8,128)(2,1)S(1)}, bf16[576,384]{1,0:T(8,128)(2,1)S(1)}, u32[]{:S(2)}, u32[]{:S(2)}) %collective-permute-start.52) | collective-permute-done | bytes 442400 | tf_op jit(solution)/shard_map/ppermute | solution.py:49
  287.8 1.3 maximum_convert_fusion.1
  (305 shorter events, 59.9 us)
Async XLA Ops:
  0.7 10.3 %collective-permute-start.4 = (bf16[192,384]{1,0:T(8,128)(2,1)}, bf16[192,384]{1,0:T(8,128)(2,1)S(1)}, u32[]{:S(2)}, u32[]{:S(2)}) collective-permute-start(bf16[192,384]{1,0:T(8,128)(2,1)} %param.27), channel_id=1, source_target_pairs={{0,3},{1,0},{2,1},{3,2},{4,7},{5,4},{6,5},{7,6},{8,11},{9,8},{10,9... | collective-permute-start | bytes 442376 | tf_op jit(solution)/shard_map/ppermute | solution.py:44
  5.8 12.7 %collective-permute-start.3 = (bf16[192,384]{1,0:T(8,128)(2,1)}, bf16[192,384]{1,0:T(8,128)(2,1)S(1)}, u32[]{:S(2)}, u32[]{:S(2)}) collective-permute-start(bf16[192,384]{1,0:T(8,128)(2,1)} %param.27), channel_id=1, source_target_pairs={{0,2},{1,3},{2,0},{3,1},{4,6},{5,7},{6,4},{7,5},{8,10},{9,11},{10,... | collective-permute-start | bytes 442376 | tf_op jit(solution)/shard_map/ppermute | solution.py:44
  5.8 12.7 %collective-permute-start.2 = (bf16[192,384]{1,0:T(8,128)(2,1)}, bf16[192,384]{1,0:T(8,128)(2,1)S(1)}, u32[]{:S(2)}, u32[]{:S(2)}) collective-permute-start(bf16[192,384]{1,0:T(8,128)(2,1)} %param.27), channel_id=1, source_target_pairs={{0,1},{1,2},{2,3},{3,0},{4,5},{5,6},{6,7},{7,4},{8,9},{9,10},{10,1... | collective-permute-start | bytes 442376 | tf_op jit(solution)/shard_map/ppermute | solution.py:44
  7.9 11.5 %collective-permute-start.1 = (bf16[576,384]{1,0:T(8,128)(2,1)S(1)}, bf16[576,384]{1,0:T(8,128)(2,1)S(1)}, u32[]{:S(2)}, u32[]{:S(2)}) collective-permute-start(bf16[576,384]{1,0:T(8,128)(2,1)S(1)} %pad_maximum_fusion.6), channel_id=1, source_target_pairs={{0,16},{16,0},{1,17},{17,1},{2,18},{18,2},{3,19},{19,3},{4,20},{20... | collective-permute-start | bytes 1327112 | tf_op jit(solution)/shard_map/ppermute | solution.py:49
  20.1 10.5 %collective-permute-start.5 = (bf16[1,512,384]{2,1,0:T(8,128)(2,1)S(1)}, bf16[1,512,384]{2,1,0:T(8,128)(2,1)S(1)}, u32[]{:S(2)}, u32[]{:S(2)}) collective-permute-start(bf16[1,512,384]{2,1,0:T(8,128)(2,1)S(1)} %bitcast.100), channel_id=1, source_target_pairs={{0,8},{4,12},{8,0},{12,4},{1,9},{5,13},{9,1},{13,5},{2,10},{6,14},... | collective-permute-start | bytes 1179656 | tf_op jit(solution)/shard_map/ppermute | solution.py:49
  31.7 6.4 %collective-permute-start.6 = (bf16[2,512,384]{2,1,0:T(8,128)(2,1)}, bf16[2,512,384]{2,1,0:T(8,128)(2,1)}, u32[]{:S(2)}, u32[]{:S(2)}) collective-permute-start(bf16[2,512,384]{2,1,0:T(8,128)(2,1)} %pad_maximum_fusion.1), channel_id=1, source_target_pairs={{0,4},{4,0},{8,12},{12,8},{1,5},{5,1},{9,13},{13,9},{2,6},{6,2},{1... | collective-permute-start | bytes 2359304 | tf_op jit(solution)/shard_map/ppermute | solution.py:49
  32.3 64.4 %collective-permute-start = (f32[]{:T(128)}, f32[]{:T(128)}, u32[]{:S(2)}, u32[]{:S(2)}) collective-permute-start(f32[]{:T(128)} %convert_element_type.210), channel_id=1, source_target_pairs={{0,16},{16,0},{1,17},{17,1},{2,18},{18,2},{3,19},{19,3},{4,20},{20... | collective-permute-start | bytes 20 | tf_op jit(solution)/shard_map/ppermute | solution.py:49
  35.8 15.9 %collective-permute-start.7 = (bf16[768,384]{1,0:T(8,128)(2,1)}, bf16[768,384]{1,0:T(8,128)(2,1)}, u32[]{:S(2)}, u32[]{:S(2)}) collective-permute-start(bf16[768,384]{1,0:T(8,128)(2,1)} %pad_maximum_fusion.4), channel_id=1, source_target_pairs={{0,16},{16,0},{1,17},{17,1},{2,18},{18,2},{3,19},{19,3},{4,20},{20... | collective-permute-start | bytes 1769480 | tf_op jit(solution)/shard_map/ppermute | solution.py:49
  53.0 16.3 %collective-permute-start.14 = (bf16[384,768]{1,0:T(8,128)(2,1)S(1)}, bf16[384,768]{1,0:T(8,128)(2,1)S(1)}, u32[]{:S(2)}, u32[]{:S(2)}) collective-permute-start(bf16[384,768]{1,0:T(8,128)(2,1)S(1)} %copy-done.26), channel_id=1, source_target_pairs={{0,16},{16,0},{1,17},{17,1},{2,18},{18,2},{3,19},{19,3},{4,20},{20... | collective-permute-start | bytes 1769480 | tf_op jit(solution)/shard_map/ppermute | solution.py:49
  54.5 6.0 %collective-permute-start.10 = (bf16[128,192]{1,0:T(8,128)(2,1)S(1)}, bf16[128,192]{1,0:T(8,128)(2,1)S(1)}, u32[]{:S(2)}, u32[]{:S(2)}) collective-permute-start(bf16[128,192]{1,0:T(8,128)(2,1)S(1)} %get-tuple-element.163), channel_id=1, source_target_pairs={{0,3},{1,0},{2,1},{3,2},{4,7},{5,4},{6,5},{7,6},{8,11},{9,8},{10,9... | collective-permute-start | bytes 147464 | tf_op jit(solution)/shard_map/ppermute | solution.py:44
  56.3 7.3 %collective-permute-start.9 = (bf16[128,192]{1,0:T(8,128)(2,1)S(1)}, bf16[128,192]{1,0:T(8,128)(2,1)S(1)}, u32[]{:S(2)}, u32[]{:S(2)}) collective-permute-start(bf16[128,192]{1,0:T(8,128)(2,1)S(1)} %get-tuple-element.164), channel_id=1, source_target_pairs={{0,2},{1,3},{2,0},{3,1},{4,6},{5,7},{6,4},{7,5},{8,10},{9,11},{10,... | collective-permute-start | bytes 147464 | tf_op jit(solution)/shard_map/ppermute | solution.py:44
  57.3 6.3 %collective-permute-start.8 = (bf16[128,192]{1,0:T(8,128)(2,1)S(1)}, bf16[128,192]{1,0:T(8,128)(2,1)S(1)}, u32[]{:S(2)}, u32[]{:S(2)}) collective-permute-start(bf16[128,192]{1,0:T(8,128)(2,1)S(1)} %get-tuple-element.165), channel_id=1, source_target_pairs={{0,1},{1,2},{2,3},{3,0},{4,5},{5,6},{6,7},{7,4},{8,9},{9,10},{10,1... | collective-permute-start | bytes 147464 | tf_op jit(solution)/shard_map/ppermute | solution.py:44
  60.5 19.8 %collective-permute-start.15 = (bf16[768,384]{1,0:T(8,128)(2,1)S(1)}, bf16[768,384]{1,0:T(8,128)(2,1)S(1)}, u32[]{:S(2)}, u32[]{:S(2)}) collective-permute-start(bf16[768,384]{1,0:T(8,128)(2,1)S(1)} %copy-done.27), channel_id=1, source_target_pairs={{0,16},{16,0},{1,17},{17,1},{2,18},{18,2},{3,19},{19,3},{4,20},{20... | collective-permute-start | bytes 1769480 | tf_op jit(solution)/shard_map/ppermute | solution.py:49
  65.0 24.1 %copy-start.31 = (bf16[128,768]{1,0:T(8,128)(2,1)}, bf16[128,768]{1,0:T(8,128)(2,1)S(1)}, u32[]{:S(2)}) copy-start(bf16[128,768]{1,0:T(8,128)(2,1)S(1)} %maximum_select_fusion.5) | copy-start | bytes 589828
  65.0 15.4 %collective-permute-start.13 = (bf16[128,768]{1,0:T(8,128)(2,1)S(1)}, bf16[128,768]{1,0:T(8,128)(2,1)S(1)}, u32[]{:S(2)}, u32[]{:S(2)}) collective-permute-start(bf16[128,768]{1,0:T(8,128)(2,1)S(1)} %maximum_select_fusion.5), channel_id=1, source_target_pairs={{0,3},{1,0},{2,1},{3,2},{4,7},{5,4},{6,5},{7,6},{8,11},{9,8},{10,9... | collective-permute-start | bytes 589832 | tf_op jit(solution)/shard_map/ppermute | solution.py:44
  66.5 17.0 %collective-permute-start.12 = (bf16[128,768]{1,0:T(8,128)(2,1)S(1)}, bf16[128,768]{1,0:T(8,128)(2,1)S(1)}, u32[]{:S(2)}, u32[]{:S(2)}) collective-permute-start(bf16[128,768]{1,0:T(8,128)(2,1)S(1)} %maximum_select_fusion.5), channel_id=1, source_target_pairs={{0,2},{1,3},{2,0},{3,1},{4,6},{5,7},{6,4},{7,5},{8,10},{9,11},{10,... | collective-permute-start | bytes 589832 | tf_op jit(solution)/shard_map/ppermute | solution.py:44
  69.2 14.3 %collective-permute-start.11 = (bf16[128,768]{1,0:T(8,128)(2,1)S(1)}, bf16[128,768]{1,0:T(8,128)(2,1)S(1)}, u32[]{:S(2)}, u32[]{:S(2)}) collective-permute-start(bf16[128,768]{1,0:T(8,128)(2,1)S(1)} %maximum_select_fusion.5), channel_id=1, source_target_pairs={{0,1},{1,2},{2,3},{3,0},{4,5},{5,6},{6,7},{7,4},{8,9},{9,10},{10,1... | collective-permute-start | bytes 589832 | tf_op jit(solution)/shard_map/ppermute | solution.py:44
  90.8 9.9 %collective-permute-start.18 = (bf16[128,768]{1,0:T(8,128)(2,1)}, bf16[128,768]{1,0:T(8,128)(2,1)}, u32[]{:S(2)}, u32[]{:S(2)}) collective-permute-start(bf16[128,768]{1,0:T(8,128)(2,1)} %get-tuple-element.137), channel_id=1, source_target_pairs={{0,1},{1,2},{2,3},{3,0},{4,5},{5,6},{6,7},{7,4},{8,9},{9,10},{10,1... | collective-permute-start | bytes 589832 | tf_op jit(solution)/shard_map/ppermute | solution.py:44
  90.8 16.2 %collective-permute-start.17 = (bf16[128,768]{1,0:T(8,128)(2,1)S(1)}, bf16[128,768]{1,0:T(8,128)(2,1)}, u32[]{:S(2)}, u32[]{:S(2)}) collective-permute-start(bf16[128,768]{1,0:T(8,128)(2,1)S(1)} %get-tuple-element.138), channel_id=1, source_target_pairs={{0,2},{1,3},{2,0},{3,1},{4,6},{5,7},{6,4},{7,5},{8,10},{9,11},{10,... | collective-permute-start | bytes 589832 | tf_op jit(solution)/shard_map/ppermute | solution.py:44
  92.5 14.5 %collective-permute-start.16 = (bf16[128,768]{1,0:T(8,128)(2,1)S(1)}, bf16[128,768]{1,0:T(8,128)(2,1)}, u32[]{:S(2)}, u32[]{:S(2)}) collective-permute-start(bf16[128,768]{1,0:T(8,128)(2,1)S(1)} %get-tuple-element.136), channel_id=1, source_target_pairs={{0,3},{1,0},{2,1},{3,2},{4,7},{5,4},{6,5},{7,6},{8,11},{9,8},{10,9... | collective-permute-start | bytes 589832 | tf_op jit(solution)/shard_map/ppermute | solution.py:44
  108.2 25.7 %copy-start.58 = (f32[512,768]{1,0:T(8,128)S(1)}, f32[512,768]{1,0:T(8,128)}, u32[]{:S(2)}) copy-start(f32[512,768]{1,0:T(8,128)} %get-tuple-element.182) | copy-start | bytes 4718596
  110.5 23.4 %copy-start.8 = (bf16[768,768]{1,0:T(8,128)(2,1)S(1)}, bf16[768,768]{1,0:T(8,128)(2,1)}, u32[]{:S(2)}) copy-start(bf16[768,768]{1,0:T(8,128)(2,1)} %copy-done.7) | copy-start | bytes 3538948
  110.5 23.4 %copy-start.57 = (f32[512,768]{1,0:T(8,128)S(1)}, f32[512,768]{1,0:T(8,128)}, u32[]{:S(2)}) copy-start(f32[512,768]{1,0:T(8,128)} %get-tuple-element.116) | copy-start | bytes 4718596
  110.9 11.6 %collective-permute-start.21 = (bf16[128,768]{1,0:T(8,128)(2,1)S(1)}, bf16[128,768]{1,0:T(8,128)(2,1)S(1)}, u32[]{:S(2)}, u32[]{:S(2)}) collective-permute-start(bf16[128,768]{1,0:T(8,128)(2,1)S(1)} %maximum_select_fusion.6), channel_id=1, source_target_pairs={{0,3},{1,0},{2,1},{3,2},{4,7},{5,4},{6,5},{7,6},{8,11},{9,8},{10,9... | collective-permute-start | bytes 589832 | tf_op jit(solution)/shard_map/ppermute | solution.py:44
  117.2 16.7 %collective-permute-start.20 = (bf16[128,768]{1,0:T(8,128)(2,1)S(1)}, bf16[128,768]{1,0:T(8,128)(2,1)S(1)}, u32[]{:S(2)}, u32[]{:S(2)}) collective-permute-start(bf16[128,768]{1,0:T(8,128)(2,1)S(1)} %maximum_select_fusion.6), channel_id=1, source_target_pairs={{0,2},{1,3},{2,0},{3,1},{4,6},{5,7},{6,4},{7,5},{8,10},{9,11},{10,... | collective-permute-start | bytes 589832 | tf_op jit(solution)/shard_map/ppermute | solution.py:44
  117.2 16.7 %collective-permute-start.19 = (bf16[128,768]{1,0:T(8,128)(2,1)S(1)}, bf16[128,768]{1,0:T(8,128)(2,1)S(1)}, u32[]{:S(2)}, u32[]{:S(2)}) collective-permute-start(bf16[128,768]{1,0:T(8,128)(2,1)S(1)} %maximum_select_fusion.6), channel_id=1, source_target_pairs={{0,1},{1,2},{2,3},{3,0},{4,5},{5,6},{6,7},{7,4},{8,9},{9,10},{10,1... | collective-permute-start | bytes 589832 | tf_op jit(solution)/shard_map/ppermute | solution.py:44
  136.1 9.8 %collective-permute-start.24 = (bf16[128,768]{1,0:T(8,128)(2,1)S(1)}, bf16[128,768]{1,0:T(8,128)(2,1)S(1)}, u32[]{:S(2)}, u32[]{:S(2)}) collective-permute-start(bf16[128,768]{1,0:T(8,128)(2,1)S(1)} %get-tuple-element.134), channel_id=1, source_target_pairs={{0,1},{1,2},{2,3},{3,0},{4,5},{5,6},{6,7},{7,4},{8,9},{9,10},{10,1... | collective-permute-start | bytes 589832 | tf_op jit(solution)/shard_map/ppermute | solution.py:44
  136.2 16.0 %collective-permute-start.23 = (bf16[128,768]{1,0:T(8,128)(2,1)S(1)}, bf16[128,768]{1,0:T(8,128)(2,1)S(1)}, u32[]{:S(2)}, u32[]{:S(2)}) collective-permute-start(bf16[128,768]{1,0:T(8,128)(2,1)S(1)} %get-tuple-element.135), channel_id=1, source_target_pairs={{0,2},{1,3},{2,0},{3,1},{4,6},{5,7},{6,4},{7,5},{8,10},{9,11},{10,... | collective-permute-start | bytes 589832 | tf_op jit(solution)/shard_map/ppermute | solution.py:44
  138.2 14.0 %collective-permute-start.22 = (bf16[128,768]{1,0:T(8,128)(2,1)S(1)}, bf16[128,768]{1,0:T(8,128)(2,1)S(1)}, u32[]{:S(2)}, u32[]{:S(2)}) collective-permute-start(bf16[128,768]{1,0:T(8,128)(2,1)S(1)} %get-tuple-element.133), channel_id=1, source_target_pairs={{0,3},{1,0},{2,1},{3,2},{4,7},{5,4},{6,5},{7,6},{8,11},{9,8},{10,9... | collective-permute-start | bytes 589832 | tf_op jit(solution)/shard_map/ppermute | solution.py:44
  142.9 24.4 %collective-permute-start.28 = (bf16[768,384]{1,0:T(8,128)(2,1)}, bf16[768,384]{1,0:T(8,128)(2,1)}, u32[]{:S(2)}, u32[]{:S(2)}) collective-permute-start(bf16[768,384]{1,0:T(8,128)(2,1)} %split.97), channel_id=1, source_target_pairs={{0,16},{16,0},{1,17},{17,1},{2,18},{18,2},{3,19},{19,3},{4,20},{20... | collective-permute-start | bytes 1769480 | tf_op jit(solution)/shard_map/ppermute | solution.py:49
  144.4 25.6 %collective-permute-start.29 = (bf16[384,768]{1,0:T(8,128)(2,1)S(1)}, bf16[384,768]{1,0:T(8,128)(2,1)}, u32[]{:S(2)}, u32[]{:S(2)}) collective-permute-start(bf16[384,768]{1,0:T(8,128)(2,1)S(1)} %split.96), channel_id=1, source_target_pairs={{0,16},{16,0},{1,17},{17,1},{2,18},{18,2},{3,19},{19,3},{4,20},{20... | collective-permute-start | bytes 1769480 | tf_op jit(solution)/shard_map/ppermute | solution.py:49
  153.5 12.4 %collective-permute-start.27 = (bf16[128,192]{1,0:T(8,128)(2,1)S(1)}, bf16[128,192]{1,0:T(8,128)(2,1)S(1)}, u32[]{:S(2)}, u32[]{:S(2)}) collective-permute-start(bf16[128,192]{1,0:T(8,128)(2,1)S(1)} %get-tuple-element.171), channel_id=1, source_target_pairs={{0,3},{1,0},{2,1},{3,2},{4,7},{5,4},{6,5},{7,6},{8,11},{9,8},{10,9... | collective-permute-start | bytes 147464 | tf_op jit(solution)/shard_map/ppermute | solution.py:44
  159.1 7.4 %collective-permute-start.26 = (bf16[128,192]{1,0:T(8,128)(2,1)S(1)}, bf16[128,192]{1,0:T(8,128)(2,1)S(1)}, u32[]{:S(2)}, u32[]{:S(2)}) collective-permute-start(bf16[128,192]{1,0:T(8,128)(2,1)S(1)} %get-tuple-element.172), channel_id=1, source_target_pairs={{0,2},{1,3},{2,0},{3,1},{4,6},{5,7},{6,4},{7,5},{8,10},{9,11},{10,... | collective-permute-start | bytes 147464 | tf_op jit(solution)/shard_map/ppermute | solution.py:44
  159.1 7.4 %collective-permute-start.25 = (bf16[128,192]{1,0:T(8,128)(2,1)S(1)}, bf16[128,192]{1,0:T(8,128)(2,1)S(1)}, u32[]{:S(2)}, u32[]{:S(2)}) collective-permute-start(bf16[128,192]{1,0:T(8,128)(2,1)S(1)} %get-tuple-element.173), channel_id=1, source_target_pairs={{0,1},{1,2},{2,3},{3,0},{4,5},{5,6},{6,7},{7,4},{8,9},{9,10},{10,1... | collective-permute-start | bytes 147464 | tf_op jit(solution)/shard_map/ppermute | solution.py:44
  165.9 17.4 %collective-permute-start.30 = (f32[12,768]{1,0:T(8,128)}, f32[12,768]{1,0:T(8,128)S(1)}, u32[]{:S(2)}, u32[]{:S(2)}) collective-permute-start(f32[12,768]{1,0:T(8,128)} %pack.1), channel_id=1, source_target_pairs={{0,16},{16,0},{1,17},{17,1},{2,18},{18,2},{3,19},{19,3},{4,20},{20... | collective-permute-start | bytes 110600 | tf_op jit(solution)/shard_map/ppermute | solution.py:49
  183.4 2.6 collective-permute-start.31
  185.0 36.7 %collective-permute-start.33 = (bf16[384,768]{1,0:T(8,128)(2,1)S(1)}, bf16[384,768]{1,0:T(8,128)(2,1)}, u32[]{:S(2)}, u32[]{:S(2)}) collective-permute-start(bf16[384,768]{1,0:T(8,128)(2,1)S(1)} %fusion.12), channel_id=1, source_target_pairs={{0,4},{4,0},{8,12},{12,8},{1,5},{5,1},{9,13},{13,9},{2,6},{6,2},{1... | collective-permute-start | bytes 1769480 | tf_op jit(solution)/shard_map/ppermute | solution.py:49
  186.2 12.2 %collective-permute-start.32 = (bf16[1,384,512]{2,1,0:T(8,128)(2,1)S(1)}, bf16[1,384,512]{2,1,0:T(8,128)(2,1)}, u32[]{:S(2)}, u32[]{:S(2)}) collective-permute-start(bf16[1,384,512]{2,1,0:T(8,128)(2,1)S(1)} %slice.305), channel_id=1, source_target_pairs={{0,8},{4,12},{8,0},{12,4},{1,9},{5,13},{9,1},{13,5},{2,10},{6,14},... | collective-permute-start | bytes 1179656 | tf_op jit(solution)/shard_map/ppermute | solution.py:49
  189.8 31.9 %collective-permute-start.34 = (bf16[768,384]{1,0:T(8,128)(2,1)}, bf16[768,384]{1,0:T(8,128)(2,1)}, u32[]{:S(2)}, u32[]{:S(2)}) collective-permute-start(bf16[768,384]{1,0:T(8,128)(2,1)} %fusion.11), channel_id=1, source_target_pairs={{0,8},{4,12},{8,0},{12,4},{1,9},{5,13},{9,1},{13,5},{2,10},{6,14},... | collective-permute-start | bytes 1769480 | tf_op jit(solution)/shard_map/ppermute | solution.py:49
  191.1 1.3 collective-permute-start.35
  191.2 14.0 %collective-permute-start.36 = (bf16[128,1536]{1,0:T(8,128)(2,1)S(1)}, bf16[128,1536]{1,0:T(8,128)(2,1)S(1)}, u32[]{:S(2)}, u32[]{:S(2)}) collective-permute-start(bf16[128,1536]{1,0:T(8,128)(2,1)S(1)} %pad_maximum_fusion.7), channel_id=1, source_target_pairs={{0,1},{1,2},{2,3},{3,0},{4,5},{5,6},{6,7},{7,4},{8,9},{9,10},{10,1... | collective-permute-start | bytes 1179656 | tf_op jit(solution)/shard_map/ppermute | solution.py:44
  192.4 29.3 %collective-permute-start.37 = (bf16[128,1536]{1,0:T(8,128)(2,1)S(1)}, bf16[128,1536]{1,0:T(8,128)(2,1)}, u32[]{:S(2)}, u32[]{:S(2)}) collective-permute-start(bf16[128,1536]{1,0:T(8,128)(2,1)S(1)} %pad_maximum_fusion.7), channel_id=1, source_target_pairs={{0,2},{1,3},{2,0},{3,1},{4,6},{5,7},{6,4},{7,5},{8,10},{9,11},{10,... | collective-permute-start | bytes 1179656 | tf_op jit(solution)/shard_map/ppermute | solution.py:44
  198.4 23.3 %collective-permute-start.38 = (bf16[128,1536]{1,0:T(8,128)(2,1)S(1)}, bf16[128,1536]{1,0:T(8,128)(2,1)}, u32[]{:S(2)}, u32[]{:S(2)}) collective-permute-start(bf16[128,1536]{1,0:T(8,128)(2,1)S(1)} %pad_maximum_fusion.7), channel_id=1, source_target_pairs={{0,3},{1,0},{2,1},{3,2},{4,7},{5,4},{6,5},{7,6},{8,11},{9,8},{10,9... | collective-permute-start | bytes 1179656 | tf_op jit(solution)/shard_map/ppermute | solution.py:44
  227.2 26.1 %collective-permute-start.41 = (bf16[128,768]{1,0:T(8,128)(2,1)S(1)}, bf16[128,768]{1,0:T(8,128)(2,1)S(1)}, u32[]{:S(2)}, u32[]{:S(2)}) collective-permute-start(bf16[128,768]{1,0:T(8,128)(2,1)S(1)} %get-tuple-element.131), channel_id=1, source_target_pairs={{0,1},{1,2},{2,3},{3,0},{4,5},{5,6},{6,7},{7,4},{8,9},{9,10},{10,1... | collective-permute-start | bytes 589832 | tf_op jit(solution)/shard_map/ppermute | solution.py:44
  236.0 17.3 %collective-permute-start.40 = (bf16[128,768]{1,0:T(8,128)(2,1)S(1)}, bf16[128,768]{1,0:T(8,128)(2,1)S(1)}, u32[]{:S(2)}, u32[]{:S(2)}) collective-permute-start(bf16[128,768]{1,0:T(8,128)(2,1)S(1)} %get-tuple-element.132), channel_id=1, source_target_pairs={{0,2},{1,3},{2,0},{3,1},{4,6},{5,7},{6,4},{7,5},{8,10},{9,11},{10,... | collective-permute-start | bytes 589832 | tf_op jit(solution)/shard_map/ppermute | solution.py:44
  236.0 17.9 %collective-permute-start.39 = (bf16[128,768]{1,0:T(8,128)(2,1)S(1)}, bf16[128,768]{1,0:T(8,128)(2,1)S(1)}, u32[]{:S(2)}, u32[]{:S(2)}) collective-permute-start(bf16[128,768]{1,0:T(8,128)(2,1)S(1)} %get-tuple-element.130), channel_id=1, source_target_pairs={{0,3},{1,0},{2,1},{3,2},{4,7},{5,4},{6,5},{7,6},{8,11},{9,8},{10,9... | collective-permute-start | bytes 589832 | tf_op jit(solution)/shard_map/ppermute | solution.py:44
  238.5 15.7 %collective-permute-start.42 = (f32[12,768]{1,0:T(8,128)S(1)}, f32[12,768]{1,0:T(8,128)S(1)}, u32[]{:S(2)}, u32[]{:S(2)}) collective-permute-start(f32[12,768]{1,0:T(8,128)S(1)} %add.311), channel_id=1, source_target_pairs={{0,8},{4,12},{8,0},{12,4},{1,9},{5,13},{9,1},{13,5},{2,10},{6,14},... | collective-permute-start | bytes 110600 | tf_op jit(solution)/shard_map/ppermute | solution.py:49
  242.9 3.7 %collective-permute-start.57 = (f32[384]{0:T(512)S(1)}, f32[384]{0:T(512)S(1)}, u32[]{:S(2)}, u32[]{:S(2)}) collective-permute-start(f32[384]{0:T(512)S(1)} %pad_maximum_fusion.17), channel_id=1, source_target_pairs={{0,8},{4,12},{8,0},{12,4},{1,9},{5,13},{9,1},{13,5},{2,10},{6,14},... | collective-permute-start | bytes 4616 | tf_op jit(solution)/shard_map/ppermute | solution.py:49
  246.7 1.2 collective-permute-start.58
  247.8 3.6 %collective-permute-start.59 = (f32[384]{0:T(512)S(1)}, f32[384]{0:T(512)S(1)}, u32[]{:S(2)}, u32[]{:S(2)}) collective-permute-start(f32[384]{0:T(512)S(1)} %add.327), channel_id=1, source_target_pairs={{0,16},{16,0},{1,17},{17,1},{2,18},{18,2},{3,19},{19,3},{4,20},{20... | collective-permute-start | bytes 4616 | tf_op jit(solution)/shard_map/ppermute | solution.py:49
  251.4 23.2 %collective-permute-start.44 = (bf16[384,768]{1,0:T(8,128)(2,1)}, bf16[384,768]{1,0:T(8,128)(2,1)}, u32[]{:S(2)}, u32[]{:S(2)}) collective-permute-start(bf16[384,768]{1,0:T(8,128)(2,1)} %add_convert_fusion.1), channel_id=1, source_target_pairs={{0,8},{4,12},{8,0},{12,4},{1,9},{5,13},{9,1},{13,5},{2,10},{6,14},... | collective-permute-start | bytes 1769480 | tf_op jit(solution)/shard_map/ppermute | solution.py:49
  253.3 32.4 %collective-permute-start.45 = (bf16[768,384]{1,0:T(8,128)(2,1)S(1)}, bf16[768,384]{1,0:T(8,128)(2,1)S(1)}, u32[]{:S(2)}, u32[]{:S(2)}) collective-permute-start(bf16[768,384]{1,0:T(8,128)(2,1)S(1)} %add_convert_fusion), channel_id=1, source_target_pairs={{0,4},{4,0},{8,12},{12,8},{1,5},{5,1},{9,13},{13,9},{2,6},{6,2},{1... | collective-permute-start | bytes 1769480 | tf_op jit(solution)/shard_map/ppermute | solution.py:49
  253.3 6.3 %collective-permute-start.54 = (bf16[192,384]{1,0:T(8,128)(2,1)S(1)}, bf16[192,384]{1,0:T(8,128)(2,1)S(1)}, u32[]{:S(2)}, u32[]{:S(2)}) collective-permute-start(bf16[192,384]{1,0:T(8,128)(2,1)S(1)} %split.99), channel_id=1, source_target_pairs={{0,16},{16,0},{1,17},{17,1},{2,18},{18,2},{3,19},{19,3},{4,20},{20... | collective-permute-start | bytes 442376 | tf_op jit(solution)/shard_map/ppermute | solution.py:49
  254.1 6.9 %collective-permute-start.47 = (f32[12,768]{1,0:T(8,128)S(1)}, f32[12,768]{1,0:T(8,128)S(1)}, u32[]{:S(2)}, u32[]{:S(2)}) collective-permute-start(f32[12,768]{1,0:T(8,128)S(1)} %add.316), channel_id=1, source_target_pairs={{0,2},{1,3},{2,0},{3,1},{4,6},{5,7},{6,4},{7,5},{8,10},{9,11},{10,... | collective-permute-start | bytes 110600 | tf_op jit(solution)/shard_map/ppermute | solution.py:49
  254.7 7.8 %collective-permute-start.48 = (f32[12,768]{1,0:T(8,128)S(1)}, f32[12,768]{1,0:T(8,128)S(1)}, u32[]{:S(2)}, u32[]{:S(2)}) collective-permute-start(f32[12,768]{1,0:T(8,128)S(1)} %add.316), channel_id=1, source_target_pairs={{0,3},{1,2},{2,1},{3,0},{4,7},{5,6},{6,5},{7,4},{8,11},{9,10},{10,... | collective-permute-start | bytes 110600 | tf_op jit(solution)/shard_map/ppermute | solution.py:49
  259.5 4.1 %collective-permute-start.46 = (f32[12,768]{1,0:T(8,128)S(1)}, f32[12,768]{1,0:T(8,128)S(1)}, u32[]{:S(2)}, u32[]{:S(2)}) collective-permute-start(f32[12,768]{1,0:T(8,128)S(1)} %add.316), channel_id=1, source_target_pairs={{0,1},{1,0},{2,3},{3,2},{4,5},{5,4},{6,7},{7,6},{8,9},{9,8},{10,11... | collective-permute-start | bytes 110600 | tf_op jit(solution)/shard_map/ppermute | solution.py:49
  261.0 10.7 %collective-permute-start.51 = (bf16[576,384]{1,0:T(8,128)(2,1)}, bf16[576,384]{1,0:T(8,128)(2,1)}, u32[]{:S(2)}, u32[]{:S(2)}) collective-permute-start(bf16[576,384]{1,0:T(8,128)(2,1)} %split.98), channel_id=1, source_target_pairs={{0,16},{16,0},{1,17},{17,1},{2,18},{18,2},{3,19},{19,3},{4,20},{20... | collective-permute-start | bytes 1327112 | tf_op jit(solution)/shard_map/ppermute | solution.py:49
  262.5 6.6 %collective-permute-start.55 = (bf16[192,384]{1,0:T(8,128)(2,1)S(1)}, bf16[192,384]{1,0:T(8,128)(2,1)S(1)}, u32[]{:S(2)}, u32[]{:S(2)}) collective-permute-start(bf16[192,384]{1,0:T(8,128)(2,1)S(1)} %fusion.51), channel_id=1, source_target_pairs={{0,8},{4,12},{8,0},{12,4},{1,9},{5,13},{9,1},{13,5},{2,10},{6,14},... | collective-permute-start | bytes 442376 | tf_op jit(solution)/shard_map/ppermute | solution.py:49
  263.6 23.2 %collective-permute-start.43 = (bf16[128,768]{1,0:T(8,128)(2,1)S(1)}, bf16[128,768]{1,0:T(8,128)(2,1)}, u32[]{:S(2)}, u32[]{:S(2)}) collective-permute-start(bf16[128,768]{1,0:T(8,128)(2,1)S(1)} %fusion.44), channel_id=1, source_target_pairs={{0,3},{1,0},{2,1},{3,2},{4,7},{5,4},{6,5},{7,6},{8,11},{9,8},{10,9... | collective-permute-start | bytes 589832 | tf_op jit(solution)/shard_map/ppermute | solution.py:44
  269.7 17.1 %collective-permute-start.50 = (bf16[128,768]{1,0:T(8,128)(2,1)S(1)}, bf16[128,768]{1,0:T(8,128)(2,1)S(1)}, u32[]{:S(2)}, u32[]{:S(2)}) collective-permute-start(bf16[128,768]{1,0:T(8,128)(2,1)S(1)} %fusion.44), channel_id=1, source_target_pairs={{0,2},{1,3},{2,0},{3,1},{4,6},{5,7},{6,4},{7,5},{8,10},{9,11},{10,... | collective-permute-start | bytes 589832 | tf_op jit(solution)/shard_map/ppermute | solution.py:44
  271.7 1.4 collective-permute-start.56
  273.1 12.4 %collective-permute-start.52 = (bf16[576,384]{1,0:T(8,128)(2,1)S(1)}, bf16[576,384]{1,0:T(8,128)(2,1)S(1)}, u32[]{:S(2)}, u32[]{:S(2)}) collective-permute-start(bf16[576,384]{1,0:T(8,128)(2,1)S(1)} %fusion.13), channel_id=1, source_target_pairs={{0,8},{4,12},{8,0},{12,4},{1,9},{5,13},{9,1},{13,5},{2,10},{6,14},... | collective-permute-start | bytes 1327112 | tf_op jit(solution)/shard_map/ppermute | solution.py:49
  274.7 12.1 %collective-permute-start.49 = (bf16[128,768]{1,0:T(8,128)(2,1)S(1)}, bf16[128,768]{1,0:T(8,128)(2,1)S(1)}, u32[]{:S(2)}, u32[]{:S(2)}) collective-permute-start(bf16[128,768]{1,0:T(8,128)(2,1)S(1)} %fusion.44), channel_id=1, source_target_pairs={{0,1},{1,2},{2,3},{3,0},{4,5},{5,6},{6,7},{7,4},{8,9},{9,10},{10,1... | collective-permute-start | bytes 589832 | tf_op jit(solution)/shard_map/ppermute | solution.py:44
  285.6 3.5 %collective-permute-start.53 = (bf16[576,384]{1,0:T(8,128)(2,1)S(1)}, bf16[576,384]{1,0:T(8,128)(2,1)S(1)}, u32[]{:S(2)}, u32[]{:S(2)}) collective-permute-start(bf16[576,384]{1,0:T(8,128)(2,1)S(1)} %add_convert_fusion.2), channel_id=1, source_target_pairs={{0,4},{4,0},{8,12},{12,8},{1,5},{5,1},{9,13},{13,9},{2,6},{6,2},{1... | collective-permute-start | bytes 1327112 | tf_op jit(solution)/shard_map/ppermute | solution.py:49
  (55 other events, 352.2 us)

commit v6 on v5

--- a/solution.py
+++ b/solution.py
@@ -33,6 +33,7 @@
 
 
 F32, BF16 = jnp.float32, jnp.bfloat16
+DP_, CTX_, TP_ = "dp", "ctx", "tp"
 
 
 def dot32(left, right, dims):
@@ -54,23 +55,23 @@
 
 
 def own_first(array):
-    if lax.axis_size("dp") != 2:
+    if lax.axis_size(DP_) != 2:
         return array
     half = array.shape[-1] // 2
     turned = jnp.concatenate([array[..., half:], array[..., :half]], -1)
-    return jnp.where(lax.axis_index("dp") == 0, array, turned)
+    return jnp.where(lax.axis_index(DP_) == 0, array, turned)
 
 
 def gather_weight(shard, dim):
-    if lax.axis_size("dp") != 2:
-        return lax.all_gather(shard, "dp", axis=dim, tiled=True)
-    return jnp.concatenate([shard, flipped(shard, "dp", 1)], dim)
+    if lax.axis_size(DP_) != 2:
+        return lax.all_gather(shard, DP_, axis=dim, tiled=True)
+    return jnp.concatenate([shard, flipped(shard, DP_, 1)], dim)
 
 
 def gather_late(shard, dim):
-    if lax.axis_size("dp") != 2:
+    if lax.axis_size(DP_) != 2:
         return gather_weight(shard, dim), lambda moved: moved
-    moved = flipped(shard, "dp", 1)
+    moved = flipped(shard, DP_, 1)
     return moved, lambda moved: jnp.concatenate([shard, moved], dim)
 
 
@@ -78,22 +79,22 @@
     def __init__(self, gradient, dim, far_first=False):
         self.bits = []
         bit = 1
-        while bit < lax.axis_size("ctx"):
+        while bit < lax.axis_size(CTX_):
             self.bits.append(bit)
             bit *= 2
         if far_first:
             self.bits.reverse()
-        if lax.axis_size("dp") == 2:
+        if lax.axis_size(DP_) == 2:
             kept, given = jnp.split(gradient, 2, dim)
-            self.kept, self.moved = kept, flipped(given.astype(BF16), "dp", 1)
+            self.kept, self.moved = kept, flipped(given.astype(BF16), DP_, 1)
         else:
             low = gradient.astype(BF16)
-            self.moved = lax.psum_scatter(low, "dp", scatter_dimension=dim, tiled=True)
+            self.moved = lax.psum_scatter(low, DP_, scatter_dimension=dim, tiled=True)
             self.kept = jnp.zeros(self.moved.shape, F32)
 
     def step(self):
         low = (self.kept.astype(F32) + self.moved.astype(F32)).astype(BF16)
-        self.kept, self.moved = low, flipped(low, "ctx", self.bits.pop(0))
+        self.kept, self.moved = low, flipped(low, CTX_, self.bits.pop(0))
 
     def total(self):
         while self.bits:
@@ -124,7 +125,7 @@
 
 
 def ctx_order():
-    order, bit = [0], lax.axis_size("ctx") // 2
+    order, bit = [0], lax.axis_size(CTX_) // 2
     while bit:
         order = order + [e ^ bit for e in order]
         bit //= 2
@@ -132,20 +133,20 @@
 
 
 def gather_parts(block, beside):
-    held, bit = [block[None]], lax.axis_size("ctx") // 2
+    held, bit = [block[None]], lax.axis_size(CTX_) // 2
     while bit:
         sent = held[0] if len(held) == 1 else jnp.concatenate(held, 0)
-        held.append(flipped(sent, "ctx", bit))
-        if bit == lax.axis_size("ctx") // 2:
+        held.append(flipped(sent, CTX_, bit))
+        if bit == lax.axis_size(CTX_) // 2:
             held[-1], beside = tie(held[-1], beside)
         bit //= 2
     return held, beside
 
 
 def scatter_parts(blocks, sent):
-    size, bit = lax.axis_size("ctx"), 1
+    size, bit = lax.axis_size(CTX_), 1
     while bit < size:
-        blocks = blocks.astype(F32) + flipped(sent.astype(BF16), "ctx", bit).astype(F32)
+        blocks = blocks.astype(F32) + flipped(sent.astype(BF16), CTX_, bit).astype(F32)
         half = blocks.shape[0] // 2
         if half:
             blocks, sent = blocks[:half], blocks[half:]
@@ -154,8 +155,8 @@
 
 
 def rows_turn(block):
-    size = lax.axis_size("tp")
-    place = lax.axis_index("tp")
+    size = lax.axis_size(TP_)
+    place = lax.axis_index(TP_)
     blocks = block.reshape((size, block.shape[0] // size) + block.shape[1:])
     return jnp.concatenate(
         [
@@ -167,20 +168,20 @@
 
 
 def rows_place(blocks):
-    size = lax.axis_size("tp")
-    place = lax.axis_index("tp")
+    size = lax.axis_size(TP_)
+    place = lax.axis_index(TP_)
     return jnp.concatenate(
         [lax.select_n(lax.rem(place - p + size, size), *blocks) for p in range(size)], 0
     )
 
 
 def rows_sum(total):
-    size = lax.axis_size("tp")
+    size = lax.axis_size(TP_)
     rows = total.shape[0] // size
     low = total.astype(BF16)
     moved = []
     for e in range(1, size):
-        moved.append(shifted(low[e * rows : (e + 1) * rows], "tp", size - e))
+        moved.append(shifted(low[e * rows : (e + 1) * rows], TP_, size - e))
     kept = total[:rows]
     for block in moved:
         kept = kept + block.astype(F32)
@@ -189,8 +190,8 @@
 
 def rows_moved(block):
     moved = []
-    for e in range(1, lax.axis_size("tp")):
-        moved.append(shifted(block, "tp", e))
+    for e in range(1, lax.axis_size(TP_)):
+        moved.append(shifted(block, TP_, e))
     return moved
 
 
@@ -199,8 +200,8 @@
 
 
 def rows_exchange(blocks):
-    size = lax.axis_size("tp")
-    return [blocks[0]] + [shifted(blocks[size - j], "tp", j) for j in range(1, size)]
+    size = lax.axis_size(TP_)
+    return [blocks[0]] + [shifted(blocks[size - j], TP_, j) for j in range(1, size)]
 
 
 TILE = 256
@@ -419,8 +420,8 @@
     width_local = w_query.shape[1]
     score_scale = 1.0 / math.sqrt(width_local // heads_local)
     seq_length = lengths[0]
-    ctx_place, tp_place = lax.axis_index("ctx"), lax.axis_index("tp")
-    tp_size = lax.axis_size("tp")
+    ctx_place, tp_place = lax.axis_index(CTX_), lax.axis_index(TP_)
+    tp_size = lax.axis_size(TP_)
     part_rows = row_count // tp_size
 
     qkv_shard = jnp.concatenate([w_query.T, w_key.T, w_value.T], 0)
@@ -441,7 +442,7 @@
     kv_all, query_scaled = gather_parts(kv_local, query_scaled)
     output_moved, join_output = gather_late(output_half, 1)
     starts = (ctx_place ^ jnp.asarray(ctx_order(), jnp.int32)) * row_count
-    all_count = VectorSum(seq_length.astype(F32), ("dp",)).total()
+    all_count = VectorSum(seq_length.astype(F32), (DP_,)).total()
 
     logits, weights, context, inverse = attend(
         query_scaled, kv_all, starts, prev_logits, limits, heads_local
@@ -469,7 +470,7 @@
     valid_rows = (own_rows(row_pos) < seq_length).astype(F32)
     deviation = result - own_rows(teacher_states[0]).astype(F32)
     local_squared = jnp.sum(valid_rows[:, None] * deviation * deviation)
-    token_total = row_count * lax.axis_size("ctx") * lax.axis_size("dp")
+    token_total = row_count * lax.axis_size(CTX_) * lax.axis_size(DP_)
     d_out = 2.0 * token_total / all_count * valid_rows[:, None] * deviation
     d_second, grad_gain_second, grad_shift_second = norm_backward(
         d_out, normed_second, spread_second, gain_second
@@ -510,7 +511,7 @@
             tp_size,
         )
     )
-    early_sum = VectorSum(packed, ("dp", "ctx"))
+    early_sum = VectorSum(packed, (DP_, CTX_))
     d_context, outer_sum.moved, inner_sum.moved = tie(
         d_context, outer_sum.moved, inner_sum.moved
     )
@@ -541,7 +542,7 @@
     output_gradient = dot32(context_turned, d_first_all, ((0,), (0,)))
     output_sum = WeightSum(output_gradient, 1, True)
     late_vector = jnp.concatenate([jnp.sum(d_query, 0), jnp.sum(d_kv[width_local:], 1)])
-    late_sum = VectorSum(late_vector, ("dp", "ctx"), True)
+    late_sum = VectorSum(late_vector, (DP_, CTX_), True)
     grad_mine = (d_first + own_first(tokens_part)).astype(BF16)
     sums = (early_sum,)
     grad_mine, *moved = tie(grad_mine, *[one.moved for one in sums])
@@ -550,7 +551,7 @@
     early = early_sum.total()
     moved = []
     for e in range(1, tp_size):
-        moved.append(flipped(early, "tp", e))
+        moved.append(flipped(early, TP_, e))
     early = [early] + moved
     while len(early) > 1:
         early = [left + right for left, right in zip(early[::2], early[1::2])]
@@ -599,20 +600,20 @@
 
 def solution(mesh):
     placed = (
-        P("dp", "ctx", None),
-        P("dp", "ctx", None),
-        P("dp"),
-        P("dp", "tp", "ctx", None),
-        P("dp", "tp"),
-        P("dp", "tp"),
-        P("dp", "tp"),
-        P("tp", "dp"),
-        P("dp", "tp"),
-        P("tp", "dp"),
-        P("tp"),
-        P("tp"),
+        P(DP_, CTX_, None),
+        P(DP_, CTX_, None),
+        P(DP_),
+        P(DP_, TP_, CTX_, None),
+        P(DP_, TP_),
+        P(DP_, TP_),
+        P(DP_, TP_),
+        P(TP_, DP_),
+        P(DP_, TP_),
+        P(TP_, DP_),
+        P(TP_),
+        P(TP_),
         P(),
-        P("tp"),
+        P(TP_),
         P(),
         P(),
         P(),
@@ -624,21 +625,21 @@
         mesh=mesh,
         in_specs=placed,
         out_specs=(
-            P("dp", "ctx", None),
-            P("dp", "tp", "ctx", None),
+            P(DP_, CTX_, None),
+            P(DP_, TP_, CTX_, None),
             P(),
-            P("dp", "ctx", None),
-            P("dp", "tp", "ctx", None),
-            P("dp", "tp"),
-            P("dp", "tp"),
-            P("dp", "tp"),
-            P("tp", "dp"),
-            P("dp", "tp"),
-            P("tp", "dp"),
-            P("tp"),
-            P("tp"),
+            P(DP_, CTX_, None),
+            P(DP_, TP_, CTX_, None),
+            P(DP_, TP_),
+            P(DP_, TP_),
+            P(DP_, TP_),
+            P(TP_, DP_),
+            P(DP_, TP_),
+            P(TP_, DP_),
+            P(TP_),
+            P(TP_),
             P(),
-            P("tp"),
+            P(TP_),
             P(),
             P(),
             P(),

time: 292 us -> 292 us (level)
  no operation moved by 1% of the time
where the time goes in v6:
time: 292 us; the launch traced here: 291 us
  waiting for transfers between devices  108 us (37%)
  starting transfers between devices  78.5 us (27%)
  other arithmetic  36.4 us (12%)
  Pallas kernels  28 us (10%)
  local copies, waits for them, and re-layouts  21.4 us (7%)
  matrix products  14.4 us (5%)
  between operations  4.94 us (2%)
    ppermute x30, waiting for transfers between devices, shifted(): lax.ppermute(block, axis, [(i, (i + step) % size) for i in range(size)])  62.7 us
    ppermute x30, starting transfers between devices, shifted(): lax.ppermute(block, axis, [(i, (i + step) % size) for i in range(size)])  53.1 us
    ppermute x30, waiting for transfers between devices, flipped(): return lax.ppermute(block, axis, [(i, i ^ bit) for i in range(size)])  45 us
    ppermute x30, starting transfers between devices, flipped(): return lax.ppermute(block, axis, [(i, i ^ bit) for i in range(size)])  25.4 us
    dot_general x13, matrix products, dot32(): lax.dot_general(left, right, (dims, ((), ())), preferred_element_type=F32)  14.4 us
    pallas_call x1, Pallas kernels, attend_back(): pl.pallas_call(partial(attend_back_kernel, heads, scale, len(kv)), grid_s...  13.3 us
    pallas_call x1, Pallas kernels, attend(): pl.pallas_call(partial(attend_kernel, heads, len(kv)), grid_spec=pltpu.Pr...  12.6 us
    convert_element_type x8, other arithmetic, step(): low = (self.kept.astype(F32) + self.moved.astype(F32)).astype(BF16)  9.17 us
  transfers between devices with their start and end apart: 60, of which 26 were waited for; matrix products, arithmetic and copies ran while one was open for 20% of the time, Pallas kernels for 10%

profile of v6, /device:TPU:0, one launch (start us, length us, event | category | flops | bytes accessed | tf_op | source)
XLA Modules:
  0.0 291.3 jit_solution(6537135933508962774)
XLA Ops:
  0.7 5.1 %collective-permute-start.4 = (bf16[192,384]{1,0:T(8,128)(2,1)}, bf16[192,384]{1,0:T(8,128)(2,1)S(1)}, u32[]{:S(2)}, u32[]{:S(2)}) collective-permute-start(bf16[192,384]{1,0:T(8,128)(2,1)} %param.27), channel_id=1, source_target_pairs={{0,3},{1,0},{2,1},{3,2},{4,7},{5,4},{6,5},{7,6},{8,11},{9,8},{10,9... | collective-permute-start | bytes 442376 | tf_op jit(solution)/shard_map/ppermute | solution.py:45
  7.9 1.6 collective-permute-start.1
  9.5 1.2 fusion.91
  11.0 7.5 %collective-permute-done.3 = bf16[192,384]{1,0:T(8,128)(2,1)S(1)} collective-permute-done((bf16[192,384]{1,0:T(8,128)(2,1)}, bf16[192,384]{1,0:T(8,128)(2,1)S(1)}, u32[]{:S(2)}, u32[]{:S(2)}) %collective-permute-start.3) | collective-permute-done | bytes 147488 | tf_op jit(solution)/shard_map/ppermute | solution.py:45
  20.1 1.6 collective-permute-start.5
  22.8 7.8 %collective-permute-done.5.refs_1_ = bf16[1,512,384]{2,1,0:T(8,128)(2,1)S(1)} collective-permute-done((bf16[1,512,384]{2,1,0:T(8,128)(2,1)S(1)}, bf16[1,512,384]{2,1,0:T(8,128)(2,1)S(1)}, u32[]{:S(2)}, u32[]{:S(2)}) %collective-permute-start.5) | collective-permute-done | bytes 393248 | tf_op jit(solution)/shard_map/ppermute | solution.py:50
  32.3 2.9 collective-permute-start
  38.0 12.6 %attend.1 = (bf16[1,3,512,2048]{3,2,1,0:T(8,128)(2,1)}, bf16[3,512,2048]{2,1,0:T(8,128)(2,1)}, bf16[512,192]{1,0:T(8,128)(2,1)}, f32[512,192]{1,0:T(8,128)}) custom-call(s32[2]{0:T(128)} %multiply_minimum_fusion.limits, s32[4]{0:T(128)} %xor_multiply_fusion.starts, bf16[512,192]{1,0:T(8,128)(2,1)} %fusion.10.query, bf16[1,3,512,2048]{3,2,1,0:T(8,128)(2,1)} %prior.1, ...), custom_call_target="tpu_custom_call" | custom-call | flops 805306368 | bytes 18874368 | tf_op jit(solution)/shard_map/attend/pallas_call | solution.py:257
  51.8 1.2 constant_dynamic-update-slice_fusion.3
  53.0 1.6 collective-permute-start.14
  54.5 1.8 collective-permute-start.10
  57.3 1.9 collective-permute-start.8
  61.1 2.5 collective-permute-done.9
  65.0 1.5 collective-permute-start.13
  66.5 2.7 collective-permute-done.14
  70.1 10.2 %collective-permute-done.15 = bf16[768,384]{1,0:T(8,128)(2,1)S(1)} collective-permute-done((bf16[768,384]{1,0:T(8,128)(2,1)S(1)}, bf16[768,384]{1,0:T(8,128)(2,1)S(1)}, u32[]{:S(2)}, u32[]{:S(2)}) %collective-permute-start.15) | collective-permute-done | bytes 589856 | tf_op jit(solution)/shard_map/ppermute | solution.py:50
  80.4 3.1 %collective-permute-done.12 = bf16[128,768]{1,0:T(8,128)(2,1)S(1)} collective-permute-done((bf16[128,768]{1,0:T(8,128)(2,1)S(1)}, bf16[128,768]{1,0:T(8,128)(2,1)S(1)}, u32[]{:S(2)}, u32[]{:S(2)}) %collective-permute-start.12) | collective-permute-done | bytes 196640 | tf_op jit(solution)/shard_map/ppermute | solution.py:45
  83.5 5.6 %multiply_convert_fusion = (bf16[512,768]{1,0:T(8,128)(2,1)S(1)}, f32[512,768]{1,0:T(8,128)}, f32[512,768]{1,0:T(8,128)}) fusion(f32[768]{0:T(1024)S(1)} %copy-done.54, bf16[768,768]{1,0:T(8,128)(2,1)S(1)} %constant_dynamic-update-slice_fusion.2, bf16[128,768]{1,0:T(8,128)(2,1)S(1)} %collective-permute-done.13, ...), kind=kOutput, calls=%fused_computation.4 | convolution fusion | flops 633077760 | bytes 5901312 | tf_op jit(solution)/shard_map/dot_general | solution.py:40
  90.8 1.7 collective-permute-start.17
  92.5 2.9 %collective-permute-start.16 = (bf16[128,768]{1,0:T(8,128)(2,1)S(1)}, bf16[128,768]{1,0:T(8,128)(2,1)}, u32[]{:S(2)}, u32[]{:S(2)}) collective-permute-start(bf16[128,768]{1,0:T(8,128)(2,1)S(1)} %get-tuple-element.136), channel_id=1, source_target_pairs={{0,3},{1,0},{2,1},{3,2},{4,7},{5,4},{6,5},{7,6},{8,11},{9,8},{10,9... | collective-permute-start | bytes 589832 | tf_op jit(solution)/shard_map/ppermute | solution.py:45
  95.4 1.3 compare_convert_fusion
  98.1 2.6 collective-permute-done.18
  100.7 6.3 %collective-permute-done.17 = bf16[128,768]{1,0:T(8,128)(2,1)} collective-permute-done((bf16[128,768]{1,0:T(8,128)(2,1)S(1)}, bf16[128,768]{1,0:T(8,128)(2,1)}, u32[]{:S(2)}, u32[]{:S(2)}) %collective-permute-start.17) | collective-permute-done | bytes 196640 | tf_op jit(solution)/shard_map/ppermute | solution.py:45
  107.0 1.2 fusion.37
  110.9 6.3 %collective-permute-start.21 = (bf16[128,768]{1,0:T(8,128)(2,1)S(1)}, bf16[128,768]{1,0:T(8,128)(2,1)S(1)}, u32[]{:S(2)}, u32[]{:S(2)}) collective-permute-start(bf16[128,768]{1,0:T(8,128)(2,1)S(1)} %maximum_select_fusion.6), channel_id=1, source_target_pairs={{0,3},{1,0},{2,1},{3,2},{4,7},{5,4},{6,5},{7,6},{8,11},{9,8},{10,9... | collective-permute-start | bytes 589832 | tf_op jit(solution)/shard_map/ppermute | solution.py:45
  117.8 4.7 %collective-permute-done.21 = bf16[128,768]{1,0:T(8,128)(2,1)S(1)} collective-permute-done((bf16[128,768]{1,0:T(8,128)(2,1)S(1)}, bf16[128,768]{1,0:T(8,128)(2,1)S(1)}, u32[]{:S(2)}, u32[]{:S(2)}) %collective-permute-start.21) | collective-permute-done | bytes 196640 | tf_op jit(solution)/shard_map/ppermute | solution.py:45
  122.5 11.4 %collective-permute-done.20 = bf16[128,768]{1,0:T(8,128)(2,1)S(1)} collective-permute-done((bf16[128,768]{1,0:T(8,128)(2,1)S(1)}, bf16[128,768]{1,0:T(8,128)(2,1)S(1)}, u32[]{:S(2)}, u32[]{:S(2)}) %collective-permute-start.20) | collective-permute-done | bytes 196640 | tf_op jit(solution)/shard_map/ppermute | solution.py:45
  134.0 1.2 fusion.104
  136.2 2.0 collective-permute-start.23
  138.2 2.9 collective-permute-start.22
  144.4 1.5 collective-permute-start.29
  145.9 6.2 %collective-permute-done.23 = bf16[128,768]{1,0:T(8,128)(2,1)S(1)} collective-permute-done((bf16[128,768]{1,0:T(8,128)(2,1)S(1)}, bf16[128,768]{1,0:T(8,128)(2,1)S(1)}, u32[]{:S(2)}, u32[]{:S(2)}) %collective-permute-start.23) | collective-permute-done | bytes 196640 | tf_op jit(solution)/shard_map/ppermute | solution.py:45
  153.5 5.6 %collective-permute-start.27 = (bf16[128,192]{1,0:T(8,128)(2,1)S(1)}, bf16[128,192]{1,0:T(8,128)(2,1)S(1)}, u32[]{:S(2)}, u32[]{:S(2)}) collective-permute-start(bf16[128,192]{1,0:T(8,128)(2,1)S(1)} %get-tuple-element.171), channel_id=1, source_target_pairs={{0,3},{1,0},{2,1},{3,2},{4,7},{5,4},{6,5},{7,6},{8,11},{9,8},{10,9... | collective-permute-start | bytes 147464 | tf_op jit(solution)/shard_map/ppermute | solution.py:45
  163.8 2.1 pack.1
  167.3 2.7 collective-permute-done.29
  170.0 13.3 %attend_back.1 = (bf16[1,3,512,2048]{3,2,1,0:T(8,128)(2,1)}, f32[512,192]{1,0:T(8,128)}, bf16[2,384,512]{2,1,0:T(8,128)(2,1)}, bf16[2,384,512]{2,1,0:T(8,128)(2,1)}) custom-call(s32[4]{0:T(128)} %xor_multiply_fusion.starts, bf16[3,512,2048]{2,1,0:T(8,128)(2,1)} %get-tuple-element.64.weights, bf16[512,192]{1,0:T(8,128)(2,1)} %get-tuple-element.58.context, ...), custom_call_target="tpu_custom_call" | custom-call | flops 2013265920 | bytes 18874368 | tf_op jit(solution)/shard_map/attend_back/pallas_call | solution.py:340
  183.4 1.6 fusion.12
  186.2 1.6 collective-permute-start.32
  187.8 2.0 fusion.11
  189.8 1.3 collective-permute-start.34
  193.0 5.4 %collective-permute-done.32 = bf16[1,384,512]{2,1,0:T(8,128)(2,1)} collective-permute-done((bf16[1,384,512]{2,1,0:T(8,128)(2,1)S(1)}, bf16[1,384,512]{2,1,0:T(8,128)(2,1)}, u32[]{:S(2)}, u32[]{:S(2)}) %collective-permute-start.32) | collective-permute-done | bytes 393248 | tf_op jit(solution)/shard_map/ppermute | solution.py:50
  201.2 2.1 convert_bitcast_fusion
  203.3 2.0 collective-permute-done.36
  205.2 16.5 %collective-permute-done.37 = bf16[128,1536]{1,0:T(8,128)(2,1)} collective-permute-done((bf16[128,1536]{1,0:T(8,128)(2,1)S(1)}, bf16[128,1536]{1,0:T(8,128)(2,1)}, u32[]{:S(2)}, u32[]{:S(2)}) %collective-permute-start.37) | collective-permute-done | bytes 393248 | tf_op jit(solution)/shard_map/ppermute | solution.py:45
  223.2 1.6 reshape.205
  224.8 1.2 constant_dynamic-slice_fusion.4
  227.2 8.8 %collective-permute-start.41 = (bf16[128,768]{1,0:T(8,128)(2,1)S(1)}, bf16[128,768]{1,0:T(8,128)(2,1)S(1)}, u32[]{:S(2)}, u32[]{:S(2)}) collective-permute-start(bf16[128,768]{1,0:T(8,128)(2,1)S(1)} %get-tuple-element.131), channel_id=1, source_target_pairs={{0,1},{1,2},{2,3},{3,0},{4,5},{5,6},{6,7},{7,4},{8,9},{9,10},{10,1... | collective-permute-start | bytes 589832 | tf_op jit(solution)/shard_map/ppermute | solution.py:45
  236.0 2.4 collective-permute-start.39
  239.3 2.0 add_convert_fusion.1
  241.3 1.4 add_convert_fusion
  242.9 1.3 collective-permute-start.57
  244.2 1.3 select_select_fusion.1
  248.4 1.3 maximum_convert_fusion
  251.4 1.2 collective-permute-start.44
  254.7 2.2 collective-permute-start.48
  256.9 2.6 collective-permute-done.54
  259.6 1.5 collective-permute-done.47
  261.0 1.4 collective-permute-start.51
  263.6 1.9 collective-permute-start.43
  267.4 1.7 collective-permute-done.55
  274.7 2.2 collective-permute-start.49
  276.8 2.4 convert_add_fusion.2
  279.2 6.3 %collective-permute-done.52 = bf16[576,384]{1,0:T(8,128)(2,1)S(1)} collective-permute-done((bf16[576,384]{1,0:T(8,128)(2,1)S(1)}, bf16[576,384]{1,0:T(8,128)(2,1)S(1)}, u32[]{:S(2)}, u32[]{:S(2)}) %collective-permute-start.52) | collective-permute-done | bytes 442400 | tf_op jit(solution)/shard_map/ppermute | solution.py:50
  287.8 1.3 maximum_convert_fusion.1
  (305 shorter events, 59.9 us)
Async XLA Ops:
  0.7 10.3 %collective-permute-start.4 = (bf16[192,384]{1,0:T(8,128)(2,1)}, bf16[192,384]{1,0:T(8,128)(2,1)S(1)}, u32[]{:S(2)}, u32[]{:S(2)}) collective-permute-start(bf16[192,384]{1,0:T(8,128)(2,1)} %param.27), channel_id=1, source_target_pairs={{0,3},{1,0},{2,1},{3,2},{4,7},{5,4},{6,5},{7,6},{8,11},{9,8},{10,9... | collective-permute-start | bytes 442376 | tf_op jit(solution)/shard_map/ppermute | solution.py:45
  5.8 12.7 %collective-permute-start.3 = (bf16[192,384]{1,0:T(8,128)(2,1)}, bf16[192,384]{1,0:T(8,128)(2,1)S(1)}, u32[]{:S(2)}, u32[]{:S(2)}) collective-permute-start(bf16[192,384]{1,0:T(8,128)(2,1)} %param.27), channel_id=1, source_target_pairs={{0,2},{1,3},{2,0},{3,1},{4,6},{5,7},{6,4},{7,5},{8,10},{9,11},{10,... | collective-permute-start | bytes 442376 | tf_op jit(solution)/shard_map/ppermute | solution.py:45
  5.8 12.7 %collective-permute-start.2 = (bf16[192,384]{1,0:T(8,128)(2,1)}, bf16[192,384]{1,0:T(8,128)(2,1)S(1)}, u32[]{:S(2)}, u32[]{:S(2)}) collective-permute-start(bf16[192,384]{1,0:T(8,128)(2,1)} %param.27), channel_id=1, source_target_pairs={{0,1},{1,2},{2,3},{3,0},{4,5},{5,6},{6,7},{7,4},{8,9},{9,10},{10,1... | collective-permute-start | bytes 442376 | tf_op jit(solution)/shard_map/ppermute | solution.py:45
  7.9 11.5 %collective-permute-start.1 = (bf16[576,384]{1,0:T(8,128)(2,1)S(1)}, bf16[576,384]{1,0:T(8,128)(2,1)S(1)}, u32[]{:S(2)}, u32[]{:S(2)}) collective-permute-start(bf16[576,384]{1,0:T(8,128)(2,1)S(1)} %pad_maximum_fusion.6), channel_id=1, source_target_pairs={{0,16},{16,0},{1,17},{17,1},{2,18},{18,2},{3,19},{19,3},{4,20},{20... | collective-permute-start | bytes 1327112 | tf_op jit(solution)/shard_map/ppermute | solution.py:50
  20.1 10.5 %collective-permute-start.5 = (bf16[1,512,384]{2,1,0:T(8,128)(2,1)S(1)}, bf16[1,512,384]{2,1,0:T(8,128)(2,1)S(1)}, u32[]{:S(2)}, u32[]{:S(2)}) collective-permute-start(bf16[1,512,384]{2,1,0:T(8,128)(2,1)S(1)} %bitcast.100), channel_id=1, source_target_pairs={{0,8},{4,12},{8,0},{12,4},{1,9},{5,13},{9,1},{13,5},{2,10},{6,14},... | collective-permute-start | bytes 1179656 | tf_op jit(solution)/shard_map/ppermute | solution.py:50
  31.7 6.4 %collective-permute-start.6 = (bf16[2,512,384]{2,1,0:T(8,128)(2,1)}, bf16[2,512,384]{2,1,0:T(8,128)(2,1)}, u32[]{:S(2)}, u32[]{:S(2)}) collective-permute-start(bf16[2,512,384]{2,1,0:T(8,128)(2,1)} %pad_maximum_fusion.1), channel_id=1, source_target_pairs={{0,4},{4,0},{8,12},{12,8},{1,5},{5,1},{9,13},{13,9},{2,6},{6,2},{1... | collective-permute-start | bytes 2359304 | tf_op jit(solution)/shard_map/ppermute | solution.py:50
  32.3 64.4 %collective-permute-start = (f32[]{:T(128)}, f32[]{:T(128)}, u32[]{:S(2)}, u32[]{:S(2)}) collective-permute-start(f32[]{:T(128)} %convert_element_type.210), channel_id=1, source_target_pairs={{0,16},{16,0},{1,17},{17,1},{2,18},{18,2},{3,19},{19,3},{4,20},{20... | collective-permute-start | bytes 20 | tf_op jit(solution)/shard_map/ppermute | solution.py:50
  35.8 15.9 %collective-permute-start.7 = (bf16[768,384]{1,0:T(8,128)(2,1)}, bf16[768,384]{1,0:T(8,128)(2,1)}, u32[]{:S(2)}, u32[]{:S(2)}) collective-permute-start(bf16[768,384]{1,0:T(8,128)(2,1)} %pad_maximum_fusion.4), channel_id=1, source_target_pairs={{0,16},{16,0},{1,17},{17,1},{2,18},{18,2},{3,19},{19,3},{4,20},{20... | collective-permute-start | bytes 1769480 | tf_op jit(solution)/shard_map/ppermute | solution.py:50
  53.0 16.3 %collective-permute-start.14 = (bf16[384,768]{1,0:T(8,128)(2,1)S(1)}, bf16[384,768]{1,0:T(8,128)(2,1)S(1)}, u32[]{:S(2)}, u32[]{:S(2)}) collective-permute-start(bf16[384,768]{1,0:T(8,128)(2,1)S(1)} %copy-done.26), channel_id=1, source_target_pairs={{0,16},{16,0},{1,17},{17,1},{2,18},{18,2},{3,19},{19,3},{4,20},{20... | collective-permute-start | bytes 1769480 | tf_op jit(solution)/shard_map/ppermute | solution.py:50
  54.5 6.0 %collective-permute-start.10 = (bf16[128,192]{1,0:T(8,128)(2,1)S(1)}, bf16[128,192]{1,0:T(8,128)(2,1)S(1)}, u32[]{:S(2)}, u32[]{:S(2)}) collective-permute-start(bf16[128,192]{1,0:T(8,128)(2,1)S(1)} %get-tuple-element.163), channel_id=1, source_target_pairs={{0,3},{1,0},{2,1},{3,2},{4,7},{5,4},{6,5},{7,6},{8,11},{9,8},{10,9... | collective-permute-start | bytes 147464 | tf_op jit(solution)/shard_map/ppermute | solution.py:45
  56.3 7.3 %collective-permute-start.9 = (bf16[128,192]{1,0:T(8,128)(2,1)S(1)}, bf16[128,192]{1,0:T(8,128)(2,1)S(1)}, u32[]{:S(2)}, u32[]{:S(2)}) collective-permute-start(bf16[128,192]{1,0:T(8,128)(2,1)S(1)} %get-tuple-element.164), channel_id=1, source_target_pairs={{0,2},{1,3},{2,0},{3,1},{4,6},{5,7},{6,4},{7,5},{8,10},{9,11},{10,... | collective-permute-start | bytes 147464 | tf_op jit(solution)/shard_map/ppermute | solution.py:45
  57.3 6.3 %collective-permute-start.8 = (bf16[128,192]{1,0:T(8,128)(2,1)S(1)}, bf16[128,192]{1,0:T(8,128)(2,1)S(1)}, u32[]{:S(2)}, u32[]{:S(2)}) collective-permute-start(bf16[128,192]{1,0:T(8,128)(2,1)S(1)} %get-tuple-element.165), channel_id=1, source_target_pairs={{0,1},{1,2},{2,3},{3,0},{4,5},{5,6},{6,7},{7,4},{8,9},{9,10},{10,1... | collective-permute-start | bytes 147464 | tf_op jit(solution)/shard_map/ppermute | solution.py:45
  60.5 19.8 %collective-permute-start.15 = (bf16[768,384]{1,0:T(8,128)(2,1)S(1)}, bf16[768,384]{1,0:T(8,128)(2,1)S(1)}, u32[]{:S(2)}, u32[]{:S(2)}) collective-permute-start(bf16[768,384]{1,0:T(8,128)(2,1)S(1)} %copy-done.27), channel_id=1, source_target_pairs={{0,16},{16,0},{1,17},{17,1},{2,18},{18,2},{3,19},{19,3},{4,20},{20... | collective-permute-start | bytes 1769480 | tf_op jit(solution)/shard_map/ppermute | solution.py:50
  65.0 24.1 %copy-start.31 = (bf16[128,768]{1,0:T(8,128)(2,1)}, bf16[128,768]{1,0:T(8,128)(2,1)S(1)}, u32[]{:S(2)}) copy-start(bf16[128,768]{1,0:T(8,128)(2,1)S(1)} %maximum_select_fusion.5) | copy-start | bytes 589828
  65.0 15.4 %collective-permute-start.13 = (bf16[128,768]{1,0:T(8,128)(2,1)S(1)}, bf16[128,768]{1,0:T(8,128)(2,1)S(1)}, u32[]{:S(2)}, u32[]{:S(2)}) collective-permute-start(bf16[128,768]{1,0:T(8,128)(2,1)S(1)} %maximum_select_fusion.5), channel_id=1, source_target_pairs={{0,3},{1,0},{2,1},{3,2},{4,7},{5,4},{6,5},{7,6},{8,11},{9,8},{10,9... | collective-permute-start | bytes 589832 | tf_op jit(solution)/shard_map/ppermute | solution.py:45
  66.5 17.0 %collective-permute-start.12 = (bf16[128,768]{1,0:T(8,128)(2,1)S(1)}, bf16[128,768]{1,0:T(8,128)(2,1)S(1)}, u32[]{:S(2)}, u32[]{:S(2)}) collective-permute-start(bf16[128,768]{1,0:T(8,128)(2,1)S(1)} %maximum_select_fusion.5), channel_id=1, source_target_pairs={{0,2},{1,3},{2,0},{3,1},{4,6},{5,7},{6,4},{7,5},{8,10},{9,11},{10,... | collective-permute-start | bytes 589832 | tf_op jit(solution)/shard_map/ppermute | solution.py:45
  69.2 14.3 %collective-permute-start.11 = (bf16[128,768]{1,0:T(8,128)(2,1)S(1)}, bf16[128,768]{1,0:T(8,128)(2,1)S(1)}, u32[]{:S(2)}, u32[]{:S(2)}) collective-permute-start(bf16[128,768]{1,0:T(8,128)(2,1)S(1)} %maximum_select_fusion.5), channel_id=1, source_target_pairs={{0,1},{1,2},{2,3},{3,0},{4,5},{5,6},{6,7},{7,4},{8,9},{9,10},{10,1... | collective-permute-start | bytes 589832 | tf_op jit(solution)/shard_map/ppermute | solution.py:45
  90.8 9.9 %collective-permute-start.18 = (bf16[128,768]{1,0:T(8,128)(2,1)}, bf16[128,768]{1,0:T(8,128)(2,1)}, u32[]{:S(2)}, u32[]{:S(2)}) collective-permute-start(bf16[128,768]{1,0:T(8,128)(2,1)} %get-tuple-element.137), channel_id=1, source_target_pairs={{0,1},{1,2},{2,3},{3,0},{4,5},{5,6},{6,7},{7,4},{8,9},{9,10},{10,1... | collective-permute-start | bytes 589832 | tf_op jit(solution)/shard_map/ppermute | solution.py:45
  90.8 16.2 %collective-permute-start.17 = (bf16[128,768]{1,0:T(8,128)(2,1)S(1)}, bf16[128,768]{1,0:T(8,128)(2,1)}, u32[]{:S(2)}, u32[]{:S(2)}) collective-permute-start(bf16[128,768]{1,0:T(8,128)(2,1)S(1)} %get-tuple-element.138), channel_id=1, source_target_pairs={{0,2},{1,3},{2,0},{3,1},{4,6},{5,7},{6,4},{7,5},{8,10},{9,11},{10,... | collective-permute-start | bytes 589832 | tf_op jit(solution)/shard_map/ppermute | solution.py:45
  92.5 14.5 %collective-permute-start.16 = (bf16[128,768]{1,0:T(8,128)(2,1)S(1)}, bf16[128,768]{1,0:T(8,128)(2,1)}, u32[]{:S(2)}, u32[]{:S(2)}) collective-permute-start(bf16[128,768]{1,0:T(8,128)(2,1)S(1)} %get-tuple-element.136), channel_id=1, source_target_pairs={{0,3},{1,0},{2,1},{3,2},{4,7},{5,4},{6,5},{7,6},{8,11},{9,8},{10,9... | collective-permute-start | bytes 589832 | tf_op jit(solution)/shard_map/ppermute | solution.py:45
  108.2 25.7 %copy-start.58 = (f32[512,768]{1,0:T(8,128)S(1)}, f32[512,768]{1,0:T(8,128)}, u32[]{:S(2)}) copy-start(f32[512,768]{1,0:T(8,128)} %get-tuple-element.182) | copy-start | bytes 4718596
  110.5 23.4 %copy-start.8 = (bf16[768,768]{1,0:T(8,128)(2,1)S(1)}, bf16[768,768]{1,0:T(8,128)(2,1)}, u32[]{:S(2)}) copy-start(bf16[768,768]{1,0:T(8,128)(2,1)} %copy-done.7) | copy-start | bytes 3538948
  110.5 23.4 %copy-start.57 = (f32[512,768]{1,0:T(8,128)S(1)}, f32[512,768]{1,0:T(8,128)}, u32[]{:S(2)}) copy-start(f32[512,768]{1,0:T(8,128)} %get-tuple-element.116) | copy-start | bytes 4718596
  110.9 11.6 %collective-permute-start.21 = (bf16[128,768]{1,0:T(8,128)(2,1)S(1)}, bf16[128,768]{1,0:T(8,128)(2,1)S(1)}, u32[]{:S(2)}, u32[]{:S(2)}) collective-permute-start(bf16[128,768]{1,0:T(8,128)(2,1)S(1)} %maximum_select_fusion.6), channel_id=1, source_target_pairs={{0,3},{1,0},{2,1},{3,2},{4,7},{5,4},{6,5},{7,6},{8,11},{9,8},{10,9... | collective-permute-start | bytes 589832 | tf_op jit(solution)/shard_map/ppermute | solution.py:45
  117.2 16.7 %collective-permute-start.20 = (bf16[128,768]{1,0:T(8,128)(2,1)S(1)}, bf16[128,768]{1,0:T(8,128)(2,1)S(1)}, u32[]{:S(2)}, u32[]{:S(2)}) collective-permute-start(bf16[128,768]{1,0:T(8,128)(2,1)S(1)} %maximum_select_fusion.6), channel_id=1, source_target_pairs={{0,2},{1,3},{2,0},{3,1},{4,6},{5,7},{6,4},{7,5},{8,10},{9,11},{10,... | collective-permute-start | bytes 589832 | tf_op jit(solution)/shard_map/ppermute | solution.py:45
  117.2 16.7 %collective-permute-start.19 = (bf16[128,768]{1,0:T(8,128)(2,1)S(1)}, bf16[128,768]{1,0:T(8,128)(2,1)S(1)}, u32[]{:S(2)}, u32[]{:S(2)}) collective-permute-start(bf16[128,768]{1,0:T(8,128)(2,1)S(1)} %maximum_select_fusion.6), channel_id=1, source_target_pairs={{0,1},{1,2},{2,3},{3,0},{4,5},{5,6},{6,7},{7,4},{8,9},{9,10},{10,1... | collective-permute-start | bytes 589832 | tf_op jit(solution)/shard_map/ppermute | solution.py:45
  136.1 9.8 %collective-permute-start.24 = (bf16[128,768]{1,0:T(8,128)(2,1)S(1)}, bf16[128,768]{1,0:T(8,128)(2,1)S(1)}, u32[]{:S(2)}, u32[]{:S(2)}) collective-permute-start(bf16[128,768]{1,0:T(8,128)(2,1)S(1)} %get-tuple-element.134), channel_id=1, source_target_pairs={{0,1},{1,2},{2,3},{3,0},{4,5},{5,6},{6,7},{7,4},{8,9},{9,10},{10,1... | collective-permute-start | bytes 589832 | tf_op jit(solution)/shard_map/ppermute | solution.py:45
  136.2 16.0 %collective-permute-start.23 = (bf16[128,768]{1,0:T(8,128)(2,1)S(1)}, bf16[128,768]{1,0:T(8,128)(2,1)S(1)}, u32[]{:S(2)}, u32[]{:S(2)}) collective-permute-start(bf16[128,768]{1,0:T(8,128)(2,1)S(1)} %get-tuple-element.135), channel_id=1, source_target_pairs={{0,2},{1,3},{2,0},{3,1},{4,6},{5,7},{6,4},{7,5},{8,10},{9,11},{10,... | collective-permute-start | bytes 589832 | tf_op jit(solution)/shard_map/ppermute | solution.py:45
  138.2 14.0 %collective-permute-start.22 = (bf16[128,768]{1,0:T(8,128)(2,1)S(1)}, bf16[128,768]{1,0:T(8,128)(2,1)S(1)}, u32[]{:S(2)}, u32[]{:S(2)}) collective-permute-start(bf16[128,768]{1,0:T(8,128)(2,1)S(1)} %get-tuple-element.133), channel_id=1, source_target_pairs={{0,3},{1,0},{2,1},{3,2},{4,7},{5,4},{6,5},{7,6},{8,11},{9,8},{10,9... | collective-permute-start | bytes 589832 | tf_op jit(solution)/shard_map/ppermute | solution.py:45
  142.9 24.4 %collective-permute-start.28 = (bf16[768,384]{1,0:T(8,128)(2,1)}, bf16[768,384]{1,0:T(8,128)(2,1)}, u32[]{:S(2)}, u32[]{:S(2)}) collective-permute-start(bf16[768,384]{1,0:T(8,128)(2,1)} %split.97), channel_id=1, source_target_pairs={{0,16},{16,0},{1,17},{17,1},{2,18},{18,2},{3,19},{19,3},{4,20},{20... | collective-permute-start | bytes 1769480 | tf_op jit(solution)/shard_map/ppermute | solution.py:50
  144.4 25.6 %collective-permute-start.29 = (bf16[384,768]{1,0:T(8,128)(2,1)S(1)}, bf16[384,768]{1,0:T(8,128)(2,1)}, u32[]{:S(2)}, u32[]{:S(2)}) collective-permute-start(bf16[384,768]{1,0:T(8,128)(2,1)S(1)} %split.96), channel_id=1, source_target_pairs={{0,16},{16,0},{1,17},{17,1},{2,18},{18,2},{3,19},{19,3},{4,20},{20... | collective-permute-start | bytes 1769480 | tf_op jit(solution)/shard_map/ppermute | solution.py:50
  153.5 12.4 %collective-permute-start.27 = (bf16[128,192]{1,0:T(8,128)(2,1)S(1)}, bf16[128,192]{1,0:T(8,128)(2,1)S(1)}, u32[]{:S(2)}, u32[]{:S(2)}) collective-permute-start(bf16[128,192]{1,0:T(8,128)(2,1)S(1)} %get-tuple-element.171), channel_id=1, source_target_pairs={{0,3},{1,0},{2,1},{3,2},{4,7},{5,4},{6,5},{7,6},{8,11},{9,8},{10,9... | collective-permute-start | bytes 147464 | tf_op jit(solution)/shard_map/ppermute | solution.py:45
  159.1 7.4 %collective-permute-start.26 = (bf16[128,192]{1,0:T(8,128)(2,1)S(1)}, bf16[128,192]{1,0:T(8,128)(2,1)S(1)}, u32[]{:S(2)}, u32[]{:S(2)}) collective-permute-start(bf16[128,192]{1,0:T(8,128)(2,1)S(1)} %get-tuple-element.172), channel_id=1, source_target_pairs={{0,2},{1,3},{2,0},{3,1},{4,6},{5,7},{6,4},{7,5},{8,10},{9,11},{10,... | collective-permute-start | bytes 147464 | tf_op jit(solution)/shard_map/ppermute | solution.py:45
  159.1 7.4 %collective-permute-start.25 = (bf16[128,192]{1,0:T(8,128)(2,1)S(1)}, bf16[128,192]{1,0:T(8,128)(2,1)S(1)}, u32[]{:S(2)}, u32[]{:S(2)}) collective-permute-start(bf16[128,192]{1,0:T(8,128)(2,1)S(1)} %get-tuple-element.173), channel_id=1, source_target_pairs={{0,1},{1,2},{2,3},{3,0},{4,5},{5,6},{6,7},{7,4},{8,9},{9,10},{10,1... | collective-permute-start | bytes 147464 | tf_op jit(solution)/shard_map/ppermute | solution.py:45
  165.9 17.4 %collective-permute-start.30 = (f32[12,768]{1,0:T(8,128)}, f32[12,768]{1,0:T(8,128)S(1)}, u32[]{:S(2)}, u32[]{:S(2)}) collective-permute-start(f32[12,768]{1,0:T(8,128)} %pack.1), channel_id=1, source_target_pairs={{0,16},{16,0},{1,17},{17,1},{2,18},{18,2},{3,19},{19,3},{4,20},{20... | collective-permute-start | bytes 110600 | tf_op jit(solution)/shard_map/ppermute | solution.py:50
  183.4 2.6 collective-permute-start.31
  185.0 36.7 %collective-permute-start.33 = (bf16[384,768]{1,0:T(8,128)(2,1)S(1)}, bf16[384,768]{1,0:T(8,128)(2,1)}, u32[]{:S(2)}, u32[]{:S(2)}) collective-permute-start(bf16[384,768]{1,0:T(8,128)(2,1)S(1)} %fusion.12), channel_id=1, source_target_pairs={{0,4},{4,0},{8,12},{12,8},{1,5},{5,1},{9,13},{13,9},{2,6},{6,2},{1... | collective-permute-start | bytes 1769480 | tf_op jit(solution)/shard_map/ppermute | solution.py:50
  186.2 12.2 %collective-permute-start.32 = (bf16[1,384,512]{2,1,0:T(8,128)(2,1)S(1)}, bf16[1,384,512]{2,1,0:T(8,128)(2,1)}, u32[]{:S(2)}, u32[]{:S(2)}) collective-permute-start(bf16[1,384,512]{2,1,0:T(8,128)(2,1)S(1)} %slice.305), channel_id=1, source_target_pairs={{0,8},{4,12},{8,0},{12,4},{1,9},{5,13},{9,1},{13,5},{2,10},{6,14},... | collective-permute-start | bytes 1179656 | tf_op jit(solution)/shard_map/ppermute | solution.py:50
  189.8 31.9 %collective-permute-start.34 = (bf16[768,384]{1,0:T(8,128)(2,1)}, bf16[768,384]{1,0:T(8,128)(2,1)}, u32[]{:S(2)}, u32[]{:S(2)}) collective-permute-start(bf16[768,384]{1,0:T(8,128)(2,1)} %fusion.11), channel_id=1, source_target_pairs={{0,8},{4,12},{8,0},{12,4},{1,9},{5,13},{9,1},{13,5},{2,10},{6,14},... | collective-permute-start | bytes 1769480 | tf_op jit(solution)/shard_map/ppermute | solution.py:50
  191.1 1.3 collective-permute-start.35
  191.2 14.0 %collective-permute-start.36 = (bf16[128,1536]{1,0:T(8,128)(2,1)S(1)}, bf16[128,1536]{1,0:T(8,128)(2,1)S(1)}, u32[]{:S(2)}, u32[]{:S(2)}) collective-permute-start(bf16[128,1536]{1,0:T(8,128)(2,1)S(1)} %pad_maximum_fusion.7), channel_id=1, source_target_pairs={{0,1},{1,2},{2,3},{3,0},{4,5},{5,6},{6,7},{7,4},{8,9},{9,10},{10,1... | collective-permute-start | bytes 1179656 | tf_op jit(solution)/shard_map/ppermute | solution.py:45
  192.4 29.3 %collective-permute-start.37 = (bf16[128,1536]{1,0:T(8,128)(2,1)S(1)}, bf16[128,1536]{1,0:T(8,128)(2,1)}, u32[]{:S(2)}, u32[]{:S(2)}) collective-permute-start(bf16[128,1536]{1,0:T(8,128)(2,1)S(1)} %pad_maximum_fusion.7), channel_id=1, source_target_pairs={{0,2},{1,3},{2,0},{3,1},{4,6},{5,7},{6,4},{7,5},{8,10},{9,11},{10,... | collective-permute-start | bytes 1179656 | tf_op jit(solution)/shard_map/ppermute | solution.py:45
  198.4 23.3 %collective-permute-start.38 = (bf16[128,1536]{1,0:T(8,128)(2,1)S(1)}, bf16[128,1536]{1,0:T(8,128)(2,1)}, u32[]{:S(2)}, u32[]{:S(2)}) collective-permute-start(bf16[128,1536]{1,0:T(8,128)(2,1)S(1)} %pad_maximum_fusion.7), channel_id=1, source_target_pairs={{0,3},{1,0},{2,1},{3,2},{4,7},{5,4},{6,5},{7,6},{8,11},{9,8},{10,9... | collective-permute-start | bytes 1179656 | tf_op jit(solution)/shard_map/ppermute | solution.py:45
  227.2 26.1 %collective-permute-start.41 = (bf16[128,768]{1,0:T(8,128)(2,1)S(1)}, bf16[128,768]{1,0:T(8,128)(2,1)S(1)}, u32[]{:S(2)}, u32[]{:S(2)}) collective-permute-start(bf16[128,768]{1,0:T(8,128)(2,1)S(1)} %get-tuple-element.131), channel_id=1, source_target_pairs={{0,1},{1,2},{2,3},{3,0},{4,5},{5,6},{6,7},{7,4},{8,9},{9,10},{10,1... | collective-permute-start | bytes 589832 | tf_op jit(solution)/shard_map/ppermute | solution.py:45
  236.0 17.3 %collective-permute-start.40 = (bf16[128,768]{1,0:T(8,128)(2,1)S(1)}, bf16[128,768]{1,0:T(8,128)(2,1)S(1)}, u32[]{:S(2)}, u32[]{:S(2)}) collective-permute-start(bf16[128,768]{1,0:T(8,128)(2,1)S(1)} %get-tuple-element.132), channel_id=1, source_target_pairs={{0,2},{1,3},{2,0},{3,1},{4,6},{5,7},{6,4},{7,5},{8,10},{9,11},{10,... | collective-permute-start | bytes 589832 | tf_op jit(solution)/shard_map/ppermute | solution.py:45
  236.0 17.9 %collective-permute-start.39 = (bf16[128,768]{1,0:T(8,128)(2,1)S(1)}, bf16[128,768]{1,0:T(8,128)(2,1)S(1)}, u32[]{:S(2)}, u32[]{:S(2)}) collective-permute-start(bf16[128,768]{1,0:T(8,128)(2,1)S(1)} %get-tuple-element.130), channel_id=1, source_target_pairs={{0,3},{1,0},{2,1},{3,2},{4,7},{5,4},{6,5},{7,6},{8,11},{9,8},{10,9... | collective-permute-start | bytes 589832 | tf_op jit(solution)/shard_map/ppermute | solution.py:45
  238.5 15.7 %collective-permute-start.42 = (f32[12,768]{1,0:T(8,128)S(1)}, f32[12,768]{1,0:T(8,128)S(1)}, u32[]{:S(2)}, u32[]{:S(2)}) collective-permute-start(f32[12,768]{1,0:T(8,128)S(1)} %add.311), channel_id=1, source_target_pairs={{0,8},{4,12},{8,0},{12,4},{1,9},{5,13},{9,1},{13,5},{2,10},{6,14},... | collective-permute-start | bytes 110600 | tf_op jit(solution)/shard_map/ppermute | solution.py:50
  242.9 3.7 %collective-permute-start.57 = (f32[384]{0:T(512)S(1)}, f32[384]{0:T(512)S(1)}, u32[]{:S(2)}, u32[]{:S(2)}) collective-permute-start(f32[384]{0:T(512)S(1)} %pad_maximum_fusion.17), channel_id=1, source_target_pairs={{0,8},{4,12},{8,0},{12,4},{1,9},{5,13},{9,1},{13,5},{2,10},{6,14},... | collective-permute-start | bytes 4616 | tf_op jit(solution)/shard_map/ppermute | solution.py:50
  246.7 1.2 collective-permute-start.58
  247.8 3.6 %collective-permute-start.59 = (f32[384]{0:T(512)S(1)}, f32[384]{0:T(512)S(1)}, u32[]{:S(2)}, u32[]{:S(2)}) collective-permute-start(f32[384]{0:T(512)S(1)} %add.327), channel_id=1, source_target_pairs={{0,16},{16,0},{1,17},{17,1},{2,18},{18,2},{3,19},{19,3},{4,20},{20... | collective-permute-start | bytes 4616 | tf_op jit(solution)/shard_map/ppermute | solution.py:50
  251.4 23.2 %collective-permute-start.44 = (bf16[384,768]{1,0:T(8,128)(2,1)}, bf16[384,768]{1,0:T(8,128)(2,1)}, u32[]{:S(2)}, u32[]{:S(2)}) collective-permute-start(bf16[384,768]{1,0:T(8,128)(2,1)} %add_convert_fusion.1), channel_id=1, source_target_pairs={{0,8},{4,12},{8,0},{12,4},{1,9},{5,13},{9,1},{13,5},{2,10},{6,14},... | collective-permute-start | bytes 1769480 | tf_op jit(solution)/shard_map/ppermute | solution.py:50
  253.3 32.4 %collective-permute-start.45 = (bf16[768,384]{1,0:T(8,128)(2,1)S(1)}, bf16[768,384]{1,0:T(8,128)(2,1)S(1)}, u32[]{:S(2)}, u32[]{:S(2)}) collective-permute-start(bf16[768,384]{1,0:T(8,128)(2,1)S(1)} %add_convert_fusion), channel_id=1, source_target_pairs={{0,4},{4,0},{8,12},{12,8},{1,5},{5,1},{9,13},{13,9},{2,6},{6,2},{1... | collective-permute-start | bytes 1769480 | tf_op jit(solution)/shard_map/ppermute | solution.py:50
  253.3 6.3 %collective-permute-start.54 = (bf16[192,384]{1,0:T(8,128)(2,1)S(1)}, bf16[192,384]{1,0:T(8,128)(2,1)S(1)}, u32[]{:S(2)}, u32[]{:S(2)}) collective-permute-start(bf16[192,384]{1,0:T(8,128)(2,1)S(1)} %split.99), channel_id=1, source_target_pairs={{0,16},{16,0},{1,17},{17,1},{2,18},{18,2},{3,19},{19,3},{4,20},{20... | collective-permute-start | bytes 442376 | tf_op jit(solution)/shard_map/ppermute | solution.py:50
  254.1 6.9 %collective-permute-start.47 = (f32[12,768]{1,0:T(8,128)S(1)}, f32[12,768]{1,0:T(8,128)S(1)}, u32[]{:S(2)}, u32[]{:S(2)}) collective-permute-start(f32[12,768]{1,0:T(8,128)S(1)} %add.316), channel_id=1, source_target_pairs={{0,2},{1,3},{2,0},{3,1},{4,6},{5,7},{6,4},{7,5},{8,10},{9,11},{10,... | collective-permute-start | bytes 110600 | tf_op jit(solution)/shard_map/ppermute | solution.py:50
  254.7 7.8 %collective-permute-start.48 = (f32[12,768]{1,0:T(8,128)S(1)}, f32[12,768]{1,0:T(8,128)S(1)}, u32[]{:S(2)}, u32[]{:S(2)}) collective-permute-start(f32[12,768]{1,0:T(8,128)S(1)} %add.316), channel_id=1, source_target_pairs={{0,3},{1,2},{2,1},{3,0},{4,7},{5,6},{6,5},{7,4},{8,11},{9,10},{10,... | collective-permute-start | bytes 110600 | tf_op jit(solution)/shard_map/ppermute | solution.py:50
  259.5 4.1 %collective-permute-start.46 = (f32[12,768]{1,0:T(8,128)S(1)}, f32[12,768]{1,0:T(8,128)S(1)}, u32[]{:S(2)}, u32[]{:S(2)}) collective-permute-start(f32[12,768]{1,0:T(8,128)S(1)} %add.316), channel_id=1, source_target_pairs={{0,1},{1,0},{2,3},{3,2},{4,5},{5,4},{6,7},{7,6},{8,9},{9,8},{10,11... | collective-permute-start | bytes 110600 | tf_op jit(solution)/shard_map/ppermute | solution.py:50
  261.0 10.7 %collective-permute-start.51 = (bf16[576,384]{1,0:T(8,128)(2,1)}, bf16[576,384]{1,0:T(8,128)(2,1)}, u32[]{:S(2)}, u32[]{:S(2)}) collective-permute-start(bf16[576,384]{1,0:T(8,128)(2,1)} %split.98), channel_id=1, source_target_pairs={{0,16},{16,0},{1,17},{17,1},{2,18},{18,2},{3,19},{19,3},{4,20},{20... | collective-permute-start | bytes 1327112 | tf_op jit(solution)/shard_map/ppermute | solution.py:50
  262.5 6.6 %collective-permute-start.55 = (bf16[192,384]{1,0:T(8,128)(2,1)S(1)}, bf16[192,384]{1,0:T(8,128)(2,1)S(1)}, u32[]{:S(2)}, u32[]{:S(2)}) collective-permute-start(bf16[192,384]{1,0:T(8,128)(2,1)S(1)} %fusion.51), channel_id=1, source_target_pairs={{0,8},{4,12},{8,0},{12,4},{1,9},{5,13},{9,1},{13,5},{2,10},{6,14},... | collective-permute-start | bytes 442376 | tf_op jit(solution)/shard_map/ppermute | solution.py:50
  263.6 23.2 %collective-permute-start.43 = (bf16[128,768]{1,0:T(8,128)(2,1)S(1)}, bf16[128,768]{1,0:T(8,128)(2,1)}, u32[]{:S(2)}, u32[]{:S(2)}) collective-permute-start(bf16[128,768]{1,0:T(8,128)(2,1)S(1)} %fusion.44), channel_id=1, source_target_pairs={{0,3},{1,0},{2,1},{3,2},{4,7},{5,4},{6,5},{7,6},{8,11},{9,8},{10,9... | collective-permute-start | bytes 589832 | tf_op jit(solution)/shard_map/ppermute | solution.py:45
  269.7 17.1 %collective-permute-start.50 = (bf16[128,768]{1,0:T(8,128)(2,1)S(1)}, bf16[128,768]{1,0:T(8,128)(2,1)S(1)}, u32[]{:S(2)}, u32[]{:S(2)}) collective-permute-start(bf16[128,768]{1,0:T(8,128)(2,1)S(1)} %fusion.44), channel_id=1, source_target_pairs={{0,2},{1,3},{2,0},{3,1},{4,6},{5,7},{6,4},{7,5},{8,10},{9,11},{10,... | collective-permute-start | bytes 589832 | tf_op jit(solution)/shard_map/ppermute | solution.py:45
  271.7 1.4 collective-permute-start.56
  273.1 12.4 %collective-permute-start.52 = (bf16[576,384]{1,0:T(8,128)(2,1)S(1)}, bf16[576,384]{1,0:T(8,128)(2,1)S(1)}, u32[]{:S(2)}, u32[]{:S(2)}) collective-permute-start(bf16[576,384]{1,0:T(8,128)(2,1)S(1)} %fusion.13), channel_id=1, source_target_pairs={{0,8},{4,12},{8,0},{12,4},{1,9},{5,13},{9,1},{13,5},{2,10},{6,14},... | collective-permute-start | bytes 1327112 | tf_op jit(solution)/shard_map/ppermute | solution.py:50
  274.7 12.1 %collective-permute-start.49 = (bf16[128,768]{1,0:T(8,128)(2,1)S(1)}, bf16[128,768]{1,0:T(8,128)(2,1)S(1)}, u32[]{:S(2)}, u32[]{:S(2)}) collective-permute-start(bf16[128,768]{1,0:T(8,128)(2,1)S(1)} %fusion.44), channel_id=1, source_target_pairs={{0,1},{1,2},{2,3},{3,0},{4,5},{5,6},{6,7},{7,4},{8,9},{9,10},{10,1... | collective-permute-start | bytes 589832 | tf_op jit(solution)/shard_map/ppermute | solution.py:45
  285.6 3.5 %collective-permute-start.53 = (bf16[576,384]{1,0:T(8,128)(2,1)S(1)}, bf16[576,384]{1,0:T(8,128)(2,1)S(1)}, u32[]{:S(2)}, u32[]{:S(2)}) collective-permute-start(bf16[576,384]{1,0:T(8,128)(2,1)S(1)} %add_convert_fusion.2), channel_id=1, source_target_pairs={{0,4},{4,0},{8,12},{12,8},{1,5},{5,1},{9,13},{13,9},{2,6},{6,2},{1... | collective-permute-start | bytes 1327112 | tf_op jit(solution)/shard_map/ppermute | solution.py:50
  (55 other events, 352.2 us)
